TPU v7x, 128 devices: a whole 4x4x4 slice. The times are simulated.
128 devices in a mesh: shard: 32 (over y, z, core), rep: 4 (over x).
Axes of the slice: x: 4, y: 4, z: 4, core: 2. Of those that a mesh axis runs over, the one named last changes fastest.
Arguments:
- feats: bfloat16 [32768, 768], P('shard'), may hold values from -6 to 6
- bases: bfloat16 [4, 768, 1024], P(None, None, 'rep'), may hold values from -0.21875 to 0.21875
- coef: bfloat16 [5, 4], replicated, may hold values from -2 to 2
- root_weight: bfloat16 [768, 1024], P(None, 'rep'), may hold values from -0.21875 to 0.21875
- slot_block: int32 [32, 32, 2], P('shard'), may hold values from 0 to 7
- recv_rel: int32 [32, 32, 2], P('shard'), may hold values from 0 to 4
- tile_slot: int32 [32, 256], P('shard'), may hold values from 0 to 63, as said below
- tile_dst: int32 [32, 256], P('shard'), may hold values from 0 to 7
- tile_adj: bfloat16 [32, 256, 128, 128], P('shard'), may hold values from 0 to 0.049804688
- d_out: bfloat16 [32768, 1024], P('shard', 'rep'), may hold values from -6 to 6
Outputs:
- output: bfloat16 [32768, 1024], P('shard', 'rep')
- grad_feats: bfloat16 [32768, 768], P(('shard', 'rep'))
- grad_bases: float32 [4, 768, 1024], P(None, 'shard', 'rep')
- grad_root: float32 [768, 1024], P('shard', 'rep')
- grad_coef: float32 [5, 4], replicated
Inputs may be any that keep to these rules, and one draw needn't show every extreme that they name: `tile_slot`: in each row (one destination device) every one of the 64 slots is named by at least one tile.
All inputs are finite; a program needn't handle non-finite values.
Results may differ from a plain program's by a relative error of at most 0.0062.
Values may be sent and summed in bfloat16 or wider, within the bound.
No kernel may reach another device: no remote copies, remote signals or barrier semaphores. Data moves between devices by JAX's collectives and lax.ppermute only.
A program may use at most 192 MiB of HBM per device.

v0:
```python
import jax
import jax.numpy as jnp
from jax import lax
from jax.sharding import PartitionSpec as P

BLK = 128


highest = lax.Precision.HIGHEST


def project_slots(source, weights):
    return jnp.einsum("snc,sco->sno", source, weights, preferred_element_type=jnp.float32).astype(
        jnp.bfloat16
    )


def body(
    feats, bases, coef, root_weight, slot_block, recv_rel, tile_slot, tile_dst, tile_adj, d_out
):
    shards = lax.axis_size("shard")
    nblocks = feats.shape[0] // BLK
    width_in = feats.shape[1]
    width_out = root_weight.shape[1]
    relations = coef.shape[0]
    capacity = slot_block.shape[2]
    slot_count = shards * capacity
    rel_weights = (
        jnp.dot(coef, bases.reshape(bases.shape[0], -1), preferred_element_type=jnp.float32)
        .astype(jnp.bfloat16)
        .reshape(relations, width_in, width_out)
    )
    feat_blocks = feats.reshape(nblocks, BLK, width_in)
    send_block = slot_block[0]
    local_rel = recv_rel[0]
    owner_rel = lax.all_to_all(local_rel, "shard", split_axis=0, concat_axis=0, tiled=True)
    tile_ids = tile_slot[0]
    dest_ids = tile_dst[0]
    adjacency = tile_adj[0]
    root_term = jnp.dot(feats, root_weight, preferred_element_type=jnp.float32)
    slot_weights = rel_weights[local_rel.reshape(-1)]
    outgoing = feat_blocks[send_block]
    incoming = lax.all_to_all(outgoing, "shard", split_axis=0, concat_axis=0, tiled=True)
    slot_msgs = project_slots(incoming.reshape(slot_count, BLK, width_in), slot_weights)
    tile_msgs = slot_msgs[tile_ids]
    weighted = jnp.einsum("tij,tjo->tio", adjacency, tile_msgs, preferred_element_type=jnp.float32)
    dst_onehot = (dest_ids[:, None] == jnp.arange(nblocks)[None, :]).astype(jnp.float32)
    neighbor_sum = jnp.einsum("tb,tio->bio", dst_onehot, weighted, precision=highest).reshape(
        -1, width_out
    )
    output = (neighbor_sum + root_term).astype(jnp.bfloat16)
    grad_rows = d_out.reshape(nblocks, BLK, width_out)[dest_ids]
    tile_grads = jnp.einsum(
        "tji,tjo->tio", adjacency, grad_rows, preferred_element_type=jnp.float32
    )
    slot_onehot = (tile_ids[:, None] == jnp.arange(slot_count)[None, :]).astype(jnp.float32)
    slot_grads = jnp.einsum("ts,tio->sio", slot_onehot, tile_grads, precision=highest).astype(
        jnp.bfloat16
    )
    slot_grads = slot_grads.reshape(shards, capacity, BLK, width_out)
    returned = lax.all_to_all(slot_grads, "shard", split_axis=0, concat_axis=0, tiled=True)
    owner_key = (owner_rel * nblocks + send_block).reshape(-1)
    owner_onehot = (owner_key[:, None] == jnp.arange(relations * nblocks)[None, :]).astype(
        jnp.bfloat16
    )
    source_grads = jnp.einsum(
        "sk,sio->kio",
        owner_onehot,
        returned.reshape(slot_count, BLK, width_out),
        preferred_element_type=jnp.float32,
    )
    source_grads = source_grads.astype(jnp.bfloat16).reshape(relations, nblocks * BLK, width_out)
    through_rel = jnp.einsum(
        "rno,rco->nc", source_grads, rel_weights, preferred_element_type=jnp.float32
    )
    feature_sum = lax.psum_scatter(
        through_rel + jnp.dot(d_out, root_weight.T, preferred_element_type=jnp.float32),
        "rep",
        scatter_dimension=0,
        tiled=True,
    )
    grad_feats = feature_sum.astype(jnp.bfloat16)
    relation_grads = jnp.einsum(
        "nc,rno->cro", feats, source_grads, preferred_element_type=jnp.float32
    )
    root_grad = jnp.dot(feats.T, d_out, preferred_element_type=jnp.float32)
    stacked = jnp.concatenate([relation_grads, root_grad[:, None, :]], axis=1)
    reduced = lax.psum_scatter(stacked, "shard", scatter_dimension=0, tiled=True)
    grad_bases = jnp.einsum(
        "rb,iro->bio", coef.astype(jnp.float32), reduced[:, :relations], precision=highest
    )
    grad_root = reduced[:, relations]
    row_count = reduced.shape[0]
    base_rows = lax.dynamic_slice_in_dim(bases, lax.axis_index("shard") * row_count, row_count, 1)
    partial_coef = jnp.einsum(
        "iro,bio->rb", reduced[:, :relations], base_rows.astype(jnp.float32), precision=highest
    )
    grad_coef = lax.psum(partial_coef, ("shard", "rep"))
    return (output, grad_feats, grad_bases, grad_root, grad_coef)


def solution(mesh):
    placed = (
        P("shard", None),
        P(None, None, "rep"),
        P(),
        P(None, "rep"),
        P("shard", None, None),
        P("shard", None, None),
        P("shard", None),
        P("shard", None),
        P("shard", None, None, None),
        P("shard", "rep"),
    )
    return jax.shard_map(
        body,
        mesh=mesh,
        in_specs=placed,
        out_specs=(
            P("shard", "rep"),
            P(("shard", "rep"), None),
            P(None, "shard", "rep"),
            P("shard", "rep"),
            P(),
        ),
        check_vma=False,
    )
```

profile of v0, /device:TPU:0, one launch (start us, length us, event | category | flops | bytes accessed | tf_op | source)
XLA Modules:
  0.0 622.9 jit_solution(11586295730918086103)
XLA Ops:
  7.2 0.0 copy-start
  7.2 1.5 copy.60
  8.7 8.4 %all-to-all-start.1 = ((s32[32,1,2]{2,1,0:T(1,128)}), s32[32,1,2]{2,1,0:T(1,128)S(1)}, u32[]{:S(2)}, u32[]{:S(2)}) async-start(s32[32,1,2]{2,1,0:T(1,128)} %copy.60), calls=%async_computation.1 | async-start | bytes 32768 | tf_op jit(solution)/shard_map/all_to_all | solution.py:36
  17.1 0.7 compare_select_fusion
  17.8 10.8 %gather_fusion.3 = bf16[256,128,256]{2,1,0:T(8,128)(2,1)} fusion(bf16[8,128,256]{2,1,0:T(8,128)(2,1)} %bitcast.87, s32[1024]{0:T(1024)S(1)} %pad_clamp_fusion), kind=kCustom, calls=%fused_computation.3 | custom fusion | bytes 33555456 | tf_op jit(solution)/shard_map/gather | solution.py:52
  28.6 20.1 %convolution_bitcast_fusion = f32[256,128,256]{1,2,0:T(8,128)} fusion(bf16[256,128,256]{2,1,0:T(8,128)(2,1)} %gather_fusion.3, bf16[1,256,128,128]{3,2,1,0:T(8,128)(2,1)} %param.18), kind=kOutput, calls=%fused_computation.5 | convolution fusion | flops 2147483648 | bytes 58720256 | tf_op jit(solution)/shard_map/tji,tjo->tio/dot_general | solution.py:53
  48.7 33.4 %copy.63 = f32[256,128,256]{2,0,1:T(8,128)} copy(f32[256,128,256]{1,2,0:T(8,128)} %convolution_bitcast_fusion) | data formatting | bytes 67108864 | tf_op jit(solution)/shard_map/tji,tjo->tio/dot_general | solution.py:53
  82.1 0.0 copy-done.9
  82.1 19.2 %convolution_convert_fusion.1 = bf16[64,128,256]{2,0,1:T(8,128)(2,1)} fusion(f32[256,128,256]{2,0,1:T(8,128)} %copy.63, s32[256]{0:T(256)S(1)} %bitcast.99), kind=kOutput, calls=%fused_computation.11 | convolution fusion | flops 6444564480 | bytes 37749760 | tf_op jit(solution)/shard_map/ts,tio->sio/dot_general | solution.py:57
  101.3 7.2 %reshape.172 = bf16[32,2,128,256]{3,1,0,2:T(2,128)(2,1)} reshape(bf16[64,128,256]{2,0,1:T(8,128)(2,1)} %convolution_convert_fusion.1) | data formatting | bytes 8388608 | tf_op jit(solution)/shard_map/reshape | solution.py:60
  108.5 8.5 %copy.64 = bf16[32,2,128,256]{3,1,2,0:T(2,128)(2,1)} copy(bf16[32,2,128,256]{3,1,0,2:T(2,128)(2,1)} %reshape.172) | data formatting | bytes 8388608 | tf_op jit(solution)/shard_map/reshape | solution.py:60
  117.0 0.0 all-to-all-done.1
  117.0 7.6 %all-to-all-start.2 = ((bf16[32,2,128,256]{3,1,2,0:T(2,128)(2,1)}), bf16[32,2,128,256]{3,1,2,0:T(2,128)(2,1)}, u32[]{:S(2)}, u32[]{:S(2)}) async-start(bf16[32,2,128,256]{3,1,2,0:T(2,128)(2,1)} %copy.64), calls=%async_computation.2 | async-start | bytes 8388608 | tf_op jit(solution)/shard_map/all_to_all | solution.py:61
  124.7 11.4 %reduce-scatter.5.cloned.1.call-start = ((), (), s32[]{:S(2)}) async-start(), calls=%async_computation.6 | async-start | bytes 6488064 | tf_op jit(solution)/shard_map/reduce_scatter | solution.py:88
  136.1 0.1 copy.61
  136.2 0.1 squeeze.21
  136.3 0.6 convolution_bitcast_fusion.3
  137.0 0.1 mul.14
  137.1 40.3 %all-to-all-done.2 = bf16[32,2,128,256]{3,1,2,0:T(2,128)(2,1)} async-done(((bf16[32,2,128,256]{3,1,2,0:T(2,128)(2,1)}), bf16[32,2,128,256]{3,1,2,0:T(2,128)(2,1)}, u32[]{:S(2)}, u32[]{:S(2)}) %all-to-all-start.2) | async-done | bytes 4194336 | tf_op jit(solution)/shard_map/all_to_all | solution.py:61
  177.4 8.9 %copy.65 = bf16[32,2,128,256]{3,1,0,2:T(2,128)(2,1)} copy(bf16[32,2,128,256]{3,1,2,0:T(2,128)(2,1)} %all-to-all-done.2) | data formatting | bytes 8388608 | tf_op jit(solution)/shard_map/all_to_all | solution.py:61
  186.3 7.2 %reshape.173 = bf16[64,128,256]{2,0,1:T(8,128)(2,1)} reshape(bf16[32,2,128,256]{3,1,0,2:T(2,128)(2,1)} %copy.65) | data formatting | bytes 8388608 | tf_op jit(solution)/shard_map/reshape | solution.py:69
  193.5 3.0 convolution_convert_fusion.3
  196.6 0.6 copy.66
  197.2 2.3 convolution_bitcast_fusion.2
  199.5 2.6 pad_maximum_fusion
  202.1 6.3 %copy.69 = f32[768,6,256]{2,1,0:T(8,128)} copy(f32[768,6,256]{0,2,1:T(8,128)} %pad_maximum_fusion) | data formatting | bytes 9437184 | tf_op jit(solution)/shard_map/concatenate | solution.py:87
  208.4 0.0 reduce-scatter.5.cloned.1.call-update
  208.4 0.1 copy.55
  208.5 0.1 reshape.177
  208.6 7.2 %gather_fusion = bf16[64,128,768]{2,1,0:T(8,128)(2,1)} fusion(bf16[8,128,768]{2,1,0:T(8,128)(2,1)S(1)} %bitcast.86, s32[1024]{0:T(1024)S(1)} %pad_clamp_fusion.3), kind=kCustom, calls=%fused_computation | custom fusion | bytes 25166080 | tf_op jit(solution)/shard_map/gather | solution.py:42
  215.8 6.7 %all-to-all-start = ((bf16[32,2,128,768]{3,2,1,0:T(8,128)(2,1)}), bf16[32,2,128,768]{3,2,1,0:T(8,128)(2,1)}, u32[]{:S(2)}, u32[]{:S(2)}) async-start(bf16[32,2,128,768]{3,2,1,0:T(8,128)(2,1)} %bitcast.90), calls=%async_computation | async-start | bytes 25165824 | tf_op jit(solution)/shard_map/all_to_all | solution.py:43
  222.5 0.0 reduce-scatter.3.cloned.1.call-start
  222.5 2.7 copy.78
  225.2 1.3 convolution_convert_fusion
  226.6 0.4 copy.84
  227.0 0.0 copy-done.5
  227.0 0.0 copy-start.6
  227.1 2.2 fusion.19
  229.3 2.3 bitcast_add_fusion
  231.6 0.0 reduce-scatter.3.cloned.1.call-update
  231.6 0.9 copy.56
  232.5 0.6 reshape_squeeze.3
  233.1 0.7 fusion.18
  233.8 0.0 copy-start.10
  233.8 0.0 copy-start.13
  233.8 10.9 %gather_fusion.1 = bf16[64,768,256]{2,1,0:T(8,128)(2,1)} fusion(bf16[5,768,256]{2,1,0:T(8,128)(2,1)S(1)} %bitcast.89, s32[1024]{0:T(1024)S(1)} %pad_clamp_fusion.2), kind=kCustom, calls=%fused_computation.1 | custom fusion | bytes 50331904 | tf_op jit(solution)/shard_map/gather | solution.py:41
  244.8 0.8 constant_dynamic-slice_fusion
  245.6 161.1 %reduce-scatter.5.cloned.1.call-done = f32[24,6,256]{2,1,0:T(8,128)} async-done(((f32[768,6,256]{2,1,0:T(8,128)}), f32[24,6,256]{2,1,0:T(8,128)}) %reduce-scatter.5.cloned.1.call-update) | async-done | bytes 147472 | tf_op jit(solution)/shard_map/reduce_scatter | solution.py:88
  406.7 1.2 convolution_bitcast_fusion.5
  408.0 38.7 %reduce-scatter.3.cloned.1.call-done = f32[256,768]{1,0:T(8,128)} async-done(((f32[1024,768]{1,0:T(8,128)}), f32[256,768]{1,0:T(8,128)}) %reduce-scatter.3.cloned.1.call-update) | async-done | bytes 786448 | tf_op jit(solution)/shard_map/reduce_scatter | solution.py:76
  446.7 1.9 convert_element_type.28
  448.6 64.9 %psum.7 = f32[5,4]{0,1:T(4,128)} all-reduce(f32[5,4]{0,1:T(4,128)S(1)} %convolution_bitcast_fusion.5), channel_id=1, replica_groups=mesh['shard'=32,'rep'=4] {'shard','rep'}, use_global_device_ids=true, to_apply=%region_2.0 | all-reduce | flops 20 | bytes 160 | tf_op jit(solution)/shard_map/psum | solution.py:98
  513.5 1.1 convolution_bitcast_fusion.4
  514.7 0.7 copy.71
  515.3 1.0 slice.18
  516.3 0.6 copy.85
  516.9 0.0 all-to-all-done
  516.9 15.7 %convolution_convert_fusion.2 = bf16[64,128,256]{2,1,0:T(8,128)(2,1)} fusion(bf16[64,128,768]{2,1,0:T(8,128)(2,1)} %bitcast.5, bf16[64,768,256]{2,1,0:T(8,128)(2,1)} %gather_fusion.1), kind=kOutput, calls=%fused_computation.12 | convolution fusion | flops 3223322624 | bytes 41943040 | tf_op jit(solution)/shard_map/snc,sco->sno/dot_general | solution.py:13
  532.6 12.0 %gather_fusion.2 = bf16[256,128,256]{2,1,0:T(8,128)(2,1)} fusion(bf16[64,128,256]{2,1,0:T(8,128)(2,1)} %convolution_convert_fusion.2, s32[1024]{0:T(1024)S(1)} %pad_clamp_fusion.1), kind=kCustom, calls=%fused_computation.2 | custom fusion | bytes 33555456 | tf_op jit(solution)/shard_map/gather | solution.py:45
  544.6 20.1 %convolution_bitcast_fusion.1 = f32[256,128,256]{1,2,0:T(8,128)} fusion(bf16[256,128,256]{2,1,0:T(8,128)(2,1)} %gather_fusion.2, bf16[1,256,128,128]{3,2,1,0:T(8,128)(2,1)} %param.18), kind=kOutput, calls=%fused_computation.6 | convolution fusion | flops 2147483648 | bytes 58720256 | tf_op jit(solution)/shard_map/tij,tjo->tio/dot_general | solution.py:46
  564.8 33.4 %copy.58 = f32[256,128,256]{2,0,1:T(8,128)} copy(f32[256,128,256]{1,2,0:T(8,128)} %convolution_bitcast_fusion.1) | data formatting | bytes 67108864 | tf_op jit(solution)/shard_map/tij,tjo->tio/dot_general | solution.py:46
  598.2 15.8 %fusion.14 = f32[8,128,256]{2,0,1:T(8,128)S(1)} fusion(f32[256,128,256]{2,0,1:T(8,128)} %copy.58, s32[256]{0:T(256)S(1)} %bitcast.98), kind=kOutput, calls=%fused_computation.35 | convolution fusion | flops 805308416 | bytes 34604032 | tf_op jit(solution)/shard_map/tb,tio->bio/dot_general | solution.py:48
  614.0 0.3 copy.59
  614.3 1.4 fusion.3
  (30 shorter events, 0.1 us)
Async XLA Ops:
  7.2 129.2 %copy-start = (bf16[1024,768]{1,0:T(8,128)(2,1)S(1)}, bf16[1024,768]{1,0:T(8,128)(2,1)}, u32[]{:S(2)}) copy-start(bf16[1024,768]{1,0:T(8,128)(2,1)} %param.10) | copy-start | bytes 4718596
  8.7 108.4 %all-to-all-start.1 = ((s32[32,1,2]{2,1,0:T(1,128)}), s32[32,1,2]{2,1,0:T(1,128)S(1)}, u32[]{:S(2)}, u32[]{:S(2)}) async-start(s32[32,1,2]{2,1,0:T(1,128)} %copy.60), calls=%async_computation.1 | async-start | bytes 32768 | tf_op jit(solution)/shard_map/all_to_all | solution.py:36
  48.7 33.4 %copy-start.9 = (s32[1,256]{1,0:T(1,128)S(1)}, s32[1,256]{1,0:T(1,128)}, u32[]{:S(2)}) copy-start(s32[1,256]{1,0:T(1,128)} %param.16) | copy-start | bytes 3076
  117.0 19.1 %copy-start.11 = (s32[1,32,2]{1,2,0:T(2,128)S(1)}, s32[1,32,2]{1,2,0:T(2,128)}, u32[]{:S(2)}) copy-start(s32[1,32,2]{1,2,0:T(2,128)} %param.14) | copy-start | bytes 772
  117.0 19.3 %copy-start.1 = (bf16[1024,256]{1,0:T(8,128)(2,1)S(1)}, bf16[1024,256]{1,0:T(8,128)(2,1)}, u32[]{:S(2)}) copy-start(bf16[1024,256]{1,0:T(8,128)(2,1)} %param.19) | copy-start | bytes 1572868
  117.0 60.4 %all-to-all-start.2 = ((bf16[32,2,128,256]{3,1,2,0:T(2,128)(2,1)}), bf16[32,2,128,256]{3,1,2,0:T(2,128)(2,1)}, u32[]{:S(2)}, u32[]{:S(2)}) async-start(bf16[32,2,128,256]{3,1,2,0:T(2,128)(2,1)} %copy.64), calls=%async_computation.2 | async-start | bytes 8388608 | tf_op jit(solution)/shard_map/all_to_all | solution.py:61
  124.7 282.1 %reduce-scatter.5.cloned.1.call-start = ((), (), s32[]{:S(2)}) async-start(), calls=%async_computation.6 | async-start | bytes 6488064 | tf_op jit(solution)/shard_map/reduce_scatter | solution.py:88
  197.2 2.3 copy-start.4
  215.8 9.4 %copy-start.12 = (bf16[5,4]{0,1:T(4,128)(2,1)S(1)}, bf16[5,4]{0,1:T(4,128)(2,1)}, u32[]{:S(2)}) copy-start(bf16[5,4]{0,1:T(4,128)(2,1)} %param.12) | copy-start | bytes 124
  215.8 301.1 %all-to-all-start = ((bf16[32,2,128,768]{3,2,1,0:T(8,128)(2,1)}), bf16[32,2,128,768]{3,2,1,0:T(8,128)(2,1)}, u32[]{:S(2)}, u32[]{:S(2)}) async-start(bf16[32,2,128,768]{3,2,1,0:T(8,128)(2,1)} %bitcast.90), calls=%async_computation | async-start | bytes 25165824 | tf_op jit(solution)/shard_map/all_to_all | solution.py:43
  222.5 224.2 %reduce-scatter.3.cloned.1.call-start = ((), (), s32[]{:S(2)}) async-start(), calls=%async_computation.5 | async-start | bytes 3932160 | tf_op jit(solution)/shard_map/reduce_scatter | solution.py:76
  225.2 1.8 copy-start.5
  227.0 2.3 copy-start.2
  227.0 2.3 copy-start.6
  231.6 2.2 copy-start.3
  233.8 11.0 %copy-start.10 = (s32[1,256]{1,0:T(1,128)S(1)}, s32[1,256]{1,0:T(1,128)}, u32[]{:S(2)}) copy-start(s32[1,256]{1,0:T(1,128)} %param.16) | copy-start | bytes 3076
  233.8 279.7 %copy-start.13 = (bf16[5,4]{0,1:T(4,128)(2,1)S(1)}, bf16[5,4]{0,1:T(4,128)(2,1)}, u32[]{:S(2)}) copy-start(bf16[5,4]{0,1:T(4,128)(2,1)} %param.12) | copy-start | bytes 124
  564.7 33.4 %copy-start.8 = (s32[1,256]{1,0:T(1,128)S(1)}, s32[1,256]{1,0:T(1,128)}, u32[]{:S(2)}) copy-start(s32[1,256]{1,0:T(1,128)} %param.17) | copy-start | bytes 3076
  598.2 16.1 %copy-start.7 = (bf16[768,256]{1,0:T(8,128)(2,1)S(1)}, bf16[768,256]{1,0:T(8,128)(2,1)}, u32[]{:S(2)}) copy-start(bf16[768,256]{1,0:T(8,128)(2,1)} %param.13) | copy-start | bytes 1179652
Sparse Core Ops, SparseCore 0:
  208.5 198.1 reduce-scatter.4
  409.3 37.3 reduce-scatter.2
where the time goes:
time: 635 us; the launch traced here: 623 us
  waiting for transfers between devices  240 us (38%)
  local copies, waits for them, and re-layouts  157 us (25%)
  matrix products  106 us (17%)
  blocking collectives  64.9 us (10%)
  starting transfers between devices  34.2 us (5%)
  between operations  14.7 us (2%)
    reduce_scatter x1, waiting for transfers between devices, body(): lax.psum_scatter(stacked, 'shard', scatter_dimension=0, tiled=True)  161 us
    psum x1, blocking collectives, body(): grad_coef = lax.psum(partial_coef, ('shard', 'rep'))  64.9 us
    all_to_all x1, waiting for transfers between devices, body(): lax.all_to_all(slot_grads, 'shard', split_axis=0, concat_axis=0, tiled=True)  40.3 us
    reduce_scatter x1, waiting for transfers between devices, body(): lax.psum_scatter(through_rel + jnp.dot(d_out, root_weight.T, preferred_el...  38.7 us
    dot_general x1, local copies, waits for them, and re-layouts, body(): jnp.einsum('tji,tjo->tio', adjacency, grad_rows, preferred_element_type=j...  33.4 us
    dot_general x1, local copies, waits for them, and re-layouts, body(): jnp.einsum('tij,tjo->tio', adjacency, tile_msgs, preferred_element_type=j...  33.4 us
    dot_general x1, matrix products, body(): jnp.einsum('tij,tjo->tio', adjacency, tile_msgs, preferred_element_type=j...  20.1 us
    dot_general x1, matrix products, body(): jnp.einsum('tji,tjo->tio', adjacency, grad_rows, preferred_element_type=j...  20.1 us
  transfers between devices with their start and end apart: 5, of which 3 were waited for; matrix products, arithmetic and copies ran while one was open for 22% of the time, Pallas kernels for 0%

commit v1 on v0

v1 whole, which is shorter than its diff:
```python
import jax
import jax.numpy as jnp
from jax import lax
from jax.experimental import pallas as pl
from jax.experimental.pallas import tpu as pltpu
from jax.sharding import PartitionSpec as P

BLK = 128
F32 = jnp.float32
BF16 = jnp.bfloat16
VMEM_LIMIT = 48 * 1024 * 1024


def params():
    return pltpu.CompilerParams(vmem_limit_bytes=VMEM_LIMIT)


def whole(shape):
    return pl.BlockSpec(shape, lambda *_: (0,) * len(shape))


def tile_grads(tile_ids, dest_ids, adjacency, grads, slots, chunk=16):
    tiles = adjacency.shape[0]
    nblocks, _, width = grads.shape

    def kernel(slot_ref, dst_ref, adj_ref, grad_ref, out_ref, acc_ref):
        step = pl.program_id(0)

        @pl.when(step == 0)
        def _():
            acc_ref[...] = jnp.zeros_like(acc_ref)

        for u in range(chunk):
            t = step * chunk + u
            part = lax.dot_general(
                adj_ref[u],
                grad_ref[dst_ref[t]],
                (((0,), (0,)), ((), ())),
                preferred_element_type=F32,
            )
            acc_ref[slot_ref[t]] += part

        @pl.when(step == pl.num_programs(0) - 1)
        def _():
            out_ref[...] = acc_ref[...].astype(BF16)

    return pl.pallas_call(
        kernel,
        name="tile_grads",
        out_shape=jax.ShapeDtypeStruct((slots, BLK, width), BF16),
        grid_spec=pltpu.PrefetchScalarGridSpec(
            num_scalar_prefetch=2,
            grid=(tiles // chunk,),
            in_specs=[
                pl.BlockSpec((chunk, BLK, BLK), lambda i, *_: (i, 0, 0)),
                whole(grads.shape),
            ],
            out_specs=whole((slots, BLK, width)),
            scratch_shapes=[pltpu.VMEM((slots, BLK, width), F32)],
        ),
        compiler_params=params(),
    )(tile_ids, dest_ids, adjacency, grads)


def tile_sums(tile_ids, dest_ids, adjacency, msgs, root_term, chunk=16):
    tiles = adjacency.shape[0]
    nblocks, _, width = root_term.shape

    def kernel(slot_ref, dst_ref, adj_ref, msg_ref, root_ref, out_ref, acc_ref):
        step = pl.program_id(0)

        @pl.when(step == 0)
        def _():
            acc_ref[...] = root_ref[...]

        for u in range(chunk):
            t = step * chunk + u
            acc_ref[dst_ref[t]] += jnp.dot(
                adj_ref[u], msg_ref[slot_ref[t]], preferred_element_type=F32
            )

        @pl.when(step == pl.num_programs(0) - 1)
        def _():
            out_ref[...] = acc_ref[...].astype(BF16)

    return pl.pallas_call(
        kernel,
        name="tile_sums",
        out_shape=jax.ShapeDtypeStruct(root_term.shape, BF16),
        grid_spec=pltpu.PrefetchScalarGridSpec(
            num_scalar_prefetch=2,
            grid=(tiles // chunk,),
            in_specs=[
                pl.BlockSpec((chunk, BLK, BLK), lambda i, *_: (i, 0, 0)),
                whole(msgs.shape),
                whole(root_term.shape),
            ],
            out_specs=whole(root_term.shape),
            scratch_shapes=[pltpu.VMEM(root_term.shape, F32)],
        ),
        compiler_params=params(),
    )(tile_ids, dest_ids, adjacency, msgs, root_term)


def project_select(keys, feats, rel_weights, nblocks):
    relations, _, width = rel_weights.shape
    slots = keys.shape[0]

    def kernel(key_ref, feat_ref, w_ref, out_ref, msg_ref):
        for r in range(relations):
            for b in range(nblocks):
                msg_ref[r * nblocks + b] = jnp.dot(
                    feat_ref[pl.ds(b * BLK, BLK), :], w_ref[r], preferred_element_type=F32
                ).astype(BF16)

        def copy(s, carry):
            out_ref[s] = msg_ref[key_ref[s]]
            return carry

        lax.fori_loop(0, slots, copy, 0)

    return pl.pallas_call(
        kernel,
        name="project_select",
        out_shape=jax.ShapeDtypeStruct((slots, BLK, width), BF16),
        grid_spec=pltpu.PrefetchScalarGridSpec(
            num_scalar_prefetch=1,
            grid=(1,),
            in_specs=[whole(feats.shape), whole(rel_weights.shape)],
            out_specs=whole((slots, BLK, width)),
            scratch_shapes=[pltpu.VMEM((relations * nblocks, BLK, width), BF16)],
        ),
        compiler_params=params(),
    )(keys, feats, rel_weights)


def sum_by_key(keys, returned, bins, chunk=8):
    slots, _, width = returned.shape

    def kernel(key_ref, ret_ref, out_ref, acc_ref):
        step = pl.program_id(0)

        @pl.when(step == 0)
        def _():
            acc_ref[...] = jnp.zeros_like(acc_ref)

        for u in range(chunk):
            acc_ref[key_ref[step * chunk + u]] += ret_ref[u].astype(F32)

        @pl.when(step == pl.num_programs(0) - 1)
        def _():
            out_ref[...] = acc_ref[...].astype(BF16)

    return pl.pallas_call(
        kernel,
        name="sum_by_key",
        out_shape=jax.ShapeDtypeStruct((bins, BLK, width), BF16),
        grid_spec=pltpu.PrefetchScalarGridSpec(
            num_scalar_prefetch=1,
            grid=(slots // chunk,),
            in_specs=[pl.BlockSpec((chunk, BLK, width), lambda i, *_: (i, 0, 0))],
            out_specs=whole((bins, BLK, width)),
            scratch_shapes=[pltpu.VMEM((bins, BLK, width), F32)],
        ),
        compiler_params=params(),
    )(keys, returned)


def exchange(x, axis, mask):
    return lax.ppermute(x, axis, [(i, i ^ mask) for i in range(lax.axis_size(axis))])


def scatter_sum(x, axis, shift, size, me):
    at = (me >> shift) & (size - 1)
    total = lax.dynamic_index_in_dim(x, at, 0, keepdims=False)
    for k in range(1, size):
        part = lax.dynamic_index_in_dim(x, at ^ k, 0, keepdims=False).astype(BF16)
        total = total + exchange(part, axis, k << shift).astype(F32)
    return total


def body(
    feats, bases, coef, root_weight, slot_block, recv_rel, tile_slot, tile_dst, tile_adj, d_out
):
    shards = lax.axis_size("shard")
    reps = lax.axis_size("rep")
    me = lax.axis_index("shard")
    my_rep = lax.axis_index("rep")
    nblocks = feats.shape[0] // BLK
    width_in = feats.shape[1]
    width = root_weight.shape[1]
    relations, nbase = coef.shape
    capacity = slot_block.shape[2]
    slots = shards * capacity

    slot_grads = tile_grads(
        tile_slot[0], tile_dst[0], tile_adj[0], d_out.reshape(nblocks, BLK, width), slots
    )
    returned = lax.all_to_all(
        slot_grads.reshape(shards, capacity * BLK, width), "shard", 0, 0, tiled=True
    )

    table = recv_rel.reshape(1, slots)
    step = 1
    while step < shards:
        table = jnp.concatenate([table, exchange(table, "shard", step)], axis=0)
        step *= 2
    mine = jnp.sum(
        jnp.where(
            jnp.arange(slots)[None, :, None]
            == (me * capacity + jnp.arange(capacity))[None, None, :],
            table[:, :, None],
            0,
        ),
        axis=1,
    )
    order = jnp.arange(shards)
    owner_rel = jnp.sum(
        jnp.where((order[:, None] ^ me) == order[None, :], 1, 0)[:, :, None] * mine[None], axis=1
    )
    keys = (owner_rel * nblocks + slot_block[0]).reshape(-1).astype(jnp.int32)

    rel_weights = (
        jnp.dot(coef, bases.reshape(nbase, -1), preferred_element_type=F32)
        .astype(BF16)
        .reshape(relations, width_in, width)
    )
    outgoing = project_select(keys, feats, rel_weights, nblocks)
    root_term = jnp.dot(feats, root_weight, preferred_element_type=F32)
    incoming = lax.all_to_all(
        outgoing.reshape(shards, capacity * BLK, width), "shard", 0, 0, tiled=True
    )

    source_grads = sum_by_key(keys, returned.reshape(slots, BLK, width), relations * nblocks)
    source_grads = source_grads.reshape(relations, nblocks * BLK, width)
    relation_grads = jnp.einsum("nc,rno->rco", feats, source_grads, preferred_element_type=F32)
    root_grad = jnp.dot(feats.T, d_out, preferred_element_type=F32)

    wide_coef = coef.astype(F32)
    partial_bases = [
        sum(wide_coef[r, b] * relation_grads[r] for r in range(relations)) for b in range(nbase)
    ]
    rows = width_in // shards
    stacked = jnp.concatenate(
        [g.reshape(shards, rows, width) for g in (*partial_bases, root_grad)], axis=1
    )
    part = scatter_sum(
        jnp.swapaxes(stacked.reshape(shards // 2, 2, -1, width), 0, 1), "shard", 0, 2, me
    )
    part = scatter_sum(part.reshape(4, shards // 8, -1, width), "shard", 3, 4, me)
    part = scatter_sum(part, "shard", 1, 4, me)
    reduced = part.reshape(nbase + 1, rows, width)
    grad_bases = reduced[:nbase]
    grad_root = reduced[nbase]

    grad_coef = jnp.sum(
        relation_grads[:, None] * bases.astype(F32)[None], axis=(2, 3)
    )
    for axis in ("shard", "rep"):
        step = 1
        while step < lax.axis_size(axis):
            grad_coef = grad_coef + exchange(grad_coef, axis, step)
            step *= 2

    through = jnp.einsum("rno,rco->nc", source_grads, rel_weights, preferred_element_type=F32)
    through = through + jnp.dot(d_out, root_weight.T, preferred_element_type=F32)
    grad_feats = scatter_sum(
        through.reshape(reps, -1, width_in), "rep", 0, reps, my_rep
    ).astype(BF16)

    output = tile_sums(
        tile_slot[0],
        tile_dst[0],
        tile_adj[0],
        incoming.reshape(slots, BLK, width),
        root_term.reshape(nblocks, BLK, width),
    ).reshape(nblocks * BLK, width)
    return (output, grad_feats, grad_bases, grad_root, grad_coef)


def solution(mesh):
    placed = (
        P("shard", None),
        P(None, None, "rep"),
        P(),
        P(None, "rep"),
        P("shard", None, None),
        P("shard", None, None),
        P("shard", None),
        P("shard", None),
        P("shard", None, None, None),
        P("shard", "rep"),
    )
    return jax.shard_map(
        body,
        mesh=mesh,
        in_specs=placed,
        out_specs=(
            P("shard", "rep"),
            P(("shard", "rep"), None),
            P(None, "shard", "rep"),
            P("shard", "rep"),
            P(),
        ),
        check_vma=False,
    )
```

time: 635 us -> 237 us (0.37); the launches traced: 623 us -> 236 us
  waiting for transfers between devices: 240 us -> 61.1 us
  local copies, waits for them, and re-layouts: 157 us -> 40.7 us
  matrix products: 106 us -> 13.3 us
  blocking collectives: 64.9 us -> 0 us
  Pallas kernels: 0 us -> 41.2 us
  other arithmetic: 5.95 us -> 34.6 us
  between operations: 14.7 us -> 1.13 us
  starting transfers between devices: 34.2 us -> 43.7 us
    reduce_scatter x2 -> x0, waiting for transfers between devices: 200 us -> none  [the longest x1 161 us: body(): lax.psum_scatter(stacked, 'shard', scatter_dimension=0, tiled=True)]
    dot_general x13 -> x5, matrix products: 104 us -> 9.33 us  [the longest x1 4.11 us: body(): jnp.einsum('nc,rno->rco', feats, source_grads, preferred_element_type=F32)]
    dot_general x3 -> x0, local copies, waits for them, and re-layouts: 67.2 us -> none  [the longest x1 33.4 us: body(): jnp.einsum('tji,tjo->tio', adjacency, grad_rows, preferred_element_type=j...]
    psum x1 -> x0, blocking collectives: 64.9 us -> none  [body(): grad_coef = lax.psum(partial_coef, ('shard', 'rep'))]
    ppermute x0 -> x22, waiting for transfers between devices: none -> 61.1 us  [exchange(): lax.ppermute(x, axis, [(i, i ^ mask) for i in range(lax.axis_size(axis))])]
    pallas_call x0 -> x4, Pallas kernels: none -> 41.2 us  [the longest x1 15.4 us: tile_sums(): pl.pallas_call(kernel, name='tile_sums', out_shape=jax.ShapeDtypeStruct(r...]
    gather x4 -> x0, local copies, waits for them, and re-layouts: 40.9 us -> none  [the longest x1 12 us: body(): tile_msgs = slot_msgs[tile_ids]]
    all_to_all x3 -> x2, waiting for transfers between devices: 40.3 us -> 0.01 us  [the longest x1 0.01 us: body(): lax.all_to_all(slot_grads.reshape(shards, capacity * BLK, width), 'shard'...]
  transfers between devices with their start and end apart: 5 -> 24, of which waited for: 3 -> 8; matrix products, arithmetic and copies ran while one was open for 22% -> 32% of each run, Pallas kernels for 0% -> 11%
where the time goes in v1:
time: 237 us; the launch traced here: 236 us
  waiting for transfers between devices  61.1 us (26%)
  starting transfers between devices  43.7 us (18%)
  Pallas kernels  41.2 us (17%)
  local copies, waits for them, and re-layouts  40.7 us (17%)
  other arithmetic  34.6 us (15%)
  matrix products  13.3 us (6%)
    ppermute x22, waiting for transfers between devices, exchange(): lax.ppermute(x, axis, [(i, i ^ mask) for i in range(lax.axis_size(axis))])  61.1 us
    ppermute x22, starting transfers between devices, exchange(): lax.ppermute(x, axis, [(i, i ^ mask) for i in range(lax.axis_size(axis))])  29.5 us
    add x4, other arithmetic, body(): sum((wide_coef[r, b] * relation_grads[r] for r in range(relations)))  25.3 us
    unnamed x63, local copies, waits for them, and re-layouts  19.7 us
    pallas_call x1, Pallas kernels, tile_sums(): pl.pallas_call(kernel, name='tile_sums', out_shape=jax.ShapeDtypeStruct(r...  15.4 us
    pallas_call x1, Pallas kernels, tile_grads(): pl.pallas_call(kernel, name='tile_grads', out_shape=jax.ShapeDtypeStruct(...  14.4 us
    add x4, local copies, waits for them, and re-layouts, body(): sum((wide_coef[r, b] * relation_grads[r] for r in range(relations)))  9.25 us
    all_to_all x1, starting transfers between devices, body(): lax.all_to_all(slot_grads.reshape(shards, capacity * BLK, width), 'shard'...  8.68 us
  transfers between devices with their start and end apart: 24, of which 8 were waited for; matrix products, arithmetic and copies ran while one was open for 32% of the time, Pallas kernels for 11%

profile of v1, /device:TPU:0, one launch (start us, length us, event | category | flops | bytes accessed | tf_op | source)
XLA Modules:
  0.0 235.7 jit_solution(7146445086164473861)
XLA Ops:
  0.7 1.1 copy-done.7
  1.7 0.7 copy-done.9
  2.4 0.7 copy-done.11
  3.1 14.4 %tile_grads.1 = bf16[64,128,256]{2,1,0:T(8,128)(2,1)S(1)} custom-call(s32[256]{0:T(256)S(1)} %bitcast.112, s32[256]{0:T(256)S(1)} %bitcast.114, bf16[256,128,128]{2,1,0:T(8,128)(2,1)} %bitcast.116, bf16[8,128,256]{2,1,0:T(8,128)(2,1)S(1)} %bitcast.111), custom_call_target="tpu_custom_call" | custom-call | tf_op jit(solution)/shard_map/tile_grads/pallas_call | solution.py:47
  17.6 2.0 copy-done.1
  19.6 8.7 %all-to-all-start.1 = ((bf16[32,256,256]{2,1,0:T(8,128)(2,1)}), bf16[32,256,256]{2,1,0:T(8,128)(2,1)}, u32[]{:S(2)}, u32[]{:S(2)}) async-start(bf16[32,256,256]{2,1,0:T(8,128)(2,1)} %bitcast.105), calls=%async_computation.1 | async-start | bytes 8388608 | tf_op jit(solution)/shard_map/all_to_all | solution.py:199
  28.8 2.8 %copy.40 = bf16[1,4,768,256]{3,1,2,0:T(4,128)(2,1)S(1)} copy(bf16[1,4,768,256]{3,2,1,0:T(8,128)(2,1)} %bitcast.123) | data formatting | bytes 3145728
  31.6 1.5 fusion.22
  33.1 2.5 %convolution_convert_fusion = bf16[5,196608]{1,0:T(8,128)(2,1)} fusion(bf16[5,4]{0,1:T(4,128)(2,1)S(1)} %copy-done.24, bf16[4,196608]{1,0:T(4,128)(2,1)S(1)} %bitcast.120), kind=kOutput, calls=%fused_computation | convolution fusion | flops 8847360 | bytes 3538984 | tf_op jit(solution)/shard_map/dot_general | solution.py:224
  35.6 1.8 collective-permute-start.1
  37.4 39.9 %collective-permute-done.1 = s32[2,64]{1,0:T(2,128)S(1)} collective-permute-done((s32[2,64]{1,0:T(2,128)S(1)}, s32[2,64]{1,0:T(2,128)S(1)}, u32[]{:S(2)}, u32[]{:S(2)}) %collective-permute-start.1) | collective-permute-done | bytes 544 | tf_op jit(solution)/shard_map/ppermute | solution.py:170
  77.4 5.1 %collective-permute-done.2 = s32[4,64]{1,0:T(4,128)S(1)} collective-permute-done((s32[4,64]{1,0:T(4,128)S(1)}, s32[4,64]{1,0:T(4,128)S(1)}, u32[]{:S(2)}, u32[]{:S(2)}) %collective-permute-start.2) | collective-permute-done | bytes 1056 | tf_op jit(solution)/shard_map/ppermute | solution.py:170
  82.5 0.7 collective-permute-start.3
  83.3 2.9 %collective-permute-done.3 = s32[8,64]{1,0:T(8,128)S(1)} collective-permute-done((s32[8,64]{1,0:T(8,128)S(1)}, s32[8,64]{1,0:T(8,128)S(1)}, u32[]{:S(2)}, u32[]{:S(2)}) %collective-permute-start.3) | collective-permute-done | bytes 2080 | tf_op jit(solution)/shard_map/ppermute | solution.py:170
  86.2 2.8 %collective-permute-start.4 = (s32[16,64]{1,0:T(8,128)S(1)}, s32[16,64]{1,0:T(8,128)S(1)}, u32[]{:S(2)}, u32[]{:S(2)}) collective-permute-start(s32[16,64]{1,0:T(8,128)S(1)} %concatenate.28), channel_id=1, source_target_pairs={{0,64},{4,68},{8,72},{12,76},{16,80},{20,84},{24,88},{28,92},{32,9... | collective-permute-start | bytes 12296 | tf_op jit(solution)/shard_map/ppermute | solution.py:170
  89.0 0.7 fusion.19
  90.3 1.9 convert_element_type.135
  92.4 2.3 copy.43
  95.3 1.4 copy-done.3
  96.7 5.3 %project_select.1 = bf16[64,128,256]{2,1,0:T(8,128)(2,1)} custom-call(s32[64]{0:T(128)S(1)} %add.216.key_ref, bf16[1024,768]{1,0:T(8,128)(2,1)S(1)} %copy-done.3, bf16[5,768,256]{2,1,0:T(8,128)(2,1)S(1)} %bitcast.106), custom_call_target="tpu_custom_call" | custom-call | tf_op jit(solution)/shard_map/project_select/pallas_call | solution.py:122
  102.0 5.5 %all-to-all-start = ((bf16[32,256,256]{2,1,0:T(8,128)(2,1)}), bf16[32,256,256]{2,1,0:T(8,128)(2,1)}, u32[]{:S(2)}, u32[]{:S(2)}) async-start(bf16[32,256,256]{2,1,0:T(8,128)(2,1)} %bitcast.118), calls=%async_computation | async-start | bytes 8388608 | tf_op jit(solution)/shard_map/all_to_all | solution.py:230
  107.5 6.0 %sum_by_key.1 = bf16[40,128,256]{2,1,0:T(8,128)(2,1)S(1)} custom-call(s32[64]{0:T(128)S(1)} %add.216.key_ref, bf16[64,128,256]{2,1,0:T(8,128)(2,1)} %bitcast.9.ret_ref), custom_call_target="tpu_custom_call" | custom-call | tf_op jit(solution)/shard_map/sum_by_key/pallas_call | solution.py:154
  113.5 1.5 copy-done.6
  115.1 4.1 %convolution_bitcast_fusion = f32[5,768,256]{1,2,0:T(8,128)} fusion(bf16[5,1024,256]{2,1,0:T(8,128)(2,1)S(1)} %bitcast.109, bf16[1024,768]{1,0:T(8,128)(2,1)S(1)} %copy-done.4), kind=kOutput, calls=%fused_computation.3 | convolution fusion | flops 2013265920 | bytes 8126464 | tf_op jit(solution)/shard_map/nc,rno->rco/dot_general | solution.py:236
  119.2 5.5 %copy.37 = f32[5,768,256]{2,1,0:T(8,128)} copy(f32[5,768,256]{1,2,0:T(8,128)} %convolution_bitcast_fusion) | data formatting | bytes 7864320 | tf_op jit(solution)/shard_map/nc,rno->rco/transpose | solution.py:236
  124.7 6.3 %multiply_add_fusion.3 = f32[1,768,256]{1,2,0:T(8,128)} fusion(f32[5,768,256]{1,2,0:T(8,128)} %convolution_bitcast_fusion, f32[]{:T(128)} %bitcast.23, f32[]{:T(128)} %bitcast.22, f32[]{:T(128)} %bitcast.21, f32[]{:T(128)} %bitcast.20, f32[]{:T(128)} %bitcast.17), kind=kLoop, calls=%fused_computation.16 | loop fusion | flops 1769472 | bytes 4718612 | tf_op jit(solution)/shard_map/add | solution.py:241
  131.0 2.3 copy.33
  133.3 6.3 %multiply_add_fusion.2 = f32[1,768,256]{1,2,0:T(8,128)} fusion(f32[5,768,256]{1,2,0:T(8,128)} %convolution_bitcast_fusion, f32[]{:T(128)} %bitcast.29, f32[]{:T(128)} %bitcast.28, f32[]{:T(128)} %bitcast.27, f32[]{:T(128)} %bitcast.26, f32[]{:T(128)} %bitcast.25), kind=kLoop, calls=%fused_computation.15 | loop fusion | flops 1769472 | bytes 4718612 | tf_op jit(solution)/shard_map/add | solution.py:241
  139.5 2.3 copy.34
  141.8 6.4 %multiply_add_fusion.1 = f32[1,768,256]{1,2,0:T(8,128)} fusion(f32[5,768,256]{1,2,0:T(8,128)} %convolution_bitcast_fusion, f32[]{:T(128)} %bitcast.35, f32[]{:T(128)} %bitcast.34, f32[]{:T(128)} %bitcast.33, f32[]{:T(128)} %bitcast.32, f32[]{:T(128)} %bitcast.31), kind=kLoop, calls=%fused_computation.14 | loop fusion | flops 1769472 | bytes 4718612 | tf_op jit(solution)/shard_map/add | solution.py:241
  148.2 2.3 copy.35
  150.6 6.4 %multiply_add_fusion = f32[1,768,256]{1,2,0:T(8,128)} fusion(f32[5,768,256]{1,2,0:T(8,128)} %convolution_bitcast_fusion, f32[]{:T(128)} %bitcast.41, f32[]{:T(128)} %bitcast.40, f32[]{:T(128)} %bitcast.39, f32[]{:T(128)} %bitcast.38, f32[]{:T(128)} %bitcast.37), kind=kLoop, calls=%fused_computation.13 | loop fusion | flops 1769472 | bytes 4718612 | tf_op jit(solution)/shard_map/add | solution.py:241
  156.9 2.3 copy.36
  159.3 1.3 constant_dynamic-update-slice_fusion.4
  160.6 1.3 constant_dynamic-update-slice_fusion.3
  162.2 1.1 fusion.1
  163.3 2.8 %copy-done.13 = f32[5,768,256]{2,1,0:T(8,128)S(1)} copy-done((f32[5,768,256]{2,1,0:T(8,128)S(1)}, f32[5,768,256]{2,1,0:T(8,128)}, u32[]{:S(2)}) %copy-start.13) | copy-done | bytes 3932184
  166.1 1.7 multiply_reduce_fusion
  167.9 1.1 collective-permute-done.15
  169.0 1.5 collective-permute-start.16
  170.5 4.0 %fusion.21 = f32[1024,768,1]{1,0,2:T(8,128)S(1)} fusion(bf16[5,1024,256]{2,1,0:T(8,128)(2,1)} %bitcast.110, bf16[5,768,256]{2,1,0:T(8,128)(2,1)S(1)} %bitcast.107), kind=kOutput, calls=%fused_computation.59 | convolution fusion | flops 2013265920 | bytes 7733248 | tf_op jit(solution)/shard_map/rno,rco->nc/dot_general | solution.py:265
  174.6 2.8 %collective-permute-start.17 = (f32[5,4]{1,0:T(8,128)S(1)}, f32[5,4]{1,0:T(8,128)S(1)}, u32[]{:S(2)}, u32[]{:S(2)}) collective-permute-start(f32[5,4]{1,0:T(8,128)S(1)} %add.263), channel_id=1, source_target_pairs={{0,16},{4,20},{8,24},{12,28},{16,0},{20,4},{24,8},{28,12},{32,48},... | collective-permute-start | bytes 248 | tf_op jit(solution)/shard_map/ppermute | solution.py:170
  177.3 1.5 bitcast_add_fusion.1
  178.8 0.9 fusion.10
  179.7 2.7 %collective-permute-start.11 = (bf16[4,120,256]{2,1,0:T(8,128)(2,1)S(1)}, bf16[4,120,256]{2,1,0:T(8,128)(2,1)S(1)}, u32[]{:S(2)}, u32[]{:S(2)}) collective-permute-start(bf16[4,120,256]{2,1,0:T(8,128)(2,1)S(1)} %get-tuple-element.14), channel_id=1, source_target_pairs={{0,96},{4,100},{8,104},{12,108},{16,112},{20,116},{24,120},{28,124... | collective-permute-start | bytes 737288 | tf_op jit(solution)/shard_map/ppermute | solution.py:170
  182.4 0.7 bitcast_add_fusion
  183.4 1.3 fusion.7
  184.7 2.1 collective-permute-done.18
  186.8 0.8 collective-permute-start.19
  187.6 2.8 %collective-permute-start.7 = (bf16[256,768]{1,0:T(8,128)(2,1)}, bf16[256,768]{1,0:T(8,128)(2,1)}, u32[]{:S(2)}, u32[]{:S(2)}) collective-permute-start(bf16[256,768]{1,0:T(8,128)(2,1)} %get-tuple-element.11), channel_id=1, source_target_pairs={{0,3},{1,2},{2,1},{3,0},{4,7},{5,6},{6,5},{7,4},{8,11},{9,10},{10,... | collective-permute-start | bytes 1179656 | tf_op jit(solution)/shard_map/ppermute | solution.py:170
  190.4 1.5 collective-permute-done.19
  191.9 1.5 collective-permute-start.20
  193.4 2.7 %collective-permute-start.6 = (bf16[256,768]{1,0:T(8,128)(2,1)}, bf16[256,768]{1,0:T(8,128)(2,1)}, u32[]{:S(2)}, u32[]{:S(2)}) collective-permute-start(bf16[256,768]{1,0:T(8,128)(2,1)} %get-tuple-element.12), channel_id=1, source_target_pairs={{0,2},{1,3},{2,0},{3,1},{4,6},{5,7},{6,4},{7,5},{8,10},{9,11},{10,... | collective-permute-start | bytes 1179656 | tf_op jit(solution)/shard_map/ppermute | solution.py:170
  196.2 2.5 %collective-permute-start.21 = (f32[5,4]{1,0:T(8,128)S(1)}, f32[5,4]{1,0:T(8,128)S(1)}, u32[]{:S(2)}, u32[]{:S(2)}) collective-permute-start(f32[5,4]{1,0:T(8,128)S(1)} %add.267), channel_id=1, source_target_pairs={{0,2},{1,3},{2,0},{3,1},{4,6},{5,7},{6,4},{7,5},{8,10},{9,11},{10,... | collective-permute-start | bytes 248 | tf_op jit(solution)/shard_map/ppermute | solution.py:170
  199.3 8.0 %collective-permute-done.21 = f32[5,4]{1,0:T(8,128)S(1)} collective-permute-done((f32[5,4]{1,0:T(8,128)S(1)}, f32[5,4]{1,0:T(8,128)S(1)}, u32[]{:S(2)}, u32[]{:S(2)}) %collective-permute-start.21) | collective-permute-done | bytes 112 | tf_op jit(solution)/shard_map/ppermute | solution.py:170
  207.3 0.8 collective-permute-start.10
  208.1 0.7 copy-done.22
  210.0 0.7 copy.38
  210.7 15.4 %tile_sums.1 = bf16[8,128,256]{2,1,0:T(8,128)(2,1)} custom-call(s32[256]{0:T(256)S(1)} %bitcast.113, s32[256]{0:T(256)S(1)} %bitcast.115, bf16[256,128,128]{2,1,0:T(8,128)(2,1)} %bitcast.117, bf16[64,128,256]{2,1,0:T(8,128)(2,1)} %bitcast.4.msg_ref, f32[8,128,256]{2,1,0:T(8,128)S(1)} %bitcast.108), custom_call_target="tpu_custom_call" | custom-call | tf_op jit(solution)/shard_map/tile_sums/pallas_call | solution.py:86
  226.1 1.2 fusion.6
  227.4 0.8 collective-permute-start.14
  228.2 1.9 collective-permute-start.13
  230.0 1.5 collective-permute-start.12
  231.6 2.4 %fusion.4 = bf16[256,768]{1,0:T(8,128)(2,1)} fusion(bf16[256,768]{1,0:T(8,128)(2,1)} %collective-permute-done.7, bf16[256,768]{1,0:T(8,128)(2,1)} %collective-permute-done.6, bf16[256,768]{1,0:T(8,128)(2,1)} %collective-permute-done.5, f32[4,256,768]{2,1,0:T(8,128)} %bitcast.122, s32[]{:T(128)S(6)} %select_n.60), kind=kLoop, calls=%fused_computation.12 | loop fusion | flops 1376256 | bytes 2359300 | tf_op jit(solution)/shard_map/convert_element_type | solution.py:269
  (105 shorter events, 6.2 us)
Async XLA Ops:
  0.6 181.8 %copy-start = (bf16[768,256]{1,0:T(8,128)(2,1)S(1)}, bf16[768,256]{1,0:T(8,128)(2,1)}, u32[]{:S(2)}) copy-start(bf16[768,256]{1,0:T(8,128)(2,1)} %param.13) | copy-start | bytes 1179652
  0.6 1.1 copy-start.7
  1.7 0.7 copy-start.9
  2.4 0.7 copy-start.11
  17.5 2.0 copy-start.1
  19.6 8.7 %copy-start.25 = (s32[1,32,2]{1,2,0:T(2,128)S(1)}, s32[1,32,2]{1,2,0:T(2,128)}, u32[]{:S(2)}) copy-start(s32[1,32,2]{1,2,0:T(2,128)} %param.15) | copy-start | bytes 772
  19.6 82.4 %all-to-all-start.1 = ((bf16[32,256,256]{2,1,0:T(8,128)(2,1)}), bf16[32,256,256]{2,1,0:T(8,128)(2,1)}, u32[]{:S(2)}, u32[]{:S(2)}) async-start(bf16[32,256,256]{2,1,0:T(8,128)(2,1)} %bitcast.105), calls=%async_computation.1 | async-start | bytes 8388608 | tf_op jit(solution)/shard_map/all_to_all | solution.py:199
  28.3 3.3 %copy-start.2 = (bf16[1024,768]{1,0:T(8,128)(2,1)S(1)}, bf16[1024,768]{1,0:T(8,128)(2,1)}, u32[]{:S(2)}) copy-start(bf16[1024,768]{1,0:T(8,128)(2,1)} %feat_ref.1) | copy-start | bytes 4718596
  28.3 3.3 %copy-start.8 = (bf16[1024,256]{1,0:T(8,128)(2,1)S(1)}, bf16[1024,256]{1,0:T(8,128)(2,1)}, u32[]{:S(2)}) copy-start(bf16[1024,256]{1,0:T(8,128)(2,1)} %param.19) | copy-start | bytes 1572868
  28.5 7.1 %collective-permute-start = (s32[1,64]{1,0:T(1,128)S(1)}, s32[1,64]{1,0:T(1,128)S(1)}, u32[]{:S(2)}, u32[]{:S(2)}) collective-permute-start(s32[1,64]{1,0:T(1,128)S(1)} %reshape.234), channel_id=1, source_target_pairs={{0,4},{4,0},{8,12},{12,8},{16,20},{20,16},{24,28},{28,24},{32,36},... | collective-permute-start | bytes 776 | tf_op jit(solution)/shard_map/ppermute | solution.py:170
  31.5 1.5 copy-start.24
  33.1 57.3 %copy-start.16 = (bf16[4,768,256]{2,1,0:T(8,128)(2,1)S(1)}, bf16[4,768,256]{2,1,0:T(8,128)(2,1)}, u32[]{:S(2)}) copy-start(bf16[4,768,256]{2,1,0:T(8,128)(2,1)} %param.11) | copy-start | bytes 4718596
  35.5 56.7 %copy-start.26 = (s32[1,32,2]{1,2,0:T(2,128)S(1)}, s32[1,32,2]{1,2,0:T(2,128)}, u32[]{:S(2)}) copy-start(s32[1,32,2]{1,2,0:T(2,128)} %param.14) | copy-start | bytes 772
  35.6 41.7 %collective-permute-start.1 = (s32[2,64]{1,0:T(2,128)S(1)}, s32[2,64]{1,0:T(2,128)S(1)}, u32[]{:S(2)}, u32[]{:S(2)}) collective-permute-start(s32[2,64]{1,0:T(2,128)S(1)} %pad_add_fusion.2), channel_id=1, source_target_pairs={{0,8},{4,12},{8,0},{12,4},{16,24},{20,28},{24,16},{28,20},{32,40},... | collective-permute-start | bytes 1544 | tf_op jit(solution)/shard_map/ppermute | solution.py:170
  77.3 5.2 %collective-permute-start.2 = (s32[4,64]{1,0:T(4,128)S(1)}, s32[4,64]{1,0:T(4,128)S(1)}, u32[]{:S(2)}, u32[]{:S(2)}) collective-permute-start(s32[4,64]{1,0:T(4,128)S(1)} %pad_add_fusion.1), channel_id=1, source_target_pairs={{0,16},{4,20},{8,24},{12,28},{16,0},{20,4},{24,8},{28,12},{32,48},... | collective-permute-start | bytes 3080 | tf_op jit(solution)/shard_map/ppermute | solution.py:170
  82.5 3.7 %collective-permute-start.3 = (s32[8,64]{1,0:T(8,128)S(1)}, s32[8,64]{1,0:T(8,128)S(1)}, u32[]{:S(2)}, u32[]{:S(2)}) collective-permute-start(s32[8,64]{1,0:T(8,128)S(1)} %pad_add_fusion), channel_id=1, source_target_pairs={{0,32},{4,36},{8,40},{12,44},{16,48},{20,52},{24,56},{28,60},{32,0... | collective-permute-start | bytes 6152 | tf_op jit(solution)/shard_map/ppermute | solution.py:170
  86.2 8.6 %collective-permute-start.4 = (s32[16,64]{1,0:T(8,128)S(1)}, s32[16,64]{1,0:T(8,128)S(1)}, u32[]{:S(2)}, u32[]{:S(2)}) collective-permute-start(s32[16,64]{1,0:T(8,128)S(1)} %concatenate.28), channel_id=1, source_target_pairs={{0,64},{4,68},{8,72},{12,76},{16,80},{20,84},{24,88},{28,92},{32,9... | collective-permute-start | bytes 12296 | tf_op jit(solution)/shard_map/ppermute | solution.py:170
  95.3 1.4 copy-start.3
  102.0 108.7 %all-to-all-start = ((bf16[32,256,256]{2,1,0:T(8,128)(2,1)}), bf16[32,256,256]{2,1,0:T(8,128)(2,1)}, u32[]{:S(2)}, u32[]{:S(2)}) async-start(bf16[32,256,256]{2,1,0:T(8,128)(2,1)} %bitcast.118), calls=%async_computation | async-start | bytes 8388608 | tf_op jit(solution)/shard_map/all_to_all | solution.py:230
  107.5 7.6 %copy-start.4 = (bf16[1024,768]{1,0:T(8,128)(2,1)S(1)}, bf16[1024,768]{1,0:T(8,128)(2,1)}, u32[]{:S(2)}) copy-start(bf16[1024,768]{1,0:T(8,128)(2,1)} %feat_ref.1) | copy-start | bytes 4718596
  113.5 1.5 copy-start.6
  159.3 2.7 %copy-start.19 = (f32[1,768,256]{2,1,0:T(8,128)S(1)}, f32[1,768,256]{2,1,0:T(8,128)}, u32[]{:S(2)}) copy-start(f32[1,768,256]{2,1,0:T(8,128)} %copy.35) | copy-start | bytes 2359300
  159.3 2.8 %copy-start.20 = (f32[1,768,256]{2,1,0:T(8,128)S(1)}, f32[1,768,256]{2,1,0:T(8,128)}, u32[]{:S(2)}) copy-start(f32[1,768,256]{2,1,0:T(8,128)} %copy.36) | copy-start | bytes 2359300
  159.3 2.8 %copy-start.21 = (f32[768,256]{1,0:T(8,128)S(1)}, f32[768,256]{1,0:T(8,128)}, u32[]{:S(2)}) copy-start(f32[768,256]{1,0:T(8,128)} %fusion.22) | copy-start | bytes 2359300
  160.6 2.7 %copy-start.14 = (f32[4,768,256]{2,1,0:T(8,128)S(1)}, f32[4,768,256]{2,1,0:T(8,128)}, u32[]{:S(2)}) copy-start(f32[4,768,256]{2,1,0:T(8,128)} %convert_element_type.135) | copy-start | bytes 9437188
  162.0 4.1 %copy-start.13 = (f32[5,768,256]{2,1,0:T(8,128)S(1)}, f32[5,768,256]{2,1,0:T(8,128)}, u32[]{:S(2)}) copy-start(f32[5,768,256]{2,1,0:T(8,128)} %copy.37) | copy-start | bytes 11796484
  162.2 5.6 %copy-start.17 = (f32[16,2,120,256]{3,2,1,0:T(8,128)}, f32[16,2,120,256]{3,2,1,0:T(8,128)S(1)}, u32[]{:S(2)}) copy-start(f32[16,2,120,256]{3,2,1,0:T(8,128)S(1)} %constant_dynamic-update-slice_fusion) | copy-start | bytes 11796484
  163.2 14.1 %collective-permute-start.8 = (bf16[16,120,256]{2,1,0:T(8,128)(2,1)}, bf16[16,120,256]{2,1,0:T(8,128)(2,1)}, u32[]{:S(2)}, u32[]{:S(2)}) collective-permute-start(bf16[16,120,256]{2,1,0:T(8,128)(2,1)} %fusion.1), channel_id=1, source_target_pairs={{0,4},{4,0},{8,12},{12,8},{16,20},{20,16},{24,28},{28,24},{32,36},... | collective-permute-start | bytes 2949128 | tf_op jit(solution)/shard_map/ppermute | solution.py:170
  167.8 1.2 collective-permute-start.15
  169.0 8.3 %copy-start.18 = (f32[16,2,120,256]{3,2,1,0:T(8,128)S(1)}, f32[16,2,120,256]{3,2,1,0:T(8,128)}, u32[]{:S(2)}) copy-start(f32[16,2,120,256]{3,2,1,0:T(8,128)} %copy-done.17) | copy-start | bytes 11796484
  169.0 5.5 %collective-permute-start.16 = (f32[5,4]{1,0:T(8,128)S(1)}, f32[5,4]{1,0:T(8,128)S(1)}, u32[]{:S(2)}, u32[]{:S(2)}) collective-permute-start(f32[5,4]{1,0:T(8,128)S(1)} %add.262), channel_id=1, source_target_pairs={{0,8},{4,12},{8,0},{12,4},{16,24},{20,28},{24,16},{28,20},{32,40},... | collective-permute-start | bytes 248 | tf_op jit(solution)/shard_map/ppermute | solution.py:170
  174.6 8.6 %collective-permute-start.17 = (f32[5,4]{1,0:T(8,128)S(1)}, f32[5,4]{1,0:T(8,128)S(1)}, u32[]{:S(2)}, u32[]{:S(2)}) collective-permute-start(f32[5,4]{1,0:T(8,128)S(1)} %add.263), channel_id=1, source_target_pairs={{0,16},{4,20},{8,24},{12,28},{16,0},{20,4},{24,8},{28,12},{32,48},... | collective-permute-start | bytes 248 | tf_op jit(solution)/shard_map/ppermute | solution.py:170
  179.7 29.7 %copy-start.5 = (bf16[1024,768]{1,0:T(8,128)(2,1)S(1)}, bf16[1024,768]{1,0:T(8,128)(2,1)}, u32[]{:S(2)}) copy-start(bf16[1024,768]{1,0:T(8,128)(2,1)} %feat_ref.1) | copy-start | bytes 4718596
  179.7 28.4 %collective-permute-start.11 = (bf16[4,120,256]{2,1,0:T(8,128)(2,1)S(1)}, bf16[4,120,256]{2,1,0:T(8,128)(2,1)S(1)}, u32[]{:S(2)}, u32[]{:S(2)}) collective-permute-start(bf16[4,120,256]{2,1,0:T(8,128)(2,1)S(1)} %get-tuple-element.14), channel_id=1, source_target_pairs={{0,96},{4,100},{8,104},{12,108},{16,112},{20,116},{24,120},{28,124... | collective-permute-start | bytes 737288 | tf_op jit(solution)/shard_map/ppermute | solution.py:170
  183.1 25.0 %copy-start.15 = (f32[1024,768]{1,0:T(8,128)}, f32[1024,768]{1,0:T(8,128)S(1)}, u32[]{:S(2)}) copy-start(f32[1024,768]{1,0:T(8,128)S(1)} %bitcast_add_fusion) | copy-start | bytes 9437188
  183.1 27.6 %copy-start.10 = (s32[1,256]{1,0:T(1,128)S(1)}, s32[1,256]{1,0:T(1,128)}, u32[]{:S(2)}) copy-start(s32[1,256]{1,0:T(1,128)} %param.16) | copy-start | bytes 3076
  183.1 27.6 %copy-start.12 = (s32[1,256]{1,0:T(1,128)S(1)}, s32[1,256]{1,0:T(1,128)}, u32[]{:S(2)}) copy-start(s32[1,256]{1,0:T(1,128)} %param.17) | copy-start | bytes 3076
  183.1 3.7 %collective-permute-start.18 = (f32[5,4]{1,0:T(8,128)S(1)}, f32[5,4]{1,0:T(8,128)S(1)}, u32[]{:S(2)}, u32[]{:S(2)}) collective-permute-start(f32[5,4]{1,0:T(8,128)S(1)} %add.264), channel_id=1, source_target_pairs={{0,32},{4,36},{8,40},{12,44},{16,48},{20,52},{24,56},{28,60},{32,0... | collective-permute-start | bytes 248 | tf_op jit(solution)/shard_map/ppermute | solution.py:170
  186.8 5.1 %collective-permute-start.19 = (f32[5,4]{1,0:T(8,128)S(1)}, f32[5,4]{1,0:T(8,128)S(1)}, u32[]{:S(2)}, u32[]{:S(2)}) collective-permute-start(f32[5,4]{1,0:T(8,128)S(1)} %add.265), channel_id=1, source_target_pairs={{0,64},{4,68},{8,72},{12,76},{16,80},{20,84},{24,88},{28,92},{32,9... | collective-permute-start | bytes 248 | tf_op jit(solution)/shard_map/ppermute | solution.py:170
  187.6 42.4 %collective-permute-start.7 = (bf16[256,768]{1,0:T(8,128)(2,1)}, bf16[256,768]{1,0:T(8,128)(2,1)}, u32[]{:S(2)}, u32[]{:S(2)}) collective-permute-start(bf16[256,768]{1,0:T(8,128)(2,1)} %get-tuple-element.11), channel_id=1, source_target_pairs={{0,3},{1,2},{2,1},{3,0},{4,7},{5,6},{6,5},{7,4},{8,11},{9,10},{10,... | collective-permute-start | bytes 1179656 | tf_op jit(solution)/shard_map/ppermute | solution.py:170
  191.9 4.2 %collective-permute-start.20 = (f32[5,4]{1,0:T(8,128)S(1)}, f32[5,4]{1,0:T(8,128)S(1)}, u32[]{:S(2)}, u32[]{:S(2)}) collective-permute-start(f32[5,4]{1,0:T(8,128)S(1)} %add.266), channel_id=1, source_target_pairs={{0,1},{1,0},{2,3},{3,2},{4,5},{5,4},{6,7},{7,6},{8,9},{9,8},{10,11... | collective-permute-start | bytes 248 | tf_op jit(solution)/shard_map/ppermute | solution.py:170
  193.4 38.1 %collective-permute-start.6 = (bf16[256,768]{1,0:T(8,128)(2,1)}, bf16[256,768]{1,0:T(8,128)(2,1)}, u32[]{:S(2)}, u32[]{:S(2)}) collective-permute-start(bf16[256,768]{1,0:T(8,128)(2,1)} %get-tuple-element.12), channel_id=1, source_target_pairs={{0,2},{1,3},{2,0},{3,1},{4,6},{5,7},{6,4},{7,5},{8,10},{9,11},{10,... | collective-permute-start | bytes 1179656 | tf_op jit(solution)/shard_map/ppermute | solution.py:170
  196.2 11.1 %collective-permute-start.21 = (f32[5,4]{1,0:T(8,128)S(1)}, f32[5,4]{1,0:T(8,128)S(1)}, u32[]{:S(2)}, u32[]{:S(2)}) collective-permute-start(f32[5,4]{1,0:T(8,128)S(1)} %add.267), channel_id=1, source_target_pairs={{0,2},{1,3},{2,0},{3,1},{4,6},{5,7},{6,4},{7,5},{8,10},{9,11},{10,... | collective-permute-start | bytes 248 | tf_op jit(solution)/shard_map/ppermute | solution.py:170
  198.7 32.9 %collective-permute-start.5 = (bf16[256,768]{1,0:T(8,128)(2,1)}, bf16[256,768]{1,0:T(8,128)(2,1)}, u32[]{:S(2)}, u32[]{:S(2)}) collective-permute-start(bf16[256,768]{1,0:T(8,128)(2,1)} %get-tuple-element.10), channel_id=1, source_target_pairs={{0,1},{1,0},{2,3},{3,2},{4,5},{5,4},{6,7},{7,6},{8,9},{9,8},{10,11... | collective-permute-start | bytes 1179656 | tf_op jit(solution)/shard_map/ppermute | solution.py:170
  207.3 18.8 %collective-permute-start.10 = (bf16[4,120,256]{2,1,0:T(8,128)(2,1)}, bf16[4,120,256]{2,1,0:T(8,128)(2,1)}, u32[]{:S(2)}, u32[]{:S(2)}) collective-permute-start(bf16[4,120,256]{2,1,0:T(8,128)(2,1)} %get-tuple-element.15), channel_id=1, source_target_pairs={{0,64},{4,68},{8,72},{12,76},{16,80},{20,84},{24,88},{28,92},{32,9... | collective-permute-start | bytes 737288 | tf_op jit(solution)/shard_map/ppermute | solution.py:170
  208.1 0.7 copy-start.22
  208.8 17.3 %collective-permute-start.9 = (bf16[4,120,256]{2,1,0:T(8,128)(2,1)}, bf16[4,120,256]{2,1,0:T(8,128)(2,1)}, u32[]{:S(2)}, u32[]{:S(2)}) collective-permute-start(bf16[4,120,256]{2,1,0:T(8,128)(2,1)} %get-tuple-element.13), channel_id=1, source_target_pairs={{0,32},{4,36},{8,40},{12,44},{16,48},{20,52},{24,56},{28,60},{32,0... | collective-permute-start | bytes 737288 | tf_op jit(solution)/shard_map/ppermute | solution.py:170
  210.7 15.4 %copy-start.23 = (bf16[4,120,256]{2,1,0:T(8,128)(2,1)S(1)}, bf16[4,120,256]{2,1,0:T(8,128)(2,1)}, u32[]{:S(2)}) copy-start(bf16[4,120,256]{2,1,0:T(8,128)(2,1)} %copy-done.22) | copy-start | bytes 737284
  227.4 6.6 %collective-permute-start.14 = (bf16[120,256]{1,0:T(8,128)(2,1)S(1)}, bf16[120,256]{1,0:T(8,128)(2,1)S(1)}, u32[]{:S(2)}, u32[]{:S(2)}) collective-permute-start(bf16[120,256]{1,0:T(8,128)(2,1)S(1)} %get-tuple-element.17), channel_id=1, source_target_pairs={{0,24},{4,28},{8,16},{12,20},{16,8},{20,12},{24,0},{28,4},{32,56},... | collective-permute-start | bytes 184328 | tf_op jit(solution)/shard_map/ppermute | solution.py:170
  228.2 5.8 %collective-permute-start.13 = (bf16[120,256]{1,0:T(8,128)(2,1)S(1)}, bf16[120,256]{1,0:T(8,128)(2,1)S(1)}, u32[]{:S(2)}, u32[]{:S(2)}) collective-permute-start(bf16[120,256]{1,0:T(8,128)(2,1)S(1)} %get-tuple-element.18), channel_id=1, source_target_pairs={{0,16},{4,20},{8,24},{12,28},{16,0},{20,4},{24,8},{28,12},{32,48},... | collective-permute-start | bytes 184328 | tf_op jit(solution)/shard_map/ppermute | solution.py:170
  230.0 4.4 %collective-permute-start.12 = (bf16[120,256]{1,0:T(8,128)(2,1)S(1)}, bf16[120,256]{1,0:T(8,128)(2,1)S(1)}, u32[]{:S(2)}, u32[]{:S(2)}) collective-permute-start(bf16[120,256]{1,0:T(8,128)(2,1)S(1)} %get-tuple-element.16), channel_id=1, source_target_pairs={{0,8},{4,12},{8,0},{12,4},{16,24},{20,28},{24,16},{28,20},{32,40},... | collective-permute-start | bytes 184328 | tf_op jit(solution)/shard_map/ppermute | solution.py:170

commit v2 on v1

v2 whole, which is shorter than its diff:
```python
import jax
import jax.numpy as jnp
from jax import lax
from jax.experimental import pallas as pl
from jax.experimental.pallas import tpu as pltpu
from jax.sharding import PartitionSpec as P

BLK = 128
F32 = jnp.float32
BF16 = jnp.bfloat16
VMEM_LIMIT = 48 * 1024 * 1024


def params():
    return pltpu.CompilerParams(vmem_limit_bytes=VMEM_LIMIT)


def whole(shape):
    return pl.BlockSpec(shape, lambda *_: (0,) * len(shape))


def tile_grads(tile_ids, dest_ids, rels, adjacency, grads, shards, chunk=16):
    tiles = adjacency.shape[0]
    nblocks, _, width = grads.shape
    slots = rels.shape[0]
    capacity = slots // shards
    rows = capacity * BLK + 8

    def kernel(slot_ref, dst_ref, rel_ref, adj_ref, grad_ref, out_ref, acc_ref):
        step = pl.program_id(0)

        @pl.when(step == 0)
        def _():
            acc_ref[...] = jnp.zeros_like(acc_ref)

        for u in range(chunk):
            t = step * chunk + u
            part = lax.dot_general(
                adj_ref[u],
                grad_ref[dst_ref[t]],
                (((0,), (0,)), ((), ())),
                preferred_element_type=F32,
            )
            acc_ref[slot_ref[t]] += part

        @pl.when(step == pl.num_programs(0) - 1)
        def _():
            row = lax.broadcasted_iota(jnp.int32, (8, width), 0)
            for o in range(shards):
                tail = jnp.zeros((8, width), F32)
                for c in range(capacity):
                    s = o * capacity + c
                    out_ref[o, pl.ds(c * BLK, BLK), :] = acc_ref[s].astype(BF16)
                    tail = jnp.where(row == c, rel_ref[s].astype(F32), tail)
                out_ref[o, pl.ds(capacity * BLK, 8), :] = tail.astype(BF16)

    return pl.pallas_call(
        kernel,
        name="tile_grads",
        out_shape=jax.ShapeDtypeStruct((shards, rows, width), BF16),
        grid_spec=pltpu.PrefetchScalarGridSpec(
            num_scalar_prefetch=3,
            grid=(tiles // chunk,),
            in_specs=[
                pl.BlockSpec((chunk, BLK, BLK), lambda i, *_: (i, 0, 0)),
                whole(grads.shape),
            ],
            out_specs=whole((shards, rows, width)),
            scratch_shapes=[pltpu.VMEM((slots, BLK, width), F32)],
        ),
        compiler_params=params(),
    )(tile_ids, dest_ids, rels, adjacency, grads)


def dense_tiles(tile_ids, dest_ids, adjacency, slots, nblocks, chunk=16, halves=2):
    tiles = adjacency.shape[0]
    per = nblocks // halves

    def kernel(slot_ref, dst_ref, adj_ref, out_ref, acc_ref):
        half = pl.program_id(0)
        step = pl.program_id(1)

        @pl.when(step == 0)
        def _():
            acc_ref[...] = jnp.zeros_like(acc_ref)

        for u in range(chunk):
            t = step * chunk + u
            local = dst_ref[t] - half * per

            @pl.when((local >= 0) & (local < per))
            def _():
                acc_ref[local, slot_ref[t]] += adj_ref[u].astype(F32)

        @pl.when(step == pl.num_programs(1) - 1)
        def _():
            def store(s, carry):
                for b in range(per):
                    out_ref[pl.ds(b * BLK, BLK), pl.ds(pl.multiple_of(s * BLK, BLK), BLK)] = (
                        acc_ref[b, s].astype(BF16)
                    )
                return carry

            lax.fori_loop(0, slots, store, 0)

    return pl.pallas_call(
        kernel,
        name="dense_tiles",
        out_shape=jax.ShapeDtypeStruct((nblocks * BLK, slots * BLK), BF16),
        grid_spec=pltpu.PrefetchScalarGridSpec(
            num_scalar_prefetch=2,
            grid=(halves, tiles // chunk),
            in_specs=[pl.BlockSpec((chunk, BLK, BLK), lambda h, i, *_: (i, 0, 0))],
            out_specs=pl.BlockSpec((per * BLK, slots * BLK), lambda h, i, *_: (h, 0)),
            scratch_shapes=[pltpu.VMEM((per, slots, BLK, BLK), F32)],
        ),
        compiler_params=params(),
    )(tile_ids, dest_ids, adjacency)


def project(feats, rel_weights, nblocks):
    relations, _, width = rel_weights.shape

    def kernel(feat_ref, w_ref, out_ref):
        for b in range(nblocks):
            out_ref[b] = jnp.dot(
                feat_ref[pl.ds(b * BLK, BLK), :], w_ref[0], preferred_element_type=F32
            ).astype(BF16)

    return pl.pallas_call(
        kernel,
        name="project",
        out_shape=jax.ShapeDtypeStruct((relations * nblocks, BLK, width), BF16),
        grid=(relations,),
        in_specs=[
            whole(feats.shape),
            pl.BlockSpec((1,) + rel_weights.shape[1:], lambda r: (r, 0, 0)),
        ],
        out_specs=pl.BlockSpec((nblocks, BLK, width), lambda r: (r, 0, 0)),
        compiler_params=params(),
    )(feats, rel_weights)


def select_blocks(keys, blocks, chunk=16):
    slots = keys.shape[0]
    _, rows, width = blocks.shape

    def kernel(key_ref, in_ref, out_ref):
        step = pl.program_id(0)
        for u in range(chunk):
            out_ref[u] = in_ref[key_ref[step * chunk + u]]

    return pl.pallas_call(
        kernel,
        name="select_blocks",
        out_shape=jax.ShapeDtypeStruct((slots, rows, width), BF16),
        grid_spec=pltpu.PrefetchScalarGridSpec(
            num_scalar_prefetch=1,
            grid=(slots // chunk,),
            in_specs=[whole(blocks.shape)],
            out_specs=pl.BlockSpec((chunk, rows, width), lambda i, *_: (i, 0, 0)),
        ),
        compiler_params=params(),
    )(keys, blocks)


def sum_by_key(keys, returned, bins, capacity, chunk=4):
    shards, rows, width = returned.shape

    def kernel(key_ref, ret_ref, out_ref, acc_ref):
        step = pl.program_id(0)

        @pl.when(step == 0)
        def _():
            acc_ref[...] = jnp.zeros_like(acc_ref)

        for u in range(chunk):
            for c in range(capacity):
                key = key_ref[(step * chunk + u) * capacity + c]
                acc_ref[key] += ret_ref[u, pl.ds(c * BLK, BLK), :].astype(F32)

        @pl.when(step == pl.num_programs(0) - 1)
        def _():
            out_ref[...] = acc_ref[...].astype(BF16)

    return pl.pallas_call(
        kernel,
        name="sum_by_key",
        out_shape=jax.ShapeDtypeStruct((bins, BLK, width), BF16),
        grid_spec=pltpu.PrefetchScalarGridSpec(
            num_scalar_prefetch=1,
            grid=(shards // chunk,),
            in_specs=[pl.BlockSpec((chunk, rows, width), lambda i, *_: (i, 0, 0))],
            out_specs=whole((bins, BLK, width)),
            scratch_shapes=[pltpu.VMEM((bins, BLK, width), F32)],
        ),
        compiler_params=params(),
    )(keys, returned)


def weight_grads(coef, feats, source_grads, d_out, bases, chunk=128):
    relations, nodes, width = source_grads.shape
    nbase, width_in, _ = bases.shape

    def kernel(coef_ref, feat_ref, src_ref, grad_ref, base_ref, out_ref, dots_ref):
        @pl.when(pl.program_id(0) == 0)
        def _():
            dots_ref[...] = jnp.zeros_like(dots_ref)

        cols = feat_ref[...].T
        for r in range(relations):
            g = jnp.dot(cols, src_ref[r], preferred_element_type=F32)
            for b in range(nbase):
                scaled = coef_ref[r * nbase + b] * g
                if r == 0:
                    out_ref[b] = scaled
                else:
                    out_ref[b] += scaled
                prod = g * base_ref[b].astype(F32)
                dots_ref[r * nbase + b] += jnp.sum(prod.reshape(-1, 8, width), axis=0)
        out_ref[nbase] = jnp.dot(cols, grad_ref[...], preferred_element_type=F32)

    return pl.pallas_call(
        kernel,
        name="weight_grads",
        out_shape=(
            jax.ShapeDtypeStruct((nbase + 1, width_in, width), F32),
            jax.ShapeDtypeStruct((relations * nbase, 8, width), F32),
        ),
        grid_spec=pltpu.PrefetchScalarGridSpec(
            num_scalar_prefetch=1,
            grid=(width_in // chunk,),
            in_specs=[
                pl.BlockSpec((nodes, chunk), lambda i, *_: (0, i)),
                whole(source_grads.shape),
                whole(d_out.shape),
                pl.BlockSpec((nbase, chunk, width), lambda i, *_: (0, i, 0)),
            ],
            out_specs=(
                pl.BlockSpec((nbase + 1, chunk, width), lambda i, *_: (0, i, 0)),
                whole((relations * nbase, 8, width)),
            ),
        ),
        compiler_params=params(),
    )(coef, feats, source_grads, d_out, bases)


def exchange(x, axis, mask):
    return lax.ppermute(x, axis, [(i, i ^ mask) for i in range(lax.axis_size(axis))])


def chunk_of(x, at, dim):
    return lax.dynamic_index_in_dim(x, at, dim, keepdims=False)


def scatter_sum(x, axis, shift, size, me, dim=0):
    at = (me >> shift) & (size - 1)
    total = chunk_of(x, at, dim)
    for k in range(1, size):
        part = chunk_of(x, at ^ k, dim).astype(BF16)
        total = total + exchange(part, axis, k << shift).astype(F32)
    return total


def scatter_sum_with(x, extra, axis, shift, size, me, dim):
    at = (me >> shift) & (size - 1)
    total = chunk_of(x, at, dim)
    width = x.shape[-1]
    count = extra.shape[0]
    high = lax.reduce_precision(extra, 8, 7)
    low = lax.reduce_precision(extra - high, 8, 7)
    line = jnp.concatenate([high, low, jnp.zeros((width - 2 * count,), F32)])
    lines = jnp.where(jnp.arange(8)[:, None] == 0, line[None], 0.0).astype(BF16)
    sums = [high + low]
    for k in range(1, size):
        part = chunk_of(x, at ^ k, dim).astype(BF16)
        sent = jnp.concatenate([part.reshape(-1, width), lines], axis=0)
        got = exchange(sent, axis, k << shift)
        total = total + got[:-8].reshape(part.shape).astype(F32)
        last = got[-8].astype(F32)
        sums.append(last[:count] + last[count : 2 * count])
    while len(sums) > 1:
        sums = [sums[i] + sums[i + 1] for i in range(0, len(sums), 2)]
    return total, sums[0]


def body(
    feats, bases, coef, root_weight, slot_block, recv_rel, tile_slot, tile_dst, tile_adj, d_out
):
    shards = lax.axis_size("shard")
    reps = lax.axis_size("rep")
    me = lax.axis_index("shard")
    my_rep = lax.axis_index("rep")
    nblocks = feats.shape[0] // BLK
    width_in = feats.shape[1]
    width = root_weight.shape[1]
    relations, nbase = coef.shape
    capacity = slot_block.shape[2]
    slots = shards * capacity

    slot_grads = tile_grads(
        tile_slot[0],
        tile_dst[0],
        recv_rel.reshape(slots),
        tile_adj[0],
        d_out.reshape(nblocks, BLK, width),
        shards,
    )
    returned = lax.all_to_all(slot_grads, "shard", 0, 0, tiled=True)

    rel_weights = (
        jnp.dot(coef, bases.reshape(nbase, -1), preferred_element_type=F32)
        .astype(BF16)
        .reshape(relations, width_in, width)
    )
    projected = project(feats, rel_weights, nblocks)
    root_term = jnp.dot(feats, root_weight, preferred_element_type=F32)
    dense = dense_tiles(tile_slot[0], tile_dst[0], tile_adj[0], slots, nblocks)

    owner_rel = returned[:, capacity * BLK : capacity * BLK + capacity, 0].astype(jnp.int32)
    keys = (owner_rel * nblocks + slot_block[0]).reshape(-1)
    outgoing = select_blocks(keys, projected)
    incoming = lax.all_to_all(
        outgoing.reshape(shards, capacity * BLK, width), "shard", 0, 0, tiled=True
    )

    source_grads = sum_by_key(keys, returned, relations * nblocks, capacity)
    source_grads = source_grads.reshape(relations, nblocks * BLK, width)
    stacked, dots = weight_grads(
        coef.astype(F32).reshape(-1), feats, source_grads, d_out, bases
    )
    dots = jnp.sum(dots, axis=(1, 2))
    dots = dots + exchange(dots, "shard", 1)
    for step in (1, 2):
        dots = dots + exchange(dots, "rep", step)

    rows = width_in // shards
    part = scatter_sum(
        stacked.reshape(nbase + 1, shards // 2, 2, rows, width), "shard", 0, 2, me, dim=2
    )
    part = part.reshape(nbase + 1, 4, shards // 8, rows, width)
    part, dots = scatter_sum_with(part, dots, "shard", 3, 4, me, dim=1)
    reduced, dots = scatter_sum_with(part, dots, "shard", 1, 4, me, dim=1)
    grad_bases = reduced[:nbase]
    grad_root = reduced[nbase]
    grad_coef = dots.reshape(relations, nbase)

    through = jnp.einsum("rno,rco->nc", source_grads, rel_weights, preferred_element_type=F32)
    through = through + jnp.dot(d_out, root_weight.T, preferred_element_type=F32)
    grad_feats = scatter_sum(
        through.reshape(reps, -1, width_in), "rep", 0, reps, my_rep
    ).astype(BF16)

    output = (
        jnp.dot(dense, incoming.reshape(slots * BLK, width), preferred_element_type=F32)
        + root_term
    ).astype(BF16)
    return (output, grad_feats, grad_bases, grad_root, grad_coef)


def solution(mesh):
    placed = (
        P("shard", None),
        P(None, None, "rep"),
        P(),
        P(None, "rep"),
        P("shard", None, None),
        P("shard", None, None),
        P("shard", None),
        P("shard", None),
        P("shard", None, None, None),
        P("shard", "rep"),
    )
    return jax.shard_map(
        body,
        mesh=mesh,
        in_specs=placed,
        out_specs=(
            P("shard", "rep"),
            P(("shard", "rep"), None),
            P(None, "shard", "rep"),
            P("shard", "rep"),
            P(),
        ),
        check_vma=False,
    )
```

time: 237 us -> 222 us (0.937)
  other arithmetic: 34.6 us -> 7.55 us
  Pallas kernels: 41.2 us -> 67.3 us
  local copies, waits for them, and re-layouts: 40.7 us -> 20.2 us
  waiting for transfers between devices: 61.1 us -> 72.7 us
  starting transfers between devices: 43.7 us -> 33.3 us
  matrix products: 13.3 us -> 19.1 us
    pallas_call x2 -> x4, Pallas kernels: 20.7 us -> 46.8 us  [the longest x1 32.5 us: dense_tiles(): pl.pallas_call(kernel, name='dense_tiles', out_shape=jax.ShapeDtypeStruct...]
    add x13 -> x6, other arithmetic: 25.4 us -> 0.91 us  [the longest x1 0.66 us: body(): keys = (owner_rel * nblocks + slot_block[0]).reshape(-1)]
    ppermute x22 -> x13, starting transfers between devices: 29.5 us -> 17.9 us  [exchange(): lax.ppermute(x, axis, [(i, i ^ mask) for i in range(lax.axis_size(axis))])]
    all_to_all x1, waiting for transfers between devices: 0.01 us -> 11.1 us  [body(): returned = lax.all_to_all(slot_grads, 'shard', 0, 0, tiled=True)]
    add x4 -> x0, local copies, waits for them, and re-layouts: 9.25 us -> none  [body(): sum((wide_coef[r, b] * relation_grads[r] for r in range(relations)))]
    unnamed x63 -> x43, local copies, waits for them, and re-layouts: 19.7 us -> 14.2 us
    transpose x1 -> x0, local copies, waits for them, and re-layouts: 5.47 us -> none  [body(): jnp.einsum('nc,rno->rco', feats, source_grads, preferred_element_type=F32)]
    dot_general x2 -> x1, matrix products: 5.62 us -> 9.31 us  [body(): jnp.dot(dense, incoming.reshape(slots * BLK, width), preferred_element_ty...]
  transfers between devices with their start and end apart: 24 -> 15, of which waited for: 8 -> 6; matrix products, arithmetic and copies ran while one was open for 32% -> 9% of each run, Pallas kernels for 11% -> 17%
where the time goes in v2:
time: 222 us; the launch traced here: 221 us
  waiting for transfers between devices  72.7 us (33%)
  Pallas kernels  67.3 us (30%)
  starting transfers between devices  33.3 us (15%)
  local copies, waits for them, and re-layouts  20.2 us (9%)
  matrix products  19.1 us (9%)
  other arithmetic  7.55 us (3%)
    ppermute x13, waiting for transfers between devices, exchange(): lax.ppermute(x, axis, [(i, i ^ mask) for i in range(lax.axis_size(axis))])  61.6 us
    pallas_call x1, Pallas kernels, dense_tiles(): pl.pallas_call(kernel, name='dense_tiles', out_shape=jax.ShapeDtypeStruct...  32.5 us
    ppermute x13, starting transfers between devices, exchange(): lax.ppermute(x, axis, [(i, i ^ mask) for i in range(lax.axis_size(axis))])  17.9 us
    pallas_call x1, Pallas kernels, tile_grads(): pl.pallas_call(kernel, name='tile_grads', out_shape=jax.ShapeDtypeStruct(...  14.5 us
    unnamed x43, local copies, waits for them, and re-layouts  14.2 us
    all_to_all x1, waiting for transfers between devices, body(): returned = lax.all_to_all(slot_grads, 'shard', 0, 0, tiled=True)  11.1 us
    dot_general x1, matrix products, body(): jnp.dot(dense, incoming.reshape(slots * BLK, width), preferred_element_ty...  9.31 us
    all_to_all x1, starting transfers between devices, body(): returned = lax.all_to_all(slot_grads, 'shard', 0, 0, tiled=True)  8.66 us
  transfers between devices with their start and end apart: 15, of which 6 were waited for; matrix products, arithmetic and copies ran while one was open for 9% of the time, Pallas kernels for 17%

profile of v2, /device:TPU:0, one launch (start us, length us, event | category | flops | bytes accessed | tf_op | source)
XLA Modules:
  0.0 221.1 jit_solution(16021679588552601135)
XLA Ops:
  0.6 0.8 copy.26
  1.5 0.1 reshape.127.rel_ref
  1.6 1.0 copy-done.8
  2.6 0.7 copy-done.12
  3.3 0.7 copy-done.14
  4.0 14.5 %tile_grads.1 = bf16[32,264,256]{2,1,0:T(8,128)(2,1)S(1)} custom-call(s32[256]{0:T(256)S(1)} %bitcast.104, s32[256]{0:T(256)S(1)} %bitcast.106, s32[64]{0:T(128)S(1)} %reshape.127.rel_ref, bf16[256,128,128]{2,1,0:T(8,128)(2,1)} %bitcast.108, bf16[8,128,256]{2,1,0:T(8,128)(2,1)S(1)} %bitcast.103), custom_call_target="tpu_custom_call" | custom-call | tf_op jit(solution)/shard_map/tile_grads/pallas_call | solution.py:57
  18.4 2.0 copy-done.1
  20.5 8.7 %all-to-all-start = ((bf16[32,264,256]{2,1,0:T(8,128)(2,1)}), bf16[32,264,256]{2,1,0:T(8,128)(2,1)}, u32[]{:S(2)}, u32[]{:S(2)}) async-start(bf16[32,264,256]{2,1,0:T(8,128)(2,1)} %copy-done.1), calls=%async_computation | async-start | bytes 8650752 | tf_op jit(solution)/shard_map/all_to_all | solution.py:309
  29.3 32.5 %dense_tiles.1 = bf16[1024,8192]{1,0:T(8,128)(2,1)} custom-call(s32[256]{0:T(256)S(1)} %bitcast.105, s32[256]{0:T(256)S(1)} %bitcast.107, bf16[256,128,128]{2,1,0:T(8,128)(2,1)} %bitcast.109), custom_call_target="tpu_custom_call" | custom-call | tf_op jit(solution)/shard_map/dense_tiles/pallas_call | solution.py:106
  61.7 0.1 copy.28
  61.8 0.1 reshape.141.coef_ref
  61.9 0.1 copy.27
  62.0 0.1 squeeze.54
  62.1 1.2 copy.40
  63.3 1.3 convolution_convert_fusion
  64.7 1.7 copy.47
  66.5 1.5 copy-done.6
  68.0 3.0 %project.1.in_ref = bf16[40,128,256]{2,1,0:T(8,128)(2,1)S(1)} custom-call(bf16[1024,768]{1,0:T(8,128)(2,1)S(1)} %copy-done.2, bf16[5,768,256]{2,1,0:T(8,128)(2,1)S(1)} %bitcast.101), custom_call_target="tpu_custom_call" | custom-call | tf_op jit(solution)/shard_map/project/pallas_call | solution.py:130
  71.0 1.4 copy-done.4
  72.4 11.1 %all-to-all-done.ret_ref = bf16[32,264,256]{2,1,0:T(8,128)(2,1)} async-done(((bf16[32,264,256]{2,1,0:T(8,128)(2,1)}), bf16[32,264,256]{2,1,0:T(8,128)(2,1)}, u32[]{:S(2)}, u32[]{:S(2)}) %all-to-all-start) | async-done | bytes 4325408 | tf_op jit(solution)/shard_map/all_to_all | solution.py:309
  83.5 2.1 multiply_reduce_fusion
  85.6 1.3 mul.12
  86.9 0.7 add.153.key_ref
  87.5 6.0 %sum_by_key.1 = bf16[40,128,256]{2,1,0:T(8,128)(2,1)S(1)} custom-call(s32[64]{0:T(128)S(1)} %add.153.key_ref, bf16[32,264,256]{2,1,0:T(8,128)(2,1)} %all-to-all-done.ret_ref), custom_call_target="tpu_custom_call" | custom-call | tf_op jit(solution)/shard_map/sum_by_key/pallas_call | solution.py:186
  93.6 1.5 copy-done.3
  95.1 8.2 %weight_grads.1 = (f32[5,768,256]{2,1,0:T(8,128)}, f32[20,8,256]{2,1,0:T(8,128)S(1)}) custom-call(f32[20]{0:T(128)S(1)} %reshape.141.coef_ref, bf16[1024,768]{1,0:T(8,128)(2,1)S(1)} %copy-done.2, bf16[5,1024,256]{2,1,0:T(8,128)(2,1)} %bitcast.98, bf16[1024,256]{1,0:T(8,128)(2,1)S(1)} %copy-done.9, bf16[4,768,256]{2,1,0:T(8,128)(2,1)S(1)} %copy-done.7), custom_call_target="tpu_custom_call" | custom-call | tf_op jit(solution)/shard_map/weight_grads/pallas_call | solution.py:223
  103.3 0.7 copy-done.11
  104.0 1.1 reduce_sum.9
  105.2 2.6 %fusion.1 = bf16[5,16,24,256]{3,2,1,0:T(8,128)(2,1)} fusion(f32[5,16,2,24,256]{4,3,2,1,0:T(8,128)} %bitcast.117, s32[]{:T(128)S(6)} %select_n.58), kind=kLoop, calls=%fused_computation.7 | loop fusion | bytes 1966084 | tf_op jit(solution)/shard_map/convert_element_type | solution.py:260
  107.9 0.5 collective-permute-start.3
  108.3 6.4 %fusion.21 = f32[1024,768,1]{1,0,2:T(8,128)} fusion(bf16[5,1024,256]{2,1,0:T(8,128)(2,1)} %bitcast.99, bf16[5,768,256]{2,1,0:T(8,128)(2,1)} %bitcast.100), kind=kOutput, calls=%fused_computation.69 | convolution fusion | flops 2013265920 | bytes 7733248 | tf_op jit(solution)/shard_map/rno,rco->nc/dot_general | solution.py:348
  114.8 1.5 collective-permute-start.5
  116.3 3.1 %select_blocks.1 = bf16[64,128,256]{2,1,0:T(8,128)(2,1)} custom-call(s32[64]{0:T(128)S(1)} %add.153.key_ref, bf16[40,128,256]{2,1,0:T(8,128)(2,1)S(1)} %copy-done.5), custom_call_target="tpu_custom_call" | custom-call | tf_op jit(solution)/shard_map/select_blocks/pallas_call | solution.py:153
  119.4 2.7 %collective-permute-start.6 = (f32[20]{0:T(128)S(1)}, f32[20]{0:T(128)S(1)}, u32[]{:S(2)}, u32[]{:S(2)}) collective-permute-start(f32[20]{0:T(128)S(1)} %add.169), channel_id=1, source_target_pairs={{0,2},{1,3},{2,0},{3,1},{4,6},{5,7},{6,4},{7,5},{8,10},{9,11},{10,... | collective-permute-start | bytes 248 | tf_op jit(solution)/shard_map/ppermute | solution.py:249
  122.2 6.7 %all-to-all-start.1 = ((bf16[32,256,256]{2,1,0:T(8,128)(2,1)}), bf16[32,256,256]{2,1,0:T(8,128)(2,1)}, u32[]{:S(2)}, u32[]{:S(2)}) async-start(bf16[32,256,256]{2,1,0:T(8,128)(2,1)} %bitcast.110), calls=%async_computation.1 | async-start | bytes 8388608 | tf_op jit(solution)/shard_map/all_to_all | solution.py:323
  128.9 0.1 pad_maximum_fusion.7
  129.1 2.0 bitcast_add_fusion.1
  131.1 0.1 bitcast_convert_fusion.2
  131.2 1.8 collective-permute-start.7
  133.0 2.7 %collective-permute-start.8 = (bf16[488,256]{1,0:T(8,128)(2,1)S(1)}, bf16[488,256]{1,0:T(8,128)(2,1)S(1)}, u32[]{:S(2)}, u32[]{:S(2)}) collective-permute-start(bf16[488,256]{1,0:T(8,128)(2,1)S(1)} %get-tuple-element.34), channel_id=1, source_target_pairs={{0,64},{4,68},{8,72},{12,76},{16,80},{20,84},{24,88},{28,92},{32,9... | collective-permute-start | bytes 749576 | tf_op jit(solution)/shard_map/ppermute | solution.py:249
  135.8 0.3 collective-permute-start.9
  136.0 0.6 bitcast_add_fusion
  136.7 0.1 fusion.7
  136.8 0.3 collective-permute-start
  137.1 1.1 collective-permute-start.2
  138.2 48.2 %collective-permute-done.7 = bf16[488,256]{1,0:T(8,128)(2,1)S(1)} collective-permute-done((bf16[488,256]{1,0:T(8,128)(2,1)S(1)}, bf16[488,256]{1,0:T(8,128)(2,1)S(1)}, u32[]{:S(2)}, u32[]{:S(2)}) %collective-permute-start.7) | collective-permute-done | bytes 249888 | tf_op jit(solution)/shard_map/ppermute | solution.py:249
  186.4 0.8 collective-permute-start.1
  187.3 5.3 %collective-permute-done.8 = bf16[488,256]{1,0:T(8,128)(2,1)S(1)} collective-permute-done((bf16[488,256]{1,0:T(8,128)(2,1)S(1)}, bf16[488,256]{1,0:T(8,128)(2,1)S(1)}, u32[]{:S(2)}, u32[]{:S(2)}) %collective-permute-start.8) | collective-permute-done | bytes 249888 | tf_op jit(solution)/shard_map/ppermute | solution.py:249
  192.6 0.1 fusion.6
  192.8 0.1 fusion.18
  192.9 0.1 pad_maximum_fusion.6
  193.1 2.4 %collective-permute-start.10 = (bf16[128,256]{1,0:T(8,128)(2,1)S(1)}, bf16[128,256]{1,0:T(8,128)(2,1)S(1)}, u32[]{:S(2)}, u32[]{:S(2)}) collective-permute-start(bf16[128,256]{1,0:T(8,128)(2,1)S(1)} %get-tuple-element.30), channel_id=1, source_target_pairs={{0,8},{4,12},{8,0},{12,4},{16,24},{20,28},{24,16},{28,20},{32,40},... | collective-permute-start | bytes 196616 | tf_op jit(solution)/shard_map/ppermute | solution.py:249
  195.5 2.6 %collective-permute-done.1 = bf16[256,768]{1,0:T(8,128)(2,1)S(1)} collective-permute-done((bf16[256,768]{1,0:T(8,128)(2,1)S(1)}, bf16[256,768]{1,0:T(8,128)(2,1)S(1)}, u32[]{:S(2)}, u32[]{:S(2)}) %collective-permute-start.1) | collective-permute-done | bytes 393248 | tf_op jit(solution)/shard_map/ppermute | solution.py:249
  198.1 1.0 fusion.4
  199.1 3.7 %collective-permute-start.11 = (bf16[128,256]{1,0:T(8,128)(2,1)S(1)}, bf16[128,256]{1,0:T(8,128)(2,1)S(1)}, u32[]{:S(2)}, u32[]{:S(2)}) collective-permute-start(bf16[128,256]{1,0:T(8,128)(2,1)S(1)} %get-tuple-element.31), channel_id=1, source_target_pairs={{0,16},{4,20},{8,24},{12,28},{16,0},{20,4},{24,8},{28,12},{32,48},... | collective-permute-start | bytes 196616 | tf_op jit(solution)/shard_map/ppermute | solution.py:249
  202.8 2.3 %collective-permute-done.11 = bf16[128,256]{1,0:T(8,128)(2,1)S(1)} collective-permute-done((bf16[128,256]{1,0:T(8,128)(2,1)S(1)}, bf16[128,256]{1,0:T(8,128)(2,1)S(1)}, u32[]{:S(2)}, u32[]{:S(2)}) %collective-permute-start.11) | collective-permute-done | bytes 65568 | tf_op jit(solution)/shard_map/ppermute | solution.py:249
  205.1 3.2 %collective-permute-done.12 = bf16[128,256]{1,0:T(8,128)(2,1)S(1)} collective-permute-done((bf16[128,256]{1,0:T(8,128)(2,1)S(1)}, bf16[128,256]{1,0:T(8,128)(2,1)S(1)}, u32[]{:S(2)}, u32[]{:S(2)}) %collective-permute-start.12) | collective-permute-done | bytes 65568 | tf_op jit(solution)/shard_map/ppermute | solution.py:249
  208.3 0.1 fusion.13
  208.3 0.1 reshape.139
  208.4 0.7 copy.36
  209.2 0.6 slice.136
  209.8 0.6 slice_bitcast_fusion
  210.4 9.3 %fusion.20 = f32[1024,256]{1,0:T(8,128)S(1)} fusion(bf16[1024,8192]{1,0:T(8,128)(2,1)} %dense_tiles.1, bf16[8192,256]{1,0:T(8,128)(2,1)} %bitcast.5), kind=kOutput, calls=%fused_computation.68 | convolution fusion | flops 4294967296 | bytes 22020096 | tf_op jit(solution)/shard_map/dot_general | solution.py:355
  219.7 1.4 fusion
  (65 shorter events, 0.6 us)
Async XLA Ops:
  0.6 135.4 %copy-start = (bf16[768,256]{1,0:T(8,128)(2,1)S(1)}, bf16[768,256]{1,0:T(8,128)(2,1)}, u32[]{:S(2)}) copy-start(bf16[768,256]{1,0:T(8,128)(2,1)} %param.13) | copy-start | bytes 1179652
  1.6 1.0 copy-start.8
  2.6 0.7 copy-start.12
  3.3 0.7 copy-start.14
  18.4 2.1 copy-start.1
  20.5 8.7 %copy-start.13 = (s32[1,256]{1,0:T(1,128)S(1)}, s32[1,256]{1,0:T(1,128)}, u32[]{:S(2)}) copy-start(s32[1,256]{1,0:T(1,128)} %param.16) | copy-start | bytes 3076
  20.5 8.7 %copy-start.15 = (s32[1,256]{1,0:T(1,128)S(1)}, s32[1,256]{1,0:T(1,128)}, u32[]{:S(2)}) copy-start(s32[1,256]{1,0:T(1,128)} %param.17) | copy-start | bytes 3076
  20.5 63.0 %all-to-all-start = ((bf16[32,264,256]{2,1,0:T(8,128)(2,1)}), bf16[32,264,256]{2,1,0:T(8,128)(2,1)}, u32[]{:S(2)}, u32[]{:S(2)}) async-start(bf16[32,264,256]{2,1,0:T(8,128)(2,1)} %copy-done.1), calls=%async_computation | async-start | bytes 8650752 | tf_op jit(solution)/shard_map/all_to_all | solution.py:309
  29.2 32.5 %copy-start.17 = (bf16[5,4]{0,1:T(4,128)(2,1)S(1)}, bf16[5,4]{0,1:T(4,128)(2,1)}, u32[]{:S(2)}) copy-start(bf16[5,4]{0,1:T(4,128)(2,1)} %param.12) | copy-start | bytes 124
  29.2 32.7 %copy-start.18 = (s32[1,32,2]{1,2,0:T(2,128)S(1)}, s32[1,32,2]{1,2,0:T(2,128)}, u32[]{:S(2)}) copy-start(s32[1,32,2]{1,2,0:T(2,128)} %param.14) | copy-start | bytes 772
  29.3 32.9 %copy-start.7 = (bf16[4,768,256]{2,1,0:T(8,128)(2,1)S(1)}, bf16[4,768,256]{2,1,0:T(8,128)(2,1)}, u32[]{:S(2)}) copy-start(bf16[4,768,256]{2,1,0:T(8,128)(2,1)} %base_ref.1) | copy-start | bytes 4718596
  64.7 1.8 copy-start.2
  66.4 1.5 copy-start.6
  71.0 1.5 copy-start.4
  87.5 7.5 %copy-start.9 = (bf16[1024,256]{1,0:T(8,128)(2,1)S(1)}, bf16[1024,256]{1,0:T(8,128)(2,1)}, u32[]{:S(2)}) copy-start(bf16[1024,256]{1,0:T(8,128)(2,1)} %grad_ref.1) | copy-start | bytes 1572868
  93.6 1.5 copy-start.3
  103.3 0.7 copy-start.11
  105.1 9.6 %collective-permute-start.4 = (f32[20]{0:T(128)S(1)}, f32[20]{0:T(128)S(1)}, u32[]{:S(2)}, u32[]{:S(2)}) collective-permute-start(f32[20]{0:T(128)S(1)} %reduce_sum.9), channel_id=1, source_target_pairs={{0,4},{4,0},{8,12},{12,8},{16,20},{20,16},{24,28},{28,24},{32,36},... | collective-permute-start | bytes 248 | tf_op jit(solution)/shard_map/ppermute | solution.py:249
  107.9 8.4 %copy-start.5 = (bf16[40,128,256]{2,1,0:T(8,128)(2,1)S(1)}, bf16[40,128,256]{2,1,0:T(8,128)(2,1)}, u32[]{:S(2)}) copy-start(bf16[40,128,256]{2,1,0:T(8,128)(2,1)} %copy-done.4) | copy-start | bytes 7864324
  107.9 21.3 %collective-permute-start.3 = (bf16[5,16,24,256]{3,2,1,0:T(8,128)(2,1)}, bf16[5,16,24,256]{3,2,1,0:T(8,128)(2,1)S(1)}, u32[]{:S(2)}, u32[]{:S(2)}) collective-permute-start(bf16[5,16,24,256]{3,2,1,0:T(8,128)(2,1)} %fusion.1), channel_id=1, source_target_pairs={{0,4},{4,0},{8,12},{12,8},{16,20},{20,16},{24,28},{28,24},{32,36},... | collective-permute-start | bytes 2949128 | tf_op jit(solution)/shard_map/ppermute | solution.py:249
  114.8 4.6 %collective-permute-start.5 = (f32[20]{0:T(128)S(1)}, f32[20]{0:T(128)S(1)}, u32[]{:S(2)}, u32[]{:S(2)}) collective-permute-start(f32[20]{0:T(128)S(1)} %add.168), channel_id=1, source_target_pairs={{0,1},{1,0},{2,3},{3,2},{4,5},{5,4},{6,7},{7,6},{8,9},{9,8},{10,11... | collective-permute-start | bytes 248 | tf_op jit(solution)/shard_map/ppermute | solution.py:249
  119.4 9.5 %collective-permute-start.6 = (f32[20]{0:T(128)S(1)}, f32[20]{0:T(128)S(1)}, u32[]{:S(2)}, u32[]{:S(2)}) collective-permute-start(f32[20]{0:T(128)S(1)} %add.169), channel_id=1, source_target_pairs={{0,2},{1,3},{2,0},{3,1},{4,6},{5,7},{6,4},{7,5},{8,10},{9,11},{10,... | collective-permute-start | bytes 248 | tf_op jit(solution)/shard_map/ppermute | solution.py:249
  122.2 88.3 %all-to-all-start.1 = ((bf16[32,256,256]{2,1,0:T(8,128)(2,1)}), bf16[32,256,256]{2,1,0:T(8,128)(2,1)}, u32[]{:S(2)}, u32[]{:S(2)}) async-start(bf16[32,256,256]{2,1,0:T(8,128)(2,1)} %bitcast.110), calls=%async_computation.1 | async-start | bytes 8388608 | tf_op jit(solution)/shard_map/all_to_all | solution.py:323
  129.1 6.9 %copy-start.10 = (bf16[1024,256]{1,0:T(8,128)(2,1)S(1)}, bf16[1024,256]{1,0:T(8,128)(2,1)}, u32[]{:S(2)}) copy-start(bf16[1024,256]{1,0:T(8,128)(2,1)} %grad_ref.1) | copy-start | bytes 1572868
  129.1 6.9 %copy-start.16 = (f32[1024,768,1]{1,0,2:T(8,128)S(1)}, f32[1024,768,1]{1,0,2:T(8,128)}, u32[]{:S(2)}) copy-start(f32[1024,768,1]{1,0,2:T(8,128)} %fusion.21) | copy-start | bytes 9437188
  131.2 55.2 %collective-permute-start.7 = (bf16[488,256]{1,0:T(8,128)(2,1)S(1)}, bf16[488,256]{1,0:T(8,128)(2,1)S(1)}, u32[]{:S(2)}, u32[]{:S(2)}) collective-permute-start(bf16[488,256]{1,0:T(8,128)(2,1)S(1)} %get-tuple-element.33), channel_id=1, source_target_pairs={{0,32},{4,36},{8,40},{12,44},{16,48},{20,52},{24,56},{28,60},{32,0... | collective-permute-start | bytes 749576 | tf_op jit(solution)/shard_map/ppermute | solution.py:249
  133.0 59.5 %collective-permute-start.8 = (bf16[488,256]{1,0:T(8,128)(2,1)S(1)}, bf16[488,256]{1,0:T(8,128)(2,1)S(1)}, u32[]{:S(2)}, u32[]{:S(2)}) collective-permute-start(bf16[488,256]{1,0:T(8,128)(2,1)S(1)} %get-tuple-element.34), channel_id=1, source_target_pairs={{0,64},{4,68},{8,72},{12,76},{16,80},{20,84},{24,88},{28,92},{32,9... | collective-permute-start | bytes 749576 | tf_op jit(solution)/shard_map/ppermute | solution.py:249
  135.8 56.8 %collective-permute-start.9 = (bf16[488,256]{1,0:T(8,128)(2,1)S(1)}, bf16[488,256]{1,0:T(8,128)(2,1)S(1)}, u32[]{:S(2)}, u32[]{:S(2)}) collective-permute-start(bf16[488,256]{1,0:T(8,128)(2,1)S(1)} %get-tuple-element.35), channel_id=1, source_target_pairs={{0,96},{4,100},{8,104},{12,108},{16,112},{20,116},{24,120},{28,124... | collective-permute-start | bytes 749576 | tf_op jit(solution)/shard_map/ppermute | solution.py:249
  136.8 58.7 %collective-permute-start = (bf16[256,768]{1,0:T(8,128)(2,1)S(1)}, bf16[256,768]{1,0:T(8,128)(2,1)S(1)}, u32[]{:S(2)}, u32[]{:S(2)}) collective-permute-start(bf16[256,768]{1,0:T(8,128)(2,1)S(1)} %get-tuple-element.21), channel_id=1, source_target_pairs={{0,1},{1,0},{2,3},{3,2},{4,5},{5,4},{6,7},{7,6},{8,9},{9,8},{10,11... | collective-permute-start | bytes 1179656 | tf_op jit(solution)/shard_map/ppermute | solution.py:249
  137.1 58.4 %collective-permute-start.2 = (bf16[256,768]{1,0:T(8,128)(2,1)S(1)}, bf16[256,768]{1,0:T(8,128)(2,1)S(1)}, u32[]{:S(2)}, u32[]{:S(2)}) collective-permute-start(bf16[256,768]{1,0:T(8,128)(2,1)S(1)} %get-tuple-element.22), channel_id=1, source_target_pairs={{0,3},{1,2},{2,1},{3,0},{4,7},{5,6},{6,5},{7,4},{8,11},{9,10},{10,... | collective-permute-start | bytes 1179656 | tf_op jit(solution)/shard_map/ppermute | solution.py:249
  186.4 11.7 %collective-permute-start.1 = (bf16[256,768]{1,0:T(8,128)(2,1)S(1)}, bf16[256,768]{1,0:T(8,128)(2,1)S(1)}, u32[]{:S(2)}, u32[]{:S(2)}) collective-permute-start(bf16[256,768]{1,0:T(8,128)(2,1)S(1)} %get-tuple-element.23), channel_id=1, source_target_pairs={{0,2},{1,3},{2,0},{3,1},{4,6},{5,7},{6,4},{7,5},{8,10},{9,11},{10,... | collective-permute-start | bytes 1179656 | tf_op jit(solution)/shard_map/ppermute | solution.py:249
  193.1 9.7 %collective-permute-start.10 = (bf16[128,256]{1,0:T(8,128)(2,1)S(1)}, bf16[128,256]{1,0:T(8,128)(2,1)S(1)}, u32[]{:S(2)}, u32[]{:S(2)}) collective-permute-start(bf16[128,256]{1,0:T(8,128)(2,1)S(1)} %get-tuple-element.30), channel_id=1, source_target_pairs={{0,8},{4,12},{8,0},{12,4},{16,24},{20,28},{24,16},{28,20},{32,40},... | collective-permute-start | bytes 196616 | tf_op jit(solution)/shard_map/ppermute | solution.py:249
  199.1 6.0 %collective-permute-start.11 = (bf16[128,256]{1,0:T(8,128)(2,1)S(1)}, bf16[128,256]{1,0:T(8,128)(2,1)S(1)}, u32[]{:S(2)}, u32[]{:S(2)}) collective-permute-start(bf16[128,256]{1,0:T(8,128)(2,1)S(1)} %get-tuple-element.31), channel_id=1, source_target_pairs={{0,16},{4,20},{8,24},{12,28},{16,0},{20,4},{24,8},{28,12},{32,48},... | collective-permute-start | bytes 196616 | tf_op jit(solution)/shard_map/ppermute | solution.py:249
  202.8 5.5 %collective-permute-start.12 = (bf16[128,256]{1,0:T(8,128)(2,1)S(1)}, bf16[128,256]{1,0:T(8,128)(2,1)S(1)}, u32[]{:S(2)}, u32[]{:S(2)}) collective-permute-start(bf16[128,256]{1,0:T(8,128)(2,1)S(1)} %get-tuple-element.32), channel_id=1, source_target_pairs={{0,24},{4,28},{8,16},{12,20},{16,8},{20,12},{24,0},{28,4},{32,56},... | collective-permute-start | bytes 196616 | tf_op jit(solution)/shard_map/ppermute | solution.py:249

commit v3 on v2

--- a/solution.py
+++ b/solution.py
@@ -45,19 +45,19 @@
 
         @pl.when(step == pl.num_programs(0) - 1)
         def _():
-            row = lax.broadcasted_iota(jnp.int32, (8, width), 0)
+            lane = lax.broadcasted_iota(jnp.int32, (8, width), 1)
             for o in range(shards):
                 tail = jnp.zeros((8, width), F32)
                 for c in range(capacity):
                     s = o * capacity + c
                     out_ref[o, pl.ds(c * BLK, BLK), :] = acc_ref[s].astype(BF16)
-                    tail = jnp.where(row == c, rel_ref[s].astype(F32), tail)
+                    tail = jnp.where(lane // BLK == c, rel_ref[s].astype(F32), tail)
                 out_ref[o, pl.ds(capacity * BLK, 8), :] = tail.astype(BF16)
 
     return pl.pallas_call(
         kernel,
         name="tile_grads",
-        out_shape=jax.ShapeDtypeStruct((shards, rows, width), BF16),
+        out_shape=pltpu.HBM((shards, rows, width), BF16),
         grid_spec=pltpu.PrefetchScalarGridSpec(
             num_scalar_prefetch=3,
             grid=(tiles // chunk,),
@@ -141,27 +141,77 @@
     )(feats, rel_weights)
 
 
-def select_blocks(keys, blocks, chunk=16):
-    slots = keys.shape[0]
-    _, rows, width = blocks.shape
-
-    def kernel(key_ref, in_ref, out_ref):
+def select_blocks(slot_block, returned, blocks, nblocks, capacity, chunk=4):
+    shards, rows, width = returned.shape
+    relations = blocks.shape[0] // nblocks
+
+    def kernel(block_ref, rel_ref, in_ref, out_ref):
         step = pl.program_id(0)
         for u in range(chunk):
-            out_ref[u] = in_ref[key_ref[step * chunk + u]]
+            for c in range(capacity):
+                block = block_ref[(step * chunk + u) * capacity + c]
+                rel = rel_ref[u, pl.ds(0, 1), pl.ds(c * BLK, BLK)].astype(F32)
+                rel = jnp.broadcast_to(rel, (BLK, BLK))
+                for j in range(width // BLK):
+                    cols = pl.ds(j * BLK, BLK)
+                    value = in_ref[block, :, cols].astype(F32)
+                    for r in range(1, relations):
+                        value = jnp.where(
+                            rel == r, in_ref[r * nblocks + block, :, cols].astype(F32), value
+                        )
+                    out_ref[u, pl.ds(c * BLK, BLK), cols] = value.astype(BF16)
 
     return pl.pallas_call(
         kernel,
         name="select_blocks",
-        out_shape=jax.ShapeDtypeStruct((slots, rows, width), BF16),
+        out_shape=jax.ShapeDtypeStruct((shards, capacity * BLK, width), BF16),
         grid_spec=pltpu.PrefetchScalarGridSpec(
             num_scalar_prefetch=1,
-            grid=(slots // chunk,),
-            in_specs=[whole(blocks.shape)],
-            out_specs=pl.BlockSpec((chunk, rows, width), lambda i, *_: (i, 0, 0)),
-        ),
-        compiler_params=params(),
-    )(keys, blocks)
+            grid=(shards // chunk,),
+            in_specs=[
+                pl.BlockSpec((chunk, 8, width), lambda i, *_: (i, capacity * BLK // 8, 0)),
+                whole(blocks.shape),
+            ],
+            out_specs=pl.BlockSpec((chunk, capacity * BLK, width), lambda i, *_: (i, 0, 0)),
+        ),
+        compiler_params=params(),
+    )(slot_block, returned, blocks)
+
+
+def add_product(base, left, right, first, steps, out_type, depth=1024):
+    nodes, width = base.shape
+    rows = right.shape[1]
+    per = depth // rows
+
+    def kernel(base_ref, left_ref, right_ref, out_ref, acc_ref):
+        step = pl.program_id(0)
+
+        @pl.when(step == 0)
+        def _():
+            acc_ref[...] = base_ref[...]
+
+        acc_ref[...] += jnp.dot(
+            left_ref[...], right_ref[...].reshape(depth, width), preferred_element_type=F32
+        )
+
+        @pl.when(step == steps - 1)
+        def _():
+            out_ref[...] = acc_ref[...].astype(out_type)
+
+    return pl.pallas_call(
+        kernel,
+        name="add_product",
+        out_shape=jax.ShapeDtypeStruct((nodes, width), out_type),
+        grid=(steps,),
+        in_specs=[
+            whole(base.shape),
+            pl.BlockSpec((nodes, depth), lambda i: (0, first + i)),
+            pl.BlockSpec((per, rows, width), lambda i: (first + i, 0, 0)),
+        ],
+        out_specs=whole((nodes, width)),
+        scratch_shapes=[pltpu.VMEM((nodes, width), F32)],
+        compiler_params=params(),
+    )(base, left, right)
 
 
 def sum_by_key(keys, returned, bins, capacity, chunk=4):
@@ -202,10 +252,10 @@
     relations, nodes, width = source_grads.shape
     nbase, width_in, _ = bases.shape
 
-    def kernel(coef_ref, feat_ref, src_ref, grad_ref, base_ref, out_ref, dots_ref):
+    def kernel(coef_ref, feat_ref, src_ref, grad_ref, base_ref, out_ref, dots_ref, acc_ref):
         @pl.when(pl.program_id(0) == 0)
         def _():
-            dots_ref[...] = jnp.zeros_like(dots_ref)
+            acc_ref[...] = jnp.zeros_like(acc_ref)
 
         cols = feat_ref[...].T
         for r in range(relations):
@@ -217,15 +267,26 @@
                 else:
                     out_ref[b] += scaled
                 prod = g * base_ref[b].astype(F32)
-                dots_ref[r * nbase + b] += jnp.sum(prod.reshape(-1, 8, width), axis=0)
+                acc_ref[r * nbase + b] += jnp.sum(prod.reshape(-1, 8, width), axis=0)
         out_ref[nbase] = jnp.dot(cols, grad_ref[...], preferred_element_type=F32)
+
+        @pl.when(pl.program_id(0) == pl.num_programs(0) - 1)
+        def _():
+            row = lax.broadcasted_iota(jnp.int32, (8, BLK), 0)
+            lane = lax.broadcasted_iota(jnp.int32, (8, BLK), 1)
+            tile = jnp.zeros((8, BLK), F32)
+            for r in range(relations):
+                for b in range(nbase):
+                    total = jnp.sum(acc_ref[r * nbase + b])
+                    tile = jnp.where((row == r) & (lane == b), total, tile)
+            dots_ref[...] = tile
 
     return pl.pallas_call(
         kernel,
         name="weight_grads",
         out_shape=(
             jax.ShapeDtypeStruct((nbase + 1, width_in, width), F32),
-            jax.ShapeDtypeStruct((relations * nbase, 8, width), F32),
+            jax.ShapeDtypeStruct((8, BLK), F32),
         ),
         grid_spec=pltpu.PrefetchScalarGridSpec(
             num_scalar_prefetch=1,
@@ -238,8 +299,9 @@
             ],
             out_specs=(
                 pl.BlockSpec((nbase + 1, chunk, width), lambda i, *_: (0, i, 0)),
-                whole((relations * nbase, 8, width)),
+                whole((8, BLK)),
             ),
+            scratch_shapes=[pltpu.VMEM((relations * nbase, 8, width), F32)],
         ),
         compiler_params=params(),
     )(coef, feats, source_grads, d_out, bases)
@@ -262,26 +324,134 @@
     return total
 
 
-def scatter_sum_with(x, extra, axis, shift, size, me, dim):
-    at = (me >> shift) & (size - 1)
-    total = chunk_of(x, at, dim)
-    width = x.shape[-1]
-    count = extra.shape[0]
-    high = lax.reduce_precision(extra, 8, 7)
-    low = lax.reduce_precision(extra - high, 8, 7)
-    line = jnp.concatenate([high, low, jnp.zeros((width - 2 * count,), F32)])
-    lines = jnp.where(jnp.arange(8)[:, None] == 0, line[None], 0.0).astype(BF16)
-    sums = [high + low]
-    for k in range(1, size):
-        part = chunk_of(x, at ^ k, dim).astype(BF16)
-        sent = jnp.concatenate([part.reshape(-1, width), lines], axis=0)
-        got = exchange(sent, axis, k << shift)
-        total = total + got[:-8].reshape(part.shape).astype(F32)
-        last = got[-8].astype(F32)
-        sums.append(last[:count] + last[count : 2 * count])
-    while len(sums) > 1:
-        sums = [sums[i] + sums[i + 1] for i in range(0, len(sums), 2)]
-    return total, sums[0]
+def two_terms(x):
+    high = x.astype(BF16)
+    low = (x - high.astype(F32)).astype(BF16)
+    return high, low
+
+
+def sum_terms(x):
+    return x[:, :BLK].astype(F32) + x[:, BLK:].astype(F32)
+
+
+def first_stage(place, stacked, got, dots, size):
+    parts, _, rest, _, rows, width = stacked.shape
+    length = parts * rest * rows
+
+    def kernel(place_ref, own_ref, got_ref, dots_ref, keep_ref, *send_refs):
+        core = place_ref[0]
+        at = place_ref[1]
+        high, low = two_terms(dots_ref[...])
+        for k in range(size):
+            for p in range(parts):
+                for q in range(rest):
+                    value = own_ref[p, at ^ k, q, core] + got_ref[p, at ^ k, q].astype(F32)
+                    if k == 0:
+                        keep_ref[p, q] = value
+                    else:
+                        send_refs[k - 1][pl.ds((p * rest + q) * rows, rows), :] = value.astype(BF16)
+            if k:
+                send_refs[k - 1][pl.ds(length, 8), pl.ds(0, BLK)] = high
+                send_refs[k - 1][pl.ds(length, 8), pl.ds(BLK, BLK)] = low
+
+    sent = (length + 8, width)
+    return pl.pallas_call(
+        kernel,
+        name="first_stage",
+        out_shape=(jax.ShapeDtypeStruct((parts, rest, rows, width), F32),)
+        + (jax.ShapeDtypeStruct(sent, BF16),) * (size - 1),
+        grid_spec=pltpu.PrefetchScalarGridSpec(
+            num_scalar_prefetch=1,
+            grid=(1,),
+            in_specs=[whole(stacked.shape), whole(got.shape), whole(dots.shape)],
+            out_specs=(whole((parts, rest, rows, width)),) + (whole(sent),) * (size - 1),
+        ),
+        compiler_params=params(),
+    )(place, stacked, got, dots)
+
+
+def second_stage(place, kept, dots, got, size):
+    parts, _, rows, width = kept.shape
+    length = parts * rows
+
+    def kernel(place_ref, own_ref, dots_ref, *refs):
+        gots = refs[: len(got)]
+        keep_ref, all_ref = refs[len(got) : len(got) + 2]
+        send_refs = refs[len(got) + 2 :]
+        at = place_ref[2]
+        high, low = two_terms(dots_ref[...])
+        sums = [high.astype(F32) + low.astype(F32)]
+        sums += [sum_terms(g[pl.ds(length * size, 8), :]) for g in gots]
+        while len(sums) > 1:
+            sums = [sums[i] + sums[i + 1] for i in range(0, len(sums), 2)]
+        all_ref[...] = sums[0]
+        high, low = two_terms(sums[0])
+        for k in range(size):
+            for p in range(parts):
+                value = own_ref[p, at ^ k]
+                start = pl.multiple_of((p * size + (at ^ k)) * rows, 8)
+                for g in gots:
+                    value = value + g[pl.ds(start, rows), :].astype(F32)
+                if k == 0:
+                    keep_ref[p] = value
+                else:
+                    send_refs[k - 1][pl.ds(p * rows, rows), :] = value.astype(BF16)
+            if k:
+                send_refs[k - 1][pl.ds(length, 8), pl.ds(0, BLK)] = high
+                send_refs[k - 1][pl.ds(length, 8), pl.ds(BLK, BLK)] = low
+
+    sent = (length + 8, width)
+    return pl.pallas_call(
+        kernel,
+        name="second_stage",
+        out_shape=(
+            jax.ShapeDtypeStruct((parts, rows, width), F32),
+            jax.ShapeDtypeStruct((8, BLK), F32),
+        )
+        + (jax.ShapeDtypeStruct(sent, BF16),) * (size - 1),
+        grid_spec=pltpu.PrefetchScalarGridSpec(
+            num_scalar_prefetch=1,
+            grid=(1,),
+            in_specs=[whole(kept.shape), whole(dots.shape)] + [whole(g.shape) for g in got],
+            out_specs=(whole((parts, rows, width)), whole((8, BLK))) + (whole(sent),) * (size - 1),
+        ),
+        compiler_params=params(),
+    )(place, kept, dots, *got)
+
+
+def last_stage(kept, dots, got, relations):
+    parts, rows, width = kept.shape
+    length = parts * rows
+    nbase = parts - 1
+
+    def kernel(own_ref, dots_ref, *refs):
+        gots = refs[: len(got)]
+        bases_ref, root_ref, coef_ref = refs[len(got) :]
+        high, low = two_terms(dots_ref[...])
+        sums = [high.astype(F32) + low.astype(F32)]
+        sums += [sum_terms(g[pl.ds(length, 8), :]) for g in gots]
+        while len(sums) > 1:
+            sums = [sums[i] + sums[i + 1] for i in range(0, len(sums), 2)]
+        coef_ref[...] = sums[0][:relations, :nbase]
+        for p in range(parts):
+            value = own_ref[p]
+            for g in gots:
+                value = value + g[pl.ds(p * rows, rows), :].astype(F32)
+            if p < nbase:
+                bases_ref[p] = value
+            else:
+                root_ref[...] = value
+
+    shapes = ((nbase, rows, width), (rows, width), (relations, nbase))
+    return pl.pallas_call(
+        kernel,
+        name="last_stage",
+        out_shape=tuple(jax.ShapeDtypeStruct(x, F32) for x in shapes),
+        grid=(1,),
+        in_specs=[whole(kept.shape), whole(dots.shape)] + [whole(g.shape) for g in got],
+        out_specs=tuple(whole(x) for x in shapes),
+        compiler_params=params(),
+    )(kept, dots, *got)
 
 
 def body(
@@ -317,33 +487,21 @@
     root_term = jnp.dot(feats, root_weight, preferred_element_type=F32)
     dense = dense_tiles(tile_slot[0], tile_dst[0], tile_adj[0], slots, nblocks)
 
-    owner_rel = returned[:, capacity * BLK : capacity * BLK + capacity, 0].astype(jnp.int32)
+    returned, dense = lax.optimization_barrier((returned, dense))
+    outgoing = select_blocks(slot_block.reshape(slots), returned, projected, nblocks, capacity)
+    outgoing, returned = lax.optimization_barrier((outgoing, returned))
+    incoming = lax.all_to_all(outgoing, "shard", 0, 0, tiled=True)
+
+    owner_rel = returned[:, capacity * BLK, :: BLK][:, :capacity].astype(jnp.int32)
     keys = (owner_rel * nblocks + slot_block[0]).reshape(-1)
-    outgoing = select_blocks(keys, projected)
-    incoming = lax.all_to_all(
-        outgoing.reshape(shards, capacity * BLK, width), "shard", 0, 0, tiled=True
-    )
-
     source_grads = sum_by_key(keys, returned, relations * nblocks, capacity)
     source_grads = source_grads.reshape(relations, nblocks * BLK, width)
     stacked, dots = weight_grads(
         coef.astype(F32).reshape(-1), feats, source_grads, d_out, bases
     )
-    dots = jnp.sum(dots, axis=(1, 2))
     dots = dots + exchange(dots, "shard", 1)
     for step in (1, 2):
         dots = dots + exchange(dots, "rep", step)
-
-    rows = width_in // shards
-    part = scatter_sum(
-        stacked.reshape(nbase + 1, shards // 2, 2, rows, width), "shard", 0, 2, me, dim=2
-    )
-    part = part.reshape(nbase + 1, 4, shards // 8, rows, width)
-    part, dots = scatter_sum_with(part, dots, "shard", 3, 4, me, dim=1)
-    reduced, dots = scatter_sum_with(part, dots, "shard", 1, 4, me, dim=1)
-    grad_bases = reduced[:nbase]
-    grad_root = reduced[nbase]
-    grad_coef = dots.reshape(relations, nbase)
 
     through = jnp.einsum("rno,rco->nc", source_grads, rel_weights, preferred_element_type=F32)
     through = through + jnp.dot(d_out, root_weight.T, preferred_element_type=F32)
@@ -351,10 +509,22 @@
         through.reshape(reps, -1, width_in), "rep", 0, reps, my_rep
     ).astype(BF16)
 
-    output = (
-        jnp.dot(dense, incoming.reshape(slots * BLK, width), preferred_element_type=F32)
-        + root_term
-    ).astype(BF16)
+    rows = width_in // shards
+    stacked = stacked.reshape(nbase + 1, 4, 4, 2, rows, width)
+    place = jnp.stack([me & 1, (me >> 3) & 3, (me >> 1) & 3]).astype(jnp.int32)
+    got = exchange(chunk_of(stacked, (me & 1) ^ 1, 3).astype(BF16), "shard", 1)
+    kept, *sends = first_stage(place, stacked, got, dots, 4)
+    grad_feats, *sends = lax.optimization_barrier((grad_feats, *sends))
+    got = [exchange(x, "shard", k << 3) for k, x in zip((1, 2, 3), sends)]
+    total_steps = slots * BLK // 1024
+    early = total_steps // 2
+    partial = add_product(root_term, dense, incoming, 0, early, F32)
+    partial, kept = lax.optimization_barrier((partial, kept))
+    kept, dots, *sends = second_stage(place, kept, dots, got, 4)
+    got = [exchange(x, "shard", k << 1) for k, x in zip((1, 2, 3), sends)]
+    partial, kept = lax.optimization_barrier((partial, kept))
+    output = add_product(partial, dense, incoming, early, total_steps - early, BF16)
+    grad_bases, grad_root, grad_coef = last_stage(kept, dots, got, relations)
     return (output, grad_feats, grad_bases, grad_root, grad_coef)
 
 

time: 222 us -> 194 us (0.87)
  waiting for transfers between devices: 72.7 us -> 33.2 us
  Pallas kernels: 67.3 us -> 90 us
  matrix products: 19.1 us -> 6.39 us
  local copies, waits for them, and re-layouts: 20.2 us -> 24.6 us
  other arithmetic: 7.55 us -> 3.89 us
    ppermute x13, waiting for transfers between devices: 61.6 us -> 23.2 us  [exchange(): lax.ppermute(x, axis, [(i, i ^ mask) for i in range(lax.axis_size(axis))])]
    pallas_call x1 -> x6, Pallas kernels: 14.5 us -> 33.2 us  [the longest x1 16.6 us: tile_grads(): pl.pallas_call(kernel, name='tile_grads', out_shape=pltpu.HBM((shards, ro...]
    dot_general x1 -> x0, matrix products: 9.31 us -> none  [body(): jnp.dot(dense, incoming.reshape(slots * BLK, width), preferred_element_ty...]
    dot_general x1, matrix products: 6.44 us -> 2.22 us  [body(): jnp.einsum('rno,rco->nc', source_grads, rel_weights, preferred_element_ty...]
    pallas_call x1, Pallas kernels: 3.14 us -> 6.67 us  [select_blocks(): pl.pallas_call(kernel, name='select_blocks', out_shape=jax.ShapeDtypeStru...]
    convert_element_type x2 -> x1, local copies, waits for them, and re-layouts: 0.13 us -> 2.66 us  [body(): got = exchange(chunk_of(stacked, me & 1 ^ 1, 3).astype(BF16), 'shard', 1)]
    unnamed x43 -> x41, local copies, waits for them, and re-layouts: 14.2 us -> 15.8 us
  transfers between devices with their start and end apart: 15 -> 15, of which waited for: 6 -> 6; matrix products, arithmetic and copies ran while one was open for 9% -> 12% of each run, Pallas kernels for 17% -> 33%
where the time goes in v3:
time: 194 us; the launch traced here: 192 us
  Pallas kernels  90 us (46%)
  waiting for transfers between devices  33.2 us (17%)
  starting transfers between devices  33.1 us (17%)
  local copies, waits for them, and re-layouts  24.6 us (13%)
  matrix products  6.39 us (3%)
  other arithmetic  3.89 us (2%)
    pallas_call x1, Pallas kernels, dense_tiles(): pl.pallas_call(kernel, name='dense_tiles', out_shape=jax.ShapeDtypeStruct...  32.5 us
    ppermute x13, waiting for transfers between devices, exchange(): lax.ppermute(x, axis, [(i, i ^ mask) for i in range(lax.axis_size(axis))])  23.2 us
    ppermute x13, starting transfers between devices, exchange(): lax.ppermute(x, axis, [(i, i ^ mask) for i in range(lax.axis_size(axis))])  17.7 us
    pallas_call x1, Pallas kernels, tile_grads(): pl.pallas_call(kernel, name='tile_grads', out_shape=pltpu.HBM((shards, ro...  16.6 us
    unnamed x41, local copies, waits for them, and re-layouts  15.8 us
    pallas_call x2, Pallas kernels, add_product(): pl.pallas_call(kernel, name='add_product', out_shape=jax.ShapeDtypeStruct...  12.6 us
    all_to_all x1, waiting for transfers between devices, body(): returned = lax.all_to_all(slot_grads, 'shard', 0, 0, tiled=True)  10 us
    all_to_all x1, starting transfers between devices, body(): returned = lax.all_to_all(slot_grads, 'shard', 0, 0, tiled=True)  8.66 us
  transfers between devices with their start and end apart: 15, of which 6 were waited for; matrix products, arithmetic and copies ran while one was open for 12% of the time, Pallas kernels for 33%

profile of v3, /device:TPU:0, one launch (start us, length us, event | category | flops | bytes accessed | tf_op | source)
XLA Modules:
  0.0 192.2 jit_solution(11170444948063465945)
XLA Ops:
  0.6 0.0 copy-start
  0.6 0.8 copy.20
  1.5 0.1 reshape.49.rel_ref
  1.6 0.0 copy-start.10
  1.6 1.0 copy-done.10
  2.6 0.7 copy-done.12
  3.3 0.7 copy-done.14
  4.0 16.6 %tile_grads.1 = bf16[32,264,256]{2,1,0:T(8,128)(2,1)} custom-call(s32[256]{0:T(256)S(1)} %bitcast.54, s32[256]{0:T(256)S(1)} %bitcast.56, s32[64]{0:T(128)S(1)} %reshape.49.rel_ref, bf16[256,128,128]{2,1,0:T(8,128)(2,1)} %bitcast.58, bf16[8,128,256]{2,1,0:T(8,128)(2,1)S(1)} %bitcast.53), custom_call_target="tpu_custom_call" | custom-call | tf_op jit(solution)/shard_map/tile_grads/pallas_call | solution.py:57
  20.6 8.7 %all-to-all-start = ((bf16[32,264,256]{2,1,0:T(8,128)(2,1)}), bf16[32,264,256]{2,1,0:T(8,128)(2,1)}, u32[]{:S(2)}, u32[]{:S(2)}) async-start(bf16[32,264,256]{2,1,0:T(8,128)(2,1)} %tile_grads.1), calls=%async_computation | async-start | bytes 8650752 | tf_op jit(solution)/shard_map/all_to_all | solution.py:479
  29.3 0.0 copy-start.8
  29.3 32.5 %dense_tiles.1.left_ref = bf16[1024,8192]{1,0:T(8,128)(2,1)} custom-call(s32[256]{0:T(256)S(1)} %bitcast.55, s32[256]{0:T(256)S(1)} %bitcast.57, bf16[256,128,128]{2,1,0:T(8,128)(2,1)} %bitcast.59), custom_call_target="tpu_custom_call" | custom-call | tf_op jit(solution)/shard_map/dense_tiles/pallas_call | solution.py:106
  61.8 1.2 copy.26
  63.0 1.3 convolution_convert_fusion
  64.4 0.0 copy-start.17
  64.4 1.7 copy.29
  66.1 0.7 copy.21
  66.8 0.8 reshape.51.block_ref
  67.6 1.5 copy-done.6
  69.2 3.0 %project.1.in_ref = bf16[40,128,256]{2,1,0:T(8,128)(2,1)S(1)} custom-call(bf16[1024,768]{1,0:T(8,128)(2,1)S(1)} %copy-done.1, bf16[5,768,256]{2,1,0:T(8,128)(2,1)S(1)} %bitcast.48), custom_call_target="tpu_custom_call" | custom-call | tf_op jit(solution)/shard_map/project/pallas_call | solution.py:130
  72.1 1.5 copy-done.4
  73.6 10.0 %all-to-all-done.rel_ref.ret_ref = bf16[32,264,256]{2,1,0:T(8,128)(2,1)} async-done(((bf16[32,264,256]{2,1,0:T(8,128)(2,1)}), bf16[32,264,256]{2,1,0:T(8,128)(2,1)}, u32[]{:S(2)}, u32[]{:S(2)}) %all-to-all-start) | async-done | bytes 4325408 | tf_op jit(solution)/shard_map/all_to_all | solution.py:479
  83.6 1.7 copy-done.5
  85.3 6.7 %select_blocks.1 = bf16[32,256,256]{2,1,0:T(8,128)(2,1)} custom-call(s32[64]{0:T(128)S(1)} %reshape.51.block_ref, bf16[32,264,256]{2,1,0:T(8,128)(2,1)} %all-to-all-done.rel_ref.ret_ref, bf16[40,128,256]{2,1,0:T(8,128)(2,1)S(1)} %copy-done.5), custom_call_target="tpu_custom_call" | custom-call | tf_op jit(solution)/shard_map/select_blocks/pallas_call | solution.py:164
  92.0 6.7 %all-to-all-start.1 = ((bf16[32,256,256]{2,1,0:T(8,128)(2,1)}), bf16[32,256,256]{2,1,0:T(8,128)(2,1)}, u32[]{:S(2)}, u32[]{:S(2)}) async-start(bf16[32,256,256]{2,1,0:T(8,128)(2,1)} %select_blocks.1), calls=%async_computation.1 | async-start | bytes 8388608 | tf_op jit(solution)/shard_map/all_to_all | solution.py:493
  98.8 0.1 copy.22
  98.9 0.1 reshape.60.coef_ref
  98.9 1.6 slice.3
  100.6 1.4 multiply_reduce_fusion
  102.0 0.8 mul.12
  102.8 0.0 copy-start.11
  102.8 6.0 %sum_by_key.1 = bf16[40,128,256]{2,1,0:T(8,128)(2,1)S(1)} custom-call(s32[64]{0:T(128)S(1)} %add.42.key_ref, bf16[32,264,256]{2,1,0:T(8,128)(2,1)} %all-to-all-done.rel_ref.ret_ref), custom_call_target="tpu_custom_call" | custom-call | tf_op jit(solution)/shard_map/sum_by_key/pallas_call | solution.py:236
  108.9 1.4 copy-done.2
  110.3 8.7 %weight_grads.1 = (f32[5,768,256]{2,1,0:T(8,128)}, f32[8,128]{1,0:T(8,128)S(1)}) custom-call(f32[20]{0:T(128)S(1)} %reshape.60.coef_ref, bf16[1024,768]{1,0:T(8,128)(2,1)S(1)} %copy-done.1, bf16[5,1024,256]{2,1,0:T(8,128)(2,1)} %bitcast.46, bf16[1024,256]{1,0:T(8,128)(2,1)S(1)} %copy-done.11, bf16[4,768,256]{2,1,0:T(8,128)(2,1)S(1)} %copy-done.8), custom_call_target="tpu_custom_call" | custom-call | tf_op jit(solution)/shard_map/weight_grads/pallas_call | solution.py:284
  119.0 2.7 %fusion = bf16[5,4,4,24,256]{4,3,2,1,0:T(8,128)(2,1)} fusion(f32[5,4,4,2,24,256]{5,4,3,2,1,0:T(8,128)} %bitcast.51, s32[]{:T(128)S(6)} %select_n.17), kind=kLoop, calls=%fused_computation.4 | loop fusion | bytes 1966084 | tf_op jit(solution)/shard_map/convert_element_type | solution.py:515
  121.6 0.2 collective-permute-start
  121.8 2.2 %fusion.8 = f32[1024,768,1]{1,0,2:T(8,128)S(1)} fusion(bf16[5,1024,256]{2,1,0:T(8,128)(2,1)S(1)} %bitcast.47, bf16[5,768,256]{2,1,0:T(8,128)(2,1)S(1)} %bitcast.49), kind=kOutput, calls=%fused_computation.18 | convolution fusion | flops 2013265920 | bytes 7733248 | tf_op jit(solution)/shard_map/rno,rco->nc/dot_general | solution.py:506
  124.1 2.3 %bitcast_add_fusion = f32[1024,768]{1,0:T(8,128)} fusion(f32[1024,768,1]{1,0,2:T(8,128)S(1)} %fusion.8, bf16[1024,256]{1,0:T(8,128)(2,1)S(1)} %copy-done.11, bf16[768,256]{1,0:T(8,128)(2,1)S(1)} %copy-done), kind=kOutput, calls=%fused_computation.1 | convolution fusion | flops 403439616 | bytes 7208960 | tf_op jit(solution)/shard_map/dot_general | solution.py:507
  126.3 2.6 %fusion.4 = (bf16[256,768]{1,0:T(8,128)(2,1)}, bf16[256,768]{1,0:T(8,128)(2,1)S(1)}, bf16[256,768]{1,0:T(8,128)(2,1)}) fusion(f32[4,256,768]{2,1,0:T(8,128)} %bitcast.11, s32[]{:T(128)S(6)} %select_n.19, s32[]{:T(128)S(6)} %select_n.21, s32[]{:T(128)S(6)} %select_n.20), kind=kLoop, calls=%fused_computation.12 | loop fusion | bytes 2359308 | tf_op jit(solution)/shard_map/convert_element_type | solution.py:322
  128.9 1.5 collective-permute-start.4
  130.4 2.7 %collective-permute-start.5 = (bf16[256,768]{1,0:T(8,128)(2,1)}, bf16[256,768]{1,0:T(8,128)(2,1)}, u32[]{:S(2)}, u32[]{:S(2)}) collective-permute-start(bf16[256,768]{1,0:T(8,128)(2,1)} %get-tuple-element.69), channel_id=1, source_target_pairs={{0,2},{1,3},{2,0},{3,1},{4,6},{5,7},{6,4},{7,5},{8,10},{9,11},{10,... | collective-permute-start | bytes 1179656 | tf_op jit(solution)/shard_map/ppermute | solution.py:311
  133.1 0.5 collective-permute-start.6
  133.6 1.2 collective-permute-done.1
  134.8 0.3 collective-permute-start.2
  135.1 13.9 %collective-permute-done.2 = f32[8,128]{1,0:T(8,128)S(1)} collective-permute-done((f32[8,128]{1,0:T(8,128)S(1)}, f32[8,128]{1,0:T(8,128)S(1)}, u32[]{:S(2)}, u32[]{:S(2)}) %collective-permute-start.2) | collective-permute-done | bytes 4128 | tf_op jit(solution)/shard_map/ppermute | solution.py:311
  149.0 3.0 %collective-permute-start.3 = (f32[8,128]{1,0:T(8,128)S(1)}, f32[8,128]{1,0:T(8,128)S(1)}, u32[]{:S(2)}, u32[]{:S(2)}) collective-permute-start(f32[8,128]{1,0:T(8,128)S(1)} %add.45), channel_id=1, source_target_pairs={{0,2},{1,3},{2,0},{3,1},{4,6},{5,7},{6,4},{7,5},{8,10},{9,11},{10,... | collective-permute-start | bytes 12296 | tf_op jit(solution)/shard_map/ppermute | solution.py:311
  152.1 0.1 pad_add_fusion.place_ref
  152.1 2.0 %collective-permute-done.3 = f32[8,128]{1,0:T(8,128)S(1)} collective-permute-done((f32[8,128]{1,0:T(8,128)S(1)}, f32[8,128]{1,0:T(8,128)S(1)}, u32[]{:S(2)}, u32[]{:S(2)}) %collective-permute-start.3) | collective-permute-done | bytes 4128 | tf_op jit(solution)/shard_map/ppermute | solution.py:311
  154.2 2.4 %fusion.3 = bf16[256,768]{1,0:T(8,128)(2,1)} fusion(bf16[256,768]{1,0:T(8,128)(2,1)} %collective-permute-done.6, bf16[256,768]{1,0:T(8,128)(2,1)} %collective-permute-done.5, bf16[256,768]{1,0:T(8,128)(2,1)} %collective-permute-done.4, f32[4,256,768]{2,1,0:T(8,128)} %bitcast.11, s32[]{:T(128)S(6)} %select_n.18), kind=kLoop, calls=%fused_computation.8 | loop fusion | flops 1376256 | bytes 2359300 | tf_op jit(solution)/shard_map/convert_element_type | solution.py:510
  156.6 2.1 %copy-done.9 = f32[5,768,256]{2,1,0:T(8,128)S(1)} copy-done((f32[5,768,256]{2,1,0:T(8,128)S(1)}, f32[5,768,256]{2,1,0:T(8,128)}, u32[]{:S(2)}) %copy-start.9) | copy-done | bytes 3932184
  158.7 1.5 first_stage.1
  160.2 1.7 collective-permute-start.7
  161.9 2.7 %collective-permute-start.8 = (bf16[488,256]{1,0:T(8,128)(2,1)}, bf16[488,256]{1,0:T(8,128)(2,1)}, u32[]{:S(2)}, u32[]{:S(2)}) collective-permute-start(bf16[488,256]{1,0:T(8,128)(2,1)} %get-tuple-element.44), channel_id=1, source_target_pairs={{0,64},{4,68},{8,72},{12,76},{16,80},{20,84},{24,88},{28,92},{32,9... | collective-permute-start | bytes 749576 | tf_op jit(solution)/shard_map/ppermute | solution.py:311
  164.6 0.3 collective-permute-start.9
  164.9 0.6 fusion.7.base_ref
  165.5 5.9 %add_product.2.base_ref = f32[1024,256]{1,0:T(8,128)S(1)} custom-call(f32[1024,256]{1,0:T(8,128)S(1)} %fusion.7.base_ref, bf16[1024,8192]{1,0:T(8,128)(2,1)} %dense_tiles.1.left_ref, bf16[32,256,256]{2,1,0:T(8,128)(2,1)} %all-to-all-done.1.right_ref), custom_call_target="tpu_custom_call" | custom-call | tf_op jit(solution)/shard_map/add_product/pallas_call | solution.py:201
  171.4 3.5 %collective-permute-done.8.refs_1_ = bf16[488,256]{1,0:T(8,128)(2,1)} collective-permute-done((bf16[488,256]{1,0:T(8,128)(2,1)}, bf16[488,256]{1,0:T(8,128)(2,1)}, u32[]{:S(2)}, u32[]{:S(2)}) %collective-permute-start.8) | collective-permute-done | bytes 249888 | tf_op jit(solution)/shard_map/ppermute | solution.py:311
  175.0 2.6 %collective-permute-done.9.refs_2_ = bf16[488,256]{1,0:T(8,128)(2,1)} collective-permute-done((bf16[488,256]{1,0:T(8,128)(2,1)}, bf16[488,256]{1,0:T(8,128)(2,1)}, u32[]{:S(2)}, u32[]{:S(2)}) %collective-permute-start.9) | collective-permute-done | bytes 249888 | tf_op jit(solution)/shard_map/ppermute | solution.py:311
  177.5 1.9 second_stage.1
  179.4 1.6 collective-permute-start.10
  180.9 2.7 %collective-permute-start.11 = (bf16[128,256]{1,0:T(8,128)(2,1)S(1)}, bf16[128,256]{1,0:T(8,128)(2,1)S(1)}, u32[]{:S(2)}, u32[]{:S(2)}) collective-permute-start(bf16[128,256]{1,0:T(8,128)(2,1)S(1)} %get-tuple-element.52), channel_id=1, source_target_pairs={{0,16},{4,20},{8,24},{12,28},{16,0},{20,4},{24,8},{28,12},{32,48},... | collective-permute-start | bytes 196616 | tf_op jit(solution)/shard_map/ppermute | solution.py:311
  183.7 0.5 collective-permute-start.12
  184.2 6.7 %add_product.3 = bf16[1024,256]{1,0:T(8,128)(2,1)} custom-call(f32[1024,256]{1,0:T(8,128)S(1)} %add_product.2.base_ref, bf16[1024,8192]{1,0:T(8,128)(2,1)} %dense_tiles.1.left_ref, bf16[32,256,256]{2,1,0:T(8,128)(2,1)} %all-to-all-done.1.right_ref), custom_call_target="tpu_custom_call" | custom-call | tf_op jit(solution)/shard_map/add_product/pallas_call | solution.py:201
  190.8 0.7 last_stage.1
  191.5 0.7 copy.24
  (37 shorter events, 0.1 us)
Async XLA Ops:
  0.6 123.4 %copy-start = (bf16[768,256]{1,0:T(8,128)(2,1)S(1)}, bf16[768,256]{1,0:T(8,128)(2,1)}, u32[]{:S(2)}) copy-start(bf16[768,256]{1,0:T(8,128)(2,1)} %param.13) | copy-start | bytes 1179652
  1.6 1.0 copy-start.10
  2.6 0.7 copy-start.12
  3.3 0.7 copy-start.14
  20.6 8.7 %copy-start.13 = (s32[1,256]{1,0:T(1,128)S(1)}, s32[1,256]{1,0:T(1,128)}, u32[]{:S(2)}) copy-start(s32[1,256]{1,0:T(1,128)} %param.16) | copy-start | bytes 3076
  20.6 8.7 %copy-start.15 = (s32[1,256]{1,0:T(1,128)S(1)}, s32[1,256]{1,0:T(1,128)}, u32[]{:S(2)}) copy-start(s32[1,256]{1,0:T(1,128)} %param.17) | copy-start | bytes 3076
  20.6 63.0 %all-to-all-start = ((bf16[32,264,256]{2,1,0:T(8,128)(2,1)}), bf16[32,264,256]{2,1,0:T(8,128)(2,1)}, u32[]{:S(2)}, u32[]{:S(2)}) async-start(bf16[32,264,256]{2,1,0:T(8,128)(2,1)} %tile_grads.1), calls=%async_computation | async-start | bytes 8650752 | tf_op jit(solution)/shard_map/all_to_all | solution.py:479
  29.3 32.5 %copy-start.8 = (bf16[4,768,256]{2,1,0:T(8,128)(2,1)S(1)}, bf16[4,768,256]{2,1,0:T(8,128)(2,1)}, u32[]{:S(2)}) copy-start(bf16[4,768,256]{2,1,0:T(8,128)(2,1)} %base_ref.1) | copy-start | bytes 4718596
  61.8 1.2 copy-start.16
  64.4 1.7 copy-start.17
  64.4 3.2 %copy-start.1 = (bf16[1024,768]{1,0:T(8,128)(2,1)S(1)}, bf16[1024,768]{1,0:T(8,128)(2,1)}, u32[]{:S(2)}) copy-start(bf16[1024,768]{1,0:T(8,128)(2,1)} %feat_ref.3) | copy-start | bytes 4718596
  67.6 1.5 copy-start.6
  72.1 1.5 copy-start.4
  83.6 1.7 copy-start.5
  92.0 73.5 %all-to-all-start.1 = ((bf16[32,256,256]{2,1,0:T(8,128)(2,1)}), bf16[32,256,256]{2,1,0:T(8,128)(2,1)}, u32[]{:S(2)}, u32[]{:S(2)}) async-start(bf16[32,256,256]{2,1,0:T(8,128)(2,1)} %select_blocks.1), calls=%async_computation.1 | async-start | bytes 8388608 | tf_op jit(solution)/shard_map/all_to_all | solution.py:493
  102.8 7.5 %copy-start.11 = (bf16[1024,256]{1,0:T(8,128)(2,1)S(1)}, bf16[1024,256]{1,0:T(8,128)(2,1)}, u32[]{:S(2)}) copy-start(bf16[1024,256]{1,0:T(8,128)(2,1)} %grad_ref.1) | copy-start | bytes 1572868
  108.8 1.5 copy-start.2
  110.3 11.5 %copy-start.3 = (bf16[40,128,256]{2,1,0:T(8,128)(2,1)S(1)}, bf16[40,128,256]{2,1,0:T(8,128)(2,1)}, u32[]{:S(2)}) copy-start(bf16[40,128,256]{2,1,0:T(8,128)(2,1)} %copy-done.2) | copy-start | bytes 7864324
  110.3 11.5 %copy-start.7 = (bf16[1,5,768,256]{3,2,1,0:T(8,128)(2,1)S(1)}, bf16[1,5,768,256]{3,2,1,0:T(8,128)(2,1)}, u32[]{:S(2)}) copy-start(bf16[1,5,768,256]{3,2,1,0:T(8,128)(2,1)} %copy.29) | copy-start | bytes 5898244
  121.6 35.0 %collective-permute-start = (bf16[5,4,4,24,256]{4,3,2,1,0:T(8,128)(2,1)}, bf16[5,4,4,24,256]{4,3,2,1,0:T(8,128)(2,1)S(1)}, u32[]{:S(2)}, u32[]{:S(2)}) collective-permute-start(bf16[5,4,4,24,256]{4,3,2,1,0:T(8,128)(2,1)} %fusion), channel_id=1, source_target_pairs={{0,4},{4,0},{8,12},{12,8},{16,20},{20,16},{24,28},{28,24},{32,36},... | collective-permute-start | bytes 2949128 | tf_op jit(solution)/shard_map/ppermute | solution.py:311
  128.9 25.2 %collective-permute-start.4 = (bf16[256,768]{1,0:T(8,128)(2,1)}, bf16[256,768]{1,0:T(8,128)(2,1)}, u32[]{:S(2)}, u32[]{:S(2)}) collective-permute-start(bf16[256,768]{1,0:T(8,128)(2,1)} %get-tuple-element.67), channel_id=1, source_target_pairs={{0,1},{1,0},{2,3},{3,2},{4,5},{5,4},{6,7},{7,6},{8,9},{9,8},{10,11... | collective-permute-start | bytes 1179656 | tf_op jit(solution)/shard_map/ppermute | solution.py:311
  130.4 23.7 %collective-permute-start.5 = (bf16[256,768]{1,0:T(8,128)(2,1)}, bf16[256,768]{1,0:T(8,128)(2,1)}, u32[]{:S(2)}, u32[]{:S(2)}) collective-permute-start(bf16[256,768]{1,0:T(8,128)(2,1)} %get-tuple-element.69), channel_id=1, source_target_pairs={{0,2},{1,3},{2,0},{3,1},{4,6},{5,7},{6,4},{7,5},{8,10},{9,11},{10,... | collective-permute-start | bytes 1179656 | tf_op jit(solution)/shard_map/ppermute | solution.py:311
  133.1 21.0 %collective-permute-start.6 = (bf16[256,768]{1,0:T(8,128)(2,1)S(1)}, bf16[256,768]{1,0:T(8,128)(2,1)}, u32[]{:S(2)}, u32[]{:S(2)}) collective-permute-start(bf16[256,768]{1,0:T(8,128)(2,1)S(1)} %get-tuple-element.68), channel_id=1, source_target_pairs={{0,3},{1,2},{2,1},{3,0},{4,7},{5,6},{6,5},{7,4},{8,11},{9,10},{10,... | collective-permute-start | bytes 1179656 | tf_op jit(solution)/shard_map/ppermute | solution.py:311
  133.6 1.2 collective-permute-start.1
  134.8 14.2 %collective-permute-start.2 = (f32[8,128]{1,0:T(8,128)S(1)}, f32[8,128]{1,0:T(8,128)S(1)}, u32[]{:S(2)}, u32[]{:S(2)}) collective-permute-start(f32[8,128]{1,0:T(8,128)S(1)} %add.44), channel_id=1, source_target_pairs={{0,1},{1,0},{2,3},{3,2},{4,5},{5,4},{6,7},{7,6},{8,9},{9,8},{10,11... | collective-permute-start | bytes 12296 | tf_op jit(solution)/shard_map/ppermute | solution.py:311
  149.0 5.1 %collective-permute-start.3 = (f32[8,128]{1,0:T(8,128)S(1)}, f32[8,128]{1,0:T(8,128)S(1)}, u32[]{:S(2)}, u32[]{:S(2)}) collective-permute-start(f32[8,128]{1,0:T(8,128)S(1)} %add.45), channel_id=1, source_target_pairs={{0,2},{1,3},{2,0},{3,1},{4,6},{5,7},{6,4},{7,5},{8,10},{9,11},{10,... | collective-permute-start | bytes 12296 | tf_op jit(solution)/shard_map/ppermute | solution.py:311
  156.6 2.1 %copy-start.9 = (f32[5,768,256]{2,1,0:T(8,128)S(1)}, f32[5,768,256]{2,1,0:T(8,128)}, u32[]{:S(2)}) copy-start(f32[5,768,256]{2,1,0:T(8,128)} %get-tuple-element.35) | copy-start | bytes 11796484
  160.2 11.2 %collective-permute-start.7 = (bf16[488,256]{1,0:T(8,128)(2,1)}, bf16[488,256]{1,0:T(8,128)(2,1)}, u32[]{:S(2)}, u32[]{:S(2)}) collective-permute-start(bf16[488,256]{1,0:T(8,128)(2,1)} %get-tuple-element.43), channel_id=1, source_target_pairs={{0,32},{4,36},{8,40},{12,44},{16,48},{20,52},{24,56},{28,60},{32,0... | collective-permute-start | bytes 749576 | tf_op jit(solution)/shard_map/ppermute | solution.py:311
  161.9 13.0 %collective-permute-start.8 = (bf16[488,256]{1,0:T(8,128)(2,1)}, bf16[488,256]{1,0:T(8,128)(2,1)}, u32[]{:S(2)}, u32[]{:S(2)}) collective-permute-start(bf16[488,256]{1,0:T(8,128)(2,1)} %get-tuple-element.44), channel_id=1, source_target_pairs={{0,64},{4,68},{8,72},{12,76},{16,80},{20,84},{24,88},{28,92},{32,9... | collective-permute-start | bytes 749576 | tf_op jit(solution)/shard_map/ppermute | solution.py:311
  164.6 12.9 %collective-permute-start.9 = (bf16[488,256]{1,0:T(8,128)(2,1)}, bf16[488,256]{1,0:T(8,128)(2,1)}, u32[]{:S(2)}, u32[]{:S(2)}) collective-permute-start(bf16[488,256]{1,0:T(8,128)(2,1)} %get-tuple-element.45), channel_id=1, source_target_pairs={{0,96},{4,100},{8,104},{12,108},{16,112},{20,116},{24,120},{28,124... | collective-permute-start | bytes 749576 | tf_op jit(solution)/shard_map/ppermute | solution.py:311
  179.4 11.5 %collective-permute-start.10 = (bf16[128,256]{1,0:T(8,128)(2,1)S(1)}, bf16[128,256]{1,0:T(8,128)(2,1)S(1)}, u32[]{:S(2)}, u32[]{:S(2)}) collective-permute-start(bf16[128,256]{1,0:T(8,128)(2,1)S(1)} %get-tuple-element.51), channel_id=1, source_target_pairs={{0,8},{4,12},{8,0},{12,4},{16,24},{20,28},{24,16},{28,20},{32,40},... | collective-permute-start | bytes 196616 | tf_op jit(solution)/shard_map/ppermute | solution.py:311
  180.9 9.9 %collective-permute-start.11 = (bf16[128,256]{1,0:T(8,128)(2,1)S(1)}, bf16[128,256]{1,0:T(8,128)(2,1)S(1)}, u32[]{:S(2)}, u32[]{:S(2)}) collective-permute-start(bf16[128,256]{1,0:T(8,128)(2,1)S(1)} %get-tuple-element.52), channel_id=1, source_target_pairs={{0,16},{4,20},{8,24},{12,28},{16,0},{20,4},{24,8},{28,12},{32,48},... | collective-permute-start | bytes 196616 | tf_op jit(solution)/shard_map/ppermute | solution.py:311
  183.7 7.2 %collective-permute-start.12 = (bf16[128,256]{1,0:T(8,128)(2,1)S(1)}, bf16[128,256]{1,0:T(8,128)(2,1)S(1)}, u32[]{:S(2)}, u32[]{:S(2)}) collective-permute-start(bf16[128,256]{1,0:T(8,128)(2,1)S(1)} %get-tuple-element.53), channel_id=1, source_target_pairs={{0,24},{4,28},{8,16},{12,20},{16,8},{20,12},{24,0},{28,4},{32,56},... | collective-permute-start | bytes 196616 | tf_op jit(solution)/shard_map/ppermute | solution.py:311

commit v4 on v3

--- a/solution.py
+++ b/solution.py
@@ -19,11 +19,11 @@
     return pl.BlockSpec(shape, lambda *_: (0,) * len(shape))
 
 
-def tile_grads(tile_ids, dest_ids, rels, adjacency, grads, shards, chunk=16):
+def tile_grads(tile_ids, dest_ids, rels, adjacency, grads, shards, chunk=64):
     tiles = adjacency.shape[0]
     nblocks, _, width = grads.shape
-    slots = rels.shape[0]
-    capacity = slots // shards
+    capacity = rels.shape[0]
+    slots = shards * capacity
     rows = capacity * BLK + 8
 
     def kernel(slot_ref, dst_ref, rel_ref, adj_ref, grad_ref, out_ref, acc_ref):
@@ -51,7 +51,7 @@
                 for c in range(capacity):
                     s = o * capacity + c
                     out_ref[o, pl.ds(c * BLK, BLK), :] = acc_ref[s].astype(BF16)
-                    tail = jnp.where(lane // BLK == c, rel_ref[s].astype(F32), tail)
+                    tail = jnp.where(lane // BLK == c, rel_ref[c, o].astype(F32), tail)
                 out_ref[o, pl.ds(capacity * BLK, 8), :] = tail.astype(BF16)
 
     return pl.pallas_call(
@@ -72,52 +72,6 @@
     )(tile_ids, dest_ids, rels, adjacency, grads)
 
 
-def dense_tiles(tile_ids, dest_ids, adjacency, slots, nblocks, chunk=16, halves=2):
-    tiles = adjacency.shape[0]
-    per = nblocks // halves
-
-    def kernel(slot_ref, dst_ref, adj_ref, out_ref, acc_ref):
-        half = pl.program_id(0)
-        step = pl.program_id(1)
-
-        @pl.when(step == 0)
-        def _():
-            acc_ref[...] = jnp.zeros_like(acc_ref)
-
-        for u in range(chunk):
-            t = step * chunk + u
-            local = dst_ref[t] - half * per
-
-            @pl.when((local >= 0) & (local < per))
-            def _():
-                acc_ref[local, slot_ref[t]] += adj_ref[u].astype(F32)
-
-        @pl.when(step == pl.num_programs(1) - 1)
-        def _():
-            def store(s, carry):
-                for b in range(per):
-                    out_ref[pl.ds(b * BLK, BLK), pl.ds(pl.multiple_of(s * BLK, BLK), BLK)] = (
-                        acc_ref[b, s].astype(BF16)
-                    )
-                return carry
-
-            lax.fori_loop(0, slots, store, 0)
-
-    return pl.pallas_call(
-        kernel,
-        name="dense_tiles",
-        out_shape=jax.ShapeDtypeStruct((nblocks * BLK, slots * BLK), BF16),
-        grid_spec=pltpu.PrefetchScalarGridSpec(
-            num_scalar_prefetch=2,
-            grid=(halves, tiles // chunk),
-            in_specs=[pl.BlockSpec((chunk, BLK, BLK), lambda h, i, *_: (i, 0, 0))],
-            out_specs=pl.BlockSpec((per * BLK, slots * BLK), lambda h, i, *_: (h, 0)),
-            scratch_shapes=[pltpu.VMEM((per, slots, BLK, BLK), F32)],
-        ),
-        compiler_params=params(),
-    )(tile_ids, dest_ids, adjacency)
-
-
 def project(feats, rel_weights, nblocks):
     relations, _, width = rel_weights.shape
 
@@ -141,92 +95,99 @@
     )(feats, rel_weights)
 
 
-def select_blocks(slot_block, returned, blocks, nblocks, capacity, chunk=4):
+def tile_sums(tile_ids, dest_ids, adjacency, msgs, root_term, chunk=64):
+    tiles = adjacency.shape[0]
+
+    def kernel(slot_ref, dst_ref, adj_ref, msg_ref, root_ref, out_ref, acc_ref):
+        step = pl.program_id(0)
+
+        @pl.when(step == 0)
+        def _():
+            acc_ref[...] = root_ref[...]
+
+        for u in range(chunk):
+            t = step * chunk + u
+            acc_ref[dst_ref[t]] += jnp.dot(
+                adj_ref[u], msg_ref[slot_ref[t]], preferred_element_type=F32
+            )
+
+        @pl.when(step == pl.num_programs(0) - 1)
+        def _():
+            out_ref[...] = acc_ref[...].astype(BF16)
+
+    return pl.pallas_call(
+        kernel,
+        name="tile_sums",
+        out_shape=jax.ShapeDtypeStruct(root_term.shape, BF16),
+        grid_spec=pltpu.PrefetchScalarGridSpec(
+            num_scalar_prefetch=2,
+            grid=(tiles // chunk,),
+            in_specs=[
+                pl.BlockSpec((chunk, BLK, BLK), lambda i, *_: (i, 0, 0)),
+                whole(msgs.shape),
+                whole(root_term.shape),
+            ],
+            out_specs=whole(root_term.shape),
+            scratch_shapes=[pltpu.VMEM(root_term.shape, F32)],
+        ),
+        compiler_params=params(),
+    )(tile_ids, dest_ids, adjacency, msgs, root_term)
+
+
+def relation_of(ref, c):
+    return jnp.max(ref[:, c * BLK : (c + 1) * BLK].astype(F32)).astype(jnp.int32)
+
+
+def select_blocks(slot_block, returned, blocks, nblocks, capacity):
+    shards, _, width = returned.shape
+
+    def kernel(block_ref, rel_ref, in_ref, out_ref, sem_ref):
+        copies = []
+        for o in range(shards):
+            for c in range(capacity):
+                key = relation_of(rel_ref[o], c) * nblocks + block_ref[c, o]
+                copy = pltpu.make_async_copy(
+                    in_ref.at[key], out_ref.at[o, pl.ds(c * BLK, BLK)], sem_ref.at[o, c]
+                )
+                copy.start()
+                copies.append(copy)
+        for copy in copies:
+            copy.wait()
+
+    return pl.pallas_call(
+        kernel,
+        name="select_blocks",
+        out_shape=pltpu.HBM((shards, capacity * BLK, width), BF16),
+        grid_spec=pltpu.PrefetchScalarGridSpec(
+            num_scalar_prefetch=1,
+            grid=(1,),
+            in_specs=[
+                pl.BlockSpec((shards, 8, width), lambda i, *_: (0, capacity * BLK // 8, 0)),
+                whole(blocks.shape),
+            ],
+            out_specs=pl.BlockSpec(memory_space=pl.ANY),
+            scratch_shapes=[pltpu.SemaphoreType.DMA((shards, capacity))],
+        ),
+        compiler_params=params(),
+    )(slot_block, returned, blocks)
+
+
+def sum_by_key(slot_block, returned, relations, nblocks, chunk=8):
     shards, rows, width = returned.shape
-    relations = blocks.shape[0] // nblocks
-
-    def kernel(block_ref, rel_ref, in_ref, out_ref):
+    capacity = slot_block.shape[0]
+    bins = relations * nblocks
+
+    def kernel(block_ref, ret_ref, out_ref, acc_ref):
         step = pl.program_id(0)
+
+        @pl.when(step == 0)
+        def _():
+            acc_ref[...] = jnp.zeros_like(acc_ref)
+
         for u in range(chunk):
             for c in range(capacity):
-                block = block_ref[(step * chunk + u) * capacity + c]
-                rel = rel_ref[u, pl.ds(0, 1), pl.ds(c * BLK, BLK)].astype(F32)
-                rel = jnp.broadcast_to(rel, (BLK, BLK))
-                for j in range(width // BLK):
-                    cols = pl.ds(j * BLK, BLK)
-                    value = in_ref[block, :, cols].astype(F32)
-                    for r in range(1, relations):
-                        value = jnp.where(
-                            rel == r, in_ref[r * nblocks + block, :, cols].astype(F32), value
-                        )
-                    out_ref[u, pl.ds(c * BLK, BLK), cols] = value.astype(BF16)
-
-    return pl.pallas_call(
-        kernel,
-        name="select_blocks",
-        out_shape=jax.ShapeDtypeStruct((shards, capacity * BLK, width), BF16),
-        grid_spec=pltpu.PrefetchScalarGridSpec(
-            num_scalar_prefetch=1,
-            grid=(shards // chunk,),
-            in_specs=[
-                pl.BlockSpec((chunk, 8, width), lambda i, *_: (i, capacity * BLK // 8, 0)),
-                whole(blocks.shape),
-            ],
-            out_specs=pl.BlockSpec((chunk, capacity * BLK, width), lambda i, *_: (i, 0, 0)),
-        ),
-        compiler_params=params(),
-    )(slot_block, returned, blocks)
-
-
-def add_product(base, left, right, first, steps, out_type, depth=1024):
-    nodes, width = base.shape
-    rows = right.shape[1]
-    per = depth // rows
-
-    def kernel(base_ref, left_ref, right_ref, out_ref, acc_ref):
-        step = pl.program_id(0)
-
-        @pl.when(step == 0)
-        def _():
-            acc_ref[...] = base_ref[...]
-
-        acc_ref[...] += jnp.dot(
-            left_ref[...], right_ref[...].reshape(depth, width), preferred_element_type=F32
-        )
-
-        @pl.when(step == steps - 1)
-        def _():
-            out_ref[...] = acc_ref[...].astype(out_type)
-
-    return pl.pallas_call(
-        kernel,
-        name="add_product",
-        out_shape=jax.ShapeDtypeStruct((nodes, width), out_type),
-        grid=(steps,),
-        in_specs=[
-            whole(base.shape),
-            pl.BlockSpec((nodes, depth), lambda i: (0, first + i)),
-            pl.BlockSpec((per, rows, width), lambda i: (first + i, 0, 0)),
-        ],
-        out_specs=whole((nodes, width)),
-        scratch_shapes=[pltpu.VMEM((nodes, width), F32)],
-        compiler_params=params(),
-    )(base, left, right)
-
-
-def sum_by_key(keys, returned, bins, capacity, chunk=4):
-    shards, rows, width = returned.shape
-
-    def kernel(key_ref, ret_ref, out_ref, acc_ref):
-        step = pl.program_id(0)
-
-        @pl.when(step == 0)
-        def _():
-            acc_ref[...] = jnp.zeros_like(acc_ref)
-
-        for u in range(chunk):
-            for c in range(capacity):
-                key = key_ref[(step * chunk + u) * capacity + c]
+                rel = relation_of(ret_ref[u, pl.ds(capacity * BLK, 8), :], c)
+                key = rel * nblocks + block_ref[c, step * chunk + u]
                 acc_ref[key] += ret_ref[u, pl.ds(c * BLK, BLK), :].astype(F32)
 
         @pl.when(step == pl.num_programs(0) - 1)
@@ -236,7 +197,7 @@
     return pl.pallas_call(
         kernel,
         name="sum_by_key",
-        out_shape=jax.ShapeDtypeStruct((bins, BLK, width), BF16),
+        out_shape=pltpu.HBM((bins, BLK, width), BF16),
         grid_spec=pltpu.PrefetchScalarGridSpec(
             num_scalar_prefetch=1,
             grid=(shards // chunk,),
@@ -245,7 +206,7 @@
             scratch_shapes=[pltpu.VMEM((bins, BLK, width), F32)],
         ),
         compiler_params=params(),
-    )(keys, returned)
+    )(slot_block, returned)
 
 
 def weight_grads(coef, feats, source_grads, d_out, bases, chunk=128):
@@ -471,7 +432,7 @@
     slot_grads = tile_grads(
         tile_slot[0],
         tile_dst[0],
-        recv_rel.reshape(slots),
+        recv_rel[0].T,
         tile_adj[0],
         d_out.reshape(nblocks, BLK, width),
         shards,
@@ -485,16 +446,13 @@
     )
     projected = project(feats, rel_weights, nblocks)
     root_term = jnp.dot(feats, root_weight, preferred_element_type=F32)
-    dense = dense_tiles(tile_slot[0], tile_dst[0], tile_adj[0], slots, nblocks)
-
-    returned, dense = lax.optimization_barrier((returned, dense))
-    outgoing = select_blocks(slot_block.reshape(slots), returned, projected, nblocks, capacity)
+
+    requested = slot_block[0].T
+    outgoing = select_blocks(requested, returned, projected, nblocks, capacity)
     outgoing, returned = lax.optimization_barrier((outgoing, returned))
     incoming = lax.all_to_all(outgoing, "shard", 0, 0, tiled=True)
 
-    owner_rel = returned[:, capacity * BLK, :: BLK][:, :capacity].astype(jnp.int32)
-    keys = (owner_rel * nblocks + slot_block[0]).reshape(-1)
-    source_grads = sum_by_key(keys, returned, relations * nblocks, capacity)
+    source_grads = sum_by_key(requested, returned, relations, nblocks)
     source_grads = source_grads.reshape(relations, nblocks * BLK, width)
     stacked, dots = weight_grads(
         coef.astype(F32).reshape(-1), feats, source_grads, d_out, bases
@@ -505,6 +463,7 @@
 
     through = jnp.einsum("rno,rco->nc", source_grads, rel_weights, preferred_element_type=F32)
     through = through + jnp.dot(d_out, root_weight.T, preferred_element_type=F32)
+    through, dots = lax.optimization_barrier((through, dots))
     grad_feats = scatter_sum(
         through.reshape(reps, -1, width_in), "rep", 0, reps, my_rep
     ).astype(BF16)
@@ -514,16 +473,19 @@
     place = jnp.stack([me & 1, (me >> 3) & 3, (me >> 1) & 3]).astype(jnp.int32)
     got = exchange(chunk_of(stacked, (me & 1) ^ 1, 3).astype(BF16), "shard", 1)
     kept, *sends = first_stage(place, stacked, got, dots, 4)
-    grad_feats, *sends = lax.optimization_barrier((grad_feats, *sends))
+    grad_feats, sends[-1] = lax.optimization_barrier((grad_feats, sends[-1]))
     got = [exchange(x, "shard", k << 3) for k, x in zip((1, 2, 3), sends)]
-    total_steps = slots * BLK // 1024
-    early = total_steps // 2
-    partial = add_product(root_term, dense, incoming, 0, early, F32)
-    partial, kept = lax.optimization_barrier((partial, kept))
     kept, dots, *sends = second_stage(place, kept, dots, got, 4)
+    root_term, *sends = lax.optimization_barrier((root_term, *sends))
     got = [exchange(x, "shard", k << 1) for k, x in zip((1, 2, 3), sends)]
-    partial, kept = lax.optimization_barrier((partial, kept))
-    output = add_product(partial, dense, incoming, early, total_steps - early, BF16)
+    output = tile_sums(
+        tile_slot[0],
+        tile_dst[0],
+        tile_adj[0],
+        incoming.reshape(slots, BLK, width),
+        root_term.reshape(nblocks, BLK, width),
+    ).reshape(nblocks * BLK, width)
+    output, kept = lax.optimization_barrier((output, kept))
     grad_bases, grad_root, grad_coef = last_stage(kept, dots, got, relations)
     return (output, grad_feats, grad_bases, grad_root, grad_coef)
 

time: 194 us -> 179 us (0.923)
  Pallas kernels: 90 us -> 44.6 us
  waiting for transfers between devices: 33.2 us -> 74.6 us
  local copies, waits for them, and re-layouts: 24.6 us -> 16.8 us
    pallas_call x5 -> x3, Pallas kernels: 57.8 us -> 20.2 us  [the longest x1 9.78 us: tile_sums(): pl.pallas_call(kernel, name='tile_sums', out_shape=jax.ShapeDtypeStruct(r...]
    all_to_all x1, waiting for transfers between devices: 10 us -> 44.6 us  [body(): returned = lax.all_to_all(slot_grads, 'shard', 0, 0, tiled=True)]
    ppermute x13, waiting for transfers between devices: 23.2 us -> 30 us  [exchange(): lax.ppermute(x, axis, [(i, i ^ mask) for i in range(lax.axis_size(axis))])]
    pallas_call x1, Pallas kernels: 16.6 us -> 10.7 us  [tile_grads(): pl.pallas_call(kernel, name='tile_grads', out_shape=pltpu.HBM((shards, ro...]
    unnamed x41, local copies, waits for them, and re-layouts: 15.8 us -> 13 us
  transfers between devices with their start and end apart: 15 -> 15, of which waited for: 6 -> 8; matrix products, arithmetic and copies ran while one was open for 12% -> 7% of each run, Pallas kernels for 33% -> 16%
where the time goes in v4:
time: 179 us; the launch traced here: 178 us
  waiting for transfers between devices  74.6 us (42%)
  Pallas kernels  44.6 us (25%)
  starting transfers between devices  33.8 us (19%)
  local copies, waits for them, and re-layouts  16.8 us (9%)
  matrix products  4.74 us (3%)
  other arithmetic  2.49 us (1%)
    all_to_all x1, waiting for transfers between devices, body(): returned = lax.all_to_all(slot_grads, 'shard', 0, 0, tiled=True)  44.6 us
    ppermute x13, waiting for transfers between devices, exchange(): lax.ppermute(x, axis, [(i, i ^ mask) for i in range(lax.axis_size(axis))])  30 us
    ppermute x13, starting transfers between devices, exchange(): lax.ppermute(x, axis, [(i, i ^ mask) for i in range(lax.axis_size(axis))])  18.4 us
    unnamed x41, local copies, waits for them, and re-layouts  13 us
    pallas_call x1, Pallas kernels, tile_grads(): pl.pallas_call(kernel, name='tile_grads', out_shape=pltpu.HBM((shards, ro...  10.7 us
    pallas_call x1, Pallas kernels, tile_sums(): pl.pallas_call(kernel, name='tile_sums', out_shape=jax.ShapeDtypeStruct(r...  9.78 us
    all_to_all x1, starting transfers between devices, body(): returned = lax.all_to_all(slot_grads, 'shard', 0, 0, tiled=True)  8.67 us
    pallas_call x1, Pallas kernels, weight_grads(): pl.pallas_call(kernel, name='weight_grads', out_shape=(jax.ShapeDtypeStru...  8.66 us
  transfers between devices with their start and end apart: 15, of which 8 were waited for; matrix products, arithmetic and copies ran while one was open for 7% of the time, Pallas kernels for 16%

profile of v4, /device:TPU:0, one launch (start us, length us, event | category | flops | bytes accessed | tf_op | source)
XLA Modules:
  0.0 178.0 jit_solution(618155368264030146)
XLA Ops:
  0.6 0.0 copy-start
  0.6 0.0 copy-start.8
  0.7 1.1 copy-done.8
  1.7 0.7 copy-done.11
  2.4 0.7 copy-done.13
  3.1 0.7 copy-done.15
  3.8 10.7 %tile_grads.1 = bf16[32,264,256]{2,1,0:T(8,128)(2,1)} custom-call(s32[256]{0:T(256)S(1)} %bitcast.64, s32[256]{0:T(256)S(1)} %bitcast.66, s32[2,32]{1,0:T(2,128)S(1)} %bitcast.68, bf16[256,128,128]{2,1,0:T(8,128)(2,1)} %bitcast.69, bf16[8,128,256]{2,1,0:T(8,128)(2,1)S(1)} %bitcast.60), custom_call_target="tpu_custom_call" | custom-call | tf_op jit(solution)/shard_map/tile_grads/pallas_call | solution.py:57
  14.5 8.7 %all-to-all-start = ((bf16[32,264,256]{2,1,0:T(8,128)(2,1)}), bf16[32,264,256]{2,1,0:T(8,128)(2,1)}, u32[]{:S(2)}, u32[]{:S(2)}) async-start(bf16[32,264,256]{2,1,0:T(8,128)(2,1)} %tile_grads.1), calls=%async_computation | async-start | bytes 8650752 | tf_op jit(solution)/shard_map/all_to_all | solution.py:440
  23.2 0.0 copy-start.18
  23.2 1.2 copy.22
  24.4 1.3 convolution_convert_fusion
  25.8 0.0 copy-start.1
  25.8 0.4 copy.25
  26.3 0.0 copy-start.10
  26.3 0.9 copy-done.1
  27.2 3.0 %project.1.in_ref = bf16[40,128,256]{2,1,0:T(8,128)(2,1)S(1)} custom-call(bf16[1024,768]{1,0:T(8,128)(2,1)S(1)} %copy-done.1, bf16[5,768,256]{2,1,0:T(8,128)(2,1)S(1)} %bitcast.55), custom_call_target="tpu_custom_call" | custom-call | tf_op jit(solution)/shard_map/project/pallas_call | solution.py:84
  30.2 1.5 copy-done.2
  31.6 1.3 copy-done.4
  32.9 44.6 %all-to-all-done.rel_ref.ret_ref = bf16[32,264,256]{2,1,0:T(8,128)(2,1)} async-done(((bf16[32,264,256]{2,1,0:T(8,128)(2,1)}), bf16[32,264,256]{2,1,0:T(8,128)(2,1)}, u32[]{:S(2)}, u32[]{:S(2)}) %all-to-all-start) | async-done | bytes 4325408 | tf_op jit(solution)/shard_map/all_to_all | solution.py:440
  77.5 1.7 copy-done.3
  79.3 4.2 %select_blocks.1 = bf16[32,256,256]{2,1,0:T(8,128)(2,1)} custom-call(s32[2,32]{1,0:T(2,128)S(1)} %bitcast.62, bf16[32,264,256]{2,1,0:T(8,128)(2,1)} %all-to-all-done.rel_ref.ret_ref, bf16[40,128,256]{2,1,0:T(8,128)(2,1)S(1)} %copy-done.3), custom_call_target="tpu_custom_call" | custom-call | tf_op jit(solution)/shard_map/select_blocks/pallas_call | solution.py:157
  83.5 6.8 %all-to-all-start.1 = ((bf16[32,256,256]{2,1,0:T(8,128)(2,1)}), bf16[32,256,256]{2,1,0:T(8,128)(2,1)}, u32[]{:S(2)}, u32[]{:S(2)}) async-start(bf16[32,256,256]{2,1,0:T(8,128)(2,1)} %select_blocks.1), calls=%async_computation.1 | async-start | bytes 8388608 | tf_op jit(solution)/shard_map/all_to_all | solution.py:453
  90.3 0.1 copy.18
  90.4 0.1 reshape.58.coef_ref
  90.4 6.2 %sum_by_key.1 = bf16[40,128,256]{2,1,0:T(8,128)(2,1)} custom-call(s32[2,32]{1,0:T(2,128)S(1)} %bitcast.63, bf16[32,264,256]{2,1,0:T(8,128)(2,1)} %all-to-all-done.rel_ref.ret_ref), custom_call_target="tpu_custom_call" | custom-call | tf_op jit(solution)/shard_map/sum_by_key/pallas_call | solution.py:197
  96.6 8.7 %weight_grads.1 = (f32[5,768,256]{2,1,0:T(8,128)}, f32[8,128]{1,0:T(8,128)S(1)}) custom-call(f32[20]{0:T(128)S(1)} %reshape.58.coef_ref, bf16[1024,768]{1,0:T(8,128)(2,1)S(1)} %copy-done.1, bf16[5,1024,256]{2,1,0:T(8,128)(2,1)} %bitcast.72, bf16[1024,256]{1,0:T(8,128)(2,1)S(1)} %copy-done.9, bf16[4,768,256]{2,1,0:T(8,128)(2,1)S(1)} %copy-done.6), custom_call_target="tpu_custom_call" | custom-call | tf_op jit(solution)/shard_map/weight_grads/pallas_call | solution.py:245
  105.3 0.2 collective-permute-start.1
  105.5 2.2 %fusion.8 = f32[1024,768,1]{1,0,2:T(8,128)S(1)} fusion(bf16[5,1024,256]{2,1,0:T(8,128)(2,1)S(1)} %bitcast.73, bf16[5,768,256]{2,1,0:T(8,128)(2,1)S(1)} %bitcast.56), kind=kOutput, calls=%fused_computation.17 | convolution fusion | flops 2013265920 | bytes 7733248 | tf_op jit(solution)/shard_map/rno,rco->nc/dot_general | solution.py:464
  107.8 1.6 collective-permute-start.2
  109.3 2.6 %fusion = bf16[5,4,4,24,256]{4,3,2,1,0:T(8,128)(2,1)} fusion(f32[5,4,4,2,24,256]{5,4,3,2,1,0:T(8,128)} %bitcast.58, s32[]{:T(128)S(6)} %select_n.17), kind=kLoop, calls=%fused_computation.4 | loop fusion | bytes 1966084 | tf_op jit(solution)/shard_map/convert_element_type | solution.py:474
  112.0 0.0 collective-permute-start
  112.0 0.0 collective-permute-done.2
  112.0 3.0 %collective-permute-start.3 = (f32[8,128]{1,0:T(8,128)S(1)}, f32[8,128]{1,0:T(8,128)S(1)}, u32[]{:S(2)}, u32[]{:S(2)}) collective-permute-start(f32[8,128]{1,0:T(8,128)S(1)} %add.41), channel_id=1, source_target_pairs={{0,2},{1,3},{2,0},{3,1},{4,6},{5,7},{6,4},{7,5},{8,10},{9,11},{10,... | collective-permute-start | bytes 12296 | tf_op jit(solution)/shard_map/ppermute | solution.py:272
  115.0 0.6 bitcast_add_fusion
  115.6 1.8 collective-permute-done.3
  117.4 1.0 fusion.4
  118.4 0.7 collective-permute-start.6
  119.1 2.6 %collective-permute-start.8 = (bf16[256,768]{1,0:T(8,128)(2,1)}, bf16[256,768]{1,0:T(8,128)(2,1)}, u32[]{:S(2)}, u32[]{:S(2)}) collective-permute-start(bf16[256,768]{1,0:T(8,128)(2,1)} %get-tuple-element.68), channel_id=1, source_target_pairs={{0,3},{1,2},{2,1},{3,0},{4,7},{5,6},{6,5},{7,4},{8,11},{9,10},{10,... | collective-permute-start | bytes 1179656 | tf_op jit(solution)/shard_map/ppermute | solution.py:272
  121.7 0.8 collective-permute-start.7
  122.5 0.1 pad_add_fusion.place_ref
  122.5 8.2 %collective-permute-done.6 = bf16[256,768]{1,0:T(8,128)(2,1)} collective-permute-done((bf16[256,768]{1,0:T(8,128)(2,1)}, bf16[256,768]{1,0:T(8,128)(2,1)}, u32[]{:S(2)}, u32[]{:S(2)}) %collective-permute-start.6) | collective-permute-done | bytes 393248 | tf_op jit(solution)/shard_map/ppermute | solution.py:272
  130.7 7.5 %collective-permute-done.8 = bf16[256,768]{1,0:T(8,128)(2,1)} collective-permute-done((bf16[256,768]{1,0:T(8,128)(2,1)}, bf16[256,768]{1,0:T(8,128)(2,1)}, u32[]{:S(2)}, u32[]{:S(2)}) %collective-permute-start.8) | collective-permute-done | bytes 393248 | tf_op jit(solution)/shard_map/ppermute | solution.py:272
  138.2 1.0 collective-permute-done.7
  139.2 2.4 %fusion.3 = bf16[256,768]{1,0:T(8,128)(2,1)} fusion(bf16[256,768]{1,0:T(8,128)(2,1)} %collective-permute-done.8, bf16[256,768]{1,0:T(8,128)(2,1)} %collective-permute-done.7, bf16[256,768]{1,0:T(8,128)(2,1)} %collective-permute-done.6, f32[4,256,768]{2,1,0:T(8,128)} %bitcast.76, s32[]{:T(128)S(6)} %select_n.18), kind=kLoop, calls=%fused_computation.8 | loop fusion | flops 1376256 | bytes 2359300 | tf_op jit(solution)/shard_map/convert_element_type | solution.py:469
  141.6 0.0 collective-permute-done.got_ref
  141.6 2.1 %copy-done.7 = f32[5,768,256]{2,1,0:T(8,128)S(1)} copy-done((f32[5,768,256]{2,1,0:T(8,128)S(1)}, f32[5,768,256]{2,1,0:T(8,128)}, u32[]{:S(2)}) %copy-start.7) | copy-done | bytes 3932184
  143.7 0.8 first_stage.1
  144.4 0.0 copy-start.12
  144.5 0.0 copy-start.14
  144.5 1.8 collective-permute-start.4
  146.2 2.7 %collective-permute-start.5 = (bf16[488,256]{1,0:T(8,128)(2,1)S(1)}, bf16[488,256]{1,0:T(8,128)(2,1)S(1)}, u32[]{:S(2)}, u32[]{:S(2)}) collective-permute-start(bf16[488,256]{1,0:T(8,128)(2,1)S(1)} %get-tuple-element.38), channel_id=1, source_target_pairs={{0,64},{4,68},{8,72},{12,76},{16,80},{20,84},{24,88},{28,92},{32,9... | collective-permute-start | bytes 749576 | tf_op jit(solution)/shard_map/ppermute | solution.py:272
  149.0 0.3 collective-permute-start.9
  149.2 0.6 fusion.7
  149.8 3.7 %collective-permute-done.4.refs_0_ = bf16[488,256]{1,0:T(8,128)(2,1)S(1)} collective-permute-done((bf16[488,256]{1,0:T(8,128)(2,1)S(1)}, bf16[488,256]{1,0:T(8,128)(2,1)S(1)}, u32[]{:S(2)}, u32[]{:S(2)}) %collective-permute-start.4) | collective-permute-done | bytes 249888 | tf_op jit(solution)/shard_map/ppermute | solution.py:272
  153.5 5.3 %collective-permute-done.5.refs_1_ = bf16[488,256]{1,0:T(8,128)(2,1)S(1)} collective-permute-done((bf16[488,256]{1,0:T(8,128)(2,1)S(1)}, bf16[488,256]{1,0:T(8,128)(2,1)S(1)}, u32[]{:S(2)}, u32[]{:S(2)}) %collective-permute-start.5) | collective-permute-done | bytes 249888 | tf_op jit(solution)/shard_map/ppermute | solution.py:272
  158.9 2.6 %collective-permute-done.9.refs_2_ = bf16[488,256]{1,0:T(8,128)(2,1)S(1)} collective-permute-done((bf16[488,256]{1,0:T(8,128)(2,1)S(1)}, bf16[488,256]{1,0:T(8,128)(2,1)S(1)}, u32[]{:S(2)}, u32[]{:S(2)}) %collective-permute-start.9) | collective-permute-done | bytes 249888 | tf_op jit(solution)/shard_map/ppermute | solution.py:272
  161.5 0.7 second_stage.1
  162.1 1.6 collective-permute-start.10
  163.7 2.7 %collective-permute-start.11 = (bf16[128,256]{1,0:T(8,128)(2,1)S(1)}, bf16[128,256]{1,0:T(8,128)(2,1)S(1)}, u32[]{:S(2)}, u32[]{:S(2)}) collective-permute-start(bf16[128,256]{1,0:T(8,128)(2,1)S(1)} %get-tuple-element.52), channel_id=1, source_target_pairs={{0,16},{4,20},{8,24},{12,28},{16,0},{20,4},{24,8},{28,12},{32,48},... | collective-permute-start | bytes 196616 | tf_op jit(solution)/shard_map/ppermute | solution.py:272
  166.4 0.5 collective-permute-start.12
  166.9 0.0 all-to-all-done.1
  166.9 9.8 %tile_sums.1 = bf16[8,128,256]{2,1,0:T(8,128)(2,1)} custom-call(s32[256]{0:T(256)S(1)} %bitcast.65, s32[256]{0:T(256)S(1)} %bitcast.67, bf16[256,128,128]{2,1,0:T(8,128)(2,1)} %bitcast.70, bf16[64,128,256]{2,1,0:T(8,128)(2,1)} %bitcast.8.msg_ref, f32[8,128,256]{2,1,0:T(8,128)S(1)} %bitcast.61), custom_call_target="tpu_custom_call" | custom-call | tf_op jit(solution)/shard_map/tile_sums/pallas_call | solution.py:118
  176.7 0.7 last_stage.1
  177.4 0.7 copy.20
  (29 shorter events, 0.1 us)
Async XLA Ops:
  0.6 114.4 %copy-start = (bf16[768,256]{1,0:T(8,128)(2,1)S(1)}, bf16[768,256]{1,0:T(8,128)(2,1)}, u32[]{:S(2)}) copy-start(bf16[768,256]{1,0:T(8,128)(2,1)} %param.13) | copy-start | bytes 1179652
  0.6 1.1 copy-start.8
  1.7 0.7 copy-start.11
  2.4 0.7 copy-start.13
  3.1 0.7 copy-start.15
  14.5 8.7 %copy-start.6 = (bf16[4,768,256]{2,1,0:T(8,128)(2,1)S(1)}, bf16[4,768,256]{2,1,0:T(8,128)(2,1)}, u32[]{:S(2)}) copy-start(bf16[4,768,256]{2,1,0:T(8,128)(2,1)} %base_ref.1) | copy-start | bytes 4718596
  14.5 63.0 %all-to-all-start = ((bf16[32,264,256]{2,1,0:T(8,128)(2,1)}), bf16[32,264,256]{2,1,0:T(8,128)(2,1)}, u32[]{:S(2)}, u32[]{:S(2)}) async-start(bf16[32,264,256]{2,1,0:T(8,128)(2,1)} %tile_grads.1), calls=%async_computation | async-start | bytes 8650752 | tf_op jit(solution)/shard_map/all_to_all | solution.py:440
  23.2 1.2 copy-start.18
  25.8 1.4 copy-start.1
  26.3 51.3 %copy-start.10 = (s32[1,32,2]{1,2,0:T(2,128)S(1)}, s32[1,32,2]{1,2,0:T(2,128)}, u32[]{:S(2)}) copy-start(s32[1,32,2]{1,2,0:T(2,128)} %param.14) | copy-start | bytes 772
  30.2 1.5 copy-start.2
  31.6 1.3 copy-start.4
  77.5 1.7 copy-start.3
  83.5 83.4 %all-to-all-start.1 = ((bf16[32,256,256]{2,1,0:T(8,128)(2,1)}), bf16[32,256,256]{2,1,0:T(8,128)(2,1)}, u32[]{:S(2)}, u32[]{:S(2)}) async-start(bf16[32,256,256]{2,1,0:T(8,128)(2,1)} %select_blocks.1), calls=%async_computation.1 | async-start | bytes 8388608 | tf_op jit(solution)/shard_map/all_to_all | solution.py:453
  90.4 6.2 %copy-start.9 = (bf16[1024,256]{1,0:T(8,128)(2,1)S(1)}, bf16[1024,256]{1,0:T(8,128)(2,1)}, u32[]{:S(2)}) copy-start(bf16[1024,256]{1,0:T(8,128)(2,1)} %grad_ref.1) | copy-start | bytes 1572868
  96.6 8.9 %copy-start.5 = (bf16[1,5,768,256]{3,2,1,0:T(8,128)(2,1)S(1)}, bf16[1,5,768,256]{3,2,1,0:T(8,128)(2,1)}, u32[]{:S(2)}) copy-start(bf16[1,5,768,256]{3,2,1,0:T(8,128)(2,1)} %copy-done.4) | copy-start | bytes 5898244
  96.6 8.9 %copy-start.16 = (bf16[40,128,256]{2,1,0:T(8,128)(2,1)S(1)}, bf16[40,128,256]{2,1,0:T(8,128)(2,1)}, u32[]{:S(2)}) copy-start(bf16[40,128,256]{2,1,0:T(8,128)(2,1)} %sum_by_key.1) | copy-start | bytes 7864324
  105.3 2.4 %collective-permute-start.1 = (f32[8,128]{1,0:T(8,128)S(1)}, f32[8,128]{1,0:T(8,128)S(1)}, u32[]{:S(2)}, u32[]{:S(2)}) collective-permute-start(f32[8,128]{1,0:T(8,128)S(1)} %get-tuple-element.34), channel_id=1, source_target_pairs={{0,4},{4,0},{8,12},{12,8},{16,20},{20,16},{24,28},{28,24},{32,36},... | collective-permute-start | bytes 12296 | tf_op jit(solution)/shard_map/ppermute | solution.py:272
  107.8 4.2 %collective-permute-start.2 = (f32[8,128]{1,0:T(8,128)S(1)}, f32[8,128]{1,0:T(8,128)S(1)}, u32[]{:S(2)}, u32[]{:S(2)}) collective-permute-start(f32[8,128]{1,0:T(8,128)S(1)} %add.40), channel_id=1, source_target_pairs={{0,1},{1,0},{2,3},{3,2},{4,5},{5,4},{6,7},{7,6},{8,9},{9,8},{10,11... | collective-permute-start | bytes 12296 | tf_op jit(solution)/shard_map/ppermute | solution.py:272
  112.0 29.6 %collective-permute-start = (bf16[5,4,4,24,256]{4,3,2,1,0:T(8,128)(2,1)}, bf16[5,4,4,24,256]{4,3,2,1,0:T(8,128)(2,1)S(1)}, u32[]{:S(2)}, u32[]{:S(2)}) collective-permute-start(bf16[5,4,4,24,256]{4,3,2,1,0:T(8,128)(2,1)} %fusion), channel_id=1, source_target_pairs={{0,4},{4,0},{8,12},{12,8},{16,20},{20,16},{24,28},{28,24},{32,36},... | collective-permute-start | bytes 2949128 | tf_op jit(solution)/shard_map/ppermute | solution.py:272
  112.0 5.3 %collective-permute-start.3 = (f32[8,128]{1,0:T(8,128)S(1)}, f32[8,128]{1,0:T(8,128)S(1)}, u32[]{:S(2)}, u32[]{:S(2)}) collective-permute-start(f32[8,128]{1,0:T(8,128)S(1)} %add.41), channel_id=1, source_target_pairs={{0,2},{1,3},{2,0},{3,1},{4,6},{5,7},{6,4},{7,5},{8,10},{9,11},{10,... | collective-permute-start | bytes 12296 | tf_op jit(solution)/shard_map/ppermute | solution.py:272
  115.6 1.8 copy-start.17
  118.4 12.3 %collective-permute-start.6 = (bf16[256,768]{1,0:T(8,128)(2,1)}, bf16[256,768]{1,0:T(8,128)(2,1)}, u32[]{:S(2)}, u32[]{:S(2)}) collective-permute-start(bf16[256,768]{1,0:T(8,128)(2,1)} %get-tuple-element.67), channel_id=1, source_target_pairs={{0,1},{1,0},{2,3},{3,2},{4,5},{5,4},{6,7},{7,6},{8,9},{9,8},{10,11... | collective-permute-start | bytes 1179656 | tf_op jit(solution)/shard_map/ppermute | solution.py:272
  119.1 19.1 %collective-permute-start.8 = (bf16[256,768]{1,0:T(8,128)(2,1)}, bf16[256,768]{1,0:T(8,128)(2,1)}, u32[]{:S(2)}, u32[]{:S(2)}) collective-permute-start(bf16[256,768]{1,0:T(8,128)(2,1)} %get-tuple-element.68), channel_id=1, source_target_pairs={{0,3},{1,2},{2,1},{3,0},{4,7},{5,6},{6,5},{7,4},{8,11},{9,10},{10,... | collective-permute-start | bytes 1179656 | tf_op jit(solution)/shard_map/ppermute | solution.py:272
  121.7 17.5 %collective-permute-start.7 = (bf16[256,768]{1,0:T(8,128)(2,1)S(1)}, bf16[256,768]{1,0:T(8,128)(2,1)}, u32[]{:S(2)}, u32[]{:S(2)}) collective-permute-start(bf16[256,768]{1,0:T(8,128)(2,1)S(1)} %get-tuple-element.69), channel_id=1, source_target_pairs={{0,2},{1,3},{2,0},{3,1},{4,6},{5,7},{6,4},{7,5},{8,10},{9,11},{10,... | collective-permute-start | bytes 1179656 | tf_op jit(solution)/shard_map/ppermute | solution.py:272
  141.6 2.1 %copy-start.7 = (f32[5,768,256]{2,1,0:T(8,128)S(1)}, f32[5,768,256]{2,1,0:T(8,128)}, u32[]{:S(2)}) copy-start(f32[5,768,256]{2,1,0:T(8,128)} %get-tuple-element.33) | copy-start | bytes 11796484
  144.4 22.5 %copy-start.12 = (s32[1,256]{1,0:T(1,128)S(1)}, s32[1,256]{1,0:T(1,128)}, u32[]{:S(2)}) copy-start(s32[1,256]{1,0:T(1,128)} %param.16) | copy-start | bytes 3076
  144.5 22.4 %copy-start.14 = (s32[1,256]{1,0:T(1,128)S(1)}, s32[1,256]{1,0:T(1,128)}, u32[]{:S(2)}) copy-start(s32[1,256]{1,0:T(1,128)} %param.17) | copy-start | bytes 3076
  144.5 9.1 %collective-permute-start.4 = (bf16[488,256]{1,0:T(8,128)(2,1)S(1)}, bf16[488,256]{1,0:T(8,128)(2,1)S(1)}, u32[]{:S(2)}, u32[]{:S(2)}) collective-permute-start(bf16[488,256]{1,0:T(8,128)(2,1)S(1)} %get-tuple-element.37), channel_id=1, source_target_pairs={{0,32},{4,36},{8,40},{12,44},{16,48},{20,52},{24,56},{28,60},{32,0... | collective-permute-start | bytes 749576 | tf_op jit(solution)/shard_map/ppermute | solution.py:272
  146.2 12.6 %collective-permute-start.5 = (bf16[488,256]{1,0:T(8,128)(2,1)S(1)}, bf16[488,256]{1,0:T(8,128)(2,1)S(1)}, u32[]{:S(2)}, u32[]{:S(2)}) collective-permute-start(bf16[488,256]{1,0:T(8,128)(2,1)S(1)} %get-tuple-element.38), channel_id=1, source_target_pairs={{0,64},{4,68},{8,72},{12,76},{16,80},{20,84},{24,88},{28,92},{32,9... | collective-permute-start | bytes 749576 | tf_op jit(solution)/shard_map/ppermute | solution.py:272
  149.0 12.5 %collective-permute-start.9 = (bf16[488,256]{1,0:T(8,128)(2,1)S(1)}, bf16[488,256]{1,0:T(8,128)(2,1)S(1)}, u32[]{:S(2)}, u32[]{:S(2)}) collective-permute-start(bf16[488,256]{1,0:T(8,128)(2,1)S(1)} %get-tuple-element.41), channel_id=1, source_target_pairs={{0,96},{4,100},{8,104},{12,108},{16,112},{20,116},{24,120},{28,124... | collective-permute-start | bytes 749576 | tf_op jit(solution)/shard_map/ppermute | solution.py:272
  162.1 14.6 %collective-permute-start.10 = (bf16[128,256]{1,0:T(8,128)(2,1)S(1)}, bf16[128,256]{1,0:T(8,128)(2,1)S(1)}, u32[]{:S(2)}, u32[]{:S(2)}) collective-permute-start(bf16[128,256]{1,0:T(8,128)(2,1)S(1)} %get-tuple-element.51), channel_id=1, source_target_pairs={{0,8},{4,12},{8,0},{12,4},{16,24},{20,28},{24,16},{28,20},{32,40},... | collective-permute-start | bytes 196616 | tf_op jit(solution)/shard_map/ppermute | solution.py:272
  163.7 13.0 %collective-permute-start.11 = (bf16[128,256]{1,0:T(8,128)(2,1)S(1)}, bf16[128,256]{1,0:T(8,128)(2,1)S(1)}, u32[]{:S(2)}, u32[]{:S(2)}) collective-permute-start(bf16[128,256]{1,0:T(8,128)(2,1)S(1)} %get-tuple-element.52), channel_id=1, source_target_pairs={{0,16},{4,20},{8,24},{12,28},{16,0},{20,4},{24,8},{28,12},{32,48},... | collective-permute-start | bytes 196616 | tf_op jit(solution)/shard_map/ppermute | solution.py:272
  166.4 10.3 %collective-permute-start.12 = (bf16[128,256]{1,0:T(8,128)(2,1)S(1)}, bf16[128,256]{1,0:T(8,128)(2,1)S(1)}, u32[]{:S(2)}, u32[]{:S(2)}) collective-permute-start(bf16[128,256]{1,0:T(8,128)(2,1)S(1)} %get-tuple-element.53), channel_id=1, source_target_pairs={{0,24},{4,28},{8,16},{12,20},{16,8},{20,12},{24,0},{28,4},{32,56},... | collective-permute-start | bytes 196616 | tf_op jit(solution)/shard_map/ppermute | solution.py:272

commit v5 on v4

--- a/solution.py
+++ b/solution.py
@@ -13,6 +13,10 @@
 
 def params():
     return pltpu.CompilerParams(vmem_limit_bytes=VMEM_LIMIT)
+
+
+def in_hbm(x):
+    return pltpu.with_memory_space_constraint(x, pltpu.HBM)
 
 
 def whole(shape):
@@ -69,7 +73,7 @@
             scratch_shapes=[pltpu.VMEM((slots, BLK, width), F32)],
         ),
         compiler_params=params(),
-    )(tile_ids, dest_ids, rels, adjacency, grads)
+    )(in_hbm(tile_ids), in_hbm(dest_ids), in_hbm(rels), adjacency, in_hbm(grads))
 
 
 def project(feats, rel_weights, nblocks):
@@ -84,7 +88,7 @@
     return pl.pallas_call(
         kernel,
         name="project",
-        out_shape=jax.ShapeDtypeStruct((relations * nblocks, BLK, width), BF16),
+        out_shape=pltpu.HBM((relations * nblocks, BLK, width), BF16),
         grid=(relations,),
         in_specs=[
             whole(feats.shape),
@@ -131,7 +135,7 @@
             scratch_shapes=[pltpu.VMEM(root_term.shape, F32)],
         ),
         compiler_params=params(),
-    )(tile_ids, dest_ids, adjacency, msgs, root_term)
+    )(in_hbm(tile_ids), in_hbm(dest_ids), adjacency, msgs, root_term)
 
 
 def relation_of(ref, c):
@@ -163,13 +167,13 @@
             grid=(1,),
             in_specs=[
                 pl.BlockSpec((shards, 8, width), lambda i, *_: (0, capacity * BLK // 8, 0)),
-                whole(blocks.shape),
+                pl.BlockSpec(memory_space=pl.ANY),
             ],
             out_specs=pl.BlockSpec(memory_space=pl.ANY),
             scratch_shapes=[pltpu.SemaphoreType.DMA((shards, capacity))],
         ),
         compiler_params=params(),
-    )(slot_block, returned, blocks)
+    )(in_hbm(slot_block), returned, in_hbm(blocks))
 
 
 def sum_by_key(slot_block, returned, relations, nblocks, chunk=8):
@@ -239,7 +243,7 @@
             for r in range(relations):
                 for b in range(nbase):
                     total = jnp.sum(acc_ref[r * nbase + b])
-                    tile = jnp.where((row == r) & (lane == b), total, tile)
+                    tile = jnp.where((row == b) & (lane == r), total, tile)
             dots_ref[...] = tile
 
     return pl.pallas_call(
@@ -393,7 +397,7 @@
         sums += [sum_terms(g[pl.ds(length, 8), :]) for g in gots]
         while len(sums) > 1:
             sums = [sums[i] + sums[i + 1] for i in range(0, len(sums), 2)]
-        coef_ref[...] = sums[0][:relations, :nbase]
+        coef_ref[...] = sums[0][:nbase, :relations]
         for p in range(parts):
             value = own_ref[p]
             for g in gots:
@@ -403,7 +407,7 @@
             else:
                 root_ref[...] = value
 
-    shapes = ((nbase, rows, width), (rows, width), (relations, nbase))
+    shapes = ((nbase, rows, width), (rows, width), (nbase, relations))
     return pl.pallas_call(
         kernel,
         name="last_stage",
@@ -463,21 +467,16 @@
 
     through = jnp.einsum("rno,rco->nc", source_grads, rel_weights, preferred_element_type=F32)
     through = through + jnp.dot(d_out, root_weight.T, preferred_element_type=F32)
-    through, dots = lax.optimization_barrier((through, dots))
-    grad_feats = scatter_sum(
-        through.reshape(reps, -1, width_in), "rep", 0, reps, my_rep
-    ).astype(BF16)
-
     rows = width_in // shards
     stacked = stacked.reshape(nbase + 1, 4, 4, 2, rows, width)
     place = jnp.stack([me & 1, (me >> 3) & 3, (me >> 1) & 3]).astype(jnp.int32)
     got = exchange(chunk_of(stacked, (me & 1) ^ 1, 3).astype(BF16), "shard", 1)
     kept, *sends = first_stage(place, stacked, got, dots, 4)
-    grad_feats, sends[-1] = lax.optimization_barrier((grad_feats, sends[-1]))
+    through, *sends = lax.optimization_barrier((through, *sends))
     got = [exchange(x, "shard", k << 3) for k, x in zip((1, 2, 3), sends)]
-    kept, dots, *sends = second_stage(place, kept, dots, got, 4)
-    root_term, *sends = lax.optimization_barrier((root_term, *sends))
-    got = [exchange(x, "shard", k << 1) for k, x in zip((1, 2, 3), sends)]
+    grad_feats = scatter_sum(
+        through.reshape(reps, -1, width_in), "rep", 0, reps, my_rep
+    ).astype(BF16)
     output = tile_sums(
         tile_slot[0],
         tile_dst[0],
@@ -485,9 +484,11 @@
         incoming.reshape(slots, BLK, width),
         root_term.reshape(nblocks, BLK, width),
     ).reshape(nblocks * BLK, width)
-    output, kept = lax.optimization_barrier((output, kept))
+    output, grad_feats, kept = lax.optimization_barrier((output, grad_feats, kept))
+    kept, dots, *sends = second_stage(place, kept, dots, got, 4)
+    got = [exchange(x, "shard", k << 1) for k, x in zip((1, 2, 3), sends)]
     grad_bases, grad_root, grad_coef = last_stage(kept, dots, got, relations)
-    return (output, grad_feats, grad_bases, grad_root, grad_coef)
+    return (output, grad_feats, grad_bases, grad_root, grad_coef.T)
 
 
 def solution(mesh):

time: 179 us -> 294 us (1.64)
  Pallas kernels: 44.6 us -> 172 us
  waiting for transfers between devices: 74.6 us -> 64.6 us
  local copies, waits for them, and re-layouts: 16.8 us -> 9.35 us
    pallas_call x1, Pallas kernels: 4.21 us -> 130 us  [select_blocks(): pl.pallas_call(kernel, name='select_blocks', out_shape=pltpu.HBM((shards,...]
    ppermute x13, waiting for transfers between devices: 30 us -> 19.7 us  [exchange(): lax.ppermute(x, axis, [(i, i ^ mask) for i in range(lax.axis_size(axis))])]
    unnamed x41 -> x28, local copies, waits for them, and re-layouts: 13 us -> 5.42 us
  transfers between devices with their start and end apart: 15 -> 15, of which waited for: 8 -> 6; matrix products, arithmetic and copies ran while one was open for 7% -> 5% of each run, Pallas kernels for 16% -> 10%
where the time goes in v5:
time: 294 us; the launch traced here: 293 us
  Pallas kernels  172 us (59%)
  waiting for transfers between devices  64.6 us (22%)
  starting transfers between devices  36.7 us (12%)
  local copies, waits for them, and re-layouts  9.35 us (3%)
  matrix products  7.09 us (2%)
    pallas_call x1, Pallas kernels, select_blocks(): pl.pallas_call(kernel, name='select_blocks', out_shape=pltpu.HBM((shards,...  130 us
    all_to_all x1, waiting for transfers between devices, body(): returned = lax.all_to_all(slot_grads, 'shard', 0, 0, tiled=True)  44.9 us
    ppermute x13, starting transfers between devices, exchange(): lax.ppermute(x, axis, [(i, i ^ mask) for i in range(lax.axis_size(axis))])  21.3 us
    ppermute x13, waiting for transfers between devices, exchange(): lax.ppermute(x, axis, [(i, i ^ mask) for i in range(lax.axis_size(axis))])  19.7 us
    pallas_call x1, Pallas kernels, tile_grads(): pl.pallas_call(kernel, name='tile_grads', out_shape=pltpu.HBM((shards, ro...  11.1 us
    pallas_call x1, Pallas kernels, tile_sums(): pl.pallas_call(kernel, name='tile_sums', out_shape=jax.ShapeDtypeStruct(r...  9.92 us
    all_to_all x1, starting transfers between devices, body(): returned = lax.all_to_all(slot_grads, 'shard', 0, 0, tiled=True)  8.66 us
    pallas_call x1, Pallas kernels, weight_grads(): pl.pallas_call(kernel, name='weight_grads', out_shape=(jax.ShapeDtypeStru...  8.36 us
  transfers between devices with their start and end apart: 15, of which 6 were waited for; matrix products, arithmetic and copies ran while one was open for 5% of the time, Pallas kernels for 10%

profile of v5, /device:TPU:0, one launch (start us, length us, event | category | flops | bytes accessed | tf_op | source)
XLA Modules:
  0.0 293.3 jit_solution(227938940365187025)
XLA Ops:
  0.6 0.0 copy-start
  0.6 11.1 %tile_grads.1 = bf16[32,264,256]{2,1,0:T(8,128)(2,1)} custom-call(s32[256]{0:T(256)} %bitcast.74, s32[256]{0:T(256)} %bitcast.76, s32[2,32]{1,0:T(2,128)} %bitcast.78, bf16[256,128,128]{2,1,0:T(8,128)(2,1)} %bitcast.65, bf16[8,128,256]{2,1,0:T(8,128)(2,1)} %bitcast.61), custom_call_target="tpu_custom_call" | custom-call | tf_op jit(solution)/shard_map/tile_grads/pallas_call | solution.py:61
  11.8 8.7 %all-to-all-start = ((bf16[32,264,256]{2,1,0:T(8,128)(2,1)}), bf16[32,264,256]{2,1,0:T(8,128)(2,1)}, u32[]{:S(2)}, u32[]{:S(2)}) async-start(bf16[32,264,256]{2,1,0:T(8,128)(2,1)} %tile_grads.1), calls=%async_computation | async-start | bytes 8650752 | tf_op jit(solution)/shard_map/all_to_all | solution.py:444
  20.4 0.0 copy-start.12
  20.4 0.0 copy-done.3
  20.5 1.2 copy.20
  21.7 0.0 copy-done.12
  21.7 1.3 convolution_convert_fusion
  23.0 0.0 copy-start.1
  23.0 0.4 copy.23
  23.5 0.9 copy-done.1
  24.4 4.2 %project.1.in_ref = bf16[40,128,256]{2,1,0:T(8,128)(2,1)} custom-call(bf16[1024,768]{1,0:T(8,128)(2,1)S(1)} %copy-done.1, bf16[5,768,256]{2,1,0:T(8,128)(2,1)S(1)} %bitcast.56), custom_call_target="tpu_custom_call" | custom-call | tf_op jit(solution)/shard_map/project/pallas_call | solution.py:88
  28.6 1.3 copy-done.2
  29.9 44.9 %all-to-all-done.rel_ref.ret_ref = bf16[32,264,256]{2,1,0:T(8,128)(2,1)} async-done(((bf16[32,264,256]{2,1,0:T(8,128)(2,1)}), bf16[32,264,256]{2,1,0:T(8,128)(2,1)}, u32[]{:S(2)}, u32[]{:S(2)}) %all-to-all-start) | async-done | bytes 4325408 | tf_op jit(solution)/shard_map/all_to_all | solution.py:444
  74.8 130.4 %select_blocks.1 = bf16[32,256,256]{2,1,0:T(8,128)(2,1)} custom-call(s32[2,32]{1,0:T(2,128)} %bitcast.63, bf16[32,264,256]{2,1,0:T(8,128)(2,1)} %all-to-all-done.rel_ref.ret_ref, bf16[40,128,256]{2,1,0:T(8,128)(2,1)} %project.1.in_ref), custom_call_target="tpu_custom_call" | custom-call | tf_op jit(solution)/shard_map/select_blocks/pallas_call | solution.py:161
  205.2 0.0 copy-start.7
  205.2 6.8 %all-to-all-start.1 = ((bf16[32,256,256]{2,1,0:T(8,128)(2,1)}), bf16[32,256,256]{2,1,0:T(8,128)(2,1)}, u32[]{:S(2)}, u32[]{:S(2)}) async-start(bf16[32,256,256]{2,1,0:T(8,128)(2,1)} %select_blocks.1), calls=%async_computation.1 | async-start | bytes 8388608 | tf_op jit(solution)/shard_map/all_to_all | solution.py:457
  212.0 0.1 copy.17
  212.1 0.1 reshape.58.coef_ref
  212.2 0.0 copy-done.7
  212.2 6.2 %sum_by_key.1 = bf16[40,128,256]{2,1,0:T(8,128)(2,1)} custom-call(s32[2,32]{1,0:T(2,128)S(1)} %bitcast.64, bf16[32,264,256]{2,1,0:T(8,128)(2,1)} %all-to-all-done.rel_ref.ret_ref), custom_call_target="tpu_custom_call" | custom-call | tf_op jit(solution)/shard_map/sum_by_key/pallas_call | solution.py:201
  218.4 8.4 %weight_grads.1 = (f32[5,768,256]{2,1,0:T(8,128)}, f32[8,128]{1,0:T(8,128)S(1)}) custom-call(f32[20]{0:T(128)S(1)} %reshape.58.coef_ref, bf16[1024,768]{1,0:T(8,128)(2,1)S(1)} %copy-done.1, bf16[5,1024,256]{2,1,0:T(8,128)(2,1)} %bitcast.68, bf16[1024,256]{1,0:T(8,128)(2,1)S(1)} %copy-done.5, bf16[4,768,256]{2,1,0:T(8,128)(2,1)S(1)} %copy-done.3), custom_call_target="tpu_custom_call" | custom-call | tf_op jit(solution)/shard_map/weight_grads/pallas_call | solution.py:249
  226.7 2.7 fusion
  229.4 0.2 collective-permute-start
  229.6 0.3 collective-permute-start.1
  229.9 0.1 pad_add_fusion.place_ref
  230.0 2.0 collective-permute-done.1
  232.0 1.5 collective-permute-start.2
  233.5 4.6 %fusion.8 = f32[1024,768,1]{1,0,2:T(8,128)S(1)} fusion(bf16[5,1024,256]{2,1,0:T(8,128)(2,1)} %bitcast.69, bf16[5,768,256]{2,1,0:T(8,128)(2,1)} %bitcast.57), kind=kOutput, calls=%fused_computation.17 | convolution fusion | flops 2013265920 | bytes 7733248 | tf_op jit(solution)/shard_map/rno,rco->nc/dot_general | solution.py:468
  238.1 0.0 collective-permute-done.2
  238.1 3.0 %collective-permute-start.3 = (f32[8,128]{1,0:T(8,128)S(1)}, f32[8,128]{1,0:T(8,128)S(1)}, u32[]{:S(2)}, u32[]{:S(2)}) collective-permute-start(f32[8,128]{1,0:T(8,128)S(1)} %add.41), channel_id=1, source_target_pairs={{0,2},{1,3},{2,0},{3,1},{4,6},{5,7},{6,4},{7,5},{8,10},{9,11},{10,... | collective-permute-start | bytes 12296 | tf_op jit(solution)/shard_map/ppermute | solution.py:276
  241.1 0.6 bitcast_add_fusion
  241.7 1.8 collective-permute-done.3
  243.5 0.0 collective-permute-done.got_ref
  243.5 0.7 first_stage.1
  244.2 0.7 copy-done.8
  244.9 0.7 copy-done.9
  245.6 0.1 copy-done.10
  245.7 1.0 fusion.4
  246.8 0.0 copy-done.11
  246.8 2.1 collective-permute-start.6
  248.9 0.6 collective-permute-start.5
  249.5 1.4 collective-permute-start.4
  250.9 0.6 fusion.7
  251.5 1.8 collective-permute-start.7
  253.2 2.7 collective-permute-start.8
  256.0 11.0 %collective-permute-done.6 = bf16[256,768]{1,0:T(8,128)(2,1)} collective-permute-done((bf16[256,768]{1,0:T(8,128)(2,1)}, bf16[256,768]{1,0:T(8,128)(2,1)}, u32[]{:S(2)}, u32[]{:S(2)}) %collective-permute-start.6) | collective-permute-done | bytes 393248 | tf_op jit(solution)/shard_map/ppermute | solution.py:276
  267.0 2.9 collective-permute-start.9
  269.9 0.0 collective-permute-done.5
  269.9 0.0 collective-permute-done.4
  269.9 2.4 fusion.3
  272.3 0.0 all-to-all-done.1
  272.3 9.9 %tile_sums.1 = bf16[8,128,256]{2,1,0:T(8,128)(2,1)} custom-call(s32[256]{0:T(256)} %bitcast.75, s32[256]{0:T(256)} %bitcast.77, bf16[256,128,128]{2,1,0:T(8,128)(2,1)} %bitcast.66, bf16[64,128,256]{2,1,0:T(8,128)(2,1)} %bitcast.8.msg_ref, f32[8,128,256]{2,1,0:T(8,128)S(1)} %bitcast.62), custom_call_target="tpu_custom_call" | custom-call | tf_op jit(solution)/shard_map/tile_sums/pallas_call | solution.py:122
  282.2 0.0 collective-permute-done.7.refs_0_
  282.2 0.0 collective-permute-done.8.refs_1_
  282.2 0.0 collective-permute-done.9.refs_2_
  282.2 0.7 second_stage.1
  282.9 1.2 collective-permute-start.10
  284.1 3.1 %collective-permute-start.11 = (bf16[128,256]{1,0:T(8,128)(2,1)S(1)}, bf16[128,256]{1,0:T(8,128)(2,1)S(1)}, u32[]{:S(2)}, u32[]{:S(2)}) collective-permute-start(bf16[128,256]{1,0:T(8,128)(2,1)S(1)} %get-tuple-element.46), channel_id=1, source_target_pairs={{0,16},{4,20},{8,24},{12,28},{16,0},{20,4},{24,8},{28,12},{32,48},... | collective-permute-start | bytes 196616 | tf_op jit(solution)/shard_map/ppermute | solution.py:276
  287.2 0.5 collective-permute-start.12
  287.7 0.0 collective-permute-done.10.refs_0_
  287.7 2.4 collective-permute-done.11.refs_1_
  290.1 2.5 collective-permute-done.12.refs_2_
  292.6 0.7 last_stage.1
  (16 shorter events, 0.0 us)
Async XLA Ops:
  0.6 240.5 %copy-start = (bf16[768,256]{1,0:T(8,128)(2,1)S(1)}, bf16[768,256]{1,0:T(8,128)(2,1)}, u32[]{:S(2)}) copy-start(bf16[768,256]{1,0:T(8,128)(2,1)} %param.13) | copy-start | bytes 1179652
  11.8 8.7 %copy-start.3 = (bf16[4,768,256]{2,1,0:T(8,128)(2,1)S(1)}, bf16[4,768,256]{2,1,0:T(8,128)(2,1)}, u32[]{:S(2)}) copy-start(bf16[4,768,256]{2,1,0:T(8,128)(2,1)} %base_ref.1) | copy-start | bytes 4718596
  11.8 63.0 %all-to-all-start = ((bf16[32,264,256]{2,1,0:T(8,128)(2,1)}), bf16[32,264,256]{2,1,0:T(8,128)(2,1)}, u32[]{:S(2)}, u32[]{:S(2)}) async-start(bf16[32,264,256]{2,1,0:T(8,128)(2,1)} %tile_grads.1), calls=%async_computation | async-start | bytes 8650752 | tf_op jit(solution)/shard_map/all_to_all | solution.py:444
  20.4 1.2 copy-start.12
  23.0 1.4 copy-start.1
  28.6 1.3 copy-start.2
  205.2 7.0 %copy-start.7 = (s32[1,32,2]{1,2,0:T(2,128)S(1)}, s32[1,32,2]{1,2,0:T(2,128)}, u32[]{:S(2)}) copy-start(s32[1,32,2]{1,2,0:T(2,128)} %param.14) | copy-start | bytes 772
  205.2 67.1 %all-to-all-start.1 = ((bf16[32,256,256]{2,1,0:T(8,128)(2,1)}), bf16[32,256,256]{2,1,0:T(8,128)(2,1)}, u32[]{:S(2)}, u32[]{:S(2)}) async-start(bf16[32,256,256]{2,1,0:T(8,128)(2,1)} %select_blocks.1), calls=%async_computation.1 | async-start | bytes 8388608 | tf_op jit(solution)/shard_map/all_to_all | solution.py:457
  212.2 6.2 %copy-start.5 = (bf16[1024,256]{1,0:T(8,128)(2,1)S(1)}, bf16[1024,256]{1,0:T(8,128)(2,1)}, u32[]{:S(2)}) copy-start(bf16[1024,256]{1,0:T(8,128)(2,1)} %grad_ref.1) | copy-start | bytes 1572868
  229.4 14.1 %collective-permute-start = (bf16[5,4,4,24,256]{4,3,2,1,0:T(8,128)(2,1)}, bf16[5,4,4,24,256]{4,3,2,1,0:T(8,128)(2,1)S(1)}, u32[]{:S(2)}, u32[]{:S(2)}) collective-permute-start(bf16[5,4,4,24,256]{4,3,2,1,0:T(8,128)(2,1)} %fusion), channel_id=1, source_target_pairs={{0,4},{4,0},{8,12},{12,8},{16,20},{20,16},{24,28},{28,24},{32,36},... | collective-permute-start | bytes 2949128 | tf_op jit(solution)/shard_map/ppermute | solution.py:276
  229.6 2.4 collective-permute-start.1
  232.0 9.1 %copy-start.6 = (bf16[1024,256]{1,0:T(8,128)(2,1)S(1)}, bf16[1024,256]{1,0:T(8,128)(2,1)}, u32[]{:S(2)}) copy-start(bf16[1024,256]{1,0:T(8,128)(2,1)} %grad_ref.1) | copy-start | bytes 1572868
  232.0 6.1 %collective-permute-start.2 = (f32[8,128]{1,0:T(8,128)S(1)}, f32[8,128]{1,0:T(8,128)S(1)}, u32[]{:S(2)}, u32[]{:S(2)}) collective-permute-start(f32[8,128]{1,0:T(8,128)S(1)} %add.40), channel_id=1, source_target_pairs={{0,1},{1,0},{2,3},{3,2},{4,5},{5,4},{6,7},{7,6},{8,9},{9,8},{10,11... | collective-permute-start | bytes 12296 | tf_op jit(solution)/shard_map/ppermute | solution.py:276
  238.1 5.4 %copy-start.4 = (f32[5,768,256]{2,1,0:T(8,128)S(1)}, f32[5,768,256]{2,1,0:T(8,128)}, u32[]{:S(2)}) copy-start(f32[5,768,256]{2,1,0:T(8,128)} %get-tuple-element.30) | copy-start | bytes 11796484
  238.1 5.4 %collective-permute-start.3 = (f32[8,128]{1,0:T(8,128)S(1)}, f32[8,128]{1,0:T(8,128)S(1)}, u32[]{:S(2)}, u32[]{:S(2)}) collective-permute-start(f32[8,128]{1,0:T(8,128)S(1)} %add.41), channel_id=1, source_target_pairs={{0,2},{1,3},{2,0},{3,1},{4,6},{5,7},{6,4},{7,5},{8,10},{9,11},{10,... | collective-permute-start | bytes 12296 | tf_op jit(solution)/shard_map/ppermute | solution.py:276
  241.7 5.1 %copy-start.11 = (f32[1024,768]{1,0:T(8,128)}, f32[1024,768]{1,0:T(8,128)S(1)}, u32[]{:S(2)}) copy-start(f32[1024,768]{1,0:T(8,128)S(1)} %bitcast_add_fusion) | copy-start | bytes 9437188
  244.2 0.7 copy-start.8
  244.9 0.7 copy-start.9
  244.9 0.8 copy-start.10
  246.8 20.2 %collective-permute-start.6 = (bf16[256,768]{1,0:T(8,128)(2,1)}, bf16[256,768]{1,0:T(8,128)(2,1)}, u32[]{:S(2)}, u32[]{:S(2)}) collective-permute-start(bf16[256,768]{1,0:T(8,128)(2,1)} %get-tuple-element.52), channel_id=1, source_target_pairs={{0,3},{1,2},{2,1},{3,0},{4,7},{5,6},{6,5},{7,4},{8,11},{9,10},{10,... | collective-permute-start | bytes 1179656 | tf_op jit(solution)/shard_map/ppermute | solution.py:276
  248.9 21.0 %collective-permute-start.5 = (bf16[256,768]{1,0:T(8,128)(2,1)}, bf16[256,768]{1,0:T(8,128)(2,1)}, u32[]{:S(2)}, u32[]{:S(2)}) collective-permute-start(bf16[256,768]{1,0:T(8,128)(2,1)} %get-tuple-element.53), channel_id=1, source_target_pairs={{0,2},{1,3},{2,0},{3,1},{4,6},{5,7},{6,4},{7,5},{8,10},{9,11},{10,... | collective-permute-start | bytes 1179656 | tf_op jit(solution)/shard_map/ppermute | solution.py:276
  249.5 20.4 %collective-permute-start.4 = (bf16[256,768]{1,0:T(8,128)(2,1)}, bf16[256,768]{1,0:T(8,128)(2,1)}, u32[]{:S(2)}, u32[]{:S(2)}) collective-permute-start(bf16[256,768]{1,0:T(8,128)(2,1)} %get-tuple-element.51), channel_id=1, source_target_pairs={{0,1},{1,0},{2,3},{3,2},{4,5},{5,4},{6,7},{7,6},{8,9},{9,8},{10,11... | collective-permute-start | bytes 1179656 | tf_op jit(solution)/shard_map/ppermute | solution.py:276
  251.5 30.8 %collective-permute-start.7 = (bf16[488,256]{1,0:T(8,128)(2,1)}, bf16[488,256]{1,0:T(8,128)(2,1)S(1)}, u32[]{:S(2)}, u32[]{:S(2)}) collective-permute-start(bf16[488,256]{1,0:T(8,128)(2,1)} %copy-done.10), channel_id=1, source_target_pairs={{0,32},{4,36},{8,40},{12,44},{16,48},{20,52},{24,56},{28,60},{32,0... | collective-permute-start | bytes 749576 | tf_op jit(solution)/shard_map/ppermute | solution.py:276
  253.2 29.0 %collective-permute-start.8 = (bf16[488,256]{1,0:T(8,128)(2,1)}, bf16[488,256]{1,0:T(8,128)(2,1)S(1)}, u32[]{:S(2)}, u32[]{:S(2)}) collective-permute-start(bf16[488,256]{1,0:T(8,128)(2,1)} %copy-done.9), channel_id=1, source_target_pairs={{0,64},{4,68},{8,72},{12,76},{16,80},{20,84},{24,88},{28,92},{32,9... | collective-permute-start | bytes 749576 | tf_op jit(solution)/shard_map/ppermute | solution.py:276
  267.0 15.3 %collective-permute-start.9 = (bf16[488,256]{1,0:T(8,128)(2,1)}, bf16[488,256]{1,0:T(8,128)(2,1)S(1)}, u32[]{:S(2)}, u32[]{:S(2)}) collective-permute-start(bf16[488,256]{1,0:T(8,128)(2,1)} %copy-done.8), channel_id=1, source_target_pairs={{0,96},{4,100},{8,104},{12,108},{16,112},{20,116},{24,120},{28,124... | collective-permute-start | bytes 749576 | tf_op jit(solution)/shard_map/ppermute | solution.py:276
  282.9 4.8 %collective-permute-start.10 = (bf16[128,256]{1,0:T(8,128)(2,1)S(1)}, bf16[128,256]{1,0:T(8,128)(2,1)S(1)}, u32[]{:S(2)}, u32[]{:S(2)}) collective-permute-start(bf16[128,256]{1,0:T(8,128)(2,1)S(1)} %get-tuple-element.45), channel_id=1, source_target_pairs={{0,8},{4,12},{8,0},{12,4},{16,24},{20,28},{24,16},{28,20},{32,40},... | collective-permute-start | bytes 196616 | tf_op jit(solution)/shard_map/ppermute | solution.py:276
  284.1 6.0 %collective-permute-start.11 = (bf16[128,256]{1,0:T(8,128)(2,1)S(1)}, bf16[128,256]{1,0:T(8,128)(2,1)S(1)}, u32[]{:S(2)}, u32[]{:S(2)}) collective-permute-start(bf16[128,256]{1,0:T(8,128)(2,1)S(1)} %get-tuple-element.46), channel_id=1, source_target_pairs={{0,16},{4,20},{8,24},{12,28},{16,0},{20,4},{24,8},{28,12},{32,48},... | collective-permute-start | bytes 196616 | tf_op jit(solution)/shard_map/ppermute | solution.py:276
  287.2 5.5 %collective-permute-start.12 = (bf16[128,256]{1,0:T(8,128)(2,1)S(1)}, bf16[128,256]{1,0:T(8,128)(2,1)S(1)}, u32[]{:S(2)}, u32[]{:S(2)}) collective-permute-start(bf16[128,256]{1,0:T(8,128)(2,1)S(1)} %get-tuple-element.47), channel_id=1, source_target_pairs={{0,24},{4,28},{8,16},{12,20},{16,8},{20,12},{24,0},{28,4},{32,56},... | collective-permute-start | bytes 196616 | tf_op jit(solution)/shard_map/ppermute | solution.py:276

commit v6 on v5

--- a/solution.py
+++ b/solution.py
@@ -145,11 +145,15 @@
 def select_blocks(slot_block, returned, blocks, nblocks, capacity):
     shards, _, width = returned.shape
 
-    def kernel(block_ref, rel_ref, in_ref, out_ref, sem_ref):
+    def kernel(block_ref, rel_ref, in_hbm_ref, out_ref, in_ref, load_ref, sem_ref):
+        load = pltpu.make_async_copy(in_hbm_ref, in_ref, load_ref)
+        load.start()
+        rels = [[relation_of(rel_ref[o], c) for c in range(capacity)] for o in range(shards)]
+        load.wait()
         copies = []
         for o in range(shards):
             for c in range(capacity):
-                key = relation_of(rel_ref[o], c) * nblocks + block_ref[c, o]
+                key = rels[o][c] * nblocks + block_ref[c, o]
                 copy = pltpu.make_async_copy(
                     in_ref.at[key], out_ref.at[o, pl.ds(c * BLK, BLK)], sem_ref.at[o, c]
                 )
@@ -170,7 +174,11 @@
                 pl.BlockSpec(memory_space=pl.ANY),
             ],
             out_specs=pl.BlockSpec(memory_space=pl.ANY),
-            scratch_shapes=[pltpu.SemaphoreType.DMA((shards, capacity))],
+            scratch_shapes=[
+                pltpu.VMEM(blocks.shape, BF16),
+                pltpu.SemaphoreType.DMA,
+                pltpu.SemaphoreType.DMA((shards, capacity)),
+            ],
         ),
         compiler_params=params(),
     )(in_hbm(slot_block), returned, in_hbm(blocks))
@@ -249,6 +257,12 @@
     return pl.pallas_call(
         kernel,
         name="weight_grads",
+        cost_estimate=pl.CostEstimate(
+            flops=2 * (relations + 1) * nodes * width_in * width,
+            transcendentals=0,
+            bytes_accessed=2 * nodes * (width_in + (relations + 1) * width)
+            + 6 * (nbase + 1) * width_in * width,
+        ),
         out_shape=(
             jax.ShapeDtypeStruct((nbase + 1, width_in, width), F32),
             jax.ShapeDtypeStruct((8, BLK), F32),
@@ -278,15 +292,6 @@
 
 def chunk_of(x, at, dim):
     return lax.dynamic_index_in_dim(x, at, dim, keepdims=False)
-
-
-def scatter_sum(x, axis, shift, size, me, dim=0):
-    at = (me >> shift) & (size - 1)
-    total = chunk_of(x, at, dim)
-    for k in range(1, size):
-        part = chunk_of(x, at ^ k, dim).astype(BF16)
-        total = total + exchange(part, axis, k << shift).astype(F32)
-    return total
 
 
 def two_terms(x):
@@ -458,6 +463,10 @@
 
     source_grads = sum_by_key(requested, returned, relations, nblocks)
     source_grads = source_grads.reshape(relations, nblocks * BLK, width)
+    through = jnp.einsum("rno,rco->nc", source_grads, rel_weights, preferred_element_type=F32)
+    through = through + jnp.dot(d_out, root_weight.T, preferred_element_type=F32)
+    through = through.reshape(reps, -1, width_in)
+    parts = [chunk_of(through, my_rep ^ k, 0).astype(BF16) for k in range(1, reps)]
     stacked, dots = weight_grads(
         coef.astype(F32).reshape(-1), feats, source_grads, d_out, bases
     )
@@ -465,18 +474,18 @@
     for step in (1, 2):
         dots = dots + exchange(dots, "rep", step)
 
-    through = jnp.einsum("rno,rco->nc", source_grads, rel_weights, preferred_element_type=F32)
-    through = through + jnp.dot(d_out, root_weight.T, preferred_element_type=F32)
+    dots, *parts = lax.optimization_barrier((dots, *parts))
+    grad_feats = chunk_of(through, my_rep, 0)
+    for k, part in zip(range(1, reps), parts):
+        grad_feats = grad_feats + exchange(part, "rep", k).astype(F32)
+    grad_feats = grad_feats.astype(BF16)
+
     rows = width_in // shards
     stacked = stacked.reshape(nbase + 1, 4, 4, 2, rows, width)
     place = jnp.stack([me & 1, (me >> 3) & 3, (me >> 1) & 3]).astype(jnp.int32)
     got = exchange(chunk_of(stacked, (me & 1) ^ 1, 3).astype(BF16), "shard", 1)
     kept, *sends = first_stage(place, stacked, got, dots, 4)
-    through, *sends = lax.optimization_barrier((through, *sends))
     got = [exchange(x, "shard", k << 3) for k, x in zip((1, 2, 3), sends)]
-    grad_feats = scatter_sum(
-        through.reshape(reps, -1, width_in), "rep", 0, reps, my_rep
-    ).astype(BF16)
     output = tile_sums(
         tile_slot[0],
         tile_dst[0],

time: 294 us -> 162 us (0.55)
  Pallas kernels: 172 us -> 48.4 us
  local copies, waits for them, and re-layouts: 9.35 us -> 4.63 us
    pallas_call x1, Pallas kernels: 130 us -> 6.16 us  [select_blocks(): pl.pallas_call(kernel, name='select_blocks', out_shape=pltpu.HBM((shards,...]
    ppermute x13, waiting for transfers between devices: 19.7 us -> 16.5 us  [exchange(): lax.ppermute(x, axis, [(i, i ^ mask) for i in range(lax.axis_size(axis))])]
  transfers between devices with their start and end apart: 15 -> 15, of which waited for: 6 -> 8; matrix products, arithmetic and copies ran while one was open for 5% -> 6% of each run, Pallas kernels for 10% -> 18%
where the time goes in v6:
time: 162 us
  waiting for transfers between devices  64.2 us (40%)
  Pallas kernels  48.4 us (30%)
  starting transfers between devices  37.7 us (23%)
  matrix products  4.75 us (3%)
  local copies, waits for them, and re-layouts  4.63 us (3%)
    all_to_all x1, waiting for transfers between devices, body(): returned = lax.all_to_all(slot_grads, 'shard', 0, 0, tiled=True)  46.1 us
    ppermute x13, starting transfers between devices, exchange(): lax.ppermute(x, axis, [(i, i ^ mask) for i in range(lax.axis_size(axis))])  22.3 us
    ppermute x13, waiting for transfers between devices, exchange(): lax.ppermute(x, axis, [(i, i ^ mask) for i in range(lax.axis_size(axis))])  16.5 us
    pallas_call x1, Pallas kernels, tile_grads(): pl.pallas_call(kernel, name='tile_grads', out_shape=pltpu.HBM((shards, ro...  11.1 us
    pallas_call x1, Pallas kernels, tile_sums(): pl.pallas_call(kernel, name='tile_sums', out_shape=jax.ShapeDtypeStruct(r...  9.92 us
    all_to_all x1, starting transfers between devices, body(): returned = lax.all_to_all(slot_grads, 'shard', 0, 0, tiled=True)  8.66 us
    pallas_call x1, Pallas kernels, weight_grads(): pl.pallas_call(kernel, name='weight_grads', cost_estimate=pl.CostEstimate...  8.47 us
    all_to_all x1, starting transfers between devices, body(): incoming = lax.all_to_all(outgoing, 'shard', 0, 0, tiled=True)  6.76 us
  transfers between devices with their start and end apart: 15, of which 8 were waited for; matrix products, arithmetic and copies ran while one was open for 6% of the time, Pallas kernels for 18%

profile of v6, /device:TPU:0, one launch (start us, length us, event | category | flops | bytes accessed | tf_op | source)
XLA Modules:
  0.0 161.6 jit_solution(14322990469132355587)
XLA Ops:
  0.6 0.0 copy-start
  0.6 11.1 %tile_grads.1 = bf16[32,264,256]{2,1,0:T(8,128)(2,1)} custom-call(s32[256]{0:T(256)} %bitcast.74, s32[256]{0:T(256)} %bitcast.76, s32[2,32]{1,0:T(2,128)} %bitcast.78, bf16[256,128,128]{2,1,0:T(8,128)(2,1)} %bitcast.65, bf16[8,128,256]{2,1,0:T(8,128)(2,1)} %bitcast.61), custom_call_target="tpu_custom_call" | custom-call | tf_op jit(solution)/shard_map/tile_grads/pallas_call | solution.py:61
  11.8 8.7 %all-to-all-start = ((bf16[32,264,256]{2,1,0:T(8,128)(2,1)}), bf16[32,264,256]{2,1,0:T(8,128)(2,1)}, u32[]{:S(2)}, u32[]{:S(2)}) async-start(bf16[32,264,256]{2,1,0:T(8,128)(2,1)} %tile_grads.1), calls=%async_computation | async-start | bytes 8650752 | tf_op jit(solution)/shard_map/all_to_all | solution.py:449
  20.4 0.0 copy-start.9
  20.5 0.0 copy-done.5
  20.5 1.2 copy.20
  21.7 0.0 copy-done.9
  21.7 1.3 convolution_convert_fusion
  23.0 0.0 copy-start.1
  23.1 0.4 copy.23
  23.5 0.9 copy-done.1
  24.5 4.2 %project.1.in_hbm_ref = bf16[40,128,256]{2,1,0:T(8,128)(2,1)} custom-call(bf16[1024,768]{1,0:T(8,128)(2,1)S(1)} %copy-done.1, bf16[5,768,256]{2,1,0:T(8,128)(2,1)S(1)} %bitcast.56), custom_call_target="tpu_custom_call" | custom-call | tf_op jit(solution)/shard_map/project/pallas_call | solution.py:88
  28.7 46.1 %all-to-all-done.rel_ref.ret_ref = bf16[32,264,256]{2,1,0:T(8,128)(2,1)} async-done(((bf16[32,264,256]{2,1,0:T(8,128)(2,1)}), bf16[32,264,256]{2,1,0:T(8,128)(2,1)}, u32[]{:S(2)}, u32[]{:S(2)}) %all-to-all-start) | async-done | bytes 4325408 | tf_op jit(solution)/shard_map/all_to_all | solution.py:449
  74.8 6.2 %select_blocks.1 = bf16[32,256,256]{2,1,0:T(8,128)(2,1)} custom-call(s32[2,32]{1,0:T(2,128)} %bitcast.63, bf16[32,264,256]{2,1,0:T(8,128)(2,1)} %all-to-all-done.rel_ref.ret_ref, bf16[40,128,256]{2,1,0:T(8,128)(2,1)} %project.1.in_hbm_ref), custom_call_target="tpu_custom_call" | custom-call | tf_op jit(solution)/shard_map/select_blocks/pallas_call | solution.py:165
  80.9 0.0 copy-start.7
  81.0 6.8 %all-to-all-start.1 = ((bf16[32,256,256]{2,1,0:T(8,128)(2,1)}), bf16[32,256,256]{2,1,0:T(8,128)(2,1)}, u32[]{:S(2)}, u32[]{:S(2)}) async-start(bf16[32,256,256]{2,1,0:T(8,128)(2,1)} %select_blocks.1), calls=%async_computation.1 | async-start | bytes 8388608 | tf_op jit(solution)/shard_map/all_to_all | solution.py:462
  87.7 0.1 copy.17
  87.8 0.1 reshape.58.coef_ref
  87.9 0.0 copy-done.7
  87.9 0.0 copy-start.6
  87.9 6.5 %sum_by_key.1 = bf16[40,128,256]{2,1,0:T(8,128)(2,1)} custom-call(s32[2,32]{1,0:T(2,128)S(1)} %bitcast.64, bf16[32,264,256]{2,1,0:T(8,128)(2,1)} %all-to-all-done.rel_ref.ret_ref), custom_call_target="tpu_custom_call" | custom-call | tf_op jit(solution)/shard_map/sum_by_key/pallas_call | solution.py:209
  94.4 0.0 copy-done.2
  94.4 0.0 copy-done.4
  94.4 8.5 %weight_grads.1 = (f32[5,768,256]{2,1,0:T(8,128)}, f32[8,128]{1,0:T(8,128)S(1)}) custom-call(f32[20]{0:T(128)S(1)} %reshape.58.coef_ref, bf16[1024,768]{1,0:T(8,128)(2,1)S(1)} %copy-done.2, bf16[5,1024,256]{2,1,0:T(8,128)(2,1)} %bitcast.71, bf16[1024,256]{1,0:T(8,128)(2,1)S(1)} %copy-done.4, bf16[4,768,256]{2,1,0:T(8,128)(2,1)S(1)} %copy-done.6), custom_call_target="tpu_custom_call" | custom-call | flops 2415919104 | bytes 10616832 | tf_op jit(solution)/shard_map/weight_grads/pallas_call | solution.py:257
  102.9 0.2 collective-permute-start
  103.1 1.7 %fusion = bf16[5,4,4,24,256]{4,3,2,1,0:T(8,128)(2,1)S(1)} fusion(f32[5,4,4,2,24,256]{5,4,3,2,1,0:T(8,128)} %bitcast.58, s32[]{:T(128)S(6)} %select_n.21), kind=kLoop, calls=%fused_computation.4 | loop fusion | bytes 1966084 | tf_op jit(solution)/shard_map/convert_element_type | solution.py:486
  104.8 0.4 collective-permute-start.6
  105.2 0.0 copy-done.8
  105.2 2.2 %fusion.8 = f32[1024,768,1]{1,0,2:T(8,128)S(1)} fusion(bf16[5,1024,256]{2,1,0:T(8,128)(2,1)S(1)} %bitcast.72, bf16[5,768,256]{2,1,0:T(8,128)(2,1)S(1)} %bitcast.57), kind=kOutput, calls=%fused_computation.17 | convolution fusion | flops 2013265920 | bytes 7733248 | tf_op jit(solution)/shard_map/rno,rco->nc/dot_general | solution.py:466
  107.4 0.0 collective-permute-done
  107.4 1.6 collective-permute-start.1
  109.0 0.6 bitcast_add_fusion
  109.6 1.5 collective-permute-done.1
  111.1 3.0 %collective-permute-start.2 = (f32[8,128]{1,0:T(8,128)S(1)}, f32[8,128]{1,0:T(8,128)S(1)}, u32[]{:S(2)}, u32[]{:S(2)}) collective-permute-start(f32[8,128]{1,0:T(8,128)S(1)} %add.41), channel_id=1, source_target_pairs={{0,2},{1,3},{2,0},{3,1},{4,6},{5,7},{6,4},{7,5},{8,10},{9,11},{10,... | collective-permute-start | bytes 12296 | tf_op jit(solution)/shard_map/ppermute | solution.py:290
  114.1 0.1 fusion.6
  114.3 2.0 %collective-permute-done.2 = f32[8,128]{1,0:T(8,128)S(1)} collective-permute-done((f32[8,128]{1,0:T(8,128)S(1)}, f32[8,128]{1,0:T(8,128)S(1)}, u32[]{:S(2)}, u32[]{:S(2)}) %collective-permute-start.2) | collective-permute-done | bytes 4128 | tf_op jit(solution)/shard_map/ppermute | solution.py:290
  116.2 2.8 %collective-permute-start.5 = (bf16[256,768]{1,0:T(8,128)(2,1)S(1)}, bf16[256,768]{1,0:T(8,128)(2,1)S(1)}, u32[]{:S(2)}, u32[]{:S(2)}) collective-permute-start(bf16[256,768]{1,0:T(8,128)(2,1)S(1)} %get-tuple-element.33), channel_id=1, source_target_pairs={{0,3},{1,2},{2,1},{3,0},{4,7},{5,6},{6,5},{7,4},{8,11},{9,10},{10,... | collective-permute-start | bytes 1179656 | tf_op jit(solution)/shard_map/ppermute | solution.py:290
  119.0 0.8 collective-permute-start.4
  119.8 0.5 collective-permute-start.3
  120.3 0.1 pad_add_fusion.place_ref
  120.4 0.6 fusion.7
  121.0 0.0 collective-permute-done.6.got_ref
  121.0 0.0 copy-done.3
  121.0 0.7 first_stage.1
  121.7 1.8 %collective-permute-start.7 = (bf16[488,256]{1,0:T(8,128)(2,1)S(1)}, bf16[488,256]{1,0:T(8,128)(2,1)S(1)}, u32[]{:S(2)}, u32[]{:S(2)}) collective-permute-start(bf16[488,256]{1,0:T(8,128)(2,1)S(1)} %get-tuple-element.40), channel_id=1, source_target_pairs={{0,32},{4,36},{8,40},{12,44},{16,48},{20,52},{24,56},{28,60},{32,0... | collective-permute-start | bytes 749576 | tf_op jit(solution)/shard_map/ppermute | solution.py:290
  123.5 2.7 %collective-permute-start.8 = (bf16[488,256]{1,0:T(8,128)(2,1)S(1)}, bf16[488,256]{1,0:T(8,128)(2,1)S(1)}, u32[]{:S(2)}, u32[]{:S(2)}) collective-permute-start(bf16[488,256]{1,0:T(8,128)(2,1)S(1)} %get-tuple-element.41), channel_id=1, source_target_pairs={{0,64},{4,68},{8,72},{12,76},{16,80},{20,84},{24,88},{28,92},{32,9... | collective-permute-start | bytes 749576 | tf_op jit(solution)/shard_map/ppermute | solution.py:290
  126.2 9.3 %collective-permute-done.5 = bf16[256,768]{1,0:T(8,128)(2,1)S(1)} collective-permute-done((bf16[256,768]{1,0:T(8,128)(2,1)S(1)}, bf16[256,768]{1,0:T(8,128)(2,1)S(1)}, u32[]{:S(2)}, u32[]{:S(2)}) %collective-permute-start.5) | collective-permute-done | bytes 393248 | tf_op jit(solution)/shard_map/ppermute | solution.py:290
  135.6 2.9 %collective-permute-start.9 = (bf16[488,256]{1,0:T(8,128)(2,1)S(1)}, bf16[488,256]{1,0:T(8,128)(2,1)S(1)}, u32[]{:S(2)}, u32[]{:S(2)}) collective-permute-start(bf16[488,256]{1,0:T(8,128)(2,1)S(1)} %get-tuple-element.42), channel_id=1, source_target_pairs={{0,96},{4,100},{8,104},{12,108},{16,112},{20,116},{24,120},{28,124... | collective-permute-start | bytes 749576 | tf_op jit(solution)/shard_map/ppermute | solution.py:290
  138.5 0.0 collective-permute-done.4
  138.5 0.0 collective-permute-done.3
  138.5 0.9 fusion.3
  139.4 1.6 all-to-all-done.1
  141.0 9.9 %tile_sums.1 = bf16[8,128,256]{2,1,0:T(8,128)(2,1)} custom-call(s32[256]{0:T(256)} %bitcast.75, s32[256]{0:T(256)} %bitcast.77, bf16[256,128,128]{2,1,0:T(8,128)(2,1)} %bitcast.66, bf16[64,128,256]{2,1,0:T(8,128)(2,1)} %bitcast.8.msg_ref, f32[8,128,256]{2,1,0:T(8,128)S(1)} %bitcast.60), custom_call_target="tpu_custom_call" | custom-call | tf_op jit(solution)/shard_map/tile_sums/pallas_call | solution.py:122
  151.0 0.0 collective-permute-done.7.refs_0_
  151.0 0.2 collective-permute-done.8.refs_1_
  151.2 0.0 collective-permute-done.9.refs_2_
  151.2 0.7 second_stage.1
  151.8 2.8 %collective-permute-start.10 = (bf16[128,256]{1,0:T(8,128)(2,1)S(1)}, bf16[128,256]{1,0:T(8,128)(2,1)S(1)}, u32[]{:S(2)}, u32[]{:S(2)}) collective-permute-start(bf16[128,256]{1,0:T(8,128)(2,1)S(1)} %get-tuple-element.45), channel_id=1, source_target_pairs={{0,8},{4,12},{8,0},{12,4},{16,24},{20,28},{24,16},{28,20},{32,40},... | collective-permute-start | bytes 196616 | tf_op jit(solution)/shard_map/ppermute | solution.py:290
  154.7 0.0 collective-permute-start.11
  154.7 2.8 %collective-permute-start.12 = (bf16[128,256]{1,0:T(8,128)(2,1)S(1)}, bf16[128,256]{1,0:T(8,128)(2,1)S(1)}, u32[]{:S(2)}, u32[]{:S(2)}) collective-permute-start(bf16[128,256]{1,0:T(8,128)(2,1)S(1)} %get-tuple-element.47), channel_id=1, source_target_pairs={{0,24},{4,28},{8,16},{12,20},{16,8},{20,12},{24,0},{28,4},{32,56},... | collective-permute-start | bytes 196616 | tf_op jit(solution)/shard_map/ppermute | solution.py:290
  157.4 0.0 collective-permute-done.10.refs_0_
  157.4 3.1 %collective-permute-done.11.refs_1_ = bf16[128,256]{1,0:T(8,128)(2,1)S(1)} collective-permute-done((bf16[128,256]{1,0:T(8,128)(2,1)S(1)}, bf16[128,256]{1,0:T(8,128)(2,1)S(1)}, u32[]{:S(2)}, u32[]{:S(2)}) %collective-permute-start.11) | collective-permute-done | bytes 65568 | tf_op jit(solution)/shard_map/ppermute | solution.py:290
  160.5 0.4 collective-permute-done.12.refs_2_
  160.9 0.7 last_stage.1
  (10 shorter events, 0.0 us)
Async XLA Ops:
  0.6 108.4 %copy-start = (bf16[768,256]{1,0:T(8,128)(2,1)S(1)}, bf16[768,256]{1,0:T(8,128)(2,1)}, u32[]{:S(2)}) copy-start(bf16[768,256]{1,0:T(8,128)(2,1)} %param.13) | copy-start | bytes 1179652
  11.8 8.7 %copy-start.5 = (bf16[4,768,256]{2,1,0:T(8,128)(2,1)S(1)}, bf16[4,768,256]{2,1,0:T(8,128)(2,1)}, u32[]{:S(2)}) copy-start(bf16[4,768,256]{2,1,0:T(8,128)(2,1)} %base_ref.1) | copy-start | bytes 4718596
  11.8 63.0 %all-to-all-start = ((bf16[32,264,256]{2,1,0:T(8,128)(2,1)}), bf16[32,264,256]{2,1,0:T(8,128)(2,1)}, u32[]{:S(2)}, u32[]{:S(2)}) async-start(bf16[32,264,256]{2,1,0:T(8,128)(2,1)} %tile_grads.1), calls=%async_computation | async-start | bytes 8650752 | tf_op jit(solution)/shard_map/all_to_all | solution.py:449
  20.4 1.2 copy-start.9
  23.0 1.4 copy-start.1
  80.9 7.0 %copy-start.7 = (s32[1,32,2]{1,2,0:T(2,128)S(1)}, s32[1,32,2]{1,2,0:T(2,128)}, u32[]{:S(2)}) copy-start(s32[1,32,2]{1,2,0:T(2,128)} %param.14) | copy-start | bytes 772
  81.0 60.1 %all-to-all-start.1 = ((bf16[32,256,256]{2,1,0:T(8,128)(2,1)}), bf16[32,256,256]{2,1,0:T(8,128)(2,1)}, u32[]{:S(2)}, u32[]{:S(2)}) async-start(bf16[32,256,256]{2,1,0:T(8,128)(2,1)} %select_blocks.1), calls=%async_computation.1 | async-start | bytes 8388608 | tf_op jit(solution)/shard_map/all_to_all | solution.py:462
  87.9 6.5 %copy-start.2 = (bf16[1024,768]{1,0:T(8,128)(2,1)S(1)}, bf16[1024,768]{1,0:T(8,128)(2,1)}, u32[]{:S(2)}) copy-start(bf16[1024,768]{1,0:T(8,128)(2,1)} %feat_ref.3) | copy-start | bytes 4718596
  87.9 6.5 %copy-start.4 = (bf16[1024,256]{1,0:T(8,128)(2,1)S(1)}, bf16[1024,256]{1,0:T(8,128)(2,1)}, u32[]{:S(2)}) copy-start(bf16[1024,256]{1,0:T(8,128)(2,1)} %grad_ref.1) | copy-start | bytes 1572868
  87.9 6.5 %copy-start.6 = (bf16[4,768,256]{2,1,0:T(8,128)(2,1)S(1)}, bf16[4,768,256]{2,1,0:T(8,128)(2,1)}, u32[]{:S(2)}) copy-start(bf16[4,768,256]{2,1,0:T(8,128)(2,1)} %base_ref.1) | copy-start | bytes 4718596
  94.4 10.8 %copy-start.8 = (bf16[40,128,256]{2,1,0:T(8,128)(2,1)S(1)}, bf16[40,128,256]{2,1,0:T(8,128)(2,1)}, u32[]{:S(2)}) copy-start(bf16[40,128,256]{2,1,0:T(8,128)(2,1)} %sum_by_key.1) | copy-start | bytes 7864324
  102.9 4.5 %collective-permute-start = (f32[8,128]{1,0:T(8,128)S(1)}, f32[8,128]{1,0:T(8,128)S(1)}, u32[]{:S(2)}, u32[]{:S(2)}) collective-permute-start(f32[8,128]{1,0:T(8,128)S(1)} %get-tuple-element.30), channel_id=1, source_target_pairs={{0,4},{4,0},{8,12},{12,8},{16,20},{20,16},{24,28},{28,24},{32,36},... | collective-permute-start | bytes 12296 | tf_op jit(solution)/shard_map/ppermute | solution.py:290
  104.8 16.2 %collective-permute-start.6 = (bf16[5,4,4,24,256]{4,3,2,1,0:T(8,128)(2,1)S(1)}, bf16[5,4,4,24,256]{4,3,2,1,0:T(8,128)(2,1)S(1)}, u32[]{:S(2)}, u32[]{:S(2)}) collective-permute-start(bf16[5,4,4,24,256]{4,3,2,1,0:T(8,128)(2,1)S(1)} %fusion), channel_id=1, source_target_pairs={{0,4},{4,0},{8,12},{12,8},{16,20},{20,16},{24,28},{28,24},{32,36},... | collective-permute-start | bytes 2949128 | tf_op jit(solution)/shard_map/ppermute | solution.py:290
  107.4 3.7 %collective-permute-start.1 = (f32[8,128]{1,0:T(8,128)S(1)}, f32[8,128]{1,0:T(8,128)S(1)}, u32[]{:S(2)}, u32[]{:S(2)}) collective-permute-start(f32[8,128]{1,0:T(8,128)S(1)} %add.40), channel_id=1, source_target_pairs={{0,1},{1,0},{2,3},{3,2},{4,5},{5,4},{6,7},{7,6},{8,9},{9,8},{10,11... | collective-permute-start | bytes 12296 | tf_op jit(solution)/shard_map/ppermute | solution.py:290
  109.6 11.4 %copy-start.3 = (f32[5,768,256]{2,1,0:T(8,128)S(1)}, f32[5,768,256]{2,1,0:T(8,128)}, u32[]{:S(2)}) copy-start(f32[5,768,256]{2,1,0:T(8,128)} %get-tuple-element.34) | copy-start | bytes 11796484
  111.1 5.1 %collective-permute-start.2 = (f32[8,128]{1,0:T(8,128)S(1)}, f32[8,128]{1,0:T(8,128)S(1)}, u32[]{:S(2)}, u32[]{:S(2)}) collective-permute-start(f32[8,128]{1,0:T(8,128)S(1)} %add.41), channel_id=1, source_target_pairs={{0,2},{1,3},{2,0},{3,1},{4,6},{5,7},{6,4},{7,5},{8,10},{9,11},{10,... | collective-permute-start | bytes 12296 | tf_op jit(solution)/shard_map/ppermute | solution.py:290
  116.2 19.4 %collective-permute-start.5 = (bf16[256,768]{1,0:T(8,128)(2,1)S(1)}, bf16[256,768]{1,0:T(8,128)(2,1)S(1)}, u32[]{:S(2)}, u32[]{:S(2)}) collective-permute-start(bf16[256,768]{1,0:T(8,128)(2,1)S(1)} %get-tuple-element.33), channel_id=1, source_target_pairs={{0,3},{1,2},{2,1},{3,0},{4,7},{5,6},{6,5},{7,4},{8,11},{9,10},{10,... | collective-permute-start | bytes 1179656 | tf_op jit(solution)/shard_map/ppermute | solution.py:290
  119.0 19.5 %collective-permute-start.4 = (bf16[256,768]{1,0:T(8,128)(2,1)S(1)}, bf16[256,768]{1,0:T(8,128)(2,1)S(1)}, u32[]{:S(2)}, u32[]{:S(2)}) collective-permute-start(bf16[256,768]{1,0:T(8,128)(2,1)S(1)} %get-tuple-element.32), channel_id=1, source_target_pairs={{0,2},{1,3},{2,0},{3,1},{4,6},{5,7},{6,4},{7,5},{8,10},{9,11},{10,... | collective-permute-start | bytes 1179656 | tf_op jit(solution)/shard_map/ppermute | solution.py:290
  119.8 18.7 %collective-permute-start.3 = (bf16[256,768]{1,0:T(8,128)(2,1)S(1)}, bf16[256,768]{1,0:T(8,128)(2,1)S(1)}, u32[]{:S(2)}, u32[]{:S(2)}) collective-permute-start(bf16[256,768]{1,0:T(8,128)(2,1)S(1)} %get-tuple-element.31), channel_id=1, source_target_pairs={{0,1},{1,0},{2,3},{3,2},{4,5},{5,4},{6,7},{7,6},{8,9},{9,8},{10,11... | collective-permute-start | bytes 1179656 | tf_op jit(solution)/shard_map/ppermute | solution.py:290
  121.7 29.3 %collective-permute-start.7 = (bf16[488,256]{1,0:T(8,128)(2,1)S(1)}, bf16[488,256]{1,0:T(8,128)(2,1)S(1)}, u32[]{:S(2)}, u32[]{:S(2)}) collective-permute-start(bf16[488,256]{1,0:T(8,128)(2,1)S(1)} %get-tuple-element.40), channel_id=1, source_target_pairs={{0,32},{4,36},{8,40},{12,44},{16,48},{20,52},{24,56},{28,60},{32,0... | collective-permute-start | bytes 749576 | tf_op jit(solution)/shard_map/ppermute | solution.py:290
  123.5 27.7 %collective-permute-start.8 = (bf16[488,256]{1,0:T(8,128)(2,1)S(1)}, bf16[488,256]{1,0:T(8,128)(2,1)S(1)}, u32[]{:S(2)}, u32[]{:S(2)}) collective-permute-start(bf16[488,256]{1,0:T(8,128)(2,1)S(1)} %get-tuple-element.41), channel_id=1, source_target_pairs={{0,64},{4,68},{8,72},{12,76},{16,80},{20,84},{24,88},{28,92},{32,9... | collective-permute-start | bytes 749576 | tf_op jit(solution)/shard_map/ppermute | solution.py:290
  135.6 15.6 %collective-permute-start.9 = (bf16[488,256]{1,0:T(8,128)(2,1)S(1)}, bf16[488,256]{1,0:T(8,128)(2,1)S(1)}, u32[]{:S(2)}, u32[]{:S(2)}) collective-permute-start(bf16[488,256]{1,0:T(8,128)(2,1)S(1)} %get-tuple-element.42), channel_id=1, source_target_pairs={{0,96},{4,100},{8,104},{12,108},{16,112},{20,116},{24,120},{28,124... | collective-permute-start | bytes 749576 | tf_op jit(solution)/shard_map/ppermute | solution.py:290
  151.8 5.6 %collective-permute-start.10 = (bf16[128,256]{1,0:T(8,128)(2,1)S(1)}, bf16[128,256]{1,0:T(8,128)(2,1)S(1)}, u32[]{:S(2)}, u32[]{:S(2)}) collective-permute-start(bf16[128,256]{1,0:T(8,128)(2,1)S(1)} %get-tuple-element.45), channel_id=1, source_target_pairs={{0,8},{4,12},{8,0},{12,4},{16,24},{20,28},{24,16},{28,20},{32,40},... | collective-permute-start | bytes 196616 | tf_op jit(solution)/shard_map/ppermute | solution.py:290
  154.7 5.8 %collective-permute-start.11 = (bf16[128,256]{1,0:T(8,128)(2,1)S(1)}, bf16[128,256]{1,0:T(8,128)(2,1)S(1)}, u32[]{:S(2)}, u32[]{:S(2)}) collective-permute-start(bf16[128,256]{1,0:T(8,128)(2,1)S(1)} %get-tuple-element.46), channel_id=1, source_target_pairs={{0,16},{4,20},{8,24},{12,28},{16,0},{20,4},{24,8},{28,12},{32,48},... | collective-permute-start | bytes 196616 | tf_op jit(solution)/shard_map/ppermute | solution.py:290
  154.7 6.3 %collective-permute-start.12 = (bf16[128,256]{1,0:T(8,128)(2,1)S(1)}, bf16[128,256]{1,0:T(8,128)(2,1)S(1)}, u32[]{:S(2)}, u32[]{:S(2)}) collective-permute-start(bf16[128,256]{1,0:T(8,128)(2,1)S(1)} %get-tuple-element.47), channel_id=1, source_target_pairs={{0,24},{4,28},{8,16},{12,20},{16,8},{20,12},{24,0},{28,4},{32,56},... | collective-permute-start | bytes 196616 | tf_op jit(solution)/shard_map/ppermute | solution.py:290

commit v7 on v6

--- a/solution.py
+++ b/solution.py
@@ -9,6 +9,8 @@
 F32 = jnp.float32
 BF16 = jnp.bfloat16
 VMEM_LIMIT = 48 * 1024 * 1024
+GROUP = 4
+GROUP_CHUNK = 12
 
 
 def params():
@@ -99,43 +101,119 @@
     )(feats, rel_weights)
 
 
-def tile_sums(tile_ids, dest_ids, adjacency, msgs, root_term, chunk=64):
-    tiles = adjacency.shape[0]
-
-    def kernel(slot_ref, dst_ref, adj_ref, msg_ref, root_ref, out_ref, acc_ref):
+def group_tables(tile_ids, dest_ids, nblocks):
+    tiles = tile_ids.shape[0]
+    groups = -(-(tiles + nblocks * (GROUP - 1)) // GROUP)
+    groups = -(-groups // GROUP_CHUNK) * GROUP_CHUNK
+    index = jnp.arange(tiles)
+    hot = (dest_ids[:, None] == jnp.arange(nblocks)[None, :]).astype(jnp.int32)
+    sizes = (jnp.sum(hot, axis=0) + GROUP - 1) // GROUP
+    blocks = jnp.arange(nblocks)
+    ends = jnp.sum(jnp.where(blocks[:, None] <= blocks[None, :], sizes[:, None], 0), axis=0)
+    same = dest_ids[:, None] == dest_ids[None, :]
+    rank = jnp.sum((same & (index[None, :] < index[:, None])).astype(jnp.int32), axis=1)
+    place = jnp.sum(hot * (ends - sizes)[None, :], axis=1) * GROUP + rank
+    here = place[None, :] == jnp.arange(groups * GROUP)[:, None]
+    tile_at = jnp.sum(jnp.where(here, index[None, :] + 1, 0), axis=1) - 1
+    slot_at = jnp.sum(jnp.where(here, tile_ids[None, :], 0), axis=1)
+    passed = (jnp.arange(groups)[:, None] >= ends[None, :]).astype(jnp.int32)
+    dest_of = jnp.minimum(jnp.sum(passed, axis=1), nblocks - 1)
+    return tile_at.astype(jnp.int32), slot_at.astype(jnp.int32), dest_of.astype(jnp.int32)
+
+
+def sort_tiles(tile_at, adjacency, chunk=GROUP * GROUP_CHUNK):
+    places = tile_at.shape[0]
+
+    def kernel(at_ref, adj_ref, out_ref):
         step = pl.program_id(0)
-
-        @pl.when(step == 0)
-        def _():
-            acc_ref[...] = root_ref[...]
-
         for u in range(chunk):
-            t = step * chunk + u
-            acc_ref[dst_ref[t]] += jnp.dot(
-                adj_ref[u], msg_ref[slot_ref[t]], preferred_element_type=F32
+            t = at_ref[step * chunk + u]
+
+            @pl.when(t >= 0)
+            def _():
+                out_ref[u] = adj_ref[jnp.maximum(t, 0)]
+
+            @pl.when(t < 0)
+            def _():
+                out_ref[u] = jnp.zeros((BLK, BLK), BF16)
+
+    return pl.pallas_call(
+        kernel,
+        name="sort_tiles",
+        out_shape=pltpu.HBM((places, BLK, BLK), BF16),
+        grid_spec=pltpu.PrefetchScalarGridSpec(
+            num_scalar_prefetch=1,
+            grid=(places // chunk,),
+            in_specs=[whole(adjacency.shape)],
+            out_specs=pl.BlockSpec((chunk, BLK, BLK), lambda i, *_: (i, 0, 0)),
+        ),
+        compiler_params=params(),
+    )(tile_at, adjacency)
+
+
+def tile_sums(slot_at, dest_of, sorted_tiles, msgs, root_term, ahead=2):
+    places = sorted_tiles.shape[0]
+    chunk = GROUP * GROUP_CHUNK
+    steps = places // chunk
+
+    def kernel(
+        slot_ref, dest_ref, root_hbm, tile_hbm, msg_hbm, out_hbm,
+        tile_ref, msg_ref, root_ref, out_ref, acc_ref, tile_sem, sem,
+    ):
+        load = pltpu.make_async_copy(msg_hbm, msg_ref, sem.at[0])
+        load.start()
+        copies = [
+            pltpu.make_async_copy(
+                tile_hbm.at[pl.ds(i * chunk, chunk)],
+                tile_ref.at[pl.ds(i * chunk, chunk)],
+                tile_sem.at[i],
             )
-
-        @pl.when(step == pl.num_programs(0) - 1)
-        def _():
-            out_ref[...] = acc_ref[...].astype(BF16)
-
+            for i in range(steps)
+        ]
+        for i in range(min(ahead, steps)):
+            copies[i].start()
+        root = pltpu.make_async_copy(root_hbm, root_ref, sem.at[1])
+        acc_ref[...] = jnp.zeros_like(acc_ref)
+        load.wait()
+        for i in range(steps):
+            if i + ahead < steps:
+                copies[i + ahead].start()
+            if i == min(1, steps - 1):
+                root.start()
+            copies[i].wait()
+            for g in range(i * GROUP_CHUNK, (i + 1) * GROUP_CHUNK):
+                at = range(g * GROUP, (g + 1) * GROUP)
+                left = jnp.concatenate([tile_ref[p] for p in at], axis=1)
+                right = jnp.concatenate([msg_ref[slot_ref[p]] for p in at], axis=0)
+                acc_ref[dest_ref[g]] += jnp.dot(left, right, preferred_element_type=F32)
+        root.wait()
+        out_ref[...] = (acc_ref[...] + root_ref[...]).astype(BF16)
+        store = pltpu.make_async_copy(out_ref, out_hbm, sem.at[2])
+        store.start()
+        store.wait()
+
+    anywhere = pl.BlockSpec(memory_space=pl.ANY)
     return pl.pallas_call(
         kernel,
         name="tile_sums",
-        out_shape=jax.ShapeDtypeStruct(root_term.shape, BF16),
+        out_shape=pltpu.HBM(root_term.shape, BF16),
         grid_spec=pltpu.PrefetchScalarGridSpec(
             num_scalar_prefetch=2,
-            grid=(tiles // chunk,),
-            in_specs=[
-                pl.BlockSpec((chunk, BLK, BLK), lambda i, *_: (i, 0, 0)),
-                whole(msgs.shape),
-                whole(root_term.shape),
+            grid=(1,),
+            in_specs=[anywhere, anywhere, anywhere],
+            out_specs=anywhere,
+            scratch_shapes=[
+                pltpu.VMEM(sorted_tiles.shape, BF16),
+                pltpu.VMEM(msgs.shape, BF16),
+                pltpu.VMEM(root_term.shape, F32),
+                pltpu.VMEM(root_term.shape, BF16),
+                pltpu.VMEM(root_term.shape, F32),
+                pltpu.SemaphoreType.DMA((steps,)),
+                pltpu.SemaphoreType.DMA((3,)),
             ],
-            out_specs=whole(root_term.shape),
-            scratch_shapes=[pltpu.VMEM(root_term.shape, F32)],
-        ),
-        compiler_params=params(),
-    )(in_hbm(tile_ids), in_hbm(dest_ids), adjacency, msgs, root_term)
+        ),
+        compiler_params=params(),
+    )(in_hbm(slot_at), in_hbm(dest_of), in_hbm(root_term), sorted_tiles, in_hbm(msgs))
 
 
 def relation_of(ref, c):
@@ -145,9 +223,14 @@
 def select_blocks(slot_block, returned, blocks, nblocks, capacity):
     shards, _, width = returned.shape
 
-    def kernel(block_ref, rel_ref, in_hbm_ref, out_ref, in_ref, load_ref, sem_ref):
-        load = pltpu.make_async_copy(in_hbm_ref, in_ref, load_ref)
+    def kernel(block_ref, ret_ref, in_hbm_ref, out_ref, rel_ref, in_ref, load_ref, sem_ref):
+        rows = pltpu.make_async_copy(
+            ret_ref.at[:, pl.ds(capacity * BLK, 8), :], rel_ref, load_ref.at[0]
+        )
+        rows.start()
+        load = pltpu.make_async_copy(in_hbm_ref, in_ref, load_ref.at[1])
         load.start()
+        rows.wait()
         rels = [[relation_of(rel_ref[o], c) for c in range(capacity)] for o in range(shards)]
         load.wait()
         copies = []
@@ -170,13 +253,14 @@
             num_scalar_prefetch=1,
             grid=(1,),
             in_specs=[
-                pl.BlockSpec((shards, 8, width), lambda i, *_: (0, capacity * BLK // 8, 0)),
+                pl.BlockSpec(memory_space=pl.ANY),
                 pl.BlockSpec(memory_space=pl.ANY),
             ],
             out_specs=pl.BlockSpec(memory_space=pl.ANY),
             scratch_shapes=[
+                pltpu.VMEM((shards, 8, width), BF16),
                 pltpu.VMEM(blocks.shape, BF16),
-                pltpu.SemaphoreType.DMA,
+                pltpu.SemaphoreType.DMA((2,)),
                 pltpu.SemaphoreType.DMA((shards, capacity)),
             ],
         ),
@@ -456,6 +540,11 @@
     projected = project(feats, rel_weights, nblocks)
     root_term = jnp.dot(feats, root_weight, preferred_element_type=F32)
 
+    tile_at, slot_at, dest_of = group_tables(tile_slot[0], tile_dst[0], nblocks)
+    sorted_tiles = sort_tiles(tile_at, tile_adj[0])
+    returned, sorted_tiles, slot_at, dest_of = lax.optimization_barrier(
+        (returned, sorted_tiles, slot_at, dest_of)
+    )
     requested = slot_block[0].T
     outgoing = select_blocks(requested, returned, projected, nblocks, capacity)
     outgoing, returned = lax.optimization_barrier((outgoing, returned))
@@ -487,9 +576,9 @@
     kept, *sends = first_stage(place, stacked, got, dots, 4)
     got = [exchange(x, "shard", k << 3) for k, x in zip((1, 2, 3), sends)]
     output = tile_sums(
-        tile_slot[0],
-        tile_dst[0],
-        tile_adj[0],
+        slot_at,
+        dest_of,
+        sorted_tiles,
         incoming.reshape(slots, BLK, width),
         root_term.reshape(nblocks, BLK, width),
     ).reshape(nblocks * BLK, width)

time: 162 us -> 161 us (level)
  waiting for transfers between devices: 64.2 us -> 51.3 us
  Pallas kernels: 48.4 us -> 56.4 us
  other arithmetic: 1 us -> 2.85 us
    all_to_all x1, waiting for transfers between devices: 46.1 us -> 34 us  [body(): returned = lax.all_to_all(slot_grads, 'shard', 0, 0, tiled=True)]
    pallas_call x1 -> x2, Pallas kernels: 9.92 us -> 19 us  [the longest x1 10.3 us: sort_tiles(): pl.pallas_call(kernel, name='sort_tiles', out_shape=pltpu.HBM((places, BL...]
  transfers between devices with their start and end apart: 15 -> 15, of which waited for: 8 -> 10; matrix products, arithmetic and copies ran while one was open for 6% -> 8% of each run, Pallas kernels for 18% -> 24%
where the time goes in v7:
time: 161 us; the launch traced here: 160 us
  Pallas kernels  56.4 us (35%)
  waiting for transfers between devices  51.3 us (32%)
  starting transfers between devices  38.6 us (24%)
  matrix products  5.75 us (4%)
  local copies, waits for them, and re-layouts  4.64 us (3%)
  other arithmetic  2.85 us (2%)
    all_to_all x1, waiting for transfers between devices, body(): returned = lax.all_to_all(slot_grads, 'shard', 0, 0, tiled=True)  34 us
    ppermute x13, starting transfers between devices, exchange(): lax.ppermute(x, axis, [(i, i ^ mask) for i in range(lax.axis_size(axis))])  23.1 us
    ppermute x13, waiting for transfers between devices, exchange(): lax.ppermute(x, axis, [(i, i ^ mask) for i in range(lax.axis_size(axis))])  16.8 us
    pallas_call x1, Pallas kernels, tile_grads(): pl.pallas_call(kernel, name='tile_grads', out_shape=pltpu.HBM((shards, ro...  11 us
    pallas_call x1, Pallas kernels, sort_tiles(): pl.pallas_call(kernel, name='sort_tiles', out_shape=pltpu.HBM((places, BL...  10.3 us
    pallas_call x1, Pallas kernels, tile_sums(): pl.pallas_call(kernel, name='tile_sums', out_shape=pltpu.HBM(root_term.sh...  8.67 us
    all_to_all x1, starting transfers between devices, body(): returned = lax.all_to_all(slot_grads, 'shard', 0, 0, tiled=True)  8.66 us
    pallas_call x1, Pallas kernels, weight_grads(): pl.pallas_call(kernel, name='weight_grads', cost_estimate=pl.CostEstimate...  8.54 us
  transfers between devices with their start and end apart: 15, of which 10 were waited for; matrix products, arithmetic and copies ran while one was open for 8% of the time, Pallas kernels for 24%

profile of v7, /device:TPU:0, one launch (start us, length us, event | category | flops | bytes accessed | tf_op | source)
XLA Modules:
  0.0 160.4 jit_solution(935937861139512534)
XLA Ops:
  0.6 0.0 copy-start
  0.6 11.0 %tile_grads.1 = bf16[32,264,256]{2,1,0:T(8,128)(2,1)} custom-call(s32[256]{0:T(256)} %bitcast.78, s32[256]{0:T(256)} %bitcast.74, s32[2,32]{1,0:T(2,128)} %bitcast.80, bf16[256,128,128]{2,1,0:T(8,128)(2,1)} %bitcast.64, bf16[8,128,256]{2,1,0:T(8,128)(2,1)} %bitcast.60), custom_call_target="tpu_custom_call" | custom-call | tf_op jit(solution)/shard_map/tile_grads/pallas_call | solution.py:63
  11.7 8.7 %all-to-all-start = ((bf16[32,264,256]{2,1,0:T(8,128)(2,1)}), bf16[32,264,256]{2,1,0:T(8,128)(2,1)}, u32[]{:S(2)}, u32[]{:S(2)}) async-start(bf16[32,264,256]{2,1,0:T(8,128)(2,1)} %tile_grads.1), calls=%async_computation | async-start | bytes 8650752 | tf_op jit(solution)/shard_map/all_to_all | solution.py:533
  20.4 0.1 convert_reduce_fusion.1
  20.5 0.1 select_reduce_fusion.3
  20.6 0.1 select_reduce_fusion.2
  20.7 0.2 convert_reduce_fusion
  20.9 0.7 select_reduce_fusion
  21.6 10.3 %sort_tiles.1.tile_hbm = bf16[288,128,128]{2,1,0:T(8,128)(2,1)} custom-call(s32[288]{0:T(512)S(1)} %broadcast_add_fusion.at_ref, bf16[256,128,128]{2,1,0:T(8,128)(2,1)} %bitcast.65), custom_call_target="tpu_custom_call" | custom-call | tf_op jit(solution)/shard_map/sort_tiles/pallas_call | solution.py:140
  32.0 1.2 copy.22
  33.2 1.3 convolution_convert_fusion
  34.6 0.0 copy-start.1
  34.6 0.4 copy.25
  35.0 0.9 copy-done.1
  36.0 4.1 %project.1.in_hbm_ref = bf16[40,128,256]{2,1,0:T(8,128)(2,1)} custom-call(bf16[1024,768]{1,0:T(8,128)(2,1)S(1)} %copy-done.1, bf16[5,768,256]{2,1,0:T(8,128)(2,1)S(1)} %bitcast.56), custom_call_target="tpu_custom_call" | custom-call | tf_op jit(solution)/shard_map/project/pallas_call | solution.py:90
  40.1 0.1 convert_reduce_fusion.2
  40.2 0.5 broadcast_minimum_fusion.dest_ref
  40.7 34.0 %all-to-all-done.ret_ref = bf16[32,264,256]{2,1,0:T(8,128)(2,1)} async-done(((bf16[32,264,256]{2,1,0:T(8,128)(2,1)}), bf16[32,264,256]{2,1,0:T(8,128)(2,1)}, u32[]{:S(2)}, u32[]{:S(2)}) %all-to-all-start) | async-done | bytes 4325408 | tf_op jit(solution)/shard_map/all_to_all | solution.py:533
  74.7 5.1 %select_blocks.1 = bf16[32,256,256]{2,1,0:T(8,128)(2,1)} custom-call(s32[2,32]{1,0:T(2,128)} %bitcast.62, bf16[32,264,256]{2,1,0:T(8,128)(2,1)} %all-to-all-done.ret_ref, bf16[40,128,256]{2,1,0:T(8,128)(2,1)} %project.1.in_hbm_ref), custom_call_target="tpu_custom_call" | custom-call | tf_op jit(solution)/shard_map/select_blocks/pallas_call | solution.py:248
  79.8 0.0 copy-start.7
  79.8 6.8 %all-to-all-start.1 = ((bf16[32,256,256]{2,1,0:T(8,128)(2,1)}), bf16[32,256,256]{2,1,0:T(8,128)(2,1)}, u32[]{:S(2)}, u32[]{:S(2)}) async-start(bf16[32,256,256]{2,1,0:T(8,128)(2,1)} %select_blocks.1), calls=%async_computation.1 | async-start | bytes 8388608 | tf_op jit(solution)/shard_map/all_to_all | solution.py:551
  86.6 0.1 copy.19
  86.7 0.1 reshape.110.coef_ref
  86.8 0.0 copy-start.6
  86.8 6.5 %sum_by_key.1 = bf16[40,128,256]{2,1,0:T(8,128)(2,1)} custom-call(s32[2,32]{1,0:T(2,128)S(1)} %bitcast.63, bf16[32,264,256]{2,1,0:T(8,128)(2,1)} %all-to-all-done.ret_ref), custom_call_target="tpu_custom_call" | custom-call | tf_op jit(solution)/shard_map/sum_by_key/pallas_call | solution.py:293
  93.3 8.5 %weight_grads.1 = (f32[5,768,256]{2,1,0:T(8,128)}, f32[8,128]{1,0:T(8,128)S(1)}) custom-call(f32[20]{0:T(128)S(1)} %reshape.110.coef_ref, bf16[1024,768]{1,0:T(8,128)(2,1)S(1)} %copy-done.2, bf16[5,1024,256]{2,1,0:T(8,128)(2,1)} %bitcast.71, bf16[1024,256]{1,0:T(8,128)(2,1)S(1)} %copy-done.4, bf16[4,768,256]{2,1,0:T(8,128)(2,1)S(1)} %copy-done.6), custom_call_target="tpu_custom_call" | custom-call | flops 2415919104 | bytes 10616832 | tf_op jit(solution)/shard_map/weight_grads/pallas_call | solution.py:341
  101.9 0.2 collective-permute-start
  102.1 1.7 %fusion = bf16[5,4,4,24,256]{4,3,2,1,0:T(8,128)(2,1)S(1)} fusion(f32[5,4,4,2,24,256]{5,4,3,2,1,0:T(8,128)} %bitcast.58, s32[]{:T(128)S(6)} %select_n.49), kind=kLoop, calls=%fused_computation.4 | loop fusion | bytes 1966084 | tf_op jit(solution)/shard_map/convert_element_type | solution.py:575
  103.7 0.4 collective-permute-start.6
  104.1 2.2 %fusion.9 = f32[1024,768,1]{1,0,2:T(8,128)S(1)} fusion(bf16[5,1024,256]{2,1,0:T(8,128)(2,1)S(1)} %bitcast.72, bf16[5,768,256]{2,1,0:T(8,128)(2,1)S(1)} %bitcast.57), kind=kOutput, calls=%fused_computation.38 | convolution fusion | flops 2013265920 | bytes 7733248 | tf_op jit(solution)/shard_map/rno,rco->nc/dot_general | solution.py:555
  106.4 0.0 collective-permute-done
  106.4 1.8 %collective-permute-start.1 = (f32[8,128]{1,0:T(8,128)S(1)}, f32[8,128]{1,0:T(8,128)S(1)}, u32[]{:S(2)}, u32[]{:S(2)}) collective-permute-start(f32[8,128]{1,0:T(8,128)S(1)} %add.87), channel_id=1, source_target_pairs={{0,1},{1,0},{2,3},{3,2},{4,5},{5,4},{6,7},{7,6},{8,9},{9,8},{10,11... | collective-permute-start | bytes 12296 | tf_op jit(solution)/shard_map/ppermute | solution.py:374
  108.2 0.6 bitcast_add_fusion
  108.8 1.5 collective-permute-done.1
  110.3 3.0 %collective-permute-start.2 = (f32[8,128]{1,0:T(8,128)S(1)}, f32[8,128]{1,0:T(8,128)S(1)}, u32[]{:S(2)}, u32[]{:S(2)}) collective-permute-start(f32[8,128]{1,0:T(8,128)S(1)} %add.88), channel_id=1, source_target_pairs={{0,2},{1,3},{2,0},{3,1},{4,6},{5,7},{6,4},{7,5},{8,10},{9,11},{10,... | collective-permute-start | bytes 12296 | tf_op jit(solution)/shard_map/ppermute | solution.py:374
  113.3 0.1 fusion.6
  113.4 2.0 %collective-permute-done.2 = f32[8,128]{1,0:T(8,128)S(1)} collective-permute-done((f32[8,128]{1,0:T(8,128)S(1)}, f32[8,128]{1,0:T(8,128)S(1)}, u32[]{:S(2)}, u32[]{:S(2)}) %collective-permute-start.2) | collective-permute-done | bytes 4128 | tf_op jit(solution)/shard_map/ppermute | solution.py:374
  115.4 1.5 collective-permute-start.3
  116.9 2.7 %collective-permute-start.4 = (bf16[256,768]{1,0:T(8,128)(2,1)S(1)}, bf16[256,768]{1,0:T(8,128)(2,1)S(1)}, u32[]{:S(2)}, u32[]{:S(2)}) collective-permute-start(bf16[256,768]{1,0:T(8,128)(2,1)S(1)} %get-tuple-element.40), channel_id=1, source_target_pairs={{0,2},{1,3},{2,0},{3,1},{4,6},{5,7},{6,4},{7,5},{8,10},{9,11},{10,... | collective-permute-start | bytes 1179656 | tf_op jit(solution)/shard_map/ppermute | solution.py:374
  119.6 0.5 collective-permute-start.5
  120.1 0.1 pad_add_fusion.place_ref
  120.2 1.6 fusion.8
  121.7 0.0 collective-permute-done.6.got_ref
  121.7 0.7 first_stage.1
  122.5 1.8 %collective-permute-start.7 = (bf16[488,256]{1,0:T(8,128)(2,1)S(1)}, bf16[488,256]{1,0:T(8,128)(2,1)S(1)}, u32[]{:S(2)}, u32[]{:S(2)}) collective-permute-start(bf16[488,256]{1,0:T(8,128)(2,1)S(1)} %get-tuple-element.48), channel_id=1, source_target_pairs={{0,32},{4,36},{8,40},{12,44},{16,48},{20,52},{24,56},{28,60},{32,0... | collective-permute-start | bytes 749576 | tf_op jit(solution)/shard_map/ppermute | solution.py:374
  124.3 2.7 %collective-permute-start.8 = (bf16[488,256]{1,0:T(8,128)(2,1)S(1)}, bf16[488,256]{1,0:T(8,128)(2,1)S(1)}, u32[]{:S(2)}, u32[]{:S(2)}) collective-permute-start(bf16[488,256]{1,0:T(8,128)(2,1)S(1)} %get-tuple-element.49), channel_id=1, source_target_pairs={{0,64},{4,68},{8,72},{12,76},{16,80},{20,84},{24,88},{28,92},{32,9... | collective-permute-start | bytes 749576 | tf_op jit(solution)/shard_map/ppermute | solution.py:374
  127.0 0.5 collective-permute-done.3
  127.4 3.0 %collective-permute-start.9 = (bf16[488,256]{1,0:T(8,128)(2,1)S(1)}, bf16[488,256]{1,0:T(8,128)(2,1)S(1)}, u32[]{:S(2)}, u32[]{:S(2)}) collective-permute-start(bf16[488,256]{1,0:T(8,128)(2,1)S(1)} %get-tuple-element.50), channel_id=1, source_target_pairs={{0,96},{4,100},{8,104},{12,108},{16,112},{20,116},{24,120},{28,124... | collective-permute-start | bytes 749576 | tf_op jit(solution)/shard_map/ppermute | solution.py:374
  130.4 5.4 %collective-permute-done.4 = bf16[256,768]{1,0:T(8,128)(2,1)S(1)} collective-permute-done((bf16[256,768]{1,0:T(8,128)(2,1)S(1)}, bf16[256,768]{1,0:T(8,128)(2,1)S(1)}, u32[]{:S(2)}, u32[]{:S(2)}) %collective-permute-start.4) | collective-permute-done | bytes 393248 | tf_op jit(solution)/shard_map/ppermute | solution.py:374
  135.8 2.6 %collective-permute-done.5 = bf16[256,768]{1,0:T(8,128)(2,1)S(1)} collective-permute-done((bf16[256,768]{1,0:T(8,128)(2,1)S(1)}, bf16[256,768]{1,0:T(8,128)(2,1)S(1)}, u32[]{:S(2)}, u32[]{:S(2)}) %collective-permute-start.5) | collective-permute-done | bytes 393248 | tf_op jit(solution)/shard_map/ppermute | solution.py:374
  138.4 0.9 fusion.3
  139.3 0.6 all-to-all-done.1
  139.9 8.7 %tile_sums.1 = bf16[8,128,256]{2,1,0:T(8,128)(2,1)} custom-call(s32[288]{0:T(512)} %get-tuple-element.32.slot_ref, s32[72]{0:T(128)} %broadcast_minimum_fusion.dest_ref, f32[8,128,256]{2,1,0:T(8,128)} %bitcast.70, bf16[288,128,128]{2,1,0:T(8,128)(2,1)} %sort_tiles.1.tile_hbm, bf16[64,128,256]{2,1,0:T(8,128)(2,1)} %bitcast.9.msg_hbm), custom_call_target="tpu_custom_call" | custom-call | tf_op jit(solution)/shard_map/tile_sums/pallas_call | solution.py:196
  148.6 0.0 collective-permute-done.7.refs_0_
  148.6 1.4 collective-permute-done.8.refs_1_
  150.0 0.0 collective-permute-done.9.refs_2_
  150.0 0.7 second_stage.1
  150.7 2.8 %collective-permute-start.10 = (bf16[128,256]{1,0:T(8,128)(2,1)S(1)}, bf16[128,256]{1,0:T(8,128)(2,1)S(1)}, u32[]{:S(2)}, u32[]{:S(2)}) collective-permute-start(bf16[128,256]{1,0:T(8,128)(2,1)S(1)} %get-tuple-element.53), channel_id=1, source_target_pairs={{0,8},{4,12},{8,0},{12,4},{16,24},{20,28},{24,16},{28,20},{32,40},... | collective-permute-start | bytes 196616 | tf_op jit(solution)/shard_map/ppermute | solution.py:374
  153.5 0.0 collective-permute-start.11
  153.5 2.8 %collective-permute-start.12 = (bf16[128,256]{1,0:T(8,128)(2,1)S(1)}, bf16[128,256]{1,0:T(8,128)(2,1)S(1)}, u32[]{:S(2)}, u32[]{:S(2)}) collective-permute-start(bf16[128,256]{1,0:T(8,128)(2,1)S(1)} %get-tuple-element.55), channel_id=1, source_target_pairs={{0,24},{4,28},{8,16},{12,20},{16,8},{20,12},{24,0},{28,4},{32,56},... | collective-permute-start | bytes 196616 | tf_op jit(solution)/shard_map/ppermute | solution.py:374
  156.3 0.0 collective-permute-done.10.refs_0_
  156.3 3.1 %collective-permute-done.11.refs_1_ = bf16[128,256]{1,0:T(8,128)(2,1)S(1)} collective-permute-done((bf16[128,256]{1,0:T(8,128)(2,1)S(1)}, bf16[128,256]{1,0:T(8,128)(2,1)S(1)}, u32[]{:S(2)}, u32[]{:S(2)}) %collective-permute-start.11) | collective-permute-done | bytes 65568 | tf_op jit(solution)/shard_map/ppermute | solution.py:374
  159.3 0.4 collective-permute-done.12.refs_2_
  159.7 0.7 last_stage.1
  (27 shorter events, 0.1 us)
Async XLA Ops:
  0.6 107.5 %copy-start = (bf16[768,256]{1,0:T(8,128)(2,1)S(1)}, bf16[768,256]{1,0:T(8,128)(2,1)}, u32[]{:S(2)}) copy-start(bf16[768,256]{1,0:T(8,128)(2,1)} %param.13) | copy-start | bytes 1179652
  11.7 8.7 %copy-start.9 = (s32[1,256]{1,0:T(1,128)S(1)}, s32[1,256]{1,0:T(1,128)}, u32[]{:S(2)}) copy-start(s32[1,256]{1,0:T(1,128)} %param.17) | copy-start | bytes 3076
  11.7 9.2 %copy-start.10 = (s32[1,256]{1,0:T(1,128)S(1)}, s32[1,256]{1,0:T(1,128)}, u32[]{:S(2)}) copy-start(s32[1,256]{1,0:T(1,128)} %param.16) | copy-start | bytes 3076
  11.7 63.0 %all-to-all-start = ((bf16[32,264,256]{2,1,0:T(8,128)(2,1)}), bf16[32,264,256]{2,1,0:T(8,128)(2,1)}, u32[]{:S(2)}, u32[]{:S(2)}) async-start(bf16[32,264,256]{2,1,0:T(8,128)(2,1)} %tile_grads.1), calls=%async_computation | async-start | bytes 8650752 | tf_op jit(solution)/shard_map/all_to_all | solution.py:533
  21.6 10.3 %copy-start.5 = (bf16[4,768,256]{2,1,0:T(8,128)(2,1)S(1)}, bf16[4,768,256]{2,1,0:T(8,128)(2,1)}, u32[]{:S(2)}) copy-start(bf16[4,768,256]{2,1,0:T(8,128)(2,1)} %base_ref.1) | copy-start | bytes 4718596
  32.0 1.2 copy-start.11
  34.6 1.4 copy-start.1
  79.8 7.0 %copy-start.7 = (s32[1,32,2]{1,2,0:T(2,128)S(1)}, s32[1,32,2]{1,2,0:T(2,128)}, u32[]{:S(2)}) copy-start(s32[1,32,2]{1,2,0:T(2,128)} %param.14) | copy-start | bytes 772
  79.8 60.1 %all-to-all-start.1 = ((bf16[32,256,256]{2,1,0:T(8,128)(2,1)}), bf16[32,256,256]{2,1,0:T(8,128)(2,1)}, u32[]{:S(2)}, u32[]{:S(2)}) async-start(bf16[32,256,256]{2,1,0:T(8,128)(2,1)} %select_blocks.1), calls=%async_computation.1 | async-start | bytes 8388608 | tf_op jit(solution)/shard_map/all_to_all | solution.py:551
  86.8 6.5 %copy-start.2 = (bf16[1024,768]{1,0:T(8,128)(2,1)S(1)}, bf16[1024,768]{1,0:T(8,128)(2,1)}, u32[]{:S(2)}) copy-start(bf16[1024,768]{1,0:T(8,128)(2,1)} %feat_ref.3) | copy-start | bytes 4718596
  86.8 6.5 %copy-start.4 = (bf16[1024,256]{1,0:T(8,128)(2,1)S(1)}, bf16[1024,256]{1,0:T(8,128)(2,1)}, u32[]{:S(2)}) copy-start(bf16[1024,256]{1,0:T(8,128)(2,1)} %grad_ref.1) | copy-start | bytes 1572868
  86.8 6.5 %copy-start.6 = (bf16[4,768,256]{2,1,0:T(8,128)(2,1)S(1)}, bf16[4,768,256]{2,1,0:T(8,128)(2,1)}, u32[]{:S(2)}) copy-start(bf16[4,768,256]{2,1,0:T(8,128)(2,1)} %base_ref.1) | copy-start | bytes 4718596
  93.3 10.8 %copy-start.8 = (bf16[40,128,256]{2,1,0:T(8,128)(2,1)S(1)}, bf16[40,128,256]{2,1,0:T(8,128)(2,1)}, u32[]{:S(2)}) copy-start(bf16[40,128,256]{2,1,0:T(8,128)(2,1)} %sum_by_key.1) | copy-start | bytes 7864324
  101.9 4.5 %collective-permute-start = (f32[8,128]{1,0:T(8,128)S(1)}, f32[8,128]{1,0:T(8,128)S(1)}, u32[]{:S(2)}, u32[]{:S(2)}) collective-permute-start(f32[8,128]{1,0:T(8,128)S(1)} %get-tuple-element.38), channel_id=1, source_target_pairs={{0,4},{4,0},{8,12},{12,8},{16,20},{20,16},{24,28},{28,24},{32,36},... | collective-permute-start | bytes 12296 | tf_op jit(solution)/shard_map/ppermute | solution.py:374
  103.7 18.0 %collective-permute-start.6 = (bf16[5,4,4,24,256]{4,3,2,1,0:T(8,128)(2,1)S(1)}, bf16[5,4,4,24,256]{4,3,2,1,0:T(8,128)(2,1)S(1)}, u32[]{:S(2)}, u32[]{:S(2)}) collective-permute-start(bf16[5,4,4,24,256]{4,3,2,1,0:T(8,128)(2,1)S(1)} %fusion), channel_id=1, source_target_pairs={{0,4},{4,0},{8,12},{12,8},{16,20},{20,16},{24,28},{28,24},{32,36},... | collective-permute-start | bytes 2949128 | tf_op jit(solution)/shard_map/ppermute | solution.py:374
  106.4 3.9 %collective-permute-start.1 = (f32[8,128]{1,0:T(8,128)S(1)}, f32[8,128]{1,0:T(8,128)S(1)}, u32[]{:S(2)}, u32[]{:S(2)}) collective-permute-start(f32[8,128]{1,0:T(8,128)S(1)} %add.87), channel_id=1, source_target_pairs={{0,1},{1,0},{2,3},{3,2},{4,5},{5,4},{6,7},{7,6},{8,9},{9,8},{10,11... | collective-permute-start | bytes 12296 | tf_op jit(solution)/shard_map/ppermute | solution.py:374
  108.8 13.0 %copy-start.3 = (f32[5,768,256]{2,1,0:T(8,128)S(1)}, f32[5,768,256]{2,1,0:T(8,128)}, u32[]{:S(2)}) copy-start(f32[5,768,256]{2,1,0:T(8,128)} %get-tuple-element.42) | copy-start | bytes 11796484
  110.3 5.1 %collective-permute-start.2 = (f32[8,128]{1,0:T(8,128)S(1)}, f32[8,128]{1,0:T(8,128)S(1)}, u32[]{:S(2)}, u32[]{:S(2)}) collective-permute-start(f32[8,128]{1,0:T(8,128)S(1)} %add.88), channel_id=1, source_target_pairs={{0,2},{1,3},{2,0},{3,1},{4,6},{5,7},{6,4},{7,5},{8,10},{9,11},{10,... | collective-permute-start | bytes 12296 | tf_op jit(solution)/shard_map/ppermute | solution.py:374
  115.4 12.1 %collective-permute-start.3 = (bf16[256,768]{1,0:T(8,128)(2,1)S(1)}, bf16[256,768]{1,0:T(8,128)(2,1)S(1)}, u32[]{:S(2)}, u32[]{:S(2)}) collective-permute-start(bf16[256,768]{1,0:T(8,128)(2,1)S(1)} %get-tuple-element.39), channel_id=1, source_target_pairs={{0,1},{1,0},{2,3},{3,2},{4,5},{5,4},{6,7},{7,6},{8,9},{9,8},{10,11... | collective-permute-start | bytes 1179656 | tf_op jit(solution)/shard_map/ppermute | solution.py:374
  116.9 18.9 %collective-permute-start.4 = (bf16[256,768]{1,0:T(8,128)(2,1)S(1)}, bf16[256,768]{1,0:T(8,128)(2,1)S(1)}, u32[]{:S(2)}, u32[]{:S(2)}) collective-permute-start(bf16[256,768]{1,0:T(8,128)(2,1)S(1)} %get-tuple-element.40), channel_id=1, source_target_pairs={{0,2},{1,3},{2,0},{3,1},{4,6},{5,7},{6,4},{7,5},{8,10},{9,11},{10,... | collective-permute-start | bytes 1179656 | tf_op jit(solution)/shard_map/ppermute | solution.py:374
  119.6 18.8 %collective-permute-start.5 = (bf16[256,768]{1,0:T(8,128)(2,1)S(1)}, bf16[256,768]{1,0:T(8,128)(2,1)S(1)}, u32[]{:S(2)}, u32[]{:S(2)}) collective-permute-start(bf16[256,768]{1,0:T(8,128)(2,1)S(1)} %get-tuple-element.41), channel_id=1, source_target_pairs={{0,3},{1,2},{2,1},{3,0},{4,7},{5,6},{6,5},{7,4},{8,11},{9,10},{10,... | collective-permute-start | bytes 1179656 | tf_op jit(solution)/shard_map/ppermute | solution.py:374
  122.5 26.1 %collective-permute-start.7 = (bf16[488,256]{1,0:T(8,128)(2,1)S(1)}, bf16[488,256]{1,0:T(8,128)(2,1)S(1)}, u32[]{:S(2)}, u32[]{:S(2)}) collective-permute-start(bf16[488,256]{1,0:T(8,128)(2,1)S(1)} %get-tuple-element.48), channel_id=1, source_target_pairs={{0,32},{4,36},{8,40},{12,44},{16,48},{20,52},{24,56},{28,60},{32,0... | collective-permute-start | bytes 749576 | tf_op jit(solution)/shard_map/ppermute | solution.py:374
  124.3 25.8 %collective-permute-start.8 = (bf16[488,256]{1,0:T(8,128)(2,1)S(1)}, bf16[488,256]{1,0:T(8,128)(2,1)S(1)}, u32[]{:S(2)}, u32[]{:S(2)}) collective-permute-start(bf16[488,256]{1,0:T(8,128)(2,1)S(1)} %get-tuple-element.49), channel_id=1, source_target_pairs={{0,64},{4,68},{8,72},{12,76},{16,80},{20,84},{24,88},{28,92},{32,9... | collective-permute-start | bytes 749576 | tf_op jit(solution)/shard_map/ppermute | solution.py:374
  127.4 22.6 %collective-permute-start.9 = (bf16[488,256]{1,0:T(8,128)(2,1)S(1)}, bf16[488,256]{1,0:T(8,128)(2,1)S(1)}, u32[]{:S(2)}, u32[]{:S(2)}) collective-permute-start(bf16[488,256]{1,0:T(8,128)(2,1)S(1)} %get-tuple-element.50), channel_id=1, source_target_pairs={{0,96},{4,100},{8,104},{12,108},{16,112},{20,116},{24,120},{28,124... | collective-permute-start | bytes 749576 | tf_op jit(solution)/shard_map/ppermute | solution.py:374
  150.7 5.6 %collective-permute-start.10 = (bf16[128,256]{1,0:T(8,128)(2,1)S(1)}, bf16[128,256]{1,0:T(8,128)(2,1)S(1)}, u32[]{:S(2)}, u32[]{:S(2)}) collective-permute-start(bf16[128,256]{1,0:T(8,128)(2,1)S(1)} %get-tuple-element.53), channel_id=1, source_target_pairs={{0,8},{4,12},{8,0},{12,4},{16,24},{20,28},{24,16},{28,20},{32,40},... | collective-permute-start | bytes 196616 | tf_op jit(solution)/shard_map/ppermute | solution.py:374
  153.5 5.8 %collective-permute-start.11 = (bf16[128,256]{1,0:T(8,128)(2,1)S(1)}, bf16[128,256]{1,0:T(8,128)(2,1)S(1)}, u32[]{:S(2)}, u32[]{:S(2)}) collective-permute-start(bf16[128,256]{1,0:T(8,128)(2,1)S(1)} %get-tuple-element.54), channel_id=1, source_target_pairs={{0,16},{4,20},{8,24},{12,28},{16,0},{20,4},{24,8},{28,12},{32,48},... | collective-permute-start | bytes 196616 | tf_op jit(solution)/shard_map/ppermute | solution.py:374
  153.5 6.2 %collective-permute-start.12 = (bf16[128,256]{1,0:T(8,128)(2,1)S(1)}, bf16[128,256]{1,0:T(8,128)(2,1)S(1)}, u32[]{:S(2)}, u32[]{:S(2)}) collective-permute-start(bf16[128,256]{1,0:T(8,128)(2,1)S(1)} %get-tuple-element.55), channel_id=1, source_target_pairs={{0,24},{4,28},{8,16},{12,20},{16,8},{20,12},{24,0},{28,4},{32,56},... | collective-permute-start | bytes 196616 | tf_op jit(solution)/shard_map/ppermute | solution.py:374

commit v8 on v7

--- a/solution.py
+++ b/solution.py
@@ -394,12 +394,15 @@
 
     def kernel(place_ref, own_ref, got_ref, dots_ref, keep_ref, *send_refs):
         core = place_ref[0]
-        at = place_ref[1]
         high, low = two_terms(dots_ref[...])
         for k in range(size):
+            role = (place_ref[1] ^ (k >> 1), place_ref[2] ^ (k & 1))
             for p in range(parts):
                 for q in range(rest):
-                    value = own_ref[p, at ^ k, q, core] + got_ref[p, at ^ k, q].astype(F32)
+                    first = 3 - role[0] if q >> 1 else role[0]
+                    second = 3 - role[1] if q & 1 else role[1]
+                    value = own_ref[p, first, second, core]
+                    value = value + got_ref[p, first, second].astype(F32)
                     if k == 0:
                         keep_ref[p, q] = value
                     else:
@@ -432,7 +435,7 @@
         gots = refs[: len(got)]
         keep_ref, all_ref = refs[len(got) : len(got) + 2]
         send_refs = refs[len(got) + 2 :]
-        at = place_ref[2]
+        at = place_ref[3]
         high, low = two_terms(dots_ref[...])
         sums = [high.astype(F32) + low.astype(F32)]
         sums += [sum_terms(g[pl.ds(length * size, 8), :]) for g in gots]
@@ -571,10 +574,12 @@
 
     rows = width_in // shards
     stacked = stacked.reshape(nbase + 1, 4, 4, 2, rows, width)
-    place = jnp.stack([me & 1, (me >> 3) & 3, (me >> 1) & 3]).astype(jnp.int32)
+    along = ((me >> 3) & 3, (me >> 1) & 3)
+    role = [(i & 1) ^ (i >> 1) for i in along]
+    place = jnp.stack([me & 1, *role, (along[0] >> 1) * 2 + (along[1] >> 1)]).astype(jnp.int32)
     got = exchange(chunk_of(stacked, (me & 1) ^ 1, 3).astype(BF16), "shard", 1)
     kept, *sends = first_stage(place, stacked, got, dots, 4)
-    got = [exchange(x, "shard", k << 3) for k, x in zip((1, 2, 3), sends)]
+    got = [exchange(x, "shard", k) for k, x in zip((2, 8, 10), sends)]
     output = tile_sums(
         slot_at,
         dest_of,
@@ -584,7 +589,7 @@
     ).reshape(nblocks * BLK, width)
     output, grad_feats, kept = lax.optimization_barrier((output, grad_feats, kept))
     kept, dots, *sends = second_stage(place, kept, dots, got, 4)
-    got = [exchange(x, "shard", k << 1) for k, x in zip((1, 2, 3), sends)]
+    got = [exchange(x, "shard", k) for k, x in zip((6, 24, 30), sends)]
     grad_bases, grad_root, grad_coef = last_stage(kept, dots, got, relations)
     return (output, grad_feats, grad_bases, grad_root, grad_coef.T)
 

time: 161 us -> 162 us (level)
  waiting for transfers between devices: 51.3 us -> 54 us
  transfers between devices with their start and end apart: 15 -> 15, of which waited for: 10 -> 7; matrix products, arithmetic and copies ran while one was open for 8% -> 8% of each run, Pallas kernels for 24% -> 24%
where the time goes in v8:
time: 162 us
  Pallas kernels  56.4 us (35%)
  waiting for transfers between devices  54 us (33%)
  starting transfers between devices  37.3 us (23%)
  matrix products  5.75 us (4%)
  local copies, waits for them, and re-layouts  4.64 us (3%)
  other arithmetic  2.85 us (2%)
    all_to_all x1, waiting for transfers between devices, body(): returned = lax.all_to_all(slot_grads, 'shard', 0, 0, tiled=True)  34 us
    ppermute x13, starting transfers between devices, exchange(): lax.ppermute(x, axis, [(i, i ^ mask) for i in range(lax.axis_size(axis))])  21.9 us
    ppermute x13, waiting for transfers between devices, exchange(): lax.ppermute(x, axis, [(i, i ^ mask) for i in range(lax.axis_size(axis))])  18 us
    pallas_call x1, Pallas kernels, tile_grads(): pl.pallas_call(kernel, name='tile_grads', out_shape=pltpu.HBM((shards, ro...  11 us
    pallas_call x1, Pallas kernels, sort_tiles(): pl.pallas_call(kernel, name='sort_tiles', out_shape=pltpu.HBM((places, BL...  10.3 us
    pallas_call x1, Pallas kernels, tile_sums(): pl.pallas_call(kernel, name='tile_sums', out_shape=pltpu.HBM(root_term.sh...  8.67 us
    all_to_all x1, starting transfers between devices, body(): returned = lax.all_to_all(slot_grads, 'shard', 0, 0, tiled=True)  8.66 us
    pallas_call x1, Pallas kernels, weight_grads(): pl.pallas_call(kernel, name='weight_grads', cost_estimate=pl.CostEstimate...  8.54 us
  transfers between devices with their start and end apart: 15, of which 7 were waited for; matrix products, arithmetic and copies ran while one was open for 8% of the time, Pallas kernels for 24%

profile of v8, /device:TPU:0, one launch (start us, length us, event | category | flops | bytes accessed | tf_op | source)
XLA Modules:
  0.0 161.9 jit_solution(10736065507980860494)
XLA Ops:
  0.6 0.0 copy-start
  0.6 11.0 %tile_grads.1 = bf16[32,264,256]{2,1,0:T(8,128)(2,1)} custom-call(s32[256]{0:T(256)} %bitcast.79, s32[256]{0:T(256)} %bitcast.75, s32[2,32]{1,0:T(2,128)} %bitcast.81, bf16[256,128,128]{2,1,0:T(8,128)(2,1)} %bitcast.65, bf16[8,128,256]{2,1,0:T(8,128)(2,1)} %bitcast.61), custom_call_target="tpu_custom_call" | custom-call | tf_op jit(solution)/shard_map/tile_grads/pallas_call | solution.py:63
  11.7 8.7 %all-to-all-start = ((bf16[32,264,256]{2,1,0:T(8,128)(2,1)}), bf16[32,264,256]{2,1,0:T(8,128)(2,1)}, u32[]{:S(2)}, u32[]{:S(2)}) async-start(bf16[32,264,256]{2,1,0:T(8,128)(2,1)} %tile_grads.1), calls=%async_computation | async-start | bytes 8650752 | tf_op jit(solution)/shard_map/all_to_all | solution.py:536
  20.4 0.1 convert_reduce_fusion.1
  20.5 0.1 select_reduce_fusion.3
  20.6 0.1 select_reduce_fusion.2
  20.7 0.2 convert_reduce_fusion
  20.9 0.7 select_reduce_fusion
  21.6 10.3 %sort_tiles.1.tile_hbm = bf16[288,128,128]{2,1,0:T(8,128)(2,1)} custom-call(s32[288]{0:T(512)S(1)} %broadcast_add_fusion.at_ref, bf16[256,128,128]{2,1,0:T(8,128)(2,1)} %bitcast.66), custom_call_target="tpu_custom_call" | custom-call | tf_op jit(solution)/shard_map/sort_tiles/pallas_call | solution.py:140
  32.0 1.2 copy.22
  33.2 1.3 convolution_convert_fusion
  34.6 0.0 copy-start.1
  34.6 0.4 copy.25
  35.0 0.9 copy-done.1
  36.0 4.1 %project.1.in_hbm_ref = bf16[40,128,256]{2,1,0:T(8,128)(2,1)} custom-call(bf16[1024,768]{1,0:T(8,128)(2,1)S(1)} %copy-done.1, bf16[5,768,256]{2,1,0:T(8,128)(2,1)S(1)} %bitcast.57), custom_call_target="tpu_custom_call" | custom-call | tf_op jit(solution)/shard_map/project/pallas_call | solution.py:90
  40.1 0.1 convert_reduce_fusion.2
  40.2 0.5 broadcast_minimum_fusion.dest_ref
  40.7 34.0 %all-to-all-done.ret_ref = bf16[32,264,256]{2,1,0:T(8,128)(2,1)} async-done(((bf16[32,264,256]{2,1,0:T(8,128)(2,1)}), bf16[32,264,256]{2,1,0:T(8,128)(2,1)}, u32[]{:S(2)}, u32[]{:S(2)}) %all-to-all-start) | async-done | bytes 4325408 | tf_op jit(solution)/shard_map/all_to_all | solution.py:536
  74.7 5.1 %select_blocks.1 = bf16[32,256,256]{2,1,0:T(8,128)(2,1)} custom-call(s32[2,32]{1,0:T(2,128)} %bitcast.63, bf16[32,264,256]{2,1,0:T(8,128)(2,1)} %all-to-all-done.ret_ref, bf16[40,128,256]{2,1,0:T(8,128)(2,1)} %project.1.in_hbm_ref), custom_call_target="tpu_custom_call" | custom-call | tf_op jit(solution)/shard_map/select_blocks/pallas_call | solution.py:248
  79.8 0.0 copy-start.7
  79.8 6.8 %all-to-all-start.1 = ((bf16[32,256,256]{2,1,0:T(8,128)(2,1)}), bf16[32,256,256]{2,1,0:T(8,128)(2,1)}, u32[]{:S(2)}, u32[]{:S(2)}) async-start(bf16[32,256,256]{2,1,0:T(8,128)(2,1)} %select_blocks.1), calls=%async_computation.1 | async-start | bytes 8388608 | tf_op jit(solution)/shard_map/all_to_all | solution.py:554
  86.6 0.1 copy.19
  86.7 0.1 reshape.110.coef_ref
  86.8 0.0 copy-start.6
  86.8 6.5 %sum_by_key.1 = bf16[40,128,256]{2,1,0:T(8,128)(2,1)} custom-call(s32[2,32]{1,0:T(2,128)S(1)} %bitcast.64, bf16[32,264,256]{2,1,0:T(8,128)(2,1)} %all-to-all-done.ret_ref), custom_call_target="tpu_custom_call" | custom-call | tf_op jit(solution)/shard_map/sum_by_key/pallas_call | solution.py:293
  93.3 8.5 %weight_grads.1 = (f32[5,768,256]{2,1,0:T(8,128)}, f32[8,128]{1,0:T(8,128)S(1)}) custom-call(f32[20]{0:T(128)S(1)} %reshape.110.coef_ref, bf16[1024,768]{1,0:T(8,128)(2,1)S(1)} %copy-done.2, bf16[5,1024,256]{2,1,0:T(8,128)(2,1)} %bitcast.72, bf16[1024,256]{1,0:T(8,128)(2,1)S(1)} %copy-done.4, bf16[4,768,256]{2,1,0:T(8,128)(2,1)S(1)} %copy-done.6), custom_call_target="tpu_custom_call" | custom-call | flops 2415919104 | bytes 10616832 | tf_op jit(solution)/shard_map/weight_grads/pallas_call | solution.py:341
  101.8 0.2 collective-permute-start
  102.0 1.7 %fusion = bf16[5,4,4,24,256]{4,3,2,1,0:T(8,128)(2,1)S(1)} fusion(f32[5,4,4,2,24,256]{5,4,3,2,1,0:T(8,128)} %bitcast.59, s32[]{:T(128)S(6)} %select_n.49), kind=kLoop, calls=%fused_computation.4 | loop fusion | bytes 1966084 | tf_op jit(solution)/shard_map/convert_element_type | solution.py:580
  103.7 0.4 collective-permute-start.6
  104.1 2.2 %fusion.9 = f32[1024,768,1]{1,0,2:T(8,128)S(1)} fusion(bf16[5,1024,256]{2,1,0:T(8,128)(2,1)S(1)} %bitcast.73, bf16[5,768,256]{2,1,0:T(8,128)(2,1)S(1)} %bitcast.58), kind=kOutput, calls=%fused_computation.38 | convolution fusion | flops 2013265920 | bytes 7733248 | tf_op jit(solution)/shard_map/rno,rco->nc/dot_general | solution.py:558
  106.4 0.0 collective-permute-done
  106.4 1.8 %collective-permute-start.1 = (f32[8,128]{1,0:T(8,128)S(1)}, f32[8,128]{1,0:T(8,128)S(1)}, u32[]{:S(2)}, u32[]{:S(2)}) collective-permute-start(f32[8,128]{1,0:T(8,128)S(1)} %add.90), channel_id=1, source_target_pairs={{0,1},{1,0},{2,3},{3,2},{4,5},{5,4},{6,7},{7,6},{8,9},{9,8},{10,11... | collective-permute-start | bytes 12296 | tf_op jit(solution)/shard_map/ppermute | solution.py:374
  108.1 0.6 bitcast_add_fusion
  108.8 1.5 collective-permute-done.1
  110.2 3.0 %collective-permute-start.2 = (f32[8,128]{1,0:T(8,128)S(1)}, f32[8,128]{1,0:T(8,128)S(1)}, u32[]{:S(2)}, u32[]{:S(2)}) collective-permute-start(f32[8,128]{1,0:T(8,128)S(1)} %add.91), channel_id=1, source_target_pairs={{0,2},{1,3},{2,0},{3,1},{4,6},{5,7},{6,4},{7,5},{8,10},{9,11},{10,... | collective-permute-start | bytes 12296 | tf_op jit(solution)/shard_map/ppermute | solution.py:374
  113.3 0.1 fusion.6
  113.4 2.0 %collective-permute-done.2 = f32[8,128]{1,0:T(8,128)S(1)} collective-permute-done((f32[8,128]{1,0:T(8,128)S(1)}, f32[8,128]{1,0:T(8,128)S(1)}, u32[]{:S(2)}, u32[]{:S(2)}) %collective-permute-start.2) | collective-permute-done | bytes 4128 | tf_op jit(solution)/shard_map/ppermute | solution.py:374
  115.4 2.8 %collective-permute-start.5 = (bf16[256,768]{1,0:T(8,128)(2,1)S(1)}, bf16[256,768]{1,0:T(8,128)(2,1)S(1)}, u32[]{:S(2)}, u32[]{:S(2)}) collective-permute-start(bf16[256,768]{1,0:T(8,128)(2,1)S(1)} %get-tuple-element.41), channel_id=1, source_target_pairs={{0,3},{1,2},{2,1},{3,0},{4,7},{5,6},{6,5},{7,4},{8,11},{9,10},{10,... | collective-permute-start | bytes 1179656 | tf_op jit(solution)/shard_map/ppermute | solution.py:374
  118.1 0.8 collective-permute-start.4
  118.9 0.5 collective-permute-start.3
  119.5 0.1 pad_add_fusion.place_ref
  119.5 1.6 fusion.8
  121.1 0.0 collective-permute-done.6.got_ref
  121.1 0.8 first_stage.1
  121.9 2.3 %collective-permute-start.7 = (bf16[488,256]{1,0:T(8,128)(2,1)S(1)}, bf16[488,256]{1,0:T(8,128)(2,1)S(1)}, u32[]{:S(2)}, u32[]{:S(2)}) collective-permute-start(bf16[488,256]{1,0:T(8,128)(2,1)S(1)} %get-tuple-element.48), channel_id=1, source_target_pairs={{0,8},{4,12},{8,0},{12,4},{16,24},{20,28},{24,16},{28,20},{32,40},... | collective-permute-start | bytes 749576 | tf_op jit(solution)/shard_map/ppermute | solution.py:374
  124.2 0.9 collective-permute-start.8
  125.1 9.6 %collective-permute-done.5 = bf16[256,768]{1,0:T(8,128)(2,1)S(1)} collective-permute-done((bf16[256,768]{1,0:T(8,128)(2,1)S(1)}, bf16[256,768]{1,0:T(8,128)(2,1)S(1)}, u32[]{:S(2)}, u32[]{:S(2)}) %collective-permute-start.5) | collective-permute-done | bytes 393248 | tf_op jit(solution)/shard_map/ppermute | solution.py:374
  134.7 2.2 %collective-permute-start.9 = (bf16[488,256]{1,0:T(8,128)(2,1)S(1)}, bf16[488,256]{1,0:T(8,128)(2,1)S(1)}, u32[]{:S(2)}, u32[]{:S(2)}) collective-permute-start(bf16[488,256]{1,0:T(8,128)(2,1)S(1)} %get-tuple-element.50), channel_id=1, source_target_pairs={{0,40},{4,44},{8,32},{12,36},{16,56},{20,60},{24,48},{28,52},{32,8... | collective-permute-start | bytes 749576 | tf_op jit(solution)/shard_map/ppermute | solution.py:374
  136.9 0.0 collective-permute-done.4
  136.9 0.0 collective-permute-done.3
  136.9 0.9 fusion.3
  137.8 2.0 %all-to-all-done.1 = bf16[32,256,256]{2,1,0:T(8,128)(2,1)} async-done(((bf16[32,256,256]{2,1,0:T(8,128)(2,1)}), bf16[32,256,256]{2,1,0:T(8,128)(2,1)}, u32[]{:S(2)}, u32[]{:S(2)}) %all-to-all-start.1) | async-done | bytes 4194336 | tf_op jit(solution)/shard_map/all_to_all | solution.py:554
  139.9 8.7 %tile_sums.1 = bf16[8,128,256]{2,1,0:T(8,128)(2,1)} custom-call(s32[288]{0:T(512)} %get-tuple-element.32.slot_ref, s32[72]{0:T(128)} %broadcast_minimum_fusion.dest_ref, f32[8,128,256]{2,1,0:T(8,128)} %bitcast.71, bf16[288,128,128]{2,1,0:T(8,128)(2,1)} %sort_tiles.1.tile_hbm, bf16[64,128,256]{2,1,0:T(8,128)(2,1)} %bitcast.9.msg_hbm), custom_call_target="tpu_custom_call" | custom-call | tf_op jit(solution)/shard_map/tile_sums/pallas_call | solution.py:196
  148.5 0.0 collective-permute-done.7.refs_0_
  148.6 0.0 collective-permute-done.8.refs_1_
  148.6 0.0 collective-permute-done.9.refs_2_
  148.6 0.7 second_stage.1
  149.2 4.2 %collective-permute-start.10 = (bf16[128,256]{1,0:T(8,128)(2,1)S(1)}, bf16[128,256]{1,0:T(8,128)(2,1)S(1)}, u32[]{:S(2)}, u32[]{:S(2)}) collective-permute-start(bf16[128,256]{1,0:T(8,128)(2,1)S(1)} %get-tuple-element.53), channel_id=1, source_target_pairs={{0,24},{4,28},{8,16},{12,20},{16,8},{20,12},{24,0},{28,4},{32,56},... | collective-permute-start | bytes 196616 | tf_op jit(solution)/shard_map/ppermute | solution.py:374
  153.5 0.1 collective-permute-start.11
  153.6 2.6 %collective-permute-start.12 = (bf16[128,256]{1,0:T(8,128)(2,1)S(1)}, bf16[128,256]{1,0:T(8,128)(2,1)S(1)}, u32[]{:S(2)}, u32[]{:S(2)}) collective-permute-start(bf16[128,256]{1,0:T(8,128)(2,1)S(1)} %get-tuple-element.55), channel_id=1, source_target_pairs={{0,120},{4,124},{8,112},{12,116},{16,104},{20,108},{24,96},{28,100... | collective-permute-start | bytes 196616 | tf_op jit(solution)/shard_map/ppermute | solution.py:374
  156.3 0.0 collective-permute-done.10.refs_0_
  156.3 2.7 %collective-permute-done.11.refs_1_ = bf16[128,256]{1,0:T(8,128)(2,1)S(1)} collective-permute-done((bf16[128,256]{1,0:T(8,128)(2,1)S(1)}, bf16[128,256]{1,0:T(8,128)(2,1)S(1)}, u32[]{:S(2)}, u32[]{:S(2)}) %collective-permute-start.11) | collective-permute-done | bytes 65568 | tf_op jit(solution)/shard_map/ppermute | solution.py:374
  159.0 2.2 %collective-permute-done.12.refs_2_ = bf16[128,256]{1,0:T(8,128)(2,1)S(1)} collective-permute-done((bf16[128,256]{1,0:T(8,128)(2,1)S(1)}, bf16[128,256]{1,0:T(8,128)(2,1)S(1)}, u32[]{:S(2)}, u32[]{:S(2)}) %collective-permute-start.12) | collective-permute-done | bytes 65568 | tf_op jit(solution)/shard_map/ppermute | solution.py:374
  161.2 0.7 last_stage.1
  (27 shorter events, 0.1 us)
Async XLA Ops:
  0.6 107.5 %copy-start = (bf16[768,256]{1,0:T(8,128)(2,1)S(1)}, bf16[768,256]{1,0:T(8,128)(2,1)}, u32[]{:S(2)}) copy-start(bf16[768,256]{1,0:T(8,128)(2,1)} %param.13) | copy-start | bytes 1179652
  11.7 8.7 %copy-start.9 = (s32[1,256]{1,0:T(1,128)S(1)}, s32[1,256]{1,0:T(1,128)}, u32[]{:S(2)}) copy-start(s32[1,256]{1,0:T(1,128)} %param.17) | copy-start | bytes 3076
  11.7 9.2 %copy-start.10 = (s32[1,256]{1,0:T(1,128)S(1)}, s32[1,256]{1,0:T(1,128)}, u32[]{:S(2)}) copy-start(s32[1,256]{1,0:T(1,128)} %param.16) | copy-start | bytes 3076
  11.7 63.0 %all-to-all-start = ((bf16[32,264,256]{2,1,0:T(8,128)(2,1)}), bf16[32,264,256]{2,1,0:T(8,128)(2,1)}, u32[]{:S(2)}, u32[]{:S(2)}) async-start(bf16[32,264,256]{2,1,0:T(8,128)(2,1)} %tile_grads.1), calls=%async_computation | async-start | bytes 8650752 | tf_op jit(solution)/shard_map/all_to_all | solution.py:536
  21.6 10.3 %copy-start.5 = (bf16[4,768,256]{2,1,0:T(8,128)(2,1)S(1)}, bf16[4,768,256]{2,1,0:T(8,128)(2,1)}, u32[]{:S(2)}) copy-start(bf16[4,768,256]{2,1,0:T(8,128)(2,1)} %base_ref.1) | copy-start | bytes 4718596
  32.0 1.2 copy-start.11
  34.6 1.4 copy-start.1
  79.8 7.0 %copy-start.7 = (s32[1,32,2]{1,2,0:T(2,128)S(1)}, s32[1,32,2]{1,2,0:T(2,128)}, u32[]{:S(2)}) copy-start(s32[1,32,2]{1,2,0:T(2,128)} %param.14) | copy-start | bytes 772
  79.8 60.0 %all-to-all-start.1 = ((bf16[32,256,256]{2,1,0:T(8,128)(2,1)}), bf16[32,256,256]{2,1,0:T(8,128)(2,1)}, u32[]{:S(2)}, u32[]{:S(2)}) async-start(bf16[32,256,256]{2,1,0:T(8,128)(2,1)} %select_blocks.1), calls=%async_computation.1 | async-start | bytes 8388608 | tf_op jit(solution)/shard_map/all_to_all | solution.py:554
  86.8 6.5 %copy-start.2 = (bf16[1024,768]{1,0:T(8,128)(2,1)S(1)}, bf16[1024,768]{1,0:T(8,128)(2,1)}, u32[]{:S(2)}) copy-start(bf16[1024,768]{1,0:T(8,128)(2,1)} %feat_ref.3) | copy-start | bytes 4718596
  86.8 6.5 %copy-start.4 = (bf16[1024,256]{1,0:T(8,128)(2,1)S(1)}, bf16[1024,256]{1,0:T(8,128)(2,1)}, u32[]{:S(2)}) copy-start(bf16[1024,256]{1,0:T(8,128)(2,1)} %grad_ref.1) | copy-start | bytes 1572868
  86.8 6.5 %copy-start.6 = (bf16[4,768,256]{2,1,0:T(8,128)(2,1)S(1)}, bf16[4,768,256]{2,1,0:T(8,128)(2,1)}, u32[]{:S(2)}) copy-start(bf16[4,768,256]{2,1,0:T(8,128)(2,1)} %base_ref.1) | copy-start | bytes 4718596
  93.3 10.8 %copy-start.8 = (bf16[40,128,256]{2,1,0:T(8,128)(2,1)S(1)}, bf16[40,128,256]{2,1,0:T(8,128)(2,1)}, u32[]{:S(2)}) copy-start(bf16[40,128,256]{2,1,0:T(8,128)(2,1)} %sum_by_key.1) | copy-start | bytes 7864324
  101.8 4.5 %collective-permute-start = (f32[8,128]{1,0:T(8,128)S(1)}, f32[8,128]{1,0:T(8,128)S(1)}, u32[]{:S(2)}, u32[]{:S(2)}) collective-permute-start(f32[8,128]{1,0:T(8,128)S(1)} %get-tuple-element.38), channel_id=1, source_target_pairs={{0,4},{4,0},{8,12},{12,8},{16,20},{20,16},{24,28},{28,24},{32,36},... | collective-permute-start | bytes 12296 | tf_op jit(solution)/shard_map/ppermute | solution.py:374
  103.7 17.4 %collective-permute-start.6 = (bf16[5,4,4,24,256]{4,3,2,1,0:T(8,128)(2,1)S(1)}, bf16[5,4,4,24,256]{4,3,2,1,0:T(8,128)(2,1)S(1)}, u32[]{:S(2)}, u32[]{:S(2)}) collective-permute-start(bf16[5,4,4,24,256]{4,3,2,1,0:T(8,128)(2,1)S(1)} %fusion), channel_id=1, source_target_pairs={{0,4},{4,0},{8,12},{12,8},{16,20},{20,16},{24,28},{28,24},{32,36},... | collective-permute-start | bytes 2949128 | tf_op jit(solution)/shard_map/ppermute | solution.py:374
  106.4 3.9 %collective-permute-start.1 = (f32[8,128]{1,0:T(8,128)S(1)}, f32[8,128]{1,0:T(8,128)S(1)}, u32[]{:S(2)}, u32[]{:S(2)}) collective-permute-start(f32[8,128]{1,0:T(8,128)S(1)} %add.90), channel_id=1, source_target_pairs={{0,1},{1,0},{2,3},{3,2},{4,5},{5,4},{6,7},{7,6},{8,9},{9,8},{10,11... | collective-permute-start | bytes 12296 | tf_op jit(solution)/shard_map/ppermute | solution.py:374
  108.8 12.4 %copy-start.3 = (f32[5,768,256]{2,1,0:T(8,128)S(1)}, f32[5,768,256]{2,1,0:T(8,128)}, u32[]{:S(2)}) copy-start(f32[5,768,256]{2,1,0:T(8,128)} %get-tuple-element.42) | copy-start | bytes 11796484
  110.2 5.1 %collective-permute-start.2 = (f32[8,128]{1,0:T(8,128)S(1)}, f32[8,128]{1,0:T(8,128)S(1)}, u32[]{:S(2)}, u32[]{:S(2)}) collective-permute-start(f32[8,128]{1,0:T(8,128)S(1)} %add.91), channel_id=1, source_target_pairs={{0,2},{1,3},{2,0},{3,1},{4,6},{5,7},{6,4},{7,5},{8,10},{9,11},{10,... | collective-permute-start | bytes 12296 | tf_op jit(solution)/shard_map/ppermute | solution.py:374
  115.4 19.4 %collective-permute-start.5 = (bf16[256,768]{1,0:T(8,128)(2,1)S(1)}, bf16[256,768]{1,0:T(8,128)(2,1)S(1)}, u32[]{:S(2)}, u32[]{:S(2)}) collective-permute-start(bf16[256,768]{1,0:T(8,128)(2,1)S(1)} %get-tuple-element.41), channel_id=1, source_target_pairs={{0,3},{1,2},{2,1},{3,0},{4,7},{5,6},{6,5},{7,4},{8,11},{9,10},{10,... | collective-permute-start | bytes 1179656 | tf_op jit(solution)/shard_map/ppermute | solution.py:374
  118.1 18.8 %collective-permute-start.4 = (bf16[256,768]{1,0:T(8,128)(2,1)S(1)}, bf16[256,768]{1,0:T(8,128)(2,1)S(1)}, u32[]{:S(2)}, u32[]{:S(2)}) collective-permute-start(bf16[256,768]{1,0:T(8,128)(2,1)S(1)} %get-tuple-element.40), channel_id=1, source_target_pairs={{0,2},{1,3},{2,0},{3,1},{4,6},{5,7},{6,4},{7,5},{8,10},{9,11},{10,... | collective-permute-start | bytes 1179656 | tf_op jit(solution)/shard_map/ppermute | solution.py:374
  118.9 18.0 %collective-permute-start.3 = (bf16[256,768]{1,0:T(8,128)(2,1)S(1)}, bf16[256,768]{1,0:T(8,128)(2,1)S(1)}, u32[]{:S(2)}, u32[]{:S(2)}) collective-permute-start(bf16[256,768]{1,0:T(8,128)(2,1)S(1)} %get-tuple-element.39), channel_id=1, source_target_pairs={{0,1},{1,0},{2,3},{3,2},{4,5},{5,4},{6,7},{7,6},{8,9},{9,8},{10,11... | collective-permute-start | bytes 1179656 | tf_op jit(solution)/shard_map/ppermute | solution.py:374
  121.9 26.7 %collective-permute-start.7 = (bf16[488,256]{1,0:T(8,128)(2,1)S(1)}, bf16[488,256]{1,0:T(8,128)(2,1)S(1)}, u32[]{:S(2)}, u32[]{:S(2)}) collective-permute-start(bf16[488,256]{1,0:T(8,128)(2,1)S(1)} %get-tuple-element.48), channel_id=1, source_target_pairs={{0,8},{4,12},{8,0},{12,4},{16,24},{20,28},{24,16},{28,20},{32,40},... | collective-permute-start | bytes 749576 | tf_op jit(solution)/shard_map/ppermute | solution.py:374
  124.2 24.4 %collective-permute-start.8 = (bf16[488,256]{1,0:T(8,128)(2,1)S(1)}, bf16[488,256]{1,0:T(8,128)(2,1)S(1)}, u32[]{:S(2)}, u32[]{:S(2)}) collective-permute-start(bf16[488,256]{1,0:T(8,128)(2,1)S(1)} %get-tuple-element.49), channel_id=1, source_target_pairs={{0,32},{4,36},{8,40},{12,44},{16,48},{20,52},{24,56},{28,60},{32,0... | collective-permute-start | bytes 749576 | tf_op jit(solution)/shard_map/ppermute | solution.py:374
  134.7 13.8 %collective-permute-start.9 = (bf16[488,256]{1,0:T(8,128)(2,1)S(1)}, bf16[488,256]{1,0:T(8,128)(2,1)S(1)}, u32[]{:S(2)}, u32[]{:S(2)}) collective-permute-start(bf16[488,256]{1,0:T(8,128)(2,1)S(1)} %get-tuple-element.50), channel_id=1, source_target_pairs={{0,40},{4,44},{8,32},{12,36},{16,56},{20,60},{24,48},{28,52},{32,8... | collective-permute-start | bytes 749576 | tf_op jit(solution)/shard_map/ppermute | solution.py:374
  149.2 7.0 %collective-permute-start.10 = (bf16[128,256]{1,0:T(8,128)(2,1)S(1)}, bf16[128,256]{1,0:T(8,128)(2,1)S(1)}, u32[]{:S(2)}, u32[]{:S(2)}) collective-permute-start(bf16[128,256]{1,0:T(8,128)(2,1)S(1)} %get-tuple-element.53), channel_id=1, source_target_pairs={{0,24},{4,28},{8,16},{12,20},{16,8},{20,12},{24,0},{28,4},{32,56},... | collective-permute-start | bytes 196616 | tf_op jit(solution)/shard_map/ppermute | solution.py:374
  153.5 5.5 %collective-permute-start.11 = (bf16[128,256]{1,0:T(8,128)(2,1)S(1)}, bf16[128,256]{1,0:T(8,128)(2,1)S(1)}, u32[]{:S(2)}, u32[]{:S(2)}) collective-permute-start(bf16[128,256]{1,0:T(8,128)(2,1)S(1)} %get-tuple-element.54), channel_id=1, source_target_pairs={{0,96},{4,100},{8,104},{12,108},{16,112},{20,116},{24,120},{28,124... | collective-permute-start | bytes 196616 | tf_op jit(solution)/shard_map/ppermute | solution.py:374
  153.6 7.6 %collective-permute-start.12 = (bf16[128,256]{1,0:T(8,128)(2,1)S(1)}, bf16[128,256]{1,0:T(8,128)(2,1)S(1)}, u32[]{:S(2)}, u32[]{:S(2)}) collective-permute-start(bf16[128,256]{1,0:T(8,128)(2,1)S(1)} %get-tuple-element.55), channel_id=1, source_target_pairs={{0,120},{4,124},{8,112},{12,116},{16,104},{20,108},{24,96},{28,100... | collective-permute-start | bytes 196616 | tf_op jit(solution)/shard_map/ppermute | solution.py:374

commit v9 on v7

--- a/solution.py
+++ b/solution.py
@@ -222,28 +222,41 @@
 
 def select_blocks(slot_block, returned, blocks, nblocks, capacity):
     shards, _, width = returned.shape
+    relations = blocks.shape[0] // nblocks
 
     def kernel(block_ref, ret_ref, in_hbm_ref, out_ref, rel_ref, in_ref, load_ref, sem_ref):
         rows = pltpu.make_async_copy(
-            ret_ref.at[:, pl.ds(capacity * BLK, 8), :], rel_ref, load_ref.at[0]
+            ret_ref.at[:, pl.ds(capacity * BLK, 8), :], rel_ref, load_ref.at[relations]
         )
         rows.start()
-        load = pltpu.make_async_copy(in_hbm_ref, in_ref, load_ref.at[1])
-        load.start()
+        loads = []
+        for r in range(relations):
+            part = pl.ds(r * nblocks, nblocks)
+            load = pltpu.make_async_copy(in_hbm_ref.at[part], in_ref.at[part], load_ref.at[r])
+            load.start()
+            loads.append(load)
         rows.wait()
         rels = [[relation_of(rel_ref[o], c) for c in range(capacity)] for o in range(shards)]
-        load.wait()
-        copies = []
+
+        def copy(o, c, r):
+            return pltpu.make_async_copy(
+                in_ref.at[r * nblocks + block_ref[c, o]],
+                out_ref.at[o, pl.ds(c * BLK, BLK)],
+                sem_ref.at[o, c],
+            )
+
+        for r in range(relations):
+            loads[r].wait()
+            for o in range(shards):
+                for c in range(capacity):
+
+                    @pl.when(rels[o][c] == r)
+                    def _():
+                        copy(o, c, r).start()
+
         for o in range(shards):
             for c in range(capacity):
-                key = rels[o][c] * nblocks + block_ref[c, o]
-                copy = pltpu.make_async_copy(
-                    in_ref.at[key], out_ref.at[o, pl.ds(c * BLK, BLK)], sem_ref.at[o, c]
-                )
-                copy.start()
-                copies.append(copy)
-        for copy in copies:
-            copy.wait()
+                copy(o, c, 0).wait()
 
     return pl.pallas_call(
         kernel,
@@ -260,7 +273,7 @@
             scratch_shapes=[
                 pltpu.VMEM((shards, 8, width), BF16),
                 pltpu.VMEM(blocks.shape, BF16),
-                pltpu.SemaphoreType.DMA((2,)),
+                pltpu.SemaphoreType.DMA((relations + 1,)),
                 pltpu.SemaphoreType.DMA((shards, capacity)),
             ],
         ),

time: 161 us -> 160 us (level)
  no operation moved by 1% of the time
where the time goes in v9:
time: 160 us
  Pallas kernels  55.8 us (35%)
  waiting for transfers between devices  51.4 us (32%)
  starting transfers between devices  38.5 us (24%)
  matrix products  5.74 us (4%)
  local copies, waits for them, and re-layouts  4.64 us (3%)
  other arithmetic  2.85 us (2%)
    all_to_all x1, waiting for transfers between devices, body(): returned = lax.all_to_all(slot_grads, 'shard', 0, 0, tiled=True)  34 us
    ppermute x13, starting transfers between devices, exchange(): lax.ppermute(x, axis, [(i, i ^ mask) for i in range(lax.axis_size(axis))])  23.1 us
    ppermute x13, waiting for transfers between devices, exchange(): lax.ppermute(x, axis, [(i, i ^ mask) for i in range(lax.axis_size(axis))])  16.8 us
    pallas_call x1, Pallas kernels, tile_grads(): pl.pallas_call(kernel, name='tile_grads', out_shape=pltpu.HBM((shards, ro...  11 us
    pallas_call x1, Pallas kernels, sort_tiles(): pl.pallas_call(kernel, name='sort_tiles', out_shape=pltpu.HBM((places, BL...  10.3 us
    pallas_call x1, Pallas kernels, tile_sums(): pl.pallas_call(kernel, name='tile_sums', out_shape=pltpu.HBM(root_term.sh...  8.68 us
    all_to_all x1, starting transfers between devices, body(): returned = lax.all_to_all(slot_grads, 'shard', 0, 0, tiled=True)  8.66 us
    pallas_call x1, Pallas kernels, weight_grads(): pl.pallas_call(kernel, name='weight_grads', cost_estimate=pl.CostEstimate...  8.54 us
  transfers between devices with their start and end apart: 15, of which 10 were waited for; matrix products, arithmetic and copies ran while one was open for 8% of the time, Pallas kernels for 24%

profile of v9, /device:TPU:0, one launch (start us, length us, event | category | flops | bytes accessed | tf_op | source)
XLA Modules:
  0.0 159.8 jit_solution(9837957518434214764)
XLA Ops:
  0.6 0.0 copy-start
  0.6 11.0 %tile_grads.1 = bf16[32,264,256]{2,1,0:T(8,128)(2,1)} custom-call(s32[256]{0:T(256)} %bitcast.78, s32[256]{0:T(256)} %bitcast.74, s32[2,32]{1,0:T(2,128)} %bitcast.80, bf16[256,128,128]{2,1,0:T(8,128)(2,1)} %bitcast.64, bf16[8,128,256]{2,1,0:T(8,128)(2,1)} %bitcast.60), custom_call_target="tpu_custom_call" | custom-call | tf_op jit(solution)/shard_map/tile_grads/pallas_call | solution.py:63
  11.7 8.7 %all-to-all-start = ((bf16[32,264,256]{2,1,0:T(8,128)(2,1)}), bf16[32,264,256]{2,1,0:T(8,128)(2,1)}, u32[]{:S(2)}, u32[]{:S(2)}) async-start(bf16[32,264,256]{2,1,0:T(8,128)(2,1)} %tile_grads.1), calls=%async_computation | async-start | bytes 8650752 | tf_op jit(solution)/shard_map/all_to_all | solution.py:546
  20.4 0.1 convert_reduce_fusion.1
  20.5 0.1 select_reduce_fusion.3
  20.6 0.1 select_reduce_fusion.2
  20.7 0.2 convert_reduce_fusion
  20.9 0.7 select_reduce_fusion
  21.6 10.3 %sort_tiles.1.tile_hbm = bf16[288,128,128]{2,1,0:T(8,128)(2,1)} custom-call(s32[288]{0:T(512)S(1)} %broadcast_add_fusion.at_ref, bf16[256,128,128]{2,1,0:T(8,128)(2,1)} %bitcast.65), custom_call_target="tpu_custom_call" | custom-call | tf_op jit(solution)/shard_map/sort_tiles/pallas_call | solution.py:140
  32.0 1.2 copy.22
  33.2 1.3 convolution_convert_fusion
  34.6 0.0 copy-start.1
  34.6 0.4 copy.25
  35.0 0.9 copy-done.1
  36.0 4.1 %project.1.in_hbm_ref = bf16[40,128,256]{2,1,0:T(8,128)(2,1)} custom-call(bf16[1024,768]{1,0:T(8,128)(2,1)S(1)} %copy-done.1, bf16[5,768,256]{2,1,0:T(8,128)(2,1)S(1)} %bitcast.56), custom_call_target="tpu_custom_call" | custom-call | tf_op jit(solution)/shard_map/project/pallas_call | solution.py:90
  40.1 0.1 convert_reduce_fusion.2
  40.2 0.5 broadcast_minimum_fusion.dest_ref
  40.7 34.0 %all-to-all-done.ret_ref = bf16[32,264,256]{2,1,0:T(8,128)(2,1)} async-done(((bf16[32,264,256]{2,1,0:T(8,128)(2,1)}), bf16[32,264,256]{2,1,0:T(8,128)(2,1)}, u32[]{:S(2)}, u32[]{:S(2)}) %all-to-all-start) | async-done | bytes 4325408 | tf_op jit(solution)/shard_map/all_to_all | solution.py:546
  74.7 4.5 %select_blocks.1 = bf16[32,256,256]{2,1,0:T(8,128)(2,1)} custom-call(s32[2,32]{1,0:T(2,128)} %bitcast.62, bf16[32,264,256]{2,1,0:T(8,128)(2,1)} %all-to-all-done.ret_ref, bf16[40,128,256]{2,1,0:T(8,128)(2,1)} %project.1.in_hbm_ref), custom_call_target="tpu_custom_call" | custom-call | tf_op jit(solution)/shard_map/select_blocks/pallas_call | solution.py:261
  79.2 0.0 copy-start.7
  79.2 6.7 %all-to-all-start.1 = ((bf16[32,256,256]{2,1,0:T(8,128)(2,1)}), bf16[32,256,256]{2,1,0:T(8,128)(2,1)}, u32[]{:S(2)}, u32[]{:S(2)}) async-start(bf16[32,256,256]{2,1,0:T(8,128)(2,1)} %select_blocks.1), calls=%async_computation.1 | async-start | bytes 8388608 | tf_op jit(solution)/shard_map/all_to_all | solution.py:564
  86.0 0.1 copy.19
  86.1 0.1 reshape.110.coef_ref
  86.2 0.0 copy-start.6
  86.2 6.5 %sum_by_key.1 = bf16[40,128,256]{2,1,0:T(8,128)(2,1)} custom-call(s32[2,32]{1,0:T(2,128)S(1)} %bitcast.63, bf16[32,264,256]{2,1,0:T(8,128)(2,1)} %all-to-all-done.ret_ref), custom_call_target="tpu_custom_call" | custom-call | tf_op jit(solution)/shard_map/sum_by_key/pallas_call | solution.py:306
  92.7 8.5 %weight_grads.1 = (f32[5,768,256]{2,1,0:T(8,128)}, f32[8,128]{1,0:T(8,128)S(1)}) custom-call(f32[20]{0:T(128)S(1)} %reshape.110.coef_ref, bf16[1024,768]{1,0:T(8,128)(2,1)S(1)} %copy-done.2, bf16[5,1024,256]{2,1,0:T(8,128)(2,1)} %bitcast.71, bf16[1024,256]{1,0:T(8,128)(2,1)S(1)} %copy-done.4, bf16[4,768,256]{2,1,0:T(8,128)(2,1)S(1)} %copy-done.6), custom_call_target="tpu_custom_call" | custom-call | flops 2415919104 | bytes 10616832 | tf_op jit(solution)/shard_map/weight_grads/pallas_call | solution.py:354
  101.2 0.2 collective-permute-start
  101.5 1.7 %fusion = bf16[5,4,4,24,256]{4,3,2,1,0:T(8,128)(2,1)S(1)} fusion(f32[5,4,4,2,24,256]{5,4,3,2,1,0:T(8,128)} %bitcast.58, s32[]{:T(128)S(6)} %select_n.49), kind=kLoop, calls=%fused_computation.4 | loop fusion | bytes 1966084 | tf_op jit(solution)/shard_map/convert_element_type | solution.py:588
  103.1 0.6 collective-permute-start.6
  103.7 2.2 %fusion.9 = f32[1024,768,1]{1,0,2:T(8,128)S(1)} fusion(bf16[5,1024,256]{2,1,0:T(8,128)(2,1)S(1)} %bitcast.72, bf16[5,768,256]{2,1,0:T(8,128)(2,1)S(1)} %bitcast.57), kind=kOutput, calls=%fused_computation.38 | convolution fusion | flops 2013265920 | bytes 7733248 | tf_op jit(solution)/shard_map/rno,rco->nc/dot_general | solution.py:568
  105.9 0.0 collective-permute-done
  106.0 1.6 collective-permute-start.1
  107.5 0.6 bitcast_add_fusion
  108.2 1.5 collective-permute-done.1
  109.6 3.0 %collective-permute-start.2 = (f32[8,128]{1,0:T(8,128)S(1)}, f32[8,128]{1,0:T(8,128)S(1)}, u32[]{:S(2)}, u32[]{:S(2)}) collective-permute-start(f32[8,128]{1,0:T(8,128)S(1)} %add.88), channel_id=1, source_target_pairs={{0,2},{1,3},{2,0},{3,1},{4,6},{5,7},{6,4},{7,5},{8,10},{9,11},{10,... | collective-permute-start | bytes 12296 | tf_op jit(solution)/shard_map/ppermute | solution.py:387
  112.7 0.1 fusion.6
  112.8 2.0 %collective-permute-done.2 = f32[8,128]{1,0:T(8,128)S(1)} collective-permute-done((f32[8,128]{1,0:T(8,128)S(1)}, f32[8,128]{1,0:T(8,128)S(1)}, u32[]{:S(2)}, u32[]{:S(2)}) %collective-permute-start.2) | collective-permute-done | bytes 4128 | tf_op jit(solution)/shard_map/ppermute | solution.py:387
  114.8 1.5 collective-permute-start.3
  116.3 2.7 %collective-permute-start.4 = (bf16[256,768]{1,0:T(8,128)(2,1)S(1)}, bf16[256,768]{1,0:T(8,128)(2,1)S(1)}, u32[]{:S(2)}, u32[]{:S(2)}) collective-permute-start(bf16[256,768]{1,0:T(8,128)(2,1)S(1)} %get-tuple-element.40), channel_id=1, source_target_pairs={{0,2},{1,3},{2,0},{3,1},{4,6},{5,7},{6,4},{7,5},{8,10},{9,11},{10,... | collective-permute-start | bytes 1179656 | tf_op jit(solution)/shard_map/ppermute | solution.py:387
  119.0 0.5 collective-permute-start.5
  119.5 0.1 pad_add_fusion.place_ref
  119.5 1.6 fusion.8
  121.1 0.0 collective-permute-done.6.got_ref
  121.1 0.7 first_stage.1
  121.8 1.8 %collective-permute-start.7 = (bf16[488,256]{1,0:T(8,128)(2,1)S(1)}, bf16[488,256]{1,0:T(8,128)(2,1)S(1)}, u32[]{:S(2)}, u32[]{:S(2)}) collective-permute-start(bf16[488,256]{1,0:T(8,128)(2,1)S(1)} %get-tuple-element.48), channel_id=1, source_target_pairs={{0,32},{4,36},{8,40},{12,44},{16,48},{20,52},{24,56},{28,60},{32,0... | collective-permute-start | bytes 749576 | tf_op jit(solution)/shard_map/ppermute | solution.py:387
  123.6 2.7 %collective-permute-start.8 = (bf16[488,256]{1,0:T(8,128)(2,1)S(1)}, bf16[488,256]{1,0:T(8,128)(2,1)S(1)}, u32[]{:S(2)}, u32[]{:S(2)}) collective-permute-start(bf16[488,256]{1,0:T(8,128)(2,1)S(1)} %get-tuple-element.49), channel_id=1, source_target_pairs={{0,64},{4,68},{8,72},{12,76},{16,80},{20,84},{24,88},{28,92},{32,9... | collective-permute-start | bytes 749576 | tf_op jit(solution)/shard_map/ppermute | solution.py:387
  126.3 0.5 collective-permute-done.3
  126.8 3.0 %collective-permute-start.9 = (bf16[488,256]{1,0:T(8,128)(2,1)S(1)}, bf16[488,256]{1,0:T(8,128)(2,1)S(1)}, u32[]{:S(2)}, u32[]{:S(2)}) collective-permute-start(bf16[488,256]{1,0:T(8,128)(2,1)S(1)} %get-tuple-element.50), channel_id=1, source_target_pairs={{0,96},{4,100},{8,104},{12,108},{16,112},{20,116},{24,120},{28,124... | collective-permute-start | bytes 749576 | tf_op jit(solution)/shard_map/ppermute | solution.py:387
  129.8 5.4 %collective-permute-done.4 = bf16[256,768]{1,0:T(8,128)(2,1)S(1)} collective-permute-done((bf16[256,768]{1,0:T(8,128)(2,1)S(1)}, bf16[256,768]{1,0:T(8,128)(2,1)S(1)}, u32[]{:S(2)}, u32[]{:S(2)}) %collective-permute-start.4) | collective-permute-done | bytes 393248 | tf_op jit(solution)/shard_map/ppermute | solution.py:387
  135.2 2.6 %collective-permute-done.5 = bf16[256,768]{1,0:T(8,128)(2,1)S(1)} collective-permute-done((bf16[256,768]{1,0:T(8,128)(2,1)S(1)}, bf16[256,768]{1,0:T(8,128)(2,1)S(1)}, u32[]{:S(2)}, u32[]{:S(2)}) %collective-permute-start.5) | collective-permute-done | bytes 393248 | tf_op jit(solution)/shard_map/ppermute | solution.py:387
  137.8 0.9 fusion.3
  138.7 0.6 all-to-all-done.1
  139.3 8.7 %tile_sums.1 = bf16[8,128,256]{2,1,0:T(8,128)(2,1)} custom-call(s32[288]{0:T(512)} %get-tuple-element.32.slot_ref, s32[72]{0:T(128)} %broadcast_minimum_fusion.dest_ref, f32[8,128,256]{2,1,0:T(8,128)} %bitcast.70, bf16[288,128,128]{2,1,0:T(8,128)(2,1)} %sort_tiles.1.tile_hbm, bf16[64,128,256]{2,1,0:T(8,128)(2,1)} %bitcast.9.msg_hbm), custom_call_target="tpu_custom_call" | custom-call | tf_op jit(solution)/shard_map/tile_sums/pallas_call | solution.py:196
  148.0 0.0 collective-permute-done.7.refs_0_
  148.0 1.4 collective-permute-done.8.refs_1_
  149.4 0.0 collective-permute-done.9.refs_2_
  149.4 0.7 second_stage.1
  150.1 2.8 %collective-permute-start.10 = (bf16[128,256]{1,0:T(8,128)(2,1)S(1)}, bf16[128,256]{1,0:T(8,128)(2,1)S(1)}, u32[]{:S(2)}, u32[]{:S(2)}) collective-permute-start(bf16[128,256]{1,0:T(8,128)(2,1)S(1)} %get-tuple-element.53), channel_id=1, source_target_pairs={{0,8},{4,12},{8,0},{12,4},{16,24},{20,28},{24,16},{28,20},{32,40},... | collective-permute-start | bytes 196616 | tf_op jit(solution)/shard_map/ppermute | solution.py:387
  152.9 0.0 collective-permute-start.11
  152.9 2.8 %collective-permute-start.12 = (bf16[128,256]{1,0:T(8,128)(2,1)S(1)}, bf16[128,256]{1,0:T(8,128)(2,1)S(1)}, u32[]{:S(2)}, u32[]{:S(2)}) collective-permute-start(bf16[128,256]{1,0:T(8,128)(2,1)S(1)} %get-tuple-element.55), channel_id=1, source_target_pairs={{0,24},{4,28},{8,16},{12,20},{16,8},{20,12},{24,0},{28,4},{32,56},... | collective-permute-start | bytes 196616 | tf_op jit(solution)/shard_map/ppermute | solution.py:387
  155.7 0.0 collective-permute-done.10.refs_0_
  155.7 3.1 %collective-permute-done.11.refs_1_ = bf16[128,256]{1,0:T(8,128)(2,1)S(1)} collective-permute-done((bf16[128,256]{1,0:T(8,128)(2,1)S(1)}, bf16[128,256]{1,0:T(8,128)(2,1)S(1)}, u32[]{:S(2)}, u32[]{:S(2)}) %collective-permute-start.11) | collective-permute-done | bytes 65568 | tf_op jit(solution)/shard_map/ppermute | solution.py:387
  158.7 0.4 collective-permute-done.12.refs_2_
  159.1 0.7 last_stage.1
  (27 shorter events, 0.1 us)
Async XLA Ops:
  0.6 106.9 %copy-start = (bf16[768,256]{1,0:T(8,128)(2,1)S(1)}, bf16[768,256]{1,0:T(8,128)(2,1)}, u32[]{:S(2)}) copy-start(bf16[768,256]{1,0:T(8,128)(2,1)} %param.13) | copy-start | bytes 1179652
  11.7 8.7 %copy-start.9 = (s32[1,256]{1,0:T(1,128)S(1)}, s32[1,256]{1,0:T(1,128)}, u32[]{:S(2)}) copy-start(s32[1,256]{1,0:T(1,128)} %param.17) | copy-start | bytes 3076
  11.7 9.2 %copy-start.10 = (s32[1,256]{1,0:T(1,128)S(1)}, s32[1,256]{1,0:T(1,128)}, u32[]{:S(2)}) copy-start(s32[1,256]{1,0:T(1,128)} %param.16) | copy-start | bytes 3076
  11.7 63.0 %all-to-all-start = ((bf16[32,264,256]{2,1,0:T(8,128)(2,1)}), bf16[32,264,256]{2,1,0:T(8,128)(2,1)}, u32[]{:S(2)}, u32[]{:S(2)}) async-start(bf16[32,264,256]{2,1,0:T(8,128)(2,1)} %tile_grads.1), calls=%async_computation | async-start | bytes 8650752 | tf_op jit(solution)/shard_map/all_to_all | solution.py:546
  21.6 10.3 %copy-start.5 = (bf16[4,768,256]{2,1,0:T(8,128)(2,1)S(1)}, bf16[4,768,256]{2,1,0:T(8,128)(2,1)}, u32[]{:S(2)}) copy-start(bf16[4,768,256]{2,1,0:T(8,128)(2,1)} %base_ref.1) | copy-start | bytes 4718596
  32.0 1.2 copy-start.11
  34.6 1.4 copy-start.1
  79.2 6.9 %copy-start.7 = (s32[1,32,2]{1,2,0:T(2,128)S(1)}, s32[1,32,2]{1,2,0:T(2,128)}, u32[]{:S(2)}) copy-start(s32[1,32,2]{1,2,0:T(2,128)} %param.14) | copy-start | bytes 772
  79.2 60.0 %all-to-all-start.1 = ((bf16[32,256,256]{2,1,0:T(8,128)(2,1)}), bf16[32,256,256]{2,1,0:T(8,128)(2,1)}, u32[]{:S(2)}, u32[]{:S(2)}) async-start(bf16[32,256,256]{2,1,0:T(8,128)(2,1)} %select_blocks.1), calls=%async_computation.1 | async-start | bytes 8388608 | tf_op jit(solution)/shard_map/all_to_all | solution.py:564
  86.2 6.5 %copy-start.2 = (bf16[1024,768]{1,0:T(8,128)(2,1)S(1)}, bf16[1024,768]{1,0:T(8,128)(2,1)}, u32[]{:S(2)}) copy-start(bf16[1024,768]{1,0:T(8,128)(2,1)} %feat_ref.3) | copy-start | bytes 4718596
  86.2 6.5 %copy-start.4 = (bf16[1024,256]{1,0:T(8,128)(2,1)S(1)}, bf16[1024,256]{1,0:T(8,128)(2,1)}, u32[]{:S(2)}) copy-start(bf16[1024,256]{1,0:T(8,128)(2,1)} %grad_ref.1) | copy-start | bytes 1572868
  86.2 6.5 %copy-start.6 = (bf16[4,768,256]{2,1,0:T(8,128)(2,1)S(1)}, bf16[4,768,256]{2,1,0:T(8,128)(2,1)}, u32[]{:S(2)}) copy-start(bf16[4,768,256]{2,1,0:T(8,128)(2,1)} %base_ref.1) | copy-start | bytes 4718596
  92.7 11.0 %copy-start.8 = (bf16[40,128,256]{2,1,0:T(8,128)(2,1)S(1)}, bf16[40,128,256]{2,1,0:T(8,128)(2,1)}, u32[]{:S(2)}) copy-start(bf16[40,128,256]{2,1,0:T(8,128)(2,1)} %sum_by_key.1) | copy-start | bytes 7864324
  101.2 4.7 %collective-permute-start = (f32[8,128]{1,0:T(8,128)S(1)}, f32[8,128]{1,0:T(8,128)S(1)}, u32[]{:S(2)}, u32[]{:S(2)}) collective-permute-start(f32[8,128]{1,0:T(8,128)S(1)} %get-tuple-element.38), channel_id=1, source_target_pairs={{0,4},{4,0},{8,12},{12,8},{16,20},{20,16},{24,28},{28,24},{32,36},... | collective-permute-start | bytes 12296 | tf_op jit(solution)/shard_map/ppermute | solution.py:387
  103.1 18.0 %collective-permute-start.6 = (bf16[5,4,4,24,256]{4,3,2,1,0:T(8,128)(2,1)S(1)}, bf16[5,4,4,24,256]{4,3,2,1,0:T(8,128)(2,1)S(1)}, u32[]{:S(2)}, u32[]{:S(2)}) collective-permute-start(bf16[5,4,4,24,256]{4,3,2,1,0:T(8,128)(2,1)S(1)} %fusion), channel_id=1, source_target_pairs={{0,4},{4,0},{8,12},{12,8},{16,20},{20,16},{24,28},{28,24},{32,36},... | collective-permute-start | bytes 2949128 | tf_op jit(solution)/shard_map/ppermute | solution.py:387
  106.0 3.7 %collective-permute-start.1 = (f32[8,128]{1,0:T(8,128)S(1)}, f32[8,128]{1,0:T(8,128)S(1)}, u32[]{:S(2)}, u32[]{:S(2)}) collective-permute-start(f32[8,128]{1,0:T(8,128)S(1)} %add.87), channel_id=1, source_target_pairs={{0,1},{1,0},{2,3},{3,2},{4,5},{5,4},{6,7},{7,6},{8,9},{9,8},{10,11... | collective-permute-start | bytes 12296 | tf_op jit(solution)/shard_map/ppermute | solution.py:387
  108.1 13.0 %copy-start.3 = (f32[5,768,256]{2,1,0:T(8,128)S(1)}, f32[5,768,256]{2,1,0:T(8,128)}, u32[]{:S(2)}) copy-start(f32[5,768,256]{2,1,0:T(8,128)} %get-tuple-element.42) | copy-start | bytes 11796484
  109.6 5.1 %collective-permute-start.2 = (f32[8,128]{1,0:T(8,128)S(1)}, f32[8,128]{1,0:T(8,128)S(1)}, u32[]{:S(2)}, u32[]{:S(2)}) collective-permute-start(f32[8,128]{1,0:T(8,128)S(1)} %add.88), channel_id=1, source_target_pairs={{0,2},{1,3},{2,0},{3,1},{4,6},{5,7},{6,4},{7,5},{8,10},{9,11},{10,... | collective-permute-start | bytes 12296 | tf_op jit(solution)/shard_map/ppermute | solution.py:387
  114.8 12.1 %collective-permute-start.3 = (bf16[256,768]{1,0:T(8,128)(2,1)S(1)}, bf16[256,768]{1,0:T(8,128)(2,1)S(1)}, u32[]{:S(2)}, u32[]{:S(2)}) collective-permute-start(bf16[256,768]{1,0:T(8,128)(2,1)S(1)} %get-tuple-element.39), channel_id=1, source_target_pairs={{0,1},{1,0},{2,3},{3,2},{4,5},{5,4},{6,7},{7,6},{8,9},{9,8},{10,11... | collective-permute-start | bytes 1179656 | tf_op jit(solution)/shard_map/ppermute | solution.py:387
  116.3 18.9 %collective-permute-start.4 = (bf16[256,768]{1,0:T(8,128)(2,1)S(1)}, bf16[256,768]{1,0:T(8,128)(2,1)S(1)}, u32[]{:S(2)}, u32[]{:S(2)}) collective-permute-start(bf16[256,768]{1,0:T(8,128)(2,1)S(1)} %get-tuple-element.40), channel_id=1, source_target_pairs={{0,2},{1,3},{2,0},{3,1},{4,6},{5,7},{6,4},{7,5},{8,10},{9,11},{10,... | collective-permute-start | bytes 1179656 | tf_op jit(solution)/shard_map/ppermute | solution.py:387
  119.0 18.8 %collective-permute-start.5 = (bf16[256,768]{1,0:T(8,128)(2,1)S(1)}, bf16[256,768]{1,0:T(8,128)(2,1)S(1)}, u32[]{:S(2)}, u32[]{:S(2)}) collective-permute-start(bf16[256,768]{1,0:T(8,128)(2,1)S(1)} %get-tuple-element.41), channel_id=1, source_target_pairs={{0,3},{1,2},{2,1},{3,0},{4,7},{5,6},{6,5},{7,4},{8,11},{9,10},{10,... | collective-permute-start | bytes 1179656 | tf_op jit(solution)/shard_map/ppermute | solution.py:387
  121.8 26.1 %collective-permute-start.7 = (bf16[488,256]{1,0:T(8,128)(2,1)S(1)}, bf16[488,256]{1,0:T(8,128)(2,1)S(1)}, u32[]{:S(2)}, u32[]{:S(2)}) collective-permute-start(bf16[488,256]{1,0:T(8,128)(2,1)S(1)} %get-tuple-element.48), channel_id=1, source_target_pairs={{0,32},{4,36},{8,40},{12,44},{16,48},{20,52},{24,56},{28,60},{32,0... | collective-permute-start | bytes 749576 | tf_op jit(solution)/shard_map/ppermute | solution.py:387
  123.6 25.8 %collective-permute-start.8 = (bf16[488,256]{1,0:T(8,128)(2,1)S(1)}, bf16[488,256]{1,0:T(8,128)(2,1)S(1)}, u32[]{:S(2)}, u32[]{:S(2)}) collective-permute-start(bf16[488,256]{1,0:T(8,128)(2,1)S(1)} %get-tuple-element.49), channel_id=1, source_target_pairs={{0,64},{4,68},{8,72},{12,76},{16,80},{20,84},{24,88},{28,92},{32,9... | collective-permute-start | bytes 749576 | tf_op jit(solution)/shard_map/ppermute | solution.py:387
  126.8 22.6 %collective-permute-start.9 = (bf16[488,256]{1,0:T(8,128)(2,1)S(1)}, bf16[488,256]{1,0:T(8,128)(2,1)S(1)}, u32[]{:S(2)}, u32[]{:S(2)}) collective-permute-start(bf16[488,256]{1,0:T(8,128)(2,1)S(1)} %get-tuple-element.50), channel_id=1, source_target_pairs={{0,96},{4,100},{8,104},{12,108},{16,112},{20,116},{24,120},{28,124... | collective-permute-start | bytes 749576 | tf_op jit(solution)/shard_map/ppermute | solution.py:387
  150.1 5.6 %collective-permute-start.10 = (bf16[128,256]{1,0:T(8,128)(2,1)S(1)}, bf16[128,256]{1,0:T(8,128)(2,1)S(1)}, u32[]{:S(2)}, u32[]{:S(2)}) collective-permute-start(bf16[128,256]{1,0:T(8,128)(2,1)S(1)} %get-tuple-element.53), channel_id=1, source_target_pairs={{0,8},{4,12},{8,0},{12,4},{16,24},{20,28},{24,16},{28,20},{32,40},... | collective-permute-start | bytes 196616 | tf_op jit(solution)/shard_map/ppermute | solution.py:387
  152.9 5.8 %collective-permute-start.11 = (bf16[128,256]{1,0:T(8,128)(2,1)S(1)}, bf16[128,256]{1,0:T(8,128)(2,1)S(1)}, u32[]{:S(2)}, u32[]{:S(2)}) collective-permute-start(bf16[128,256]{1,0:T(8,128)(2,1)S(1)} %get-tuple-element.54), channel_id=1, source_target_pairs={{0,16},{4,20},{8,24},{12,28},{16,0},{20,4},{24,8},{28,12},{32,48},... | collective-permute-start | bytes 196616 | tf_op jit(solution)/shard_map/ppermute | solution.py:387
  152.9 6.2 %collective-permute-start.12 = (bf16[128,256]{1,0:T(8,128)(2,1)S(1)}, bf16[128,256]{1,0:T(8,128)(2,1)S(1)}, u32[]{:S(2)}, u32[]{:S(2)}) collective-permute-start(bf16[128,256]{1,0:T(8,128)(2,1)S(1)} %get-tuple-element.55), channel_id=1, source_target_pairs={{0,24},{4,28},{8,16},{12,20},{16,8},{20,12},{24,0},{28,4},{32,56},... | collective-permute-start | bytes 196616 | tf_op jit(solution)/shard_map/ppermute | solution.py:387

commit v10 on v9

--- a/solution.py
+++ b/solution.py
@@ -402,7 +402,7 @@
 
 
 def first_stage(place, stacked, got, dots, size):
-    parts, _, rest, _, rows, width = stacked.shape
+    parts, rest, _, _, rows, width = stacked.shape
     length = parts * rest * rows
 
     def kernel(place_ref, own_ref, got_ref, dots_ref, keep_ref, *send_refs):
@@ -412,7 +412,7 @@
         for k in range(size):
             for p in range(parts):
                 for q in range(rest):
-                    value = own_ref[p, at ^ k, q, core] + got_ref[p, at ^ k, q].astype(F32)
+                    value = own_ref[p, q, at ^ k, core] + got_ref[p, q, at ^ k].astype(F32)
                     if k == 0:
                         keep_ref[p, q] = value
                     else:
@@ -584,10 +584,10 @@
 
     rows = width_in // shards
     stacked = stacked.reshape(nbase + 1, 4, 4, 2, rows, width)
-    place = jnp.stack([me & 1, (me >> 3) & 3, (me >> 1) & 3]).astype(jnp.int32)
+    place = jnp.stack([me & 1, (me >> 1) & 3, (me >> 3) & 3]).astype(jnp.int32)
     got = exchange(chunk_of(stacked, (me & 1) ^ 1, 3).astype(BF16), "shard", 1)
     kept, *sends = first_stage(place, stacked, got, dots, 4)
-    got = [exchange(x, "shard", k << 3) for k, x in zip((1, 2, 3), sends)]
+    got = [exchange(x, "shard", k << 1) for k, x in zip((1, 2, 3), sends)]
     output = tile_sums(
         slot_at,
         dest_of,
@@ -597,7 +597,7 @@
     ).reshape(nblocks * BLK, width)
     output, grad_feats, kept = lax.optimization_barrier((output, grad_feats, kept))
     kept, dots, *sends = second_stage(place, kept, dots, got, 4)
-    got = [exchange(x, "shard", k << 1) for k, x in zip((1, 2, 3), sends)]
+    got = [exchange(x, "shard", k << 3) for k, x in zip((1, 2, 3), sends)]
     grad_bases, grad_root, grad_coef = last_stage(kept, dots, got, relations)
     return (output, grad_feats, grad_bases, grad_root, grad_coef.T)
 

time: 160 us -> 159 us (level)
  transfers between devices with their start and end apart: 15 -> 15, of which waited for: 10 -> 9; matrix products, arithmetic and copies ran while one was open for 8% -> 8% of each run, Pallas kernels for 24% -> 25%
where the time goes in v10:
time: 159 us
  Pallas kernels  55.8 us (35%)
  waiting for transfers between devices  51.1 us (32%)
  starting transfers between devices  37.7 us (24%)
  matrix products  5.74 us (4%)
  local copies, waits for them, and re-layouts  4.64 us (3%)
  other arithmetic  2.85 us (2%)
    all_to_all x1, waiting for transfers between devices, body(): returned = lax.all_to_all(slot_grads, 'shard', 0, 0, tiled=True)  34 us
    ppermute x13, starting transfers between devices, exchange(): lax.ppermute(x, axis, [(i, i ^ mask) for i in range(lax.axis_size(axis))])  22.3 us
    ppermute x13, waiting for transfers between devices, exchange(): lax.ppermute(x, axis, [(i, i ^ mask) for i in range(lax.axis_size(axis))])  17 us
    pallas_call x1, Pallas kernels, tile_grads(): pl.pallas_call(kernel, name='tile_grads', out_shape=pltpu.HBM((shards, ro...  11 us
    pallas_call x1, Pallas kernels, sort_tiles(): pl.pallas_call(kernel, name='sort_tiles', out_shape=pltpu.HBM((places, BL...  10.3 us
    pallas_call x1, Pallas kernels, tile_sums(): pl.pallas_call(kernel, name='tile_sums', out_shape=pltpu.HBM(root_term.sh...  8.69 us
    all_to_all x1, starting transfers between devices, body(): returned = lax.all_to_all(slot_grads, 'shard', 0, 0, tiled=True)  8.66 us
    pallas_call x1, Pallas kernels, weight_grads(): pl.pallas_call(kernel, name='weight_grads', cost_estimate=pl.CostEstimate...  8.53 us
  transfers between devices with their start and end apart: 15, of which 9 were waited for; matrix products, arithmetic and copies ran while one was open for 8% of the time, Pallas kernels for 25%

profile of v10, /device:TPU:0, one launch (start us, length us, event | category | flops | bytes accessed | tf_op | source)
XLA Modules:
  0.0 158.7 jit_solution(15271384692056189898)
XLA Ops:
  0.6 0.0 copy-start
  0.6 11.0 %tile_grads.1 = bf16[32,264,256]{2,1,0:T(8,128)(2,1)} custom-call(s32[256]{0:T(256)} %bitcast.78, s32[256]{0:T(256)} %bitcast.74, s32[2,32]{1,0:T(2,128)} %bitcast.80, bf16[256,128,128]{2,1,0:T(8,128)(2,1)} %bitcast.64, bf16[8,128,256]{2,1,0:T(8,128)(2,1)} %bitcast.60), custom_call_target="tpu_custom_call" | custom-call | tf_op jit(solution)/shard_map/tile_grads/pallas_call | solution.py:63
  11.7 8.7 %all-to-all-start = ((bf16[32,264,256]{2,1,0:T(8,128)(2,1)}), bf16[32,264,256]{2,1,0:T(8,128)(2,1)}, u32[]{:S(2)}, u32[]{:S(2)}) async-start(bf16[32,264,256]{2,1,0:T(8,128)(2,1)} %tile_grads.1), calls=%async_computation | async-start | bytes 8650752 | tf_op jit(solution)/shard_map/all_to_all | solution.py:546
  20.4 0.1 convert_reduce_fusion.1
  20.5 0.1 select_reduce_fusion.3
  20.6 0.1 select_reduce_fusion.2
  20.7 0.2 convert_reduce_fusion
  20.9 0.7 select_reduce_fusion
  21.6 10.3 %sort_tiles.1.tile_hbm = bf16[288,128,128]{2,1,0:T(8,128)(2,1)} custom-call(s32[288]{0:T(512)S(1)} %broadcast_add_fusion.at_ref, bf16[256,128,128]{2,1,0:T(8,128)(2,1)} %bitcast.65), custom_call_target="tpu_custom_call" | custom-call | tf_op jit(solution)/shard_map/sort_tiles/pallas_call | solution.py:140
  32.0 1.2 copy.22
  33.2 1.3 convolution_convert_fusion
  34.6 0.0 copy-start.1
  34.6 0.4 copy.25
  35.0 0.9 copy-done.1
  36.0 4.1 %project.1.in_hbm_ref = bf16[40,128,256]{2,1,0:T(8,128)(2,1)} custom-call(bf16[1024,768]{1,0:T(8,128)(2,1)S(1)} %copy-done.1, bf16[5,768,256]{2,1,0:T(8,128)(2,1)S(1)} %bitcast.56), custom_call_target="tpu_custom_call" | custom-call | tf_op jit(solution)/shard_map/project/pallas_call | solution.py:90
  40.1 0.1 convert_reduce_fusion.2
  40.2 0.5 broadcast_minimum_fusion.dest_ref
  40.7 34.0 %all-to-all-done.ret_ref = bf16[32,264,256]{2,1,0:T(8,128)(2,1)} async-done(((bf16[32,264,256]{2,1,0:T(8,128)(2,1)}), bf16[32,264,256]{2,1,0:T(8,128)(2,1)}, u32[]{:S(2)}, u32[]{:S(2)}) %all-to-all-start) | async-done | bytes 4325408 | tf_op jit(solution)/shard_map/all_to_all | solution.py:546
  74.7 4.5 %select_blocks.1 = bf16[32,256,256]{2,1,0:T(8,128)(2,1)} custom-call(s32[2,32]{1,0:T(2,128)} %bitcast.62, bf16[32,264,256]{2,1,0:T(8,128)(2,1)} %all-to-all-done.ret_ref, bf16[40,128,256]{2,1,0:T(8,128)(2,1)} %project.1.in_hbm_ref), custom_call_target="tpu_custom_call" | custom-call | tf_op jit(solution)/shard_map/select_blocks/pallas_call | solution.py:261
  79.2 0.0 copy-start.7
  79.2 6.7 %all-to-all-start.1 = ((bf16[32,256,256]{2,1,0:T(8,128)(2,1)}), bf16[32,256,256]{2,1,0:T(8,128)(2,1)}, u32[]{:S(2)}, u32[]{:S(2)}) async-start(bf16[32,256,256]{2,1,0:T(8,128)(2,1)} %select_blocks.1), calls=%async_computation.1 | async-start | bytes 8388608 | tf_op jit(solution)/shard_map/all_to_all | solution.py:564
  85.9 0.1 copy.19
  86.0 0.1 reshape.110.coef_ref
  86.1 0.0 copy-start.6
  86.1 6.5 %sum_by_key.1 = bf16[40,128,256]{2,1,0:T(8,128)(2,1)} custom-call(s32[2,32]{1,0:T(2,128)S(1)} %bitcast.63, bf16[32,264,256]{2,1,0:T(8,128)(2,1)} %all-to-all-done.ret_ref), custom_call_target="tpu_custom_call" | custom-call | tf_op jit(solution)/shard_map/sum_by_key/pallas_call | solution.py:306
  92.7 8.5 %weight_grads.1 = (f32[5,768,256]{2,1,0:T(8,128)}, f32[8,128]{1,0:T(8,128)S(1)}) custom-call(f32[20]{0:T(128)S(1)} %reshape.110.coef_ref, bf16[1024,768]{1,0:T(8,128)(2,1)S(1)} %copy-done.2, bf16[5,1024,256]{2,1,0:T(8,128)(2,1)} %bitcast.71, bf16[1024,256]{1,0:T(8,128)(2,1)S(1)} %copy-done.4, bf16[4,768,256]{2,1,0:T(8,128)(2,1)S(1)} %copy-done.6), custom_call_target="tpu_custom_call" | custom-call | flops 2415919104 | bytes 10616832 | tf_op jit(solution)/shard_map/weight_grads/pallas_call | solution.py:354
  101.2 0.2 collective-permute-start
  101.4 1.7 %fusion = bf16[5,4,4,24,256]{4,3,2,1,0:T(8,128)(2,1)S(1)} fusion(f32[5,4,4,2,24,256]{5,4,3,2,1,0:T(8,128)} %bitcast.58, s32[]{:T(128)S(6)} %select_n.49), kind=kLoop, calls=%fused_computation.4 | loop fusion | bytes 1966084 | tf_op jit(solution)/shard_map/convert_element_type | solution.py:588
  103.1 0.6 collective-permute-start.6
  103.7 2.2 %fusion.9 = f32[1024,768,1]{1,0,2:T(8,128)S(1)} fusion(bf16[5,1024,256]{2,1,0:T(8,128)(2,1)S(1)} %bitcast.72, bf16[5,768,256]{2,1,0:T(8,128)(2,1)S(1)} %bitcast.57), kind=kOutput, calls=%fused_computation.38 | convolution fusion | flops 2013265920 | bytes 7733248 | tf_op jit(solution)/shard_map/rno,rco->nc/dot_general | solution.py:568
  105.9 0.0 collective-permute-done
  105.9 1.6 collective-permute-start.1
  107.5 0.6 bitcast_add_fusion
  108.1 1.5 collective-permute-done.1
  109.6 3.0 %collective-permute-start.2 = (f32[8,128]{1,0:T(8,128)S(1)}, f32[8,128]{1,0:T(8,128)S(1)}, u32[]{:S(2)}, u32[]{:S(2)}) collective-permute-start(f32[8,128]{1,0:T(8,128)S(1)} %add.88), channel_id=1, source_target_pairs={{0,2},{1,3},{2,0},{3,1},{4,6},{5,7},{6,4},{7,5},{8,10},{9,11},{10,... | collective-permute-start | bytes 12296 | tf_op jit(solution)/shard_map/ppermute | solution.py:387
  112.6 0.1 fusion.6
  112.8 2.0 %collective-permute-done.2 = f32[8,128]{1,0:T(8,128)S(1)} collective-permute-done((f32[8,128]{1,0:T(8,128)S(1)}, f32[8,128]{1,0:T(8,128)S(1)}, u32[]{:S(2)}, u32[]{:S(2)}) %collective-permute-start.2) | collective-permute-done | bytes 4128 | tf_op jit(solution)/shard_map/ppermute | solution.py:387
  114.7 1.5 collective-permute-start.3
  116.2 2.7 %collective-permute-start.4 = (bf16[256,768]{1,0:T(8,128)(2,1)S(1)}, bf16[256,768]{1,0:T(8,128)(2,1)S(1)}, u32[]{:S(2)}, u32[]{:S(2)}) collective-permute-start(bf16[256,768]{1,0:T(8,128)(2,1)S(1)} %get-tuple-element.40), channel_id=1, source_target_pairs={{0,2},{1,3},{2,0},{3,1},{4,6},{5,7},{6,4},{7,5},{8,10},{9,11},{10,... | collective-permute-start | bytes 1179656 | tf_op jit(solution)/shard_map/ppermute | solution.py:387
  118.9 0.5 collective-permute-start.5
  119.4 0.1 pad_add_fusion.place_ref
  119.5 1.6 fusion.8
  121.1 0.0 collective-permute-done.6.got_ref
  121.1 0.7 first_stage.1
  121.8 2.4 %collective-permute-start.7 = (bf16[488,256]{1,0:T(8,128)(2,1)S(1)}, bf16[488,256]{1,0:T(8,128)(2,1)S(1)}, u32[]{:S(2)}, u32[]{:S(2)}) collective-permute-start(bf16[488,256]{1,0:T(8,128)(2,1)S(1)} %get-tuple-element.48), channel_id=1, source_target_pairs={{0,8},{4,12},{8,0},{12,4},{16,24},{20,28},{24,16},{28,20},{32,40},... | collective-permute-start | bytes 749576 | tf_op jit(solution)/shard_map/ppermute | solution.py:387
  124.2 2.1 %collective-permute-start.8 = (bf16[488,256]{1,0:T(8,128)(2,1)S(1)}, bf16[488,256]{1,0:T(8,128)(2,1)S(1)}, u32[]{:S(2)}, u32[]{:S(2)}) collective-permute-start(bf16[488,256]{1,0:T(8,128)(2,1)S(1)} %get-tuple-element.49), channel_id=1, source_target_pairs={{0,16},{4,20},{8,24},{12,28},{16,0},{20,4},{24,8},{28,12},{32,48},... | collective-permute-start | bytes 749576 | tf_op jit(solution)/shard_map/ppermute | solution.py:387
  126.3 0.5 collective-permute-done.3
  126.8 2.9 %collective-permute-start.9 = (bf16[488,256]{1,0:T(8,128)(2,1)S(1)}, bf16[488,256]{1,0:T(8,128)(2,1)S(1)}, u32[]{:S(2)}, u32[]{:S(2)}) collective-permute-start(bf16[488,256]{1,0:T(8,128)(2,1)S(1)} %get-tuple-element.50), channel_id=1, source_target_pairs={{0,24},{4,28},{8,16},{12,20},{16,8},{20,12},{24,0},{28,4},{32,56},... | collective-permute-start | bytes 749576 | tf_op jit(solution)/shard_map/ppermute | solution.py:387
  129.7 5.5 %collective-permute-done.4 = bf16[256,768]{1,0:T(8,128)(2,1)S(1)} collective-permute-done((bf16[256,768]{1,0:T(8,128)(2,1)S(1)}, bf16[256,768]{1,0:T(8,128)(2,1)S(1)}, u32[]{:S(2)}, u32[]{:S(2)}) %collective-permute-start.4) | collective-permute-done | bytes 393248 | tf_op jit(solution)/shard_map/ppermute | solution.py:387
  135.2 2.6 %collective-permute-done.5 = bf16[256,768]{1,0:T(8,128)(2,1)S(1)} collective-permute-done((bf16[256,768]{1,0:T(8,128)(2,1)S(1)}, bf16[256,768]{1,0:T(8,128)(2,1)S(1)}, u32[]{:S(2)}, u32[]{:S(2)}) %collective-permute-start.5) | collective-permute-done | bytes 393248 | tf_op jit(solution)/shard_map/ppermute | solution.py:387
  137.7 0.9 fusion.3
  138.7 0.1 all-to-all-done.1
  138.8 8.7 %tile_sums.1 = bf16[8,128,256]{2,1,0:T(8,128)(2,1)} custom-call(s32[288]{0:T(512)} %get-tuple-element.32.slot_ref, s32[72]{0:T(128)} %broadcast_minimum_fusion.dest_ref, f32[8,128,256]{2,1,0:T(8,128)} %bitcast.70, bf16[288,128,128]{2,1,0:T(8,128)(2,1)} %sort_tiles.1.tile_hbm, bf16[64,128,256]{2,1,0:T(8,128)(2,1)} %bitcast.9.msg_hbm), custom_call_target="tpu_custom_call" | custom-call | tf_op jit(solution)/shard_map/tile_sums/pallas_call | solution.py:196
  147.5 0.0 collective-permute-done.7.refs_0_
  147.5 0.0 collective-permute-done.8.refs_1_
  147.5 0.0 collective-permute-done.9.refs_2_
  147.5 0.7 second_stage.1
  148.2 1.6 %collective-permute-start.10 = (bf16[128,256]{1,0:T(8,128)(2,1)S(1)}, bf16[128,256]{1,0:T(8,128)(2,1)S(1)}, u32[]{:S(2)}, u32[]{:S(2)}) collective-permute-start(bf16[128,256]{1,0:T(8,128)(2,1)S(1)} %get-tuple-element.53), channel_id=1, source_target_pairs={{0,32},{4,36},{8,40},{12,44},{16,48},{20,52},{24,56},{28,60},{32,0... | collective-permute-start | bytes 196616 | tf_op jit(solution)/shard_map/ppermute | solution.py:387
  149.8 2.7 %collective-permute-start.11 = (bf16[128,256]{1,0:T(8,128)(2,1)S(1)}, bf16[128,256]{1,0:T(8,128)(2,1)S(1)}, u32[]{:S(2)}, u32[]{:S(2)}) collective-permute-start(bf16[128,256]{1,0:T(8,128)(2,1)S(1)} %get-tuple-element.54), channel_id=1, source_target_pairs={{0,64},{4,68},{8,72},{12,76},{16,80},{20,84},{24,88},{28,92},{32,9... | collective-permute-start | bytes 196616 | tf_op jit(solution)/shard_map/ppermute | solution.py:387
  152.5 0.4 collective-permute-start.12
  153.0 0.0 collective-permute-done.10.refs_0_
  153.0 2.7 %collective-permute-done.11.refs_1_ = bf16[128,256]{1,0:T(8,128)(2,1)S(1)} collective-permute-done((bf16[128,256]{1,0:T(8,128)(2,1)S(1)}, bf16[128,256]{1,0:T(8,128)(2,1)S(1)}, u32[]{:S(2)}, u32[]{:S(2)}) %collective-permute-start.11) | collective-permute-done | bytes 65568 | tf_op jit(solution)/shard_map/ppermute | solution.py:387
  155.7 2.3 %collective-permute-done.12.refs_2_ = bf16[128,256]{1,0:T(8,128)(2,1)S(1)} collective-permute-done((bf16[128,256]{1,0:T(8,128)(2,1)S(1)}, bf16[128,256]{1,0:T(8,128)(2,1)S(1)}, u32[]{:S(2)}, u32[]{:S(2)}) %collective-permute-start.12) | collective-permute-done | bytes 65568 | tf_op jit(solution)/shard_map/ppermute | solution.py:387
  158.0 0.7 last_stage.1
  (27 shorter events, 0.1 us)
Async XLA Ops:
  0.6 106.9 %copy-start = (bf16[768,256]{1,0:T(8,128)(2,1)S(1)}, bf16[768,256]{1,0:T(8,128)(2,1)}, u32[]{:S(2)}) copy-start(bf16[768,256]{1,0:T(8,128)(2,1)} %param.13) | copy-start | bytes 1179652
  11.7 8.7 %copy-start.9 = (s32[1,256]{1,0:T(1,128)S(1)}, s32[1,256]{1,0:T(1,128)}, u32[]{:S(2)}) copy-start(s32[1,256]{1,0:T(1,128)} %param.17) | copy-start | bytes 3076
  11.7 9.2 %copy-start.10 = (s32[1,256]{1,0:T(1,128)S(1)}, s32[1,256]{1,0:T(1,128)}, u32[]{:S(2)}) copy-start(s32[1,256]{1,0:T(1,128)} %param.16) | copy-start | bytes 3076
  11.7 63.0 %all-to-all-start = ((bf16[32,264,256]{2,1,0:T(8,128)(2,1)}), bf16[32,264,256]{2,1,0:T(8,128)(2,1)}, u32[]{:S(2)}, u32[]{:S(2)}) async-start(bf16[32,264,256]{2,1,0:T(8,128)(2,1)} %tile_grads.1), calls=%async_computation | async-start | bytes 8650752 | tf_op jit(solution)/shard_map/all_to_all | solution.py:546
  21.6 10.3 %copy-start.5 = (bf16[4,768,256]{2,1,0:T(8,128)(2,1)S(1)}, bf16[4,768,256]{2,1,0:T(8,128)(2,1)}, u32[]{:S(2)}) copy-start(bf16[4,768,256]{2,1,0:T(8,128)(2,1)} %base_ref.1) | copy-start | bytes 4718596
  32.0 1.2 copy-start.11
  34.6 1.4 copy-start.1
  79.2 7.0 %copy-start.7 = (s32[1,32,2]{1,2,0:T(2,128)S(1)}, s32[1,32,2]{1,2,0:T(2,128)}, u32[]{:S(2)}) copy-start(s32[1,32,2]{1,2,0:T(2,128)} %param.14) | copy-start | bytes 772
  79.2 59.6 %all-to-all-start.1 = ((bf16[32,256,256]{2,1,0:T(8,128)(2,1)}), bf16[32,256,256]{2,1,0:T(8,128)(2,1)}, u32[]{:S(2)}, u32[]{:S(2)}) async-start(bf16[32,256,256]{2,1,0:T(8,128)(2,1)} %select_blocks.1), calls=%async_computation.1 | async-start | bytes 8388608 | tf_op jit(solution)/shard_map/all_to_all | solution.py:564
  86.1 6.5 %copy-start.2 = (bf16[1024,768]{1,0:T(8,128)(2,1)S(1)}, bf16[1024,768]{1,0:T(8,128)(2,1)}, u32[]{:S(2)}) copy-start(bf16[1024,768]{1,0:T(8,128)(2,1)} %feat_ref.3) | copy-start | bytes 4718596
  86.1 6.5 %copy-start.4 = (bf16[1024,256]{1,0:T(8,128)(2,1)S(1)}, bf16[1024,256]{1,0:T(8,128)(2,1)}, u32[]{:S(2)}) copy-start(bf16[1024,256]{1,0:T(8,128)(2,1)} %grad_ref.1) | copy-start | bytes 1572868
  86.1 6.5 %copy-start.6 = (bf16[4,768,256]{2,1,0:T(8,128)(2,1)S(1)}, bf16[4,768,256]{2,1,0:T(8,128)(2,1)}, u32[]{:S(2)}) copy-start(bf16[4,768,256]{2,1,0:T(8,128)(2,1)} %base_ref.1) | copy-start | bytes 4718596
  92.7 11.0 %copy-start.8 = (bf16[40,128,256]{2,1,0:T(8,128)(2,1)S(1)}, bf16[40,128,256]{2,1,0:T(8,128)(2,1)}, u32[]{:S(2)}) copy-start(bf16[40,128,256]{2,1,0:T(8,128)(2,1)} %sum_by_key.1) | copy-start | bytes 7864324
  101.2 4.7 %collective-permute-start = (f32[8,128]{1,0:T(8,128)S(1)}, f32[8,128]{1,0:T(8,128)S(1)}, u32[]{:S(2)}, u32[]{:S(2)}) collective-permute-start(f32[8,128]{1,0:T(8,128)S(1)} %get-tuple-element.38), channel_id=1, source_target_pairs={{0,4},{4,0},{8,12},{12,8},{16,20},{20,16},{24,28},{28,24},{32,36},... | collective-permute-start | bytes 12296 | tf_op jit(solution)/shard_map/ppermute | solution.py:387
  103.1 18.0 %collective-permute-start.6 = (bf16[5,4,4,24,256]{4,3,2,1,0:T(8,128)(2,1)S(1)}, bf16[5,4,4,24,256]{4,3,2,1,0:T(8,128)(2,1)S(1)}, u32[]{:S(2)}, u32[]{:S(2)}) collective-permute-start(bf16[5,4,4,24,256]{4,3,2,1,0:T(8,128)(2,1)S(1)} %fusion), channel_id=1, source_target_pairs={{0,4},{4,0},{8,12},{12,8},{16,20},{20,16},{24,28},{28,24},{32,36},... | collective-permute-start | bytes 2949128 | tf_op jit(solution)/shard_map/ppermute | solution.py:387
  105.9 3.7 %collective-permute-start.1 = (f32[8,128]{1,0:T(8,128)S(1)}, f32[8,128]{1,0:T(8,128)S(1)}, u32[]{:S(2)}, u32[]{:S(2)}) collective-permute-start(f32[8,128]{1,0:T(8,128)S(1)} %add.87), channel_id=1, source_target_pairs={{0,1},{1,0},{2,3},{3,2},{4,5},{5,4},{6,7},{7,6},{8,9},{9,8},{10,11... | collective-permute-start | bytes 12296 | tf_op jit(solution)/shard_map/ppermute | solution.py:387
  108.1 13.0 %copy-start.3 = (f32[5,768,256]{2,1,0:T(8,128)S(1)}, f32[5,768,256]{2,1,0:T(8,128)}, u32[]{:S(2)}) copy-start(f32[5,768,256]{2,1,0:T(8,128)} %get-tuple-element.42) | copy-start | bytes 11796484
  109.6 5.1 %collective-permute-start.2 = (f32[8,128]{1,0:T(8,128)S(1)}, f32[8,128]{1,0:T(8,128)S(1)}, u32[]{:S(2)}, u32[]{:S(2)}) collective-permute-start(f32[8,128]{1,0:T(8,128)S(1)} %add.88), channel_id=1, source_target_pairs={{0,2},{1,3},{2,0},{3,1},{4,6},{5,7},{6,4},{7,5},{8,10},{9,11},{10,... | collective-permute-start | bytes 12296 | tf_op jit(solution)/shard_map/ppermute | solution.py:387
  114.7 12.1 %collective-permute-start.3 = (bf16[256,768]{1,0:T(8,128)(2,1)S(1)}, bf16[256,768]{1,0:T(8,128)(2,1)S(1)}, u32[]{:S(2)}, u32[]{:S(2)}) collective-permute-start(bf16[256,768]{1,0:T(8,128)(2,1)S(1)} %get-tuple-element.39), channel_id=1, source_target_pairs={{0,1},{1,0},{2,3},{3,2},{4,5},{5,4},{6,7},{7,6},{8,9},{9,8},{10,11... | collective-permute-start | bytes 1179656 | tf_op jit(solution)/shard_map/ppermute | solution.py:387
  116.2 19.0 %collective-permute-start.4 = (bf16[256,768]{1,0:T(8,128)(2,1)S(1)}, bf16[256,768]{1,0:T(8,128)(2,1)S(1)}, u32[]{:S(2)}, u32[]{:S(2)}) collective-permute-start(bf16[256,768]{1,0:T(8,128)(2,1)S(1)} %get-tuple-element.40), channel_id=1, source_target_pairs={{0,2},{1,3},{2,0},{3,1},{4,6},{5,7},{6,4},{7,5},{8,10},{9,11},{10,... | collective-permute-start | bytes 1179656 | tf_op jit(solution)/shard_map/ppermute | solution.py:387
  118.9 18.8 %collective-permute-start.5 = (bf16[256,768]{1,0:T(8,128)(2,1)S(1)}, bf16[256,768]{1,0:T(8,128)(2,1)S(1)}, u32[]{:S(2)}, u32[]{:S(2)}) collective-permute-start(bf16[256,768]{1,0:T(8,128)(2,1)S(1)} %get-tuple-element.41), channel_id=1, source_target_pairs={{0,3},{1,2},{2,1},{3,0},{4,7},{5,6},{6,5},{7,4},{8,11},{9,10},{10,... | collective-permute-start | bytes 1179656 | tf_op jit(solution)/shard_map/ppermute | solution.py:387
  121.8 25.6 %collective-permute-start.7 = (bf16[488,256]{1,0:T(8,128)(2,1)S(1)}, bf16[488,256]{1,0:T(8,128)(2,1)S(1)}, u32[]{:S(2)}, u32[]{:S(2)}) collective-permute-start(bf16[488,256]{1,0:T(8,128)(2,1)S(1)} %get-tuple-element.48), channel_id=1, source_target_pairs={{0,8},{4,12},{8,0},{12,4},{16,24},{20,28},{24,16},{28,20},{32,40},... | collective-permute-start | bytes 749576 | tf_op jit(solution)/shard_map/ppermute | solution.py:387
  124.2 23.3 %collective-permute-start.8 = (bf16[488,256]{1,0:T(8,128)(2,1)S(1)}, bf16[488,256]{1,0:T(8,128)(2,1)S(1)}, u32[]{:S(2)}, u32[]{:S(2)}) collective-permute-start(bf16[488,256]{1,0:T(8,128)(2,1)S(1)} %get-tuple-element.49), channel_id=1, source_target_pairs={{0,16},{4,20},{8,24},{12,28},{16,0},{20,4},{24,8},{28,12},{32,48},... | collective-permute-start | bytes 749576 | tf_op jit(solution)/shard_map/ppermute | solution.py:387
  126.8 20.7 %collective-permute-start.9 = (bf16[488,256]{1,0:T(8,128)(2,1)S(1)}, bf16[488,256]{1,0:T(8,128)(2,1)S(1)}, u32[]{:S(2)}, u32[]{:S(2)}) collective-permute-start(bf16[488,256]{1,0:T(8,128)(2,1)S(1)} %get-tuple-element.50), channel_id=1, source_target_pairs={{0,24},{4,28},{8,16},{12,20},{16,8},{20,12},{24,0},{28,4},{32,56},... | collective-permute-start | bytes 749576 | tf_op jit(solution)/shard_map/ppermute | solution.py:387
  148.2 4.8 %collective-permute-start.10 = (bf16[128,256]{1,0:T(8,128)(2,1)S(1)}, bf16[128,256]{1,0:T(8,128)(2,1)S(1)}, u32[]{:S(2)}, u32[]{:S(2)}) collective-permute-start(bf16[128,256]{1,0:T(8,128)(2,1)S(1)} %get-tuple-element.53), channel_id=1, source_target_pairs={{0,32},{4,36},{8,40},{12,44},{16,48},{20,52},{24,56},{28,60},{32,0... | collective-permute-start | bytes 196616 | tf_op jit(solution)/shard_map/ppermute | solution.py:387
  149.8 5.9 %collective-permute-start.11 = (bf16[128,256]{1,0:T(8,128)(2,1)S(1)}, bf16[128,256]{1,0:T(8,128)(2,1)S(1)}, u32[]{:S(2)}, u32[]{:S(2)}) collective-permute-start(bf16[128,256]{1,0:T(8,128)(2,1)S(1)} %get-tuple-element.54), channel_id=1, source_target_pairs={{0,64},{4,68},{8,72},{12,76},{16,80},{20,84},{24,88},{28,92},{32,9... | collective-permute-start | bytes 196616 | tf_op jit(solution)/shard_map/ppermute | solution.py:387
  152.5 5.5 %collective-permute-start.12 = (bf16[128,256]{1,0:T(8,128)(2,1)S(1)}, bf16[128,256]{1,0:T(8,128)(2,1)S(1)}, u32[]{:S(2)}, u32[]{:S(2)}) collective-permute-start(bf16[128,256]{1,0:T(8,128)(2,1)S(1)} %get-tuple-element.55), channel_id=1, source_target_pairs={{0,96},{4,100},{8,104},{12,108},{16,112},{20,116},{24,120},{28,124... | collective-permute-start | bytes 196616 | tf_op jit(solution)/shard_map/ppermute | solution.py:387
